TPU v7x, 256 devices: a whole 4x4x8 slice. The times are simulated.
256 devices in a mesh: grp: 8 (over x_lo, y), ep: 32 (over z, x_hi, core).
Axes of the slice: x: 4 (x_hi: 2, x_lo: 2; x = x_hi * 2 + x_lo), y: 4, z: 8, core: 2. Of those that a mesh axis runs over, the one named last changes fastest.
Arguments:
- tokens: bfloat16 [32768, 2048], P(('grp', 'ep')), may hold values from -6 to 6
- routes: int32 [32768, 6], P(('grp', 'ep')), may hold values from 0 to 31, all different within a row; in each aligned block of 128 rows (0 to 127, 128 to 255, ...) at most 32 rows name the same one
- route_gain: float32 [32768, 6], P(('grp', 'ep')), may hold values from 0.05 to 0.6
- gate_weight: bfloat16 [32, 2048, 768], P('ep', 'grp'), may hold values from -0.125 to 0.125
- up_weight: bfloat16 [32, 2048, 768], P('ep', 'grp'), may hold values from -0.125 to 0.125
- down_weight: bfloat16 [32, 768, 2048], P('ep', None, 'grp'), may hold values from -0.21875 to 0.21875
- norm_gain: float32 [2048], replicated, may hold values from 0.25 to 1.75
- query_weight: bfloat16 [2048, 1536], P(None, 'grp'), may hold values from -0.125 to 0.125
Outputs:
- mixed: bfloat16 [32768, 2048], P(('grp', 'ep'))
- query: bfloat16 [32768, 1536], P(('grp', 'ep'))
Inputs may be any that keep to these rules, and one draw needn't show every extreme that they name: `routes`: each row names 6 different experts. Among the 128 rows of one device no expert is named by more than 32 rows, a bound that some of them reach.
All inputs are finite; a program needn't handle non-finite values.
Results may differ from a plain program's by a relative error of at most 0.0053.
Values may be sent and summed in bfloat16 or wider, within the bound.
No kernel may reach another device: no remote copies, remote signals or barrier semaphores. Data moves between devices by JAX's collectives and lax.ppermute only.
A program may use at most 128 MiB of HBM per device.

v0:
```python
import jax
import jax.numpy as jnp
from jax import lax
from jax.sharding import PartitionSpec as P


def shards(
    tokens, routes, route_gain, gate_weight, up_weight, down_weight, norm_gain, query_weight
):
    ep_count = lax.axis_size("ep")
    tok_rows = tokens.shape[0]
    width = tokens.shape[1]
    choose = routes.shape[1]
    capacity = 8 * tok_rows // ep_count
    flat = routes.reshape(-1)
    onehot = (flat[:, None] == jnp.arange(ep_count, dtype=jnp.int32)[None, :]).astype(jnp.int32)
    counted = jnp.cumsum(onehot, axis=0)
    rank = jnp.sum(onehot * (counted - 1), axis=1)
    slot = flat * capacity + rank
    repeated = jnp.repeat(tokens, choose, axis=0)
    outbound = jnp.zeros((ep_count * capacity, width), jnp.bfloat16).at[slot].set(repeated)
    arrived = lax.all_to_all(outbound, "ep", split_axis=0, concat_axis=0, tiled=True)
    gate = jnp.dot(
        arrived,
        lax.all_gather(gate_weight[0], "grp", axis=0, tiled=True),
        preferred_element_type=jnp.float32,
    )
    up = jnp.dot(
        arrived,
        lax.all_gather(up_weight[0], "grp", axis=0, tiled=True),
        preferred_element_type=jnp.float32,
    )
    hidden = (jax.nn.silu(gate) * up).astype(jnp.bfloat16)
    answers = jnp.dot(
        hidden,
        lax.all_gather(down_weight[0], "grp", axis=1, tiled=True),
        preferred_element_type=jnp.float32,
    ).astype(jnp.bfloat16)
    returned = lax.all_to_all(answers, "ep", split_axis=0, concat_axis=0, tiled=True)
    picked = returned[slot].reshape(tok_rows, choose, width).astype(jnp.float32)
    total = tokens.astype(jnp.float32) + jnp.sum(picked * route_gain[:, :, None], axis=1)
    square = jnp.mean(total * total, axis=-1, keepdims=True)
    normed = (total * lax.rsqrt(square + 1e-06) * norm_gain).astype(jnp.bfloat16)
    query = jnp.dot(
        normed,
        lax.all_gather(query_weight, "grp", axis=1, tiled=True),
        preferred_element_type=jnp.float32,
    ).astype(jnp.bfloat16)
    return (total.astype(jnp.bfloat16), query)


def solution(mesh):
    placed = (
        P(("grp", "ep"), None),
        P(("grp", "ep"), None),
        P(("grp", "ep"), None),
        P("ep", "grp", None),
        P("ep", "grp", None),
        P("ep", None, "grp"),
        P(),
        P(None, "grp"),
    )
    return jax.shard_map(
        shards,
        mesh=mesh,
        in_specs=placed,
        out_specs=(P(("grp", "ep"), None), P(("grp", "ep"), None)),
        check_vma=False,
    )
```

profile of v0, /device:TPU:1, one launch (start us, length us, event | category | flops | bytes accessed | tf_op | source)
XLA Modules:
  0.0 352.4 jit_solution(9262614193327806445)
XLA Ops:
  7.2 0.0 all-gather.12.cloned.1.call-start
  7.2 0.7 all-gather.12.cloned.1.call-update
  7.9 0.0 all-gather.10.cloned.1.call-start
  7.9 0.7 all-gather.10.cloned.1.call-update
  8.6 0.8 copy.12
  9.4 0.1 eq.29
  9.6 0.1 eq.25
  9.7 1.7 reduce-window.6
  11.5 0.3 slice_reduce_fusion
  11.8 0.7 broadcast_multiply_fusion
  12.5 0.1 copy.11
  12.6 0.1 mul.55
  12.7 3.6 %broadcast_in_dim.5 = bf16[128,6,2048]{2,1,0:T(8,128)(2,1)} broadcast(bf16[128,2048]{1,0:T(8,128)(2,1)} %param.8), dimensions={0,2} | broadcast | bytes 3670016 | tf_op jit(solution)/shard_map/broadcast_in_dim | solution.py:20
  16.4 4.9 %reshape.87 = bf16[768,2048]{1,0:T(8,128)(2,1)S(1)} reshape(bf16[128,6,2048]{2,1,0:T(8,128)(2,1)} %broadcast_in_dim.5) | data formatting | bytes 6291456 | tf_op jit(solution)/shard_map/reshape | solution.py:20
  21.2 0.1 fusion.15
  21.4 9.4 %scatter_custom_fusion = bf16[1024,2048]{1,0:T(8,128)(2,1)} fusion(s32[768]{0:T(1024)S(1)} %fusion.17, bf16[768,2048]{1,0:T(8,128)(2,1)S(1)} %reshape.87, bf16[]{:T(256)} %constant.9.clone.1), kind=kCustom, calls=%fused_computation.11 | custom fusion | bytes 4194306 | tf_op jit(solution)/shard_map/scatter | solution.py:21
  30.8 12.6 %all-to-all-start = ((bf16[32,32,2048]{2,1,0:T(8,128)(2,1)}), bf16[32,32,2048]{2,1,0:T(8,128)(2,1)}, u32[]{:S(2)}, u32[]{:S(2)}) async-start(bf16[32,32,2048]{2,1,0:T(8,128)(2,1)} %bitcast.36), calls=%async_computation | async-start | bytes 8388608 | tf_op jit(solution)/shard_map/all_to_all | solution.py:22
  43.4 0.0 all-gather.14.cloned.1.call-start
  43.5 0.7 all-gather.14.cloned.1.call-update
  44.2 0.2 all-gather.8.cloned.1.call-start
  44.4 0.3 all-gather.8.cloned.1.call-update
  44.7 34.4 %all-gather.12.cloned.1.call-done = bf16[1,2048,768]{2,1,0:T(8,128)(2,1)} async-done(((bf16[1,256,768]{2,1,0:T(8,128)(2,1)}), bf16[1,2048,768]{2,1,0:T(8,128)(2,1)}) %all-gather.12.cloned.1.call-update) | async-done | bytes 3145744 | tf_op jit(solution)/shard_map/all_gather | solution.py:30
  79.2 58.3 %all-to-all-done = bf16[32,32,2048]{2,1,0:T(8,128)(2,1)} async-done(((bf16[32,32,2048]{2,1,0:T(8,128)(2,1)}), bf16[32,32,2048]{2,1,0:T(8,128)(2,1)}, u32[]{:S(2)}, u32[]{:S(2)}) %all-to-all-start) | async-done | bytes 4194336 | tf_op jit(solution)/shard_map/all_to_all | solution.py:22
  137.5 6.2 %fusion.1 = f32[1024,768]{1,0:T(8,128)S(1)} fusion(bf16[1024,2048]{1,0:T(8,128)(2,1)} %bitcast.2, bf16[1,2048,768]{2,1,0:T(8,128)(2,1)} %all-gather.12.cloned.1.call-done), kind=kOutput, calls=%fused_computation.5 | convolution fusion | flops 3221225472 | bytes 10485760 | tf_op jit(solution)/shard_map/dot_general | solution.py:28
  143.7 2.9 all-gather.10.cloned.1.call-done
  146.6 53.4 %all-gather.14.cloned.1.call-done = bf16[1,768,2048]{2,1,0:T(8,128)(2,1)} async-done(((bf16[1,768,256]{2,1,0:T(8,128)(2,1)}), bf16[1,768,2048]{2,1,0:T(8,128)(2,1)}) %all-gather.14.cloned.1.call-update) | async-done | bytes 3145744 | tf_op jit(solution)/shard_map/all_gather | solution.py:36
  200.0 12.8 %convolution_convert_fusion = bf16[1024,2048]{1,0:T(8,128)(2,1)} fusion(bf16[1,768,2048]{2,1,0:T(8,128)(2,1)} %all-gather.14.cloned.1.call-done, f32[1024,768]{1,0:T(8,128)S(1)} %fusion.1, bf16[1024,2048]{1,0:T(8,128)(2,1)} %bitcast.2, bf16[1,2048,768]{2,1,0:T(8,128)(2,1)} %all-gather.10.cloned.1.call-done), kind=kOutput, calls=%fused_computation.3 | convolution fusion | flops 6449266688 | bytes 17825792 | tf_op jit(solution)/shard_map/dot_general | solution.py:34
  212.8 0.0 copy-start.2
  212.8 12.9 %all-to-all-start.1 = ((bf16[32,32,2048]{2,1,0:T(8,128)(2,1)}), bf16[32,32,2048]{2,1,0:T(8,128)(2,1)}, u32[]{:S(2)}, u32[]{:S(2)}) async-start(bf16[32,32,2048]{2,1,0:T(8,128)(2,1)} %bitcast.37), calls=%async_computation.1 | async-start | bytes 8388608 | tf_op jit(solution)/shard_map/all_to_all | solution.py:39
  225.7 0.0 copy-done.2
  225.7 0.1 copy.15
  225.8 93.9 %all-to-all-done.1 = bf16[32,32,2048]{2,1,0:T(8,128)(2,1)} async-done(((bf16[32,32,2048]{2,1,0:T(8,128)(2,1)}), bf16[32,32,2048]{2,1,0:T(8,128)(2,1)}, u32[]{:S(2)}, u32[]{:S(2)}) %all-to-all-start.1) | async-done | bytes 4194336 | tf_op jit(solution)/shard_map/all_to_all | solution.py:39
  319.7 9.1 %gather_fusion = bf16[768,2048]{1,0:T(8,128)(2,1)S(1)} fusion(bf16[1024,2048]{1,0:T(8,128)(2,1)} %bitcast.7, s32[1024]{0:T(1024)S(1)} %pad_clamp_fusion), kind=kCustom, calls=%fused_computation | custom fusion | bytes 6294528 | tf_op jit(solution)/shard_map/gather | solution.py:40
  328.8 3.7 %reshape.74 = f32[128,6,2048]{2,1,0:T(8,128)} reshape(bf16[768,2048]{1,0:T(8,128)(2,1)S(1)} %gather_fusion) | data formatting | bytes 9437184 | tf_op jit(solution)/shard_map/convert_element_type | solution.py:40
  332.5 0.0 copy-start
  332.5 0.0 copy-start.1
  332.5 6.6 %multiply_reduce_fusion = f32[128,2048]{1,0:T(8,128)S(1)} fusion(f32[128,6,2048]{2,1,0:T(8,128)} %reshape.74, f32[128,6]{1,0:T(8,128)S(1)} %copy.15), kind=kLoop, calls=%fused_computation.2 | loop fusion | flops 2883584 | bytes 7343104 | tf_op jit(solution)/shard_map/reduce_sum | solution.py:41
  339.1 0.0 copy-done
  339.2 0.9 multiply_reduce_fusion.1
  340.1 0.0 all-gather.8.cloned.1.call-done
  340.1 0.0 copy-done.1
  340.1 5.7 %convolution_convert_fusion.1 = bf16[128,1536]{1,0:T(8,128)(2,1)} fusion(bf16[2048,1536]{0,1:T(8,128)(2,1)} %all-gather.8.cloned.1.call-done, f32[2048]{0:T(1024)S(1)} %copy-done.1, f32[128]{0:T(128)S(1)} %add_rsqrt_fusion, f32[128,2048]{1,0:T(8,128)S(1)} %multiply_reduce_fusion, bf16[128,2048]{1,0:T(8,128)(2,1)S(1)} %copy-done), kind=kOutput, calls=%fused_computation.10 | convolution fusion | flops 806813696 | bytes 8266240 | tf_op jit(solution)/shard_map/dot_general | solution.py:44
  (5 shorter events, 0.1 us)
Async XLA Ops:
  7.2 72.0 %all-gather.12.cloned.1.call-start = ((), (), s32[]{:S(2)}) async-start(), calls=%async_computation.4 | async-start | bytes 3538944 | tf_op jit(solution)/shard_map/all_gather | solution.py:30
  7.9 138.7 %all-gather.10.cloned.1.call-start = ((), (), s32[]{:S(2)}) async-start(), calls=%async_computation.3 | async-start | bytes 3538944 | tf_op jit(solution)/shard_map/all_gather | solution.py:25
  30.8 106.7 %all-to-all-start = ((bf16[32,32,2048]{2,1,0:T(8,128)(2,1)}), bf16[32,32,2048]{2,1,0:T(8,128)(2,1)}, u32[]{:S(2)}, u32[]{:S(2)}) async-start(bf16[32,32,2048]{2,1,0:T(8,128)(2,1)} %bitcast.36), calls=%async_computation | async-start | bytes 8388608 | tf_op jit(solution)/shard_map/all_to_all | solution.py:22
  43.4 156.6 %all-gather.14.cloned.1.call-start = ((), (), s32[]{:S(2)}) async-start(), calls=%async_computation.5 | async-start | bytes 3538944 | tf_op jit(solution)/shard_map/all_gather | solution.py:36
  44.2 295.9 %all-gather.8.cloned.1.call-start = ((), (), s32[]{:S(2)}) async-start(), calls=%async_computation.2 | async-start | bytes 7077888 | tf_op jit(solution)/shard_map/all_gather | solution.py:46
  212.8 12.9 %copy-start.2 = (f32[128,6]{0,1:T(8,128)S(1)}, f32[128,6]{0,1:T(8,128)}, u32[]{:S(2)}) copy-start(f32[128,6]{0,1:T(8,128)} %param.10) | copy-start | bytes 9220
  212.8 107.0 %all-to-all-start.1 = ((bf16[32,32,2048]{2,1,0:T(8,128)(2,1)}), bf16[32,32,2048]{2,1,0:T(8,128)(2,1)}, u32[]{:S(2)}, u32[]{:S(2)}) async-start(bf16[32,32,2048]{2,1,0:T(8,128)(2,1)} %bitcast.37), calls=%async_computation.1 | async-start | bytes 8388608 | tf_op jit(solution)/shard_map/all_to_all | solution.py:39
  332.5 6.6 %copy-start = (bf16[128,2048]{1,0:T(8,128)(2,1)S(1)}, bf16[128,2048]{1,0:T(8,128)(2,1)}, u32[]{:S(2)}) copy-start(bf16[128,2048]{1,0:T(8,128)(2,1)} %param.8) | copy-start | bytes 1572868
  332.5 7.6 %copy-start.1 = (f32[2048]{0:T(1024)S(1)}, f32[2048]{0:T(1024)}, u32[]{:S(2)}) copy-start(f32[2048]{0:T(1024)} %param.14) | copy-start | bytes 24580
Sparse Core Ops, SparseCore 0:
  9.8 69.3 all-gather.11
  81.0 65.5 all-gather.9
  148.3 51.6 all-gather.13
  201.6 123.8 all-gather.7
where the time goes:
time: 355 us; the launch traced here: 352 us
  waiting for transfers between devices  245 us (69%)
  local copies, waits for them, and re-layouts  32.4 us (9%)
  starting transfers between devices  25.9 us (7%)
  matrix products  24.7 us (7%)
  between operations  13.9 us (4%)
  other arithmetic  10.1 us (3%)
    all_to_all x1, waiting for transfers between devices, shards(): lax.all_to_all(answers, 'ep', split_axis=0, concat_axis=0, tiled=True)  93.9 us
    all_to_all x1, waiting for transfers between devices, shards(): lax.all_to_all(outbound, 'ep', split_axis=0, concat_axis=0, tiled=True)  58.3 us
    all_gather x1, waiting for transfers between devices, shards(): lax.all_gather(down_weight[0], 'grp', axis=1, tiled=True)  53.4 us
    all_gather x1, waiting for transfers between devices, shards(): lax.all_gather(up_weight[0], 'grp', axis=0, tiled=True)  34.4 us
    all_to_all x1, starting transfers between devices, shards(): lax.all_to_all(answers, 'ep', split_axis=0, concat_axis=0, tiled=True)  12.9 us
    dot_general x1, matrix products, shards(): jnp.dot(hidden, lax.all_gather(down_weight[0], 'grp', axis=1, tiled=True)...  12.8 us
    all_to_all x1, starting transfers between devices, shards(): lax.all_to_all(outbound, 'ep', split_axis=0, concat_axis=0, tiled=True)  12.6 us
    scatter x1, local copies, waits for them, and re-layouts, shards(): jnp.zeros((ep_count * capacity, width), jnp.bfloat16).at[slot].set(repeated)  9.4 us
  transfers between devices with their start and end apart: 6, of which 5 were waited for; matrix products, arithmetic and copies ran while one was open for 17% of the time, Pallas kernels for 0%

commit v1 on v0

v1 whole, which is shorter than its diff:
```python
import functools

import jax
import jax.numpy as jnp
from jax import lax
from jax.experimental import pallas as pl
from jax.experimental.pallas import tpu as pltpu
from jax.sharding import Mesh, PartitionSpec as P

BF = jnp.bfloat16
F32 = jnp.float32
SLOTS = 32
ANY = pl.BlockSpec(memory_space=pl.ANY)
SMEM = pl.BlockSpec(memory_space=pltpu.SMEM)
VMEM = pl.BlockSpec(memory_space=pltpu.VMEM)
FIRST = (2, 6, 1, 7, 0)
SECOND = (4, 3, 5)


def params(mib):
    return pltpu.CompilerParams(vmem_limit_bytes=mib << 20)


def cost(flops, size):
    return pl.CostEstimate(flops=flops, bytes_accessed=size, transcendentals=0)


def shift(x, axis, by):
    n = lax.axis_size(axis)
    return lax.ppermute(x, axis, [(i, (i + by) % n) for i in range(n)])


def swap(x, axes, k):
    n = lax.axis_size(axes)
    return lax.ppermute(x, axes, [(i, i ^ k) for i in range(n)])


def table_kernel(place, table, code, gain, match):
    z, me = place[0], place[1]
    for s in range(8):
        block = table[lax.rem(z - s + 8, 8)]
        for k in range(4):
            expert = (4 * z + lax.bitwise_xor(me, k)).astype(F32)
            hit = block[0:6] == expert
            row = slice(4 * s + k, 4 * s + k + 1)
            match[row] = jnp.sum(jnp.where(hit, 1.0, 0.0), axis=0, keepdims=True)
            gain[row] = jnp.sum(jnp.where(hit, block[6:12], 0.0), axis=0, keepdims=True)
    chosen = match[...]
    before = lax.broadcasted_iota(jnp.int32, (128, 128), 0) < lax.broadcasted_iota(jnp.int32, (128, 128), 1)
    rank = jnp.dot(chosen.astype(BF), jnp.where(before, 1.0, 0.0).astype(BF), preferred_element_type=F32)
    code[...] = jnp.where(chosen > 0.5, rank, -1.0)


def make_table(place, table):
    return pl.pallas_call(
        table_kernel,
        out_shape=(jax.ShapeDtypeStruct((32, 128), F32),) * 2,
        in_specs=[SMEM, VMEM],
        out_specs=(VMEM, VMEM),
        scratch_shapes=[pltpu.VMEM((32, 128), F32)],
        cost_estimate=cost(1 << 20, 1 << 17),
    )(place, table)


def chosen_rows(code, s):
    slot = lax.broadcasted_iota(jnp.int32, (SLOTS, 128), 0).astype(F32)
    return [code[4 * s + k : 4 * s + k + 1, :] == slot for k in range(4)]


def select_kernel(blocks, *refs):
    code, refs = refs[0], list(refs[1:])
    outs = refs[-5:-1]
    joined = refs[-1]
    at = 0
    for b, s in enumerate(blocks):
        if s == 4:
            joined[0:64] = refs[at][...]
            joined[64:128] = refs[at + 1][...]
            source, at = joined[...], at + 2
        else:
            source, at = refs[at][...], at + 1
        onehot = jnp.concatenate([jnp.where(hit, 1.0, 0.0).astype(BF) for hit in chosen_rows(code, s)], axis=0)
        rows = jnp.dot(onehot, source, preferred_element_type=F32).astype(BF)
        for k in range(4):
            outs[k][b * SLOTS : (b + 1) * SLOTS] = rows[k * SLOTS : (k + 1) * SLOTS]


def select(blocks, code, sources):
    width, step = sources[0].shape[1], 512
    rows = len(blocks) * SLOTS
    return pl.pallas_call(
        functools.partial(select_kernel, blocks),
        out_shape=(jax.ShapeDtypeStruct((rows, width), BF),) * 4,
        grid=(width // step,),
        in_specs=[pl.BlockSpec((32, 128), lambda j: (0, 0))]
        + [pl.BlockSpec((x.shape[0], step), lambda j: (0, j)) for x in sources],
        out_specs=(pl.BlockSpec((rows, step), lambda j: (0, j)),) * 4,
        scratch_shapes=[pltpu.VMEM((128, step), BF)],
        compiler_params=params(32),
        cost_estimate=cost(len(blocks) << 26, len(blocks) << 20),
    )(code, *sources)


def hidden_kernel(n_rows, offsets, *refs):
    pieces, weights, out = refs[:4], refs[4:14], refs[14]
    x, gate, up, sems = refs[15:]
    half = 256
    copies = []

    def copy(src, dst):
        c = pltpu.make_async_copy(src, dst, sems.at[len(copies)])
        c.start()
        copies.append(c)

    for ring in range(2):
        whole = weights[5 * ring : 5 * ring + 3]
        for i in range(3):
            off = pl.multiple_of(offsets[4 * ring + i], half)
            copy(whole[i].at[0:half], gate.at[pl.ds(off, half)])
            copy(whole[i].at[half : 2 * half], up.at[pl.ds(off, half)])
        off = pl.multiple_of(offsets[4 * ring + 3], half)
        copy(weights[5 * ring + 3], gate.at[pl.ds(off, half)])
        copy(weights[5 * ring + 4], up.at[pl.ds(off, half)])
    for k in range(4):
        copy(pieces[k], x.at[k * n_rows : (k + 1) * n_rows])
    for c in copies:
        c.wait()

    @pl.loop(0, gate.shape[1] // 256)
    def _(j):
        cols = pl.ds(pl.multiple_of(j * 256, 256), 256)
        g = jnp.dot(x[...], gate[:, cols], preferred_element_type=F32)
        u = jnp.dot(x[...], up[:, cols], preferred_element_type=F32)
        out[:, cols] = (g / (1.0 + jnp.exp(-g)) * u).astype(BF)


def hidden_of(offsets, pieces, weights):
    n_rows, width = pieces[0].shape
    units = weights[0].shape[1]
    return pl.pallas_call(
        functools.partial(hidden_kernel, n_rows),
        out_shape=jax.ShapeDtypeStruct((4 * n_rows, units), BF),
        in_specs=[SMEM] + [ANY] * (len(pieces) + len(weights)),
        out_specs=VMEM,
        scratch_shapes=[
            pltpu.VMEM((4 * n_rows, width), BF),
            pltpu.VMEM((width, units), BF),
            pltpu.VMEM((width, units), BF),
            pltpu.SemaphoreType.DMA((20,)),
        ],
        compiler_params=params(40),
        cost_estimate=cost(16 * n_rows * width * units, 8 << 20),
    )(offsets, *pieces, *weights)


def answer_kernel(sizes, offsets, *refs):
    hidden, weights = refs[0], refs[1:11]
    outs, (down, sems) = refs[11:-2], refs[-2:]
    copies = []

    def copy(src, dst):
        c = pltpu.make_async_copy(src, dst, sems.at[len(copies)])
        c.start()
        copies.append(c)

    half = down.shape[0] // 2
    for ring in range(2):
        for i in range(3):
            cols = pl.ds(pl.multiple_of(offsets[4 * ring + i], 256), 256)
            copy(weights[5 * ring + i], down.at[:, cols])
        cols = pl.ds(pl.multiple_of(offsets[4 * ring + 3], 256), 256)
        copy(weights[5 * ring + 3], down.at[0:half, cols])
        copy(weights[5 * ring + 4], down.at[half : 2 * half, cols])
    for c in copies:
        c.wait()
    total = sum(sizes)

    @pl.loop(0, down.shape[1] // 256)
    def _(j):
        cols = pl.ds(pl.multiple_of(j * 256, 256), 256)
        answer = jnp.dot(hidden[...], down[:, cols], preferred_element_type=F32).astype(BF)
        for k in range(4):
            at = k * total
            for i, size in enumerate(sizes):
                outs[4 * i + k][:, cols] = answer[at : at + size]
                at += size


def answers_of(sizes, offsets, hidden, weights):
    width = 8 * weights[0].shape[1]
    units = hidden.shape[1]
    shapes = [jax.ShapeDtypeStruct((size, width), BF) for size in sizes for _ in range(4)]
    out = pl.pallas_call(
        functools.partial(answer_kernel, sizes),
        out_shape=tuple(shapes),
        in_specs=[SMEM, VMEM] + [ANY] * len(weights),
        out_specs=(VMEM,) * len(shapes),
        scratch_shapes=[pltpu.VMEM((units, width), BF), pltpu.SemaphoreType.DMA((10,))],
        compiler_params=params(40),
        cost_estimate=cost(2 * hidden.shape[0] * width * units, 8 << 20),
    )(offsets, hidden, *weights)
    return [out[4 * i : 4 * i + 4] for i in range(len(sizes))]


def combined(code, gain, s, answers):
    weight = jnp.concatenate(
        [jnp.where(hit, gain[4 * s + k : 4 * s + k + 1, :], 0.0) for k, hit in enumerate(chosen_rows(code, s))], axis=0
    )
    high = weight.astype(BF)
    low = (weight - high.astype(F32)).astype(BF)
    rows = jnp.concatenate(answers, axis=0)
    dims = (((0,), (0,)), ((), ()))
    return lax.dot_general(high, rows, dims, preferred_element_type=F32) + lax.dot_general(
        low, rows, dims, preferred_element_type=F32
    )


def combine_kernel(blocks, start, n_in, code, gain, *refs):
    answers, arrived, outs = refs[:4], refs[4 : 4 + n_in], refs[4 + n_in :]
    for i, s in enumerate(blocks):
        rows = slice(start + i * SLOTS, start + (i + 1) * SLOTS)
        total = combined(code, gain, s, [a[rows] for a in answers])
        if s == 4:
            outs[0][...] = total[0:64].astype(BF)
            outs[1][...] = total[64:128].astype(BF)
        elif s == 3:
            outs[i][0:64] = (total[0:64] + arrived[i][...].astype(F32)).astype(BF)
            outs[i][64:128] = total[64:128].astype(BF)
        elif s == 5:
            outs[i][0:64] = total[0:64].astype(BF)
            outs[i][64:128] = (total[64:128] + arrived[i][...].astype(F32)).astype(BF)
        else:
            outs[i][...] = (total + arrived[i][...].astype(F32)).astype(BF)


def combine(blocks, start, code, gain, answers, arrived):
    width, step = answers[0].shape[1], 512
    height = 64 if blocks == (4,) else 128
    whole = pl.BlockSpec((32, 128), lambda j: (0, 0))
    return pl.pallas_call(
        functools.partial(combine_kernel, blocks, start, len(arrived)),
        out_shape=(jax.ShapeDtypeStruct((height, width), BF),) * 2,
        grid=(width // step,),
        in_specs=[whole, whole]
        + [pl.BlockSpec((x.shape[0], step), lambda j: (0, j)) for x in (*answers, *arrived)],
        out_specs=(pl.BlockSpec((height, step), lambda j: (0, j)),) * 2,
        compiler_params=params(32),
        cost_estimate=cost(len(blocks) << 27, 2 << 20),
    )(code, gain, *answers, *arrived)


def final_kernel(start, offsets, code, gain, a0, a1, a2, a3, tokens, left, right, norm, q0, q1, mixed, query, total, normed, held, sems):
    copies = [pltpu.make_async_copy(q, held.at[i], sems.at[i]) for i, q in enumerate((q0, q1))]
    for c in copies:
        c.start()
    width, step = tokens.shape[1], 512
    square = jnp.zeros((128, 1), F32)
    for j in range(width // step):
        cols = slice(j * step, (j + 1) * step)
        part = combined(code, gain, 0, [a[start : start + SLOTS, cols] for a in (a0, a1, a2, a3)])
        part = part + tokens[:, cols].astype(F32)
        part = part + left[:, cols].astype(F32) + right[:, cols].astype(F32)
        mixed[:, cols] = part.astype(BF)
        total[:, cols] = part
        square = square + jnp.sum(part * part, axis=1, keepdims=True)
    scale = lax.rsqrt(square / width + 1e-06)
    for j in range(width // step):
        cols = slice(j * step, (j + 1) * step)
        normed[:, cols] = (total[:, cols] * scale * norm[:, cols]).astype(BF)
    for c in copies:
        c.wait()
    half = width // 2
    sides = [normed[:, pl.ds(pl.multiple_of(offsets[i], half), half)] for i in range(2)]
    dims = (((1,), (1,)), ((), ()))
    tile = 256
    for j in range(query.shape[1] // tile):
        cols = slice(j * tile, (j + 1) * tile)
        out = lax.dot_general(sides[0], held[0, cols], dims, preferred_element_type=F32)
        out = out + lax.dot_general(sides[1], held[1, cols], dims, preferred_element_type=F32)
        query[:, cols] = out.astype(BF)


def final(start, offsets, code, gain, answers, tokens, left, right, norm, q0, q1):
    rows, width = tokens.shape
    features = q0.shape[0]
    return pl.pallas_call(
        functools.partial(final_kernel, start),
        out_shape=(jax.ShapeDtypeStruct((rows, width), BF), jax.ShapeDtypeStruct((rows, features), BF)),
        in_specs=[SMEM] + [VMEM] * 10 + [ANY] * 2,
        out_specs=(VMEM, VMEM),
        scratch_shapes=[
            pltpu.VMEM((rows, width), F32),
            pltpu.VMEM((rows, width), BF),
            pltpu.VMEM((2, features, width // 2), BF),
            pltpu.SemaphoreType.DMA((2,)),
        ],
        compiler_params=params(40),
        cost_estimate=cost(2 * rows * width * features, 8 << 20),
    )(offsets, code, gain, *answers, tokens, left, right, norm, q0, q1)


def ring_of_four(x, half):
    up, down = shift(x, "y", 1), shift(x, "y", -1)
    return [x, up, down, shift(up[:half], "y", 1), shift(down[half:], "y", -1)]


def shards(tokens, routes, route_gain, gate_weight, up_weight, down_weight, norm_gain, query_weight):
    xl, y, z, c = (lax.axis_index(a) for a in ("xl", "y", "z", "c"))
    me = 2 * lax.axis_index("xh") + c
    plane = ("xh", "c")
    around = [xl * 4 + lax.rem(y + d, 4) for d in (0, 3, 1, 2)]
    across = [(1 - xl) * 4 + lax.rem(y + d, 4) for d in (0, 3, 1, 2)]
    offsets = (256 * jnp.stack(around + across)).astype(jnp.int32)
    place = jnp.stack([z, me]).astype(jnp.int32)

    table = lax.all_gather(jnp.concatenate([routes.T.astype(F32), route_gain.T], axis=0), "z")
    code, gain = make_table(place, table)

    up1, down1 = shift(tokens, "z", 1), shift(tokens, "z", -1)
    gate_up = jnp.concatenate([gate_weight[0], up_weight[0]], axis=0)
    other = swap(gate_up, "xl", 1)
    wide = ring_of_four(gate_up, 256) + ring_of_four(other, 256)
    up2, down2 = shift(up1, "z", 1), shift(down1, "z", -1)
    tall = down_weight[0]
    narrow = ring_of_four(tall, 384) + ring_of_four(swap(tall, "xl", 1), 384)

    sent = select(FIRST, code, [up2, down2, up1, down1, tokens])
    rows_a = [sent[0]] + [swap(sent[k], plane, k) for k in (1, 2, 3)]
    up3, down3 = shift(up2, "z", 1), shift(down2, "z", -1)
    up4, down4 = shift(up3[:64], "z", 1), shift(down3[64:], "z", -1)
    sent = select(SECOND, code, [up4, down4, up3, down3])
    rows_b = [sent[0]] + [swap(sent[k], plane, k) for k in (1, 2, 3)]

    hidden_a = hidden_of(offsets, rows_a, wide)
    hidden_b = hidden_of(offsets, rows_b, wide)
    ans4, ans3 = answers_of((32, 64), offsets, hidden_b, narrow)
    ans2, ans1 = answers_of((64, 96), offsets, hidden_a, narrow)

    half = query_weight.shape[0] // 2
    share = lax.dynamic_slice(query_weight.T, (0, c * half), (query_weight.shape[1], half))
    share, _ = lax.optimization_barrier((share, wide[8]))
    q_own = lax.all_gather(share, ("xl", "y"), axis=0, tiled=True)
    q_other = swap(q_own, "c", 1)
    sides = (half * jnp.stack([c, 1 - c])).astype(jnp.int32)

    def back(pieces):
        return [pieces[0]] + [swap(pieces[k], plane, k) for k in (1, 2, 3)]

    ans4, ans3, ans2, ans1 = back(ans4), back(ans3), back(ans2), back(ans1)
    low, high = combine((4,), 0, code, gain, ans4, [])
    low, high = shift(low, "z", -1), shift(high, "z", 1)
    low, high = combine((3, 5), 0, code, gain, ans3, [low, high])
    low, high = shift(low, "z", -1), shift(high, "z", 1)
    low, high = combine((2, 6), 0, code, gain, ans2, [low, high])
    low, high = shift(low, "z", -1), shift(high, "z", 1)
    low, high = combine((1, 7), 0, code, gain, ans1, [low, high])
    low, high = shift(low, "z", -1), shift(high, "z", 1)
    return final(64, sides, code, gain, ans1, tokens, low, high, norm_gain[None, :], q_own, q_other)


def solution(mesh):
    fine = Mesh(mesh.devices.reshape(2, 4, 8, 2, 2), ("xl", "y", "z", "xh", "c"))
    grp, ep = ("xl", "y"), ("z", "xh", "c")
    placed = (
        P(grp + ep, None),
        P(grp + ep, None),
        P(grp + ep, None),
        P(ep, grp, None),
        P(ep, grp, None),
        P(ep, None, grp),
        P(),
        P(None, grp),
    )
    return jax.shard_map(
        shards,
        mesh=fine,
        in_specs=placed,
        out_specs=(P(grp + ep, None), P(grp + ep, None)),
        check_vma=False,
    )
```

time: 355 us -> 388 us (1.093)
  waiting for transfers between devices: 245 us -> 173 us
  starting transfers between devices: 25.9 us -> 89.2 us
  Pallas kernels: 0 us -> 46 us
  matrix products: 24.7 us -> 0 us
  blocking collectives: 0 us -> 22.4 us
  other arithmetic: 10.1 us -> 2.46 us
    ppermute x0 -> x53, waiting for transfers between devices: none -> 173 us  [the longest x32 96.6 us: shift(): return lax.ppermute(x, axis, [(i, (i + by) % n) for i in range(n)])]
    all_to_all x2 -> x0, waiting for transfers between devices: 152 us -> none  [the longest x1 93.9 us: shards(): lax.all_to_all(answers, 'ep', split_axis=0, concat_axis=0, tiled=True)]
    all_gather x4 -> x1, waiting for transfers between devices: 90.8 us -> 0.01 us  [shards(): q_own = lax.all_gather(share, ('xl', 'y'), axis=0, tiled=True)]
    ppermute x0 -> x53, starting transfers between devices: none -> 89.1 us  [the longest x21 49.7 us: swap(): return lax.ppermute(x, axes, [(i, i ^ k) for i in range(n)])]
    pallas_call x0 -> x12, Pallas kernels: none -> 46 us  [the longest x2 15.2 us: hidden_of(): pl.pallas_call(functools.partial(hidden_kernel, n_rows), out_shape=jax.Sh...]
    all_to_all x2 -> x0, starting transfers between devices: 25.6 us -> none  [the longest x1 12.9 us: shards(): lax.all_to_all(answers, 'ep', split_axis=0, concat_axis=0, tiled=True)]
    dot_general x3 -> x0, matrix products: 24.7 us -> none  [the longest x1 12.8 us: shards(): jnp.dot(hidden, lax.all_gather(down_weight[0], 'grp', axis=1, tiled=True)...]
    all_gather x0 -> x1, blocking collectives: none -> 22.4 us  [shards(): lax.all_gather(jnp.concatenate([routes.T.astype(F32), route_gain.T], axis...]
  transfers between devices with their start and end apart: 6 -> 54, of which waited for: 5 -> 17; matrix products, arithmetic and copies ran while one was open for 17% -> 4% of each run, Pallas kernels for 0% -> 10%
where the time goes in v1:
time: 388 us; the launch traced here: 383 us
  waiting for transfers between devices  173 us (45%)
  starting transfers between devices  89.2 us (23%)
  Pallas kernels  46 us (12%)
  local copies, waits for them, and re-layouts  35.1 us (9%)
  blocking collectives  22.4 us (6%)
  between operations  14.7 us (4%)
    ppermute x32, waiting for transfers between devices, shift(): return lax.ppermute(x, axis, [(i, (i + by) % n) for i in range(n)])  96.6 us
    ppermute x21, waiting for transfers between devices, swap(): return lax.ppermute(x, axes, [(i, i ^ k) for i in range(n)])  76.4 us
    ppermute x21, starting transfers between devices, swap(): return lax.ppermute(x, axes, [(i, i ^ k) for i in range(n)])  49.7 us
    ppermute x32, starting transfers between devices, shift(): return lax.ppermute(x, axis, [(i, (i + by) % n) for i in range(n)])  39.5 us
    all_gather x1, blocking collectives, shards(): lax.all_gather(jnp.concatenate([routes.T.astype(F32), route_gain.T], axis...  22.4 us
    unnamed x102, local copies, waits for them, and re-layouts  20 us
    pallas_call x2, Pallas kernels, hidden_of(): pl.pallas_call(functools.partial(hidden_kernel, n_rows), out_shape=jax.Sh...  15.2 us
    slice x8, local copies, waits for them, and re-layouts, ring_of_four(): return [x, up, down, shift(up[:half], 'y', 1), shift(down[half:], 'y', -1)]  12.8 us
  transfers between devices with their start and end apart: 54, of which 17 were waited for; matrix products, arithmetic and copies ran while one was open for 4% of the time, Pallas kernels for 10%

profile of v1, /device:TPU:1, one launch (start us, length us, event | category | flops | bytes accessed | tf_op | source)
XLA Modules:
  0.0 382.9 jit_solution(7073087012932013143)
XLA Ops:
  8.5 2.1 collective-permute-start.11
  10.6 15.9 %collective-permute-done.11.refs_9_ = bf16[512,768]{1,0:T(8,128)(2,1)S(1)} collective-permute-done((bf16[512,768]{1,0:T(8,128)(2,1)S(1)}, bf16[512,768]{1,0:T(8,128)(2,1)S(1)}, u32[]{:S(2)}, u32[]{:S(2)}) %collective-permute-start.11) | collective-permute-done | bytes 786464 | tf_op jit(solution)/shard_map/ppermute | solution.py:35
  27.5 2.6 collective-permute-start.12
  30.1 17.7 %collective-permute-done.12.refs_10_ = bf16[512,768]{1,0:T(8,128)(2,1)S(1)} collective-permute-done((bf16[512,768]{1,0:T(8,128)(2,1)S(1)}, bf16[512,768]{1,0:T(8,128)(2,1)S(1)}, u32[]{:S(2)}, u32[]{:S(2)}) %collective-permute-start.12) | collective-permute-done | bytes 786464 | tf_op jit(solution)/shard_map/ppermute | solution.py:30
  49.5 9.0 %collective-permute-done.14.refs_12_ = bf16[256,768]{1,0:T(8,128)(2,1)S(1)} collective-permute-done((bf16[256,768]{1,0:T(8,128)(2,1)}, bf16[256,768]{1,0:T(8,128)(2,1)S(1)}, u32[]{:S(2)}, u32[]{:S(2)}) %collective-permute-start.14) | collective-permute-done | bytes 393248 | tf_op jit(solution)/shard_map/ppermute | solution.py:30
  59.8 4.0 %collective-permute-start.2 = (bf16[128,2048]{1,0:T(8,128)(2,1)S(1)}, bf16[128,2048]{1,0:T(8,128)(2,1)S(1)}, u32[]{:S(2)}, u32[]{:S(2)}) collective-permute-start(bf16[128,2048]{1,0:T(8,128)(2,1)S(1)} %copy-done.2), channel_id=1, source_target_pairs={{0,28},{4,0},{8,4},{12,8},{16,12},{20,16},{24,20},{28,24},{1,29},{... | collective-permute-start | bytes 1572872 | tf_op jit(solution)/shard_map/ppermute | solution.py:30
  63.8 8.8 %collective-permute-done.refs_3_ = bf16[128,2048]{1,0:T(8,128)(2,1)S(1)} collective-permute-done((bf16[128,2048]{1,0:T(8,128)(2,1)S(1)}, bf16[128,2048]{1,0:T(8,128)(2,1)S(1)}, u32[]{:S(2)}, u32[]{:S(2)}) %collective-permute-start) | collective-permute-done | bytes 524320 | tf_op jit(solution)/shard_map/ppermute | solution.py:30
  73.5 2.7 collective-permute-start.3
  77.0 6.4 %collective-permute-done.1.refs_1_ = bf16[128,2048]{1,0:T(8,128)(2,1)S(1)} collective-permute-done((bf16[128,2048]{1,0:T(8,128)(2,1)S(1)}, bf16[128,2048]{1,0:T(8,128)(2,1)S(1)}, u32[]{:S(2)}, u32[]{:S(2)}) %collective-permute-start.1) | collective-permute-done | bytes 524320 | tf_op jit(solution)/shard_map/ppermute | solution.py:30
  84.2 2.7 collective-permute-start.13
  86.9 2.7 collective-permute-start.33
  89.7 4.2 %collective-permute-done.31.refs_3_ = bf16[128,2048]{1,0:T(8,128)(2,1)S(1)} collective-permute-done((bf16[128,2048]{1,0:T(8,128)(2,1)S(1)}, bf16[128,2048]{1,0:T(8,128)(2,1)S(1)}, u32[]{:S(2)}, u32[]{:S(2)}) %collective-permute-start.31) | collective-permute-done | bytes 524320 | tf_op jit(solution)/shard_map/ppermute | solution.py:30
  96.5 18.3 %collective-permute-done.8.refs_6_ = bf16[512,768]{1,0:T(8,128)(2,1)S(1)} collective-permute-done((bf16[512,768]{1,0:T(8,128)(2,1)S(1)}, bf16[512,768]{1,0:T(8,128)(2,1)S(1)}, u32[]{:S(2)}, u32[]{:S(2)}) %collective-permute-start.8) | collective-permute-done | bytes 786464 | tf_op jit(solution)/shard_map/ppermute | solution.py:30
  118.7 3.8 %collective-permute-done.7.refs_5_ = bf16[512,768]{1,0:T(8,128)(2,1)} collective-permute-done((bf16[512,768]{1,0:T(8,128)(2,1)S(1)}, bf16[512,768]{1,0:T(8,128)(2,1)}, u32[]{:S(2)}, u32[]{:S(2)}) %collective-permute-start.7) | collective-permute-done | bytes 786464 | tf_op jit(solution)/shard_map/ppermute | solution.py:30
  122.5 13.6 %collective-permute-done.13.refs_11_ = bf16[512,768]{1,0:T(8,128)(2,1)} collective-permute-done((bf16[512,768]{1,0:T(8,128)(2,1)}, bf16[512,768]{1,0:T(8,128)(2,1)}, u32[]{:S(2)}, u32[]{:S(2)}) %collective-permute-start.13) | collective-permute-done | bytes 786464 | tf_op jit(solution)/shard_map/ppermute | solution.py:30
  140.5 22.4 %all-gather.1.table = f32[8,12,128]{2,1,0:T(8,128)} all-gather(f32[1,12,128]{2,1,0:T(8,128)S(1)} %maximum_bitcast_fusion), channel_id=2, replica_groups=mesh['xl'=2,'y'=4,'z'=8,'xh'=2,'c'=2] {'z'}, dimensions={0}, use_global_device_ids=true | all-gather | bytes 55296 | tf_op jit(solution)/shard_map/all_gather | solution.py:316
  169.7 3.8 shard_map.99
  174.2 2.7 collective-permute-start.15
  176.9 10.0 %collective-permute-start.35 = (bf16[96,2048]{1,0:T(8,128)(2,1)}, bf16[96,2048]{1,0:T(8,128)(2,1)}, u32[]{:S(2)}, u32[]{:S(2)}) collective-permute-start(bf16[96,2048]{1,0:T(8,128)(2,1)} %get-tuple-element.52), channel_id=1, source_target_pairs={{0,1},{1,0},{2,3},{3,2},{4,5},{5,4},{6,7},{7,6},{8,9},{9,8},{10,11... | collective-permute-start | bytes 1179656 | tf_op jit(solution)/shard_map/ppermute | solution.py:35
  186.9 2.7 collective-permute-start.36
  204.5 2.7 collective-permute-start.19
  207.1 2.7 collective-permute-start.24
  216.1 7.0 %shard_map.100.refs_0_ = bf16[384,768]{1,0:T(8,128)(2,1)S(1)} custom-call(s32[8]{0:T(128)S(1)} %copy-done.47, bf16[96,2048]{1,0:T(8,128)(2,1)S(1)} %copy-done.39, bf16[96,2048]{1,0:T(8,128)(2,1)} %collective-permute-done.35.refs_1_, bf16[96,2048]{1,0:T(8,128)(2,1)} %collective-permute-done.36.refs_2_, bf16[96,2048]{1,0:T(8,128)(2,1)} %collective-permute-done.37.refs_3_, ...), custom_call_target="tpu_custom_call" | custom-call | flops 2415919104 | bytes 8388608 | tf_op jit(solution)/shard_map/pallas_call | solution.py:140
  223.2 8.9 %collective-permute-start.4 = (bf16[160,2048]{1,0:T(8,128)(2,1)S(1)}, bf16[160,2048]{1,0:T(8,128)(2,1)S(1)}, u32[]{:S(2)}, u32[]{:S(2)}) collective-permute-start(bf16[160,2048]{1,0:T(8,128)(2,1)S(1)} %copy-done.34), channel_id=1, source_target_pairs={{0,1},{1,0},{2,3},{3,2},{4,5},{5,4},{6,7},{7,6},{8,9},{9,8},{10,11... | collective-permute-start | bytes 1966088 | tf_op jit(solution)/shard_map/ppermute | solution.py:35
  233.8 4.9 %shard_map.101 = (bf16[32,2048]{1,0:T(8,128)(2,1)S(1)}, bf16[32,2048]{1,0:T(8,128)(2,1)S(1)}, bf16[32,2048]{1,0:T(8,128)(2,1)S(1)}, bf16[32,2048]{1,0:T(8,128)(2...) custom-call(s32[8]{0:T(128)S(1)} %copy-done.48, ...), custom_call_target="tpu_custom_call" | custom-call | flops 1207959552 | bytes 8388608 | tf_op jit(solution)/shard_map/pallas_call | solution.py:193
  239.3 2.7 collective-permute-start.5
  242.6 2.7 collective-permute-start.42
  245.2 28.7 %collective-permute-done.42.refs_2_ = bf16[32,2048]{1,0:T(8,128)(2,1)S(1)} collective-permute-done((bf16[32,2048]{1,0:T(8,128)(2,1)S(1)}, bf16[32,2048]{1,0:T(8,128)(2,1)S(1)}, u32[]{:S(2)}, u32[]{:S(2)}) %collective-permute-start.42) | collective-permute-done | bytes 131104 | tf_op jit(solution)/shard_map/ppermute | solution.py:35
  274.0 3.4 collective-permute-start.43
  277.4 4.3 %collective-permute-done.43.refs_3_ = bf16[32,2048]{1,0:T(8,128)(2,1)S(1)} collective-permute-done((bf16[32,2048]{1,0:T(8,128)(2,1)S(1)}, bf16[32,2048]{1,0:T(8,128)(2,1)S(1)}, u32[]{:S(2)}, u32[]{:S(2)}) %collective-permute-start.43) | collective-permute-done | bytes 131104 | tf_op jit(solution)/shard_map/ppermute | solution.py:35
  283.3 2.6 collective-permute-start.39
  288.3 8.2 %shard_map.97.refs_0_ = bf16[640,768]{1,0:T(8,128)(2,1)S(1)} custom-call(s32[8]{0:T(128)S(1)} %copy-done.48, bf16[160,2048]{1,0:T(8,128)(2,1)S(1)} %copy-done.28, bf16[160,2048]{1,0:T(8,128)(2,1)S(1)} %collective-permute-done.4.refs_1_, bf16[160,2048]{1,0:T(8,128)(2,1)S(1)} %collective-permute-done.5.refs_2_, ...), custom_call_target="tpu_custom_call" | custom-call | flops 4026531840 | bytes 8388608 | tf_op jit(solution)/shard_map/pallas_call | solution.py:140
  296.6 5.7 %shard_map.98 = (bf16[64,2048]{1,0:T(8,128)(2,1)S(1)}, bf16[64,2048]{1,0:T(8,128)(2,1)S(1)}, bf16[64,2048]{1,0:T(8,128)(2,1)S(1)}, bf16[64,2048]{1,0:T(8,128)(2,...) custom-call(s32[8]{0:T(128)S(1)} %copy-done.48, ...), custom_call_target="tpu_custom_call" | custom-call | flops 2013265920 | bytes 8388608 | tf_op jit(solution)/shard_map/pallas_call | solution.py:193
  304.5 2.9 collective-permute-start.46
  307.5 2.5 collective-permute-start.29
  310.9 5.6 %collective-permute-done.29.refs_2_ = bf16[64,2048]{1,0:T(8,128)(2,1)S(1)} collective-permute-done((bf16[64,2048]{1,0:T(8,128)(2,1)S(1)}, bf16[64,2048]{1,0:T(8,128)(2,1)S(1)}, u32[]{:S(2)}, u32[]{:S(2)}) %collective-permute-start.29) | collective-permute-done | bytes 262176 | tf_op jit(solution)/shard_map/ppermute | solution.py:35
  316.6 2.1 collective-permute-start.25
  318.6 4.0 %collective-permute-done.30.refs_3_ = bf16[64,2048]{1,0:T(8,128)(2,1)S(1)} collective-permute-done((bf16[64,2048]{1,0:T(8,128)(2,1)S(1)}, bf16[64,2048]{1,0:T(8,128)(2,1)S(1)}, u32[]{:S(2)}, u32[]{:S(2)}) %collective-permute-start.30) | collective-permute-done | bytes 262176 | tf_op jit(solution)/shard_map/ppermute | solution.py:35
  324.3 2.8 collective-permute-start.48
  327.0 2.5 collective-permute-start.26
  330.1 9.3 %collective-permute-done.26.refs_2_.a2 = bf16[96,2048]{1,0:T(8,128)(2,1)S(1)} collective-permute-done((bf16[96,2048]{1,0:T(8,128)(2,1)S(1)}, bf16[96,2048]{1,0:T(8,128)(2,1)S(1)}, u32[]{:S(2)}, u32[]{:S(2)}) %collective-permute-start.26) | collective-permute-done | bytes 393248 | tf_op jit(solution)/shard_map/ppermute | solution.py:35
  339.4 8.4 %collective-permute-done.27.refs_3_.a3 = bf16[96,2048]{1,0:T(8,128)(2,1)S(1)} collective-permute-done((bf16[96,2048]{1,0:T(8,128)(2,1)S(1)}, bf16[96,2048]{1,0:T(8,128)(2,1)S(1)}, u32[]{:S(2)}, u32[]{:S(2)}) %collective-permute-start.27) | collective-permute-done | bytes 393248 | tf_op jit(solution)/shard_map/ppermute | solution.py:35
  347.8 2.6 shard_map.105
  350.4 2.7 collective-permute-start.50
  353.1 11.5 %collective-permute-done.50.left = bf16[128,2048]{1,0:T(8,128)(2,1)S(1)} collective-permute-done((bf16[128,2048]{1,0:T(8,128)(2,1)}, bf16[128,2048]{1,0:T(8,128)(2,1)S(1)}, u32[]{:S(2)}, u32[]{:S(2)}) %collective-permute-start.50) | collective-permute-done | bytes 524320 | tf_op jit(solution)/shard_map/ppermute | solution.py:30
  364.6 3.1 collective-permute-done.51.right
  367.7 1.9 copy-done.1
  369.6 6.2 %shard_map.106 = (bf16[128,2048]{1,0:T(8,128)(2,1)}, bf16[128,1536]{1,0:T(8,128)(2,1)}) custom-call(s32[2]{0:T(128)S(1)} %add_multiply_fusion.offsets, f32[32,128]{1,0:T(8,128)S(1)} %copy-done.3, f32[32,128]{1,0:T(8,128)S(1)} %copy-done.14, bf16[96,2048]{1,0:T(8,128)(2,1)S(1)} %get-tuple-element.43.refs_0_.a0, ...), custom_call_target="tpu_custom_call" | custom-call | flops 805306368 | bytes 8388608 | tf_op jit(solution)/shard_map/pallas_call | solution.py:286
  (194 shorter events, 59.3 us)
Async XLA Ops:
  7.2 202.6 %all-gather.4.cloned.1.call-start = ((), (), s32[]{:S(2)}) async-start(), calls=%async_computation | async-start | bytes 3538944 | tf_op jit(solution)/shard_map/all_gather | solution.py:342
  8.5 18.1 %collective-permute-start.11 = (bf16[512,768]{1,0:T(8,128)(2,1)S(1)}, bf16[512,768]{1,0:T(8,128)(2,1)S(1)}, u32[]{:S(2)}, u32[]{:S(2)}) collective-permute-start(bf16[512,768]{1,0:T(8,128)(2,1)S(1)} %pad_maximum_fusion.refs_4_), channel_id=1, source_target_pairs={{0,128},{128,0},{1,129},{129,1},{2,130},{130,2},{3,131},{131,3},{4... | collective-permute-start | bytes 2359304 | tf_op jit(solution)/shard_map/ppermute | solution.py:35
  27.5 20.3 %collective-permute-start.12 = (bf16[512,768]{1,0:T(8,128)(2,1)S(1)}, bf16[512,768]{1,0:T(8,128)(2,1)S(1)}, u32[]{:S(2)}, u32[]{:S(2)}) collective-permute-start(bf16[512,768]{1,0:T(8,128)(2,1)S(1)} %collective-permute-done.11.refs_9_), channel_id=1, source_target_pairs={{0,32},{32,64},{64,96},{96,0},{1,33},{33,65},{65,97},{97,1},{2,34}... | collective-permute-start | bytes 2359304 | tf_op jit(solution)/shard_map/ppermute | solution.py:30
  48.7 9.8 %collective-permute-start.14 = (bf16[256,768]{1,0:T(8,128)(2,1)}, bf16[256,768]{1,0:T(8,128)(2,1)S(1)}, u32[]{:S(2)}, u32[]{:S(2)}) collective-permute-start(bf16[256,768]{1,0:T(8,128)(2,1)} %slice.42), channel_id=1, source_target_pairs={{0,32},{32,64},{64,96},{96,0},{1,33},{33,65},{65,97},{97,1},{2,34}... | collective-permute-start | bytes 1179656 | tf_op jit(solution)/shard_map/ppermute | solution.py:30
  58.5 14.1 %collective-permute-start = (bf16[128,2048]{1,0:T(8,128)(2,1)S(1)}, bf16[128,2048]{1,0:T(8,128)(2,1)S(1)}, u32[]{:S(2)}, u32[]{:S(2)}) collective-permute-start(bf16[128,2048]{1,0:T(8,128)(2,1)S(1)} %copy-done.2), channel_id=1, source_target_pairs={{0,4},{4,8},{8,12},{12,16},{16,20},{20,24},{24,28},{28,0},{1,5},{5... | collective-permute-start | bytes 1572872 | tf_op jit(solution)/shard_map/ppermute | solution.py:30
  59.8 13.7 %collective-permute-start.2 = (bf16[128,2048]{1,0:T(8,128)(2,1)S(1)}, bf16[128,2048]{1,0:T(8,128)(2,1)S(1)}, u32[]{:S(2)}, u32[]{:S(2)}) collective-permute-start(bf16[128,2048]{1,0:T(8,128)(2,1)S(1)} %copy-done.2), channel_id=1, source_target_pairs={{0,28},{4,0},{8,4},{12,8},{16,12},{20,16},{24,20},{28,24},{1,29},{... | collective-permute-start | bytes 1572872 | tf_op jit(solution)/shard_map/ppermute | solution.py:30
  72.7 10.8 %collective-permute-start.1 = (bf16[128,2048]{1,0:T(8,128)(2,1)S(1)}, bf16[128,2048]{1,0:T(8,128)(2,1)S(1)}, u32[]{:S(2)}, u32[]{:S(2)}) collective-permute-start(bf16[128,2048]{1,0:T(8,128)(2,1)S(1)} %collective-permute-done.refs_3_), channel_id=1, source_target_pairs={{0,4},{4,8},{8,12},{12,16},{16,20},{20,24},{24,28},{28,0},{1,5},{5... | collective-permute-start | bytes 1572872 | tf_op jit(solution)/shard_map/ppermute | solution.py:30
  73.5 13.4 %collective-permute-start.3 = (bf16[128,2048]{1,0:T(8,128)(2,1)S(1)}, bf16[128,2048]{1,0:T(8,128)(2,1)S(1)}, u32[]{:S(2)}, u32[]{:S(2)}) collective-permute-start(bf16[128,2048]{1,0:T(8,128)(2,1)S(1)} %collective-permute-done.2.refs_4_), channel_id=1, source_target_pairs={{0,28},{4,0},{8,4},{12,8},{16,12},{20,16},{24,20},{28,24},{1,29},{... | collective-permute-start | bytes 1572872 | tf_op jit(solution)/shard_map/ppermute | solution.py:30
  77.0 37.9 %collective-permute-start.8 = (bf16[512,768]{1,0:T(8,128)(2,1)S(1)}, bf16[512,768]{1,0:T(8,128)(2,1)S(1)}, u32[]{:S(2)}, u32[]{:S(2)}) collective-permute-start(bf16[512,768]{1,0:T(8,128)(2,1)S(1)} %pad_maximum_fusion.refs_4_), channel_id=1, source_target_pairs={{0,96},{32,0},{64,32},{96,64},{1,97},{33,1},{65,33},{97,65},{2,98}... | collective-permute-start | bytes 2359304 | tf_op jit(solution)/shard_map/ppermute | solution.py:30
  83.4 10.4 %collective-permute-start.31 = (bf16[128,2048]{1,0:T(8,128)(2,1)S(1)}, bf16[128,2048]{1,0:T(8,128)(2,1)S(1)}, u32[]{:S(2)}, u32[]{:S(2)}) collective-permute-start(bf16[128,2048]{1,0:T(8,128)(2,1)S(1)} %collective-permute-done.1.refs_1_), channel_id=1, source_target_pairs={{0,4},{4,8},{8,12},{12,16},{16,20},{20,24},{24,28},{28,0},{1,5},{5... | collective-permute-start | bytes 1572872 | tf_op jit(solution)/shard_map/ppermute | solution.py:30
  84.2 38.3 %collective-permute-start.7 = (bf16[512,768]{1,0:T(8,128)(2,1)S(1)}, bf16[512,768]{1,0:T(8,128)(2,1)}, u32[]{:S(2)}, u32[]{:S(2)}) collective-permute-start(bf16[512,768]{1,0:T(8,128)(2,1)S(1)} %pad_maximum_fusion.refs_4_), channel_id=1, source_target_pairs={{0,32},{32,64},{64,96},{96,0},{1,33},{33,65},{65,97},{97,1},{2,34}... | collective-permute-start | bytes 2359304 | tf_op jit(solution)/shard_map/ppermute | solution.py:30
  84.2 52.0 %collective-permute-start.13 = (bf16[512,768]{1,0:T(8,128)(2,1)}, bf16[512,768]{1,0:T(8,128)(2,1)}, u32[]{:S(2)}, u32[]{:S(2)}) collective-permute-start(bf16[512,768]{1,0:T(8,128)(2,1)} %copy-done.24), channel_id=1, source_target_pairs={{0,96},{32,0},{64,32},{96,64},{1,97},{33,1},{65,33},{97,65},{2,98}... | collective-permute-start | bytes 2359304 | tf_op jit(solution)/shard_map/ppermute | solution.py:30
  93.8 24.6 %collective-permute-start.20 = (bf16[768,256]{1,0:T(8,128)(2,1)}, bf16[768,256]{1,0:T(8,128)(2,1)}, u32[]{:S(2)}, u32[]{:S(2)}) collective-permute-start(bf16[768,256]{1,0:T(8,128)(2,1)} %bitcast.24), channel_id=1, source_target_pairs={{0,128},{128,0},{1,129},{129,1},{2,130},{130,2},{3,131},{131,3},{4... | collective-permute-start | bytes 1179656 | tf_op jit(solution)/shard_map/ppermute | solution.py:35
  95.8 41.7 %collective-permute-start.32 = (bf16[64,2048]{1,0:T(8,128)(2,1)}, bf16[64,2048]{1,0:T(8,128)(2,1)S(1)}, u32[]{:S(2)}, u32[]{:S(2)}) collective-permute-start(bf16[64,2048]{1,0:T(8,128)(2,1)} %slice.48), channel_id=1, source_target_pairs={{0,4},{4,8},{8,12},{12,16},{16,20},{20,24},{24,28},{28,0},{1,5},{5... | collective-permute-start | bytes 786440 | tf_op jit(solution)/shard_map/ppermute | solution.py:30
  115.7 23.4 %collective-permute-start.34 = (bf16[64,2048]{1,0:T(8,128)(2,1)}, bf16[64,2048]{1,0:T(8,128)(2,1)}, u32[]{:S(2)}, u32[]{:S(2)}) collective-permute-start(bf16[64,2048]{1,0:T(8,128)(2,1)} %slice.49), channel_id=1, source_target_pairs={{0,28},{4,0},{8,4},{12,8},{16,12},{20,16},{24,20},{28,24},{1,29},{... | collective-permute-start | bytes 786440 | tf_op jit(solution)/shard_map/ppermute | solution.py:30
  118.4 55.8 %collective-permute-start.16 = (bf16[768,256]{1,0:T(8,128)(2,1)}, bf16[768,256]{1,0:T(8,128)(2,1)}, u32[]{:S(2)}, u32[]{:S(2)}) collective-permute-start(bf16[768,256]{1,0:T(8,128)(2,1)} %bitcast.25), channel_id=1, source_target_pairs={{0,32},{32,64},{64,96},{96,0},{1,33},{33,65},{65,97},{97,1},{2,34}... | collective-permute-start | bytes 1179656 | tf_op jit(solution)/shard_map/ppermute | solution.py:30
  122.5 51.7 %collective-permute-start.17 = (bf16[768,256]{1,0:T(8,128)(2,1)}, bf16[768,256]{1,0:T(8,128)(2,1)}, u32[]{:S(2)}, u32[]{:S(2)}) collective-permute-start(bf16[768,256]{1,0:T(8,128)(2,1)} %bitcast.26), channel_id=1, source_target_pairs={{0,96},{32,0},{64,32},{96,64},{1,97},{33,1},{65,33},{97,65},{2,98}... | collective-permute-start | bytes 1179656 | tf_op jit(solution)/shard_map/ppermute | solution.py:30
  136.2 40.7 %collective-permute-start.21 = (bf16[768,256]{1,0:T(8,128)(2,1)}, bf16[768,256]{1,0:T(8,128)(2,1)}, u32[]{:S(2)}, u32[]{:S(2)}) collective-permute-start(bf16[768,256]{1,0:T(8,128)(2,1)} %collective-permute-done.20.refs_6_), channel_id=1, source_target_pairs={{0,32},{32,64},{64,96},{96,0},{1,33},{33,65},{65,97},{97,1},{2,34}... | collective-permute-start | bytes 1179656 | tf_op jit(solution)/shard_map/ppermute | solution.py:30
  137.5 49.4 %collective-permute-start.22 = (bf16[768,256]{1,0:T(8,128)(2,1)}, bf16[768,256]{1,0:T(8,128)(2,1)}, u32[]{:S(2)}, u32[]{:S(2)}) collective-permute-start(bf16[768,256]{1,0:T(8,128)(2,1)} %collective-permute-done.20.refs_6_), channel_id=1, source_target_pairs={{0,96},{32,0},{64,32},{96,64},{1,97},{33,1},{65,33},{97,65},{2,98}... | collective-permute-start | bytes 1179656 | tf_op jit(solution)/shard_map/ppermute | solution.py:30
  139.1 50.5 %collective-permute-start.10 = (bf16[256,768]{1,0:T(8,128)(2,1)}, bf16[256,768]{1,0:T(8,128)(2,1)}, u32[]{:S(2)}, u32[]{:S(2)}) collective-permute-start(bf16[256,768]{1,0:T(8,128)(2,1)} %slice.41), channel_id=1, source_target_pairs={{0,96},{32,0},{64,32},{96,64},{1,97},{33,1},{65,33},{97,65},{2,98}... | collective-permute-start | bytes 1179656 | tf_op jit(solution)/shard_map/ppermute | solution.py:30
  174.2 30.2 %collective-permute-start.9 = (bf16[256,768]{1,0:T(8,128)(2,1)}, bf16[256,768]{1,0:T(8,128)(2,1)}, u32[]{:S(2)}, u32[]{:S(2)}) collective-permute-start(bf16[256,768]{1,0:T(8,128)(2,1)} %slice.40), channel_id=1, source_target_pairs={{0,32},{32,64},{64,96},{96,0},{1,33},{33,65},{65,97},{97,1},{2,34}... | collective-permute-start | bytes 1179656 | tf_op jit(solution)/shard_map/ppermute | solution.py:30
  174.2 30.2 %collective-permute-start.15 = (bf16[256,768]{1,0:T(8,128)(2,1)}, bf16[256,768]{1,0:T(8,128)(2,1)}, u32[]{:S(2)}, u32[]{:S(2)}) collective-permute-start(bf16[256,768]{1,0:T(8,128)(2,1)} %slice.43), channel_id=1, source_target_pairs={{0,96},{32,0},{64,32},{96,64},{1,97},{33,1},{65,33},{97,65},{2,98}... | collective-permute-start | bytes 1179656 | tf_op jit(solution)/shard_map/ppermute | solution.py:30
  176.9 30.2 %collective-permute-start.35 = (bf16[96,2048]{1,0:T(8,128)(2,1)}, bf16[96,2048]{1,0:T(8,128)(2,1)}, u32[]{:S(2)}, u32[]{:S(2)}) collective-permute-start(bf16[96,2048]{1,0:T(8,128)(2,1)} %get-tuple-element.52), channel_id=1, source_target_pairs={{0,1},{1,0},{2,3},{3,2},{4,5},{5,4},{6,7},{7,6},{8,9},{9,8},{10,11... | collective-permute-start | bytes 1179656 | tf_op jit(solution)/shard_map/ppermute | solution.py:35
  186.9 20.3 %collective-permute-start.36 = (bf16[96,2048]{1,0:T(8,128)(2,1)}, bf16[96,2048]{1,0:T(8,128)(2,1)}, u32[]{:S(2)}, u32[]{:S(2)}) collective-permute-start(bf16[96,2048]{1,0:T(8,128)(2,1)} %get-tuple-element.53), channel_id=1, source_target_pairs={{0,2},{1,3},{2,0},{3,1},{4,6},{5,7},{6,4},{7,5},{8,10},{9,11},{10,... | collective-permute-start | bytes 1179656 | tf_op jit(solution)/shard_map/ppermute | solution.py:35
  189.6 20.2 %collective-permute-start.37 = (bf16[96,2048]{1,0:T(8,128)(2,1)}, bf16[96,2048]{1,0:T(8,128)(2,1)}, u32[]{:S(2)}, u32[]{:S(2)}) collective-permute-start(bf16[96,2048]{1,0:T(8,128)(2,1)} %get-tuple-element.54), channel_id=1, source_target_pairs={{0,3},{1,2},{2,1},{3,0},{4,7},{5,6},{6,5},{7,4},{8,11},{9,10},{10,... | collective-permute-start | bytes 1179656 | tf_op jit(solution)/shard_map/ppermute | solution.py:35
  204.5 18.6 %collective-permute-start.18 = (bf16[384,256]{1,0:T(8,128)(2,1)}, bf16[384,256]{1,0:T(8,128)(2,1)S(1)}, u32[]{:S(2)}, u32[]{:S(2)}) collective-permute-start(bf16[384,256]{1,0:T(8,128)(2,1)} %slice.44), channel_id=1, source_target_pairs={{0,32},{32,64},{64,96},{96,0},{1,33},{33,65},{65,97},{97,1},{2,34}... | collective-permute-start | bytes 589832 | tf_op jit(solution)/shard_map/ppermute | solution.py:30
  204.5 27.7 %collective-permute-start.19 = (bf16[384,256]{1,0:T(8,128)(2,1)}, bf16[384,256]{1,0:T(8,128)(2,1)S(1)}, u32[]{:S(2)}, u32[]{:S(2)}) collective-permute-start(bf16[384,256]{1,0:T(8,128)(2,1)} %slice.45), channel_id=1, source_target_pairs={{0,96},{32,0},{64,32},{96,64},{1,97},{33,1},{65,33},{97,65},{2,98}... | collective-permute-start | bytes 589832 | tf_op jit(solution)/shard_map/ppermute | solution.py:30
  207.1 25.0 %collective-permute-start.23 = (bf16[384,256]{1,0:T(8,128)(2,1)}, bf16[384,256]{1,0:T(8,128)(2,1)S(1)}, u32[]{:S(2)}, u32[]{:S(2)}) collective-permute-start(bf16[384,256]{1,0:T(8,128)(2,1)} %slice.46), channel_id=1, source_target_pairs={{0,32},{32,64},{64,96},{96,0},{1,33},{33,65},{65,97},{97,1},{2,34}... | collective-permute-start | bytes 589832 | tf_op jit(solution)/shard_map/ppermute | solution.py:30
  207.1 25.7 %collective-permute-start.24 = (bf16[384,256]{1,0:T(8,128)(2,1)}, bf16[384,256]{1,0:T(8,128)(2,1)}, u32[]{:S(2)}, u32[]{:S(2)}) collective-permute-start(bf16[384,256]{1,0:T(8,128)(2,1)} %slice.47), channel_id=1, source_target_pairs={{0,96},{32,0},{64,32},{96,64},{1,97},{33,1},{65,33},{97,65},{2,98}... | collective-permute-start | bytes 589832 | tf_op jit(solution)/shard_map/ppermute | solution.py:30
  209.8 157.9 %collective-permute-start.52 = (bf16[1536,1024]{1,0:T(8,128)(2,1)}, bf16[1536,1024]{1,0:T(8,128)(2,1)}, u32[]{:S(2)}, u32[]{:S(2)}) collective-permute-start(bf16[1536,1024]{1,0:T(8,128)(2,1)} %all-gather.4.cloned.1.call-done.q0), channel_id=1, source_target_pairs={{0,1},{1,0},{2,3},{3,2},{4,5},{5,4},{6,7},{7,6},{8,9},{9,8},{10,11... | collective-permute-start | bytes 9437192 | tf_op jit(solution)/shard_map/ppermute | solution.py:35
  223.2 60.1 %collective-permute-start.4 = (bf16[160,2048]{1,0:T(8,128)(2,1)S(1)}, bf16[160,2048]{1,0:T(8,128)(2,1)S(1)}, u32[]{:S(2)}, u32[]{:S(2)}) collective-permute-start(bf16[160,2048]{1,0:T(8,128)(2,1)S(1)} %copy-done.34), channel_id=1, source_target_pairs={{0,1},{1,0},{2,3},{3,2},{4,5},{5,4},{6,7},{7,6},{8,9},{9,8},{10,11... | collective-permute-start | bytes 1966088 | tf_op jit(solution)/shard_map/ppermute | solution.py:35
  239.3 46.6 %collective-permute-start.5 = (bf16[160,2048]{1,0:T(8,128)(2,1)S(1)}, bf16[160,2048]{1,0:T(8,128)(2,1)S(1)}, u32[]{:S(2)}, u32[]{:S(2)}) collective-permute-start(bf16[160,2048]{1,0:T(8,128)(2,1)S(1)} %copy-done.32), channel_id=1, source_target_pairs={{0,2},{1,3},{2,0},{3,1},{4,6},{5,7},{6,4},{7,5},{8,10},{9,11},{10,... | collective-permute-start | bytes 1966088 | tf_op jit(solution)/shard_map/ppermute | solution.py:35
  242.0 44.7 %collective-permute-start.6 = (bf16[160,2048]{1,0:T(8,128)(2,1)S(1)}, bf16[160,2048]{1,0:T(8,128)(2,1)S(1)}, u32[]{:S(2)}, u32[]{:S(2)}) collective-permute-start(bf16[160,2048]{1,0:T(8,128)(2,1)S(1)} %copy-done.30), channel_id=1, source_target_pairs={{0,3},{1,2},{2,1},{3,0},{4,7},{5,6},{6,5},{7,4},{8,11},{9,10},{10,... | collective-permute-start | bytes 1966088 | tf_op jit(solution)/shard_map/ppermute | solution.py:35
  242.6 31.4 %collective-permute-start.42 = (bf16[32,2048]{1,0:T(8,128)(2,1)S(1)}, bf16[32,2048]{1,0:T(8,128)(2,1)S(1)}, u32[]{:S(2)}, u32[]{:S(2)}) collective-permute-start(bf16[32,2048]{1,0:T(8,128)(2,1)S(1)} %get-tuple-element.61), channel_id=1, source_target_pairs={{0,2},{1,3},{2,0},{3,1},{4,6},{5,7},{6,4},{7,5},{8,10},{9,11},{10,... | collective-permute-start | bytes 393224 | tf_op jit(solution)/shard_map/ppermute | solution.py:35
  283.3 19.0 %collective-permute-start.39 = (bf16[64,2048]{1,0:T(8,128)(2,1)S(1)}, bf16[64,2048]{1,0:T(8,128)(2,1)S(1)}, u32[]{:S(2)}, u32[]{:S(2)}) collective-permute-start(bf16[64,2048]{1,0:T(8,128)(2,1)S(1)} %get-tuple-element.57), channel_id=1, source_target_pairs={{0,2},{1,3},{2,0},{3,1},{4,6},{5,7},{6,4},{7,5},{8,10},{9,11},{10,... | collective-permute-start | bytes 786440 | tf_op jit(solution)/shard_map/ppermute | solution.py:35
  285.9 17.0 %collective-permute-start.40 = (bf16[64,2048]{1,0:T(8,128)(2,1)S(1)}, bf16[64,2048]{1,0:T(8,128)(2,1)S(1)}, u32[]{:S(2)}, u32[]{:S(2)}) collective-permute-start(bf16[64,2048]{1,0:T(8,128)(2,1)S(1)} %get-tuple-element.58), channel_id=1, source_target_pairs={{0,3},{1,2},{2,1},{3,0},{4,7},{5,6},{6,5},{7,4},{8,11},{9,10},{10,... | collective-permute-start | bytes 786440 | tf_op jit(solution)/shard_map/ppermute | solution.py:35
  286.7 16.2 %collective-permute-start.44 = (bf16[64,2048]{1,0:T(8,128)(2,1)S(1)}, bf16[64,2048]{1,0:T(8,128)(2,1)S(1)}, u32[]{:S(2)}, u32[]{:S(2)}) collective-permute-start(bf16[64,2048]{1,0:T(8,128)(2,1)S(1)} %get-tuple-element.63), channel_id=1, source_target_pairs={{0,28},{4,0},{8,4},{12,8},{16,12},{20,16},{24,20},{28,24},{1,29},{... | collective-permute-start | bytes 786440 | tf_op jit(solution)/shard_map/ppermute | solution.py:30
  288.3 14.7 %collective-permute-start.45 = (bf16[64,2048]{1,0:T(8,128)(2,1)S(1)}, bf16[64,2048]{1,0:T(8,128)(2,1)S(1)}, u32[]{:S(2)}, u32[]{:S(2)}) collective-permute-start(bf16[64,2048]{1,0:T(8,128)(2,1)S(1)} %get-tuple-element.64), channel_id=1, source_target_pairs={{0,4},{4,8},{8,12},{12,16},{16,20},{20,24},{24,28},{28,0},{1,5},{5... | collective-permute-start | bytes 786440 | tf_op jit(solution)/shard_map/ppermute | solution.py:30
  304.5 18.1 %collective-permute-start.46 = (bf16[128,2048]{1,0:T(8,128)(2,1)S(1)}, bf16[128,2048]{1,0:T(8,128)(2,1)S(1)}, u32[]{:S(2)}, u32[]{:S(2)}) collective-permute-start(bf16[128,2048]{1,0:T(8,128)(2,1)S(1)} %get-tuple-element.65), channel_id=1, source_target_pairs={{0,28},{4,0},{8,4},{12,8},{16,12},{20,16},{24,20},{28,24},{1,29},{... | collective-permute-start | bytes 1572872 | tf_op jit(solution)/shard_map/ppermute | solution.py:30
  307.5 15.2 %collective-permute-start.47 = (bf16[128,2048]{1,0:T(8,128)(2,1)S(1)}, bf16[128,2048]{1,0:T(8,128)(2,1)S(1)}, u32[]{:S(2)}, u32[]{:S(2)}) collective-permute-start(bf16[128,2048]{1,0:T(8,128)(2,1)S(1)} %get-tuple-element.66), channel_id=1, source_target_pairs={{0,4},{4,8},{8,12},{12,16},{16,20},{20,24},{24,28},{28,0},{1,5},{5... | collective-permute-start | bytes 1572872 | tf_op jit(solution)/shard_map/ppermute | solution.py:30
  310.0 12.6 %collective-permute-start.30 = (bf16[64,2048]{1,0:T(8,128)(2,1)S(1)}, bf16[64,2048]{1,0:T(8,128)(2,1)S(1)}, u32[]{:S(2)}, u32[]{:S(2)}) collective-permute-start(bf16[64,2048]{1,0:T(8,128)(2,1)S(1)} %get-tuple-element.50), channel_id=1, source_target_pairs={{0,3},{1,2},{2,1},{3,0},{4,7},{5,6},{6,5},{7,4},{8,11},{9,10},{10,... | collective-permute-start | bytes 786440 | tf_op jit(solution)/shard_map/ppermute | solution.py:35
  316.6 13.0 %collective-permute-start.25 = (bf16[96,2048]{1,0:T(8,128)(2,1)S(1)}, bf16[96,2048]{1,0:T(8,128)(2,1)S(1)}, u32[]{:S(2)}, u32[]{:S(2)}) collective-permute-start(bf16[96,2048]{1,0:T(8,128)(2,1)S(1)} %get-tuple-element.44), channel_id=1, source_target_pairs={{0,1},{1,0},{2,3},{3,2},{4,5},{5,4},{6,7},{7,6},{8,9},{9,8},{10,11... | collective-permute-start | bytes 1179656 | tf_op jit(solution)/shard_map/ppermute | solution.py:35
  324.3 23.6 %collective-permute-start.48 = (bf16[128,2048]{1,0:T(8,128)(2,1)S(1)}, bf16[128,2048]{1,0:T(8,128)(2,1)S(1)}, u32[]{:S(2)}, u32[]{:S(2)}) collective-permute-start(bf16[128,2048]{1,0:T(8,128)(2,1)S(1)} %get-tuple-element.67), channel_id=1, source_target_pairs={{0,28},{4,0},{8,4},{12,8},{16,12},{20,16},{24,20},{28,24},{1,29},{... | collective-permute-start | bytes 1572872 | tf_op jit(solution)/shard_map/ppermute | solution.py:30
  327.0 20.8 %collective-permute-start.49 = (bf16[128,2048]{1,0:T(8,128)(2,1)S(1)}, bf16[128,2048]{1,0:T(8,128)(2,1)S(1)}, u32[]{:S(2)}, u32[]{:S(2)}) collective-permute-start(bf16[128,2048]{1,0:T(8,128)(2,1)S(1)} %get-tuple-element.68), channel_id=1, source_target_pairs={{0,4},{4,8},{8,12},{12,16},{16,20},{20,24},{24,28},{28,0},{1,5},{5... | collective-permute-start | bytes 1572872 | tf_op jit(solution)/shard_map/ppermute | solution.py:30
  327.0 12.4 %collective-permute-start.26 = (bf16[96,2048]{1,0:T(8,128)(2,1)S(1)}, bf16[96,2048]{1,0:T(8,128)(2,1)S(1)}, u32[]{:S(2)}, u32[]{:S(2)}) collective-permute-start(bf16[96,2048]{1,0:T(8,128)(2,1)S(1)} %get-tuple-element.45), channel_id=1, source_target_pairs={{0,2},{1,3},{2,0},{3,1},{4,6},{5,7},{6,4},{7,5},{8,10},{9,11},{10,... | collective-permute-start | bytes 1179656 | tf_op jit(solution)/shard_map/ppermute | solution.py:35
  329.5 18.3 %collective-permute-start.27 = (bf16[96,2048]{1,0:T(8,128)(2,1)S(1)}, bf16[96,2048]{1,0:T(8,128)(2,1)S(1)}, u32[]{:S(2)}, u32[]{:S(2)}) collective-permute-start(bf16[96,2048]{1,0:T(8,128)(2,1)S(1)} %get-tuple-element.46), channel_id=1, source_target_pairs={{0,3},{1,2},{2,1},{3,0},{4,7},{5,6},{6,5},{7,4},{8,11},{9,10},{10,... | collective-permute-start | bytes 1179656 | tf_op jit(solution)/shard_map/ppermute | solution.py:35
  350.4 14.2 %collective-permute-start.50 = (bf16[128,2048]{1,0:T(8,128)(2,1)}, bf16[128,2048]{1,0:T(8,128)(2,1)S(1)}, u32[]{:S(2)}, u32[]{:S(2)}) collective-permute-start(bf16[128,2048]{1,0:T(8,128)(2,1)} %get-tuple-element.69), channel_id=1, source_target_pairs={{0,28},{4,0},{8,4},{12,8},{16,12},{20,16},{24,20},{28,24},{1,29},{... | collective-permute-start | bytes 1572872 | tf_op jit(solution)/shard_map/ppermute | solution.py:30
  353.1 14.7 %collective-permute-start.51 = (bf16[128,2048]{1,0:T(8,128)(2,1)}, bf16[128,2048]{1,0:T(8,128)(2,1)}, u32[]{:S(2)}, u32[]{:S(2)}) collective-permute-start(bf16[128,2048]{1,0:T(8,128)(2,1)} %get-tuple-element.70), channel_id=1, source_target_pairs={{0,4},{4,8},{8,12},{12,16},{16,20},{20,24},{24,28},{28,0},{1,5},{5... | collective-permute-start | bytes 1572872 | tf_op jit(solution)/shard_map/ppermute | solution.py:30
  (57 other events, 1119.8 us)
Sparse Core Ops, SparseCore 0:
  58.7 68.2 all-gather.3

commit v2 on v1

v2 whole, which is shorter than its diff:
```python
import functools

import jax
import jax.numpy as jnp
from jax import lax
from jax.experimental import pallas as pl
from jax.experimental.pallas import tpu as pltpu
from jax.sharding import Mesh, PartitionSpec as P

BF = jnp.bfloat16
F32 = jnp.float32
SLOTS = 32
ANY = pl.BlockSpec(memory_space=pltpu.HBM)
SMEM = pl.BlockSpec(memory_space=pltpu.SMEM)
VMEM = pl.BlockSpec(memory_space=pltpu.VMEM)
FIRST = (2, 6, 1, 7, 0)
SECOND = (4, 3, 5)


def params(mib):
    return pltpu.CompilerParams(vmem_limit_bytes=mib << 20)


def cost(flops, size):
    return pl.CostEstimate(flops=flops, bytes_accessed=size, transcendentals=0)


def shift(x, axis, by):
    n = lax.axis_size(axis)
    return lax.ppermute(x, axis, [(i, (i + by) % n) for i in range(n)])


def swap(x, axes, k):
    n = lax.axis_size(axes)
    return lax.ppermute(x, axes, [(i, i ^ k) for i in range(n)])


def prepare_kernel(tokens, routes, gain, gate, up, down, block, weights, extra, sems):
    copies = []

    def copy(src, dst):
        c = pltpu.make_async_copy(src, dst, sems.at[len(copies)])
        c.start()
        copies.append(c)

    rows = tokens.shape[0]
    copy(tokens, block.at[0:rows])
    for j in range(3):
        copy(gate.at[:, 256 * j : 256 * (j + 1)], weights.at[256 * j : 256 * (j + 1)])
        copy(up.at[:, 256 * j : 256 * (j + 1)], weights.at[768 + 256 * j : 768 + 256 * (j + 1)])
    copy(down, weights.at[1536:2304])
    extra[...] = jnp.zeros_like(extra)
    g = gain[...]
    high = g.astype(BF)
    rest = g - high.astype(F32)
    middle = rest.astype(BF)
    low = (rest - middle.astype(F32)).astype(BF)
    for i, part in enumerate((routes[...].astype(F32).astype(BF), high, middle, low)):
        extra[0:6, 128 * i : 128 * (i + 1)] = part
    copy(extra, block.at[rows : rows + 16])
    for c in copies:
        c.wait()


def prepare(tokens, routes, gain, gate, up, down):
    rows, width = tokens.shape
    return pl.pallas_call(
        prepare_kernel,
        out_shape=(jax.ShapeDtypeStruct((rows + 16, width), BF), jax.ShapeDtypeStruct((2304, 256), BF)),
        in_specs=[ANY, VMEM, VMEM, ANY, ANY, ANY],
        out_specs=(ANY, ANY),
        scratch_shapes=[pltpu.VMEM((16, width), BF), pltpu.SemaphoreType.DMA((9,))],
        compiler_params=params(62),
        cost_estimate=cost(1 << 16, 4 << 20),
    )(tokens, routes, gain, gate, up, down)


def chosen_rows(code, i):
    slot = lax.broadcasted_iota(jnp.int32, (SLOTS, 128), 0).astype(F32)
    return [code[4 * i + k : 4 * i + k + 1, :] == slot for k in range(4)]


def select_kernel(blocks, n_in, place, *refs):
    sources, extras, refs = refs[:n_in], refs[n_in : n_in + len(blocks)], refs[n_in + len(blocks) :]
    outs, (code, gain, match, joined) = refs[:4], refs[4:]

    @pl.when(pl.program_id(0) == 0)
    def _():
        z, me = place[0], place[1]
        for i, extra in enumerate(extras):
            block = extra[...].astype(F32)
            routes = block[0:6, 0:128]
            gains = block[0:6, 128:256] + block[0:6, 256:384] + block[0:6, 384:512]
            for k in range(4):
                expert = (4 * z + lax.bitwise_xor(me, k)).astype(F32)
                hit = routes == expert
                row = slice(4 * i + k, 4 * i + k + 1)
                match[row] = jnp.sum(jnp.where(hit, 1.0, 0.0), axis=0, keepdims=True)
                gain[row] = jnp.sum(jnp.where(hit, gains, 0.0), axis=0, keepdims=True)
        chosen = match[...]
        before = lax.broadcasted_iota(jnp.int32, (128, 128), 0) < lax.broadcasted_iota(jnp.int32, (128, 128), 1)
        rank = jnp.dot(chosen.astype(BF), jnp.where(before, 1.0, 0.0).astype(BF), preferred_element_type=F32)
        code[...] = jnp.where(chosen > 0.5, rank, -1.0)

    at = 0
    for i, s in enumerate(blocks):
        if s == 4:
            joined[0:64] = sources[at][0:64]
            joined[64:128] = sources[at + 1][0:64]
            source, at = joined[...], at + 2
        else:
            source, at = sources[at][0:128], at + 1
        onehot = jnp.concatenate([jnp.where(hit, 1.0, 0.0).astype(BF) for hit in chosen_rows(code, i)], axis=0)
        rows = jnp.dot(onehot, source, preferred_element_type=F32).astype(BF)
        for k in range(4):
            outs[k][i * SLOTS : (i + 1) * SLOTS] = rows[k * SLOTS : (k + 1) * SLOTS]


def select(blocks, place, sources):
    width, step = sources[0].shape[1], 512
    n, rows = len(blocks), len(blocks) * SLOTS
    holders = [x for x in sources if x.shape[0] > 64]
    below = [pl.BlockSpec((16, step), functools.partial(lambda i, j: (i, 0), x.shape[0] // 16 - 1)) for x in holders]
    out = pl.pallas_call(
        functools.partial(select_kernel, blocks, len(sources)),
        out_shape=(jax.ShapeDtypeStruct((rows, width), BF),) * 4 + (jax.ShapeDtypeStruct((4 * n, 128), F32),) * 2,
        grid=(width // step,),
        in_specs=[SMEM] + [pl.BlockSpec((x.shape[0], step), lambda j: (0, j)) for x in sources] + below,
        out_specs=(pl.BlockSpec((rows, step), lambda j: (0, j)),) * 4 + (pl.BlockSpec((4 * n, 128), lambda j: (0, 0)),) * 2,
        scratch_shapes=[pltpu.VMEM((4 * n, 128), F32), pltpu.VMEM((128, step), BF)],
        compiler_params=params(62),
        cost_estimate=cost(n << 26, n << 20),
    )(place, *sources, *holders)
    return out[:4], out[4], out[5]


def hidden_kernel(n_rows, offsets, *refs):
    pieces, weights, out = refs[:4], refs[4:14], refs[14]
    x, gate, up, sems = refs[15:]
    copies = []

    def copy(src, dst):
        c = pltpu.make_async_copy(src, dst, sems.at[len(copies)])
        c.start()
        copies.append(c)

    for ring in range(2):
        whole, far = weights[5 * ring : 5 * ring + 3], weights[5 * ring + 3 : 5 * ring + 5]
        for i in range(4):
            rows = pl.ds(pl.multiple_of(offsets[4 * ring + i], 256), 256)
            for j in range(3):
                cols = slice(256 * j, 256 * (j + 1))
                if i < 3:
                    copy(whole[i].at[cols], gate.at[rows, cols])
                    copy(whole[i].at[768 + 256 * j : 768 + 256 * (j + 1)], up.at[rows, cols])
                else:
                    copy(far[0].at[cols], gate.at[rows, cols])
                    copy(far[1].at[cols], up.at[rows, cols])
    for k in range(4):
        copy(pieces[k], x.at[k * n_rows : (k + 1) * n_rows])
    for c in copies:
        c.wait()

    @pl.loop(0, gate.shape[1] // 256)
    def _(j):
        cols = pl.ds(pl.multiple_of(j * 256, 256), 256)
        g = jnp.dot(x[...], gate[:, cols], preferred_element_type=F32)
        u = jnp.dot(x[...], up[:, cols], preferred_element_type=F32)
        out[:, cols] = (g / (1.0 + jnp.exp(-g)) * u).astype(BF)


def hidden_of(offsets, pieces, weights):
    n_rows, width = pieces[0].shape
    units = 768
    return pl.pallas_call(
        functools.partial(hidden_kernel, n_rows),
        out_shape=jax.ShapeDtypeStruct((4 * n_rows, units), BF),
        in_specs=[SMEM] + [ANY] * (len(pieces) + len(weights)),
        out_specs=VMEM,
        scratch_shapes=[
            pltpu.VMEM((4 * n_rows, width), BF),
            pltpu.VMEM((width, units), BF),
            pltpu.VMEM((width, units), BF),
            pltpu.SemaphoreType.DMA((52,)),
        ],
        compiler_params=params(62),
        cost_estimate=cost(16 * n_rows * width * units, 8 << 20),
    )(offsets, *pieces, *weights)


def answer_kernel(sizes, offsets, *refs):
    hidden, weights = refs[0], refs[1:11]
    outs, (down, sems) = refs[11:-2], refs[-2:]
    copies = []

    def copy(src, dst):
        c = pltpu.make_async_copy(src, dst, sems.at[len(copies)])
        c.start()
        copies.append(c)

    half = down.shape[0] // 2
    for ring in range(2):
        for i in range(3):
            cols = pl.ds(pl.multiple_of(offsets[4 * ring + i], 256), 256)
            copy(weights[5 * ring + i].at[1536:2304], down.at[:, cols])
        cols = pl.ds(pl.multiple_of(offsets[4 * ring + 3], 256), 256)
        copy(weights[5 * ring + 3], down.at[0:half, cols])
        copy(weights[5 * ring + 4], down.at[half : 2 * half, cols])
    for c in copies:
        c.wait()
    total = sum(sizes)

    @pl.loop(0, down.shape[1] // 256)
    def _(j):
        cols = pl.ds(pl.multiple_of(j * 256, 256), 256)
        answer = jnp.dot(hidden[...], down[:, cols], preferred_element_type=F32).astype(BF)
        for k in range(4):
            at = k * total
            for i, size in enumerate(sizes):
                outs[4 * i + k][:, cols] = answer[at : at + size]
                at += size


def answers_of(sizes, offsets, hidden, weights):
    width = 8 * weights[0].shape[1]
    units = hidden.shape[1]
    shapes = [jax.ShapeDtypeStruct((size, width), BF) for size in sizes for _ in range(4)]
    out = pl.pallas_call(
        functools.partial(answer_kernel, sizes),
        out_shape=tuple(shapes),
        in_specs=[SMEM, VMEM] + [ANY] * len(weights),
        out_specs=(VMEM,) * len(shapes),
        scratch_shapes=[pltpu.VMEM((units, width), BF), pltpu.SemaphoreType.DMA((10,))],
        compiler_params=params(62),
        cost_estimate=cost(2 * hidden.shape[0] * width * units, 8 << 20),
    )(offsets, hidden, *weights)
    return [out[4 * i : 4 * i + 4] for i in range(len(sizes))]


def combined(code, gain, i, answers):
    weight = jnp.concatenate(
        [jnp.where(hit, gain[4 * i + k : 4 * i + k + 1, :], 0.0) for k, hit in enumerate(chosen_rows(code, i))], axis=0
    )
    high = weight.astype(BF)
    low = (weight - high.astype(F32)).astype(BF)
    rows = jnp.concatenate(answers, axis=0)
    dims = (((0,), (0,)), ((), ()))
    return lax.dot_general(high, rows, dims, preferred_element_type=F32) + lax.dot_general(
        low, rows, dims, preferred_element_type=F32
    )


def combine_kernel(blocks, first, start, n_in, code, gain, *refs):
    answers, arrived, outs = refs[:4], refs[4 : 4 + n_in], refs[4 + n_in :]
    for i, s in enumerate(blocks):
        rows = slice(start + i * SLOTS, start + (i + 1) * SLOTS)
        total = combined(code, gain, first + i, [a[rows] for a in answers])
        if s == 4:
            outs[0][...] = total[0:64].astype(BF)
            outs[1][...] = total[64:128].astype(BF)
        elif s == 3:
            outs[i][0:64] = (total[0:64] + arrived[i][...].astype(F32)).astype(BF)
            outs[i][64:128] = total[64:128].astype(BF)
        elif s == 5:
            outs[i][0:64] = total[0:64].astype(BF)
            outs[i][64:128] = (total[64:128] + arrived[i][...].astype(F32)).astype(BF)
        else:
            outs[i][...] = (total + arrived[i][...].astype(F32)).astype(BF)


def combine(blocks, first, start, code, gain, answers, arrived):
    width, step = answers[0].shape[1], 512
    height = 64 if blocks == (4,) else 128
    whole = pl.BlockSpec(code.shape, lambda j: (0, 0))
    return pl.pallas_call(
        functools.partial(combine_kernel, blocks, first, start, len(arrived)),
        out_shape=(jax.ShapeDtypeStruct((height, width), BF),) * 2,
        grid=(width // step,),
        in_specs=[whole, whole]
        + [pl.BlockSpec((x.shape[0], step), lambda j: (0, j)) for x in (*answers, *arrived)],
        out_specs=(pl.BlockSpec((height, step), lambda j: (0, j)),) * 2,
        compiler_params=params(62),
        cost_estimate=cost(len(blocks) << 27, 2 << 20),
    )(code, gain, *answers, *arrived)


def final_kernel(start, offsets, code, gain, a0, a1, a2, a3, tokens, left, right, norm, q0, q1, mixed, query, total, normed, held, sems):
    copies = [pltpu.make_async_copy(q, held.at[i], sems.at[i]) for i, q in enumerate((q0, q1))]
    for c in copies:
        c.start()
    width, step = tokens.shape[1], 512
    square = jnp.zeros((128, 1), F32)
    for j in range(width // step):
        cols = slice(j * step, (j + 1) * step)
        part = combined(code, gain, 4, [a[start : start + SLOTS, cols] for a in (a0, a1, a2, a3)])
        part = part + tokens[:, cols].astype(F32)
        part = part + left[:, cols].astype(F32) + right[:, cols].astype(F32)
        mixed[:, cols] = part.astype(BF)
        total[:, cols] = part
        square = square + jnp.sum(part * part, axis=1, keepdims=True)
    scale = lax.rsqrt(square / width + 1e-06)
    for j in range(width // step):
        cols = slice(j * step, (j + 1) * step)
        normed[:, cols] = (total[:, cols] * scale * norm[:, cols]).astype(BF)
    for c in copies:
        c.wait()
    half = width // 2
    sides = [normed[:, pl.ds(pl.multiple_of(offsets[i], half), half)] for i in range(2)]
    dims = (((1,), (1,)), ((), ()))

    @pl.loop(0, query.shape[1] // 256)
    def _(j):
        cols = pl.ds(pl.multiple_of(j * 256, 256), 256)
        out = lax.dot_general(sides[0], held[0, cols], dims, preferred_element_type=F32)
        out = out + lax.dot_general(sides[1], held[1, cols], dims, preferred_element_type=F32)
        query[:, cols] = out.astype(BF)


def final(start, offsets, code, gain, answers, tokens, left, right, norm, q0, q1):
    rows, width = tokens.shape
    features = q0.shape[0]
    return pl.pallas_call(
        functools.partial(final_kernel, start),
        out_shape=(jax.ShapeDtypeStruct((rows, width), BF), jax.ShapeDtypeStruct((rows, features), BF)),
        in_specs=[SMEM] + [VMEM] * 10 + [ANY] * 2,
        out_specs=(VMEM, VMEM),
        scratch_shapes=[
            pltpu.VMEM((rows, width), F32),
            pltpu.VMEM((rows, width), BF),
            pltpu.VMEM((2, features, width // 2), BF),
            pltpu.SemaphoreType.DMA((2,)),
        ],
        compiler_params=params(62),
        cost_estimate=cost(2 * rows * width * features, 8 << 20),
    )(offsets, code, gain, *answers, tokens, left, right, norm, q0, q1)


def shards(tokens, routes, route_gain, gate_weight, up_weight, down_weight, norm_gain, query_weight):
    xl, y, z, c = (lax.axis_index(a) for a in ("xl", "y", "z", "c"))
    me = 2 * lax.axis_index("xh") + c
    plane = ("xh", "c")
    around = [xl * 4 + lax.rem(y + d, 4) for d in (0, 3, 1, 2)]
    across = [(1 - xl) * 4 + lax.rem(y + d, 4) for d in (0, 3, 1, 2)]
    offsets = (256 * jnp.stack(around + across)).astype(jnp.int32)
    place = jnp.stack([z, me]).astype(jnp.int32)
    hold = lax.optimization_barrier

    def exchange(pieces):
        return tuple(swap(pieces[k], plane, k) for k in (1, 2, 3))

    block, own = prepare(tokens, routes.T, route_gain.T, gate_weight[0], up_weight[0], down_weight[0])

    up1, down1 = shift(block, "z", 1), shift(block, "z", -1)
    own_u, own_d, other = shift(own, "y", 1), shift(own, "y", -1), swap(own, "xl", 1)
    up2, down2 = shift(up1, "z", 1), shift(down1, "z", -1)
    up1, down1, up2, down2, own_u, own_d, other = hold((up1, down1, up2, down2, own_u, own_d, other))

    oth_u, oth_d = shift(other, "y", 1), shift(other, "y", -1)
    sent_a, code_a, gain_a = select(FIRST, place, [up2, down2, up1, down1, block])
    got_a = exchange(sent_a)
    up3, down3 = shift(up2, "z", 1), shift(down2, "z", -1)
    up4, down4 = shift(up3[:64], "z", 1), shift(down3[64:], "z", -1)
    near = (own_u[:768], own_d[768:1536], own_u[1536:1920], own_d[1920:])
    oth_u, oth_d, got_a, up3, down3, up4, down4, near = hold((oth_u, oth_d, got_a, up3, down3, up4, down4, near))

    far = (shift(near[0], "y", 1), shift(near[1], "y", -1), shift(oth_u[:768], "y", 1), shift(oth_d[768:1536], "y", -1))
    sent_b, code_b, gain_b = select(SECOND, place, [up4, down4, up3, down3])
    got_b = exchange(sent_b)
    half = query_weight.shape[0] // 2
    share = lax.dynamic_slice(query_weight.T, (0, c * half), (query_weight.shape[1], half))
    near = near[2:] + (oth_u[1536:1920], oth_d[1920:])
    far, got_b, near, share = hold((far, got_b, near, share))

    q_own = lax.all_gather(share, ("xl", "y"), axis=0, tiled=True)
    low = tuple(shift(x, "y", d) for x, d in zip(near, (1, -1, 1, -1)))
    wide = [own, own_u, own_d, far[0], far[1], other, oth_u, oth_d, far[2], far[3]]
    hidden_a = hidden_of(offsets, (sent_a[0],) + got_a, wide)
    hidden_b = hidden_of(offsets, (sent_b[0],) + got_b, wide)
    low, hidden_a, hidden_b = hold((low, hidden_a, hidden_b))
    narrow = [own, own_u, own_d, low[0], low[1], other, oth_u, oth_d, low[2], low[3]]

    ans4, ans3 = answers_of((32, 64), offsets, hidden_b, narrow)
    ans2, ans1 = answers_of((64, 96), offsets, hidden_a, narrow)
    got4 = exchange(ans4)
    got4, ans3, ans2, ans1 = hold((got4, ans3, ans2, ans1))
    low, high = combine((4,), 0, 0, code_b, gain_b, (ans4[0],) + got4, [])
    low, high, got3 = shift(low, "z", -1), shift(high, "z", 1), exchange(ans3)
    low, high, got3, ans2 = hold((low, high, got3, ans2))
    low, high = combine((3, 5), 1, 0, code_b, gain_b, (ans3[0],) + got3, [low, high])
    low, high, got2 = shift(low, "z", -1), shift(high, "z", 1), exchange(ans2)
    low, high, got2, ans1 = hold((low, high, got2, ans1))
    low, high = combine((2, 6), 0, 0, code_a, gain_a, (ans2[0],) + got2, [low, high])
    low, high, got1 = shift(low, "z", -1), shift(high, "z", 1), exchange(ans1)
    low, high, got1, q_own = hold((low, high, got1, q_own))
    got1 = (ans1[0],) + got1
    low, high = combine((1, 7), 2, 0, code_a, gain_a, got1, [low, high])
    low, high, q_other = shift(low, "z", -1), shift(high, "z", 1), swap(q_own, "c", 1)
    sides = (half * jnp.stack([c, 1 - c])).astype(jnp.int32)
    return final(64, sides, code_a, gain_a, got1, tokens, low, high, norm_gain[None, :], q_own, q_other)


def solution(mesh):
    fine = Mesh(mesh.devices.reshape(2, 4, 8, 2, 2), ("xl", "y", "z", "xh", "c"))
    grp, ep = ("xl", "y"), ("z", "xh", "c")
    placed = (
        P(grp + ep, None),
        P(grp + ep, None),
        P(grp + ep, None),
        P(ep, grp, None),
        P(ep, grp, None),
        P(ep, None, grp),
        P(),
        P(None, grp),
    )
    return jax.shard_map(
        shards,
        mesh=fine,
        in_specs=placed,
        out_specs=(P(grp + ep, None), P(grp + ep, None)),
        check_vma=False,
    )
```

time: 388 us -> 371 us (0.956)
  Pallas kernels: 46 us -> 121 us
  waiting for transfers between devices: 173 us -> 114 us
  blocking collectives: 22.4 us -> 0 us
  local copies, waits for them, and re-layouts: 35.1 us -> 21.1 us
    pallas_call x7, Pallas kernels: 14.1 us -> 79.1 us  [the longest x1 53.6 us: prepare(): pl.pallas_call(prepare_kernel, out_shape=(jax.ShapeDtypeStruct((rows + 16...]
    ppermute x32 -> x28, waiting for transfers between devices: 96.6 us -> 47.4 us  [shift(): return lax.ppermute(x, axis, [(i, (i + by) % n) for i in range(n)])]
    all_gather x1 -> x0, blocking collectives: 22.4 us -> none  [shards(): lax.all_gather(jnp.concatenate([routes.T.astype(F32), route_gain.T], axis...]
    unnamed x102 -> x70, local copies, waits for them, and re-layouts: 20 us -> 6.68 us
    ppermute x21 -> x20, waiting for transfers between devices: 76.4 us -> 66.8 us  [swap(): return lax.ppermute(x, axes, [(i, i ^ k) for i in range(n)])]
    ppermute x21 -> x20, starting transfers between devices: 49.7 us -> 55.1 us  [swap(): return lax.ppermute(x, axes, [(i, i ^ k) for i in range(n)])]
    pallas_call x2, Pallas kernels: 10.6 us -> 14.7 us  [answers_of(): pl.pallas_call(functools.partial(answer_kernel, sizes), out_shape=tuple(s...]
    ppermute x32 -> x28, starting transfers between devices: 39.5 us -> 37.6 us  [shift(): return lax.ppermute(x, axis, [(i, (i + by) % n) for i in range(n)])]
  transfers between devices with their start and end apart: 54 -> 49, of which waited for: 17 -> 22; matrix products, arithmetic and copies ran while one was open for 4% -> 4% of each run, Pallas kernels for 10% -> 15%
where the time goes in v2:
time: 371 us; the launch traced here: 366 us
  Pallas kernels  121 us (33%)
  waiting for transfers between devices  114 us (31%)
  starting transfers between devices  92.8 us (25%)
  local copies, waits for them, and re-layouts  21.1 us (6%)
  between operations  14.6 us (4%)
    ppermute x20, waiting for transfers between devices, swap(): return lax.ppermute(x, axes, [(i, i ^ k) for i in range(n)])  66.8 us
    ppermute x20, starting transfers between devices, swap(): return lax.ppermute(x, axes, [(i, i ^ k) for i in range(n)])  55.1 us
    pallas_call x1, Pallas kernels, prepare(): pl.pallas_call(prepare_kernel, out_shape=(jax.ShapeDtypeStruct((rows + 16...  53.6 us
    ppermute x28, waiting for transfers between devices, shift(): return lax.ppermute(x, axis, [(i, (i + by) % n) for i in range(n)])  47.4 us
    ppermute x28, starting transfers between devices, shift(): return lax.ppermute(x, axis, [(i, (i + by) % n) for i in range(n)])  37.6 us
    pallas_call x2, Pallas kernels, hidden_of(): pl.pallas_call(functools.partial(hidden_kernel, n_rows), out_shape=jax.Sh...  18.9 us
    pallas_call x4, Pallas kernels, combine(): pl.pallas_call(functools.partial(combine_kernel, blocks, first, start, le...  16.1 us
    pallas_call x2, Pallas kernels, answers_of(): pl.pallas_call(functools.partial(answer_kernel, sizes), out_shape=tuple(s...  14.7 us
  transfers between devices with their start and end apart: 49, of which 22 were waited for; matrix products, arithmetic and copies ran while one was open for 4% of the time, Pallas kernels for 15%

profile of v2, /device:TPU:1, one launch (start us, length us, event | category | flops | bytes accessed | tf_op | source)
XLA Modules:
  0.0 365.8 jit_solution(3915189080865902831)
XLA Ops:
  7.2 53.6 %shard_map.95 = (bf16[144,2048]{1,0:T(8,128)(2,1)}, bf16[2304,256]{1,0:T(8,128)(2,1)}) custom-call(bf16[128,2048]{1,0:T(8,128)(2,1)} %tokens.3, s32[6,128]{1,0:T(8,128)} %bitcast.24, f32[6,128]{1,0:T(8,128)} %bitcast.25, bf16[256,768]{1,0:T(8,128)(2,1)} %bitcast.20, bf16[256,768]{1,0:T(8,128)(2,1)} %bitcast.21, bf16[768,256]{1,0:T(8,128)(2,1)} %bitcast.22), custom_call_target="tpu_custom_call" | custom-call | flops 65536 | bytes 4194304 | tf_op jit(solution)/shard_map/pallas_call | solution.py:67
  60.8 2.2 collective-permute-start.4
  67.4 3.9 %collective-permute-start.1 = (bf16[144,2048]{1,0:T(8,128)(2,1)}, bf16[144,2048]{1,0:T(8,128)(2,1)S(1)}, u32[]{:S(2)}, u32[]{:S(2)}) collective-permute-start(bf16[144,2048]{1,0:T(8,128)(2,1)} %get-tuple-element.117.refs_4_.refs_9_), channel_id=1, source_target_pairs={{0,28},{4,0},{8,4},{12,8},{16,12},{20,16},{24,20},{28,24},{1,29},{... | collective-permute-start | bytes 1769480 | tf_op jit(solution)/shard_map/ppermute | solution.py:30
  71.3 11.6 %collective-permute-done.refs_2_.refs_7_ = bf16[144,2048]{1,0:T(8,128)(2,1)S(1)} collective-permute-done((bf16[144,2048]{1,0:T(8,128)(2,1)}, bf16[144,2048]{1,0:T(8,128)(2,1)S(1)}, u32[]{:S(2)}, u32[]{:S(2)}) %collective-permute-start) | collective-permute-done | bytes 589856 | tf_op jit(solution)/shard_map/ppermute | solution.py:30
  82.9 3.3 collective-permute-start.3
  89.6 3.0 collective-permute-done.6.refs_9_.refs_6_
  92.6 4.8 %collective-permute-done.2.refs_0_.refs_5_ = bf16[144,2048]{1,0:T(8,128)(2,1)} collective-permute-done((bf16[144,2048]{1,0:T(8,128)(2,1)S(1)}, bf16[144,2048]{1,0:T(8,128)(2,1)}, u32[]{:S(2)}, u32[]{:S(2)}) %collective-permute-start.2) | collective-permute-done | bytes 589856 | tf_op jit(solution)/shard_map/ppermute | solution.py:30
  97.3 2.7 collective-permute-start.13
  100.0 2.7 collective-permute-start.8
  103.4 5.0 %shard_map.96 = (bf16[160,2048]{1,0:T(8,128)(2,1)}, bf16[160,2048]{1,0:T(8,128)(2,1)}, bf16[160,2048]{1,0:T(8,128)(2,1)}, bf16[160,2048]{1,0:T(8,128)(2,1)}, f32[20,128]{1,0:T(8,128)}, /*index=5*/f32[20,128]{1,0:T(8,128)}) custom-call(s32[2]{0:T(128)} %pad_add_fusion.place, bf16[144,2048]{1,0:T(8,128)(2,1)} %collective-permute-done.2.refs_0_.refs_5_, ...), custom_call_target="tpu_custom_call" | custom-call | flops 335544320 | bytes 5242880 | tf_op jit(solution)/shard_map/pallas_call | solution.py:124
  108.4 2.5 collective-permute-start.10
  110.9 5.3 %collective-permute-start.11 = (bf16[160,2048]{1,0:T(8,128)(2,1)}, bf16[160,2048]{1,0:T(8,128)(2,1)S(1)}, u32[]{:S(2)}, u32[]{:S(2)}) collective-permute-start(bf16[160,2048]{1,0:T(8,128)(2,1)} %get-tuple-element.128), channel_id=1, source_target_pairs={{0,3},{1,2},{2,1},{3,0},{4,7},{5,6},{6,5},{7,4},{8,11},{9,10},{10,... | collective-permute-start | bytes 1966088 | tf_op jit(solution)/shard_map/ppermute | solution.py:35
  118.3 4.0 %collective-permute-done.10.refs_2_ = bf16[160,2048]{1,0:T(8,128)(2,1)S(1)} collective-permute-done((bf16[160,2048]{1,0:T(8,128)(2,1)}, bf16[160,2048]{1,0:T(8,128)(2,1)S(1)}, u32[]{:S(2)}, u32[]{:S(2)}) %collective-permute-start.10) | collective-permute-done | bytes 655392 | tf_op jit(solution)/shard_map/ppermute | solution.py:35
  123.2 2.4 collective-permute-start.15
  126.6 14.1 %collective-permute-done.11.refs_3_ = bf16[160,2048]{1,0:T(8,128)(2,1)S(1)} collective-permute-done((bf16[160,2048]{1,0:T(8,128)(2,1)}, bf16[160,2048]{1,0:T(8,128)(2,1)S(1)}, u32[]{:S(2)}, u32[]{:S(2)}) %collective-permute-start.11) | collective-permute-done | bytes 655392 | tf_op jit(solution)/shard_map/ppermute | solution.py:35
  145.8 4.6 %collective-permute-done.14.refs_0_ = bf16[64,2048]{1,0:T(8,128)(2,1)S(1)} collective-permute-done((bf16[64,2048]{1,0:T(8,128)(2,1)S(1)}, bf16[64,2048]{1,0:T(8,128)(2,1)S(1)}, u32[]{:S(2)}, u32[]{:S(2)}) %collective-permute-start.14) | collective-permute-done | bytes 262176 | tf_op jit(solution)/shard_map/ppermute | solution.py:30
  151.2 4.4 %shard_map.97 = (bf16[96,2048]{1,0:T(8,128)(2,1)}, bf16[96,2048]{1,0:T(8,128)(2,1)}, bf16[96,2048]{1,0:T(8,128)(2,1)}, bf16[96,2048]{1,0:T(8,128)(2,1)}, f32[12,128]{1,0:T(8,128)}, /*index=5*/f32[12,128]{1,0:T(8,128)}) custom-call(s32[2]{0:T(128)} %pad_add_fusion.place, bf16[64,2048]{1,0:T(8,128)(2,1)} %copy-done.26, ...), custom_call_target="tpu_custom_call" | custom-call | flops 201326592 | bytes 3145728 | tf_op jit(solution)/shard_map/pallas_call | solution.py:124
  156.0 3.3 collective-permute-start.22
  162.9 2.7 collective-permute-start.19
  165.6 2.9 collective-permute-done.21.refs_2_
  172.7 4.4 %collective-permute-done.22.refs_3_ = bf16[96,2048]{1,0:T(8,128)(2,1)S(1)} collective-permute-done((bf16[96,2048]{1,0:T(8,128)(2,1)}, bf16[96,2048]{1,0:T(8,128)(2,1)S(1)}, u32[]{:S(2)}, u32[]{:S(2)}) %collective-permute-start.22) | collective-permute-done | bytes 393248 | tf_op jit(solution)/shard_map/ppermute | solution.py:35
  177.0 4.6 %collective-permute-done.16.refs_7_ = bf16[768,256]{1,0:T(8,128)(2,1)S(1)} collective-permute-done((bf16[768,256]{1,0:T(8,128)(2,1)}, bf16[768,256]{1,0:T(8,128)(2,1)S(1)}, u32[]{:S(2)}, u32[]{:S(2)}) %collective-permute-start.16) | collective-permute-done | bytes 393248 | tf_op jit(solution)/shard_map/ppermute | solution.py:30
  183.8 3.3 collective-permute-start.24
  187.1 2.7 collective-permute-start.26
  189.8 10.5 %shard_map.98.refs_0_ = bf16[640,768]{1,0:T(8,128)(2,1)} custom-call(s32[8]{0:T(128)} %broadcast_multiply_fusion.offsets, bf16[160,2048]{1,0:T(8,128)(2,1)} %get-tuple-element.150.refs_0_, bf16[160,2048]{1,0:T(8,128)(2,1)} %copy-done.34, bf16[160,2048]{1,0:T(8,128)(2,1)} %copy-done.32, bf16[160,2048]{1,0:T(8,128)(2,1)} %copy-done.33, ...), custom_call_target="tpu_custom_call" | custom-call | flops 4026531840 | bytes 8388608 | tf_op jit(solution)/shard_map/pallas_call | solution.py:175
  200.3 8.4 %shard_map.99.refs_0_ = bf16[384,768]{1,0:T(8,128)(2,1)} custom-call(s32[8]{0:T(128)} %broadcast_multiply_fusion.offsets, bf16[96,2048]{1,0:T(8,128)(2,1)} %get-tuple-element.158.refs_0_, bf16[96,2048]{1,0:T(8,128)(2,1)} %copy-done.15, bf16[96,2048]{1,0:T(8,128)(2,1)} %collective-permute-done.21.refs_2_, bf16[96,2048]{1,0:T(8,128)(2,1)} %copy-done.16, ...), custom_call_target="tpu_custom_call" | custom-call | flops 2415919104 | bytes 8388608 | tf_op jit(solution)/shard_map/pallas_call | solution.py:175
  210.3 6.7 %shard_map.100 = (bf16[32,2048]{1,0:T(8,128)(2,1)}, bf16[32,2048]{1,0:T(8,128)(2,1)}, bf16[32,2048]{1,0:T(8,128)(2,1)}, bf16[32,2048]{1,0:T(8,128)(2,1)}, bf16[6...) custom-call(s32[8]{0:T(128)} %broadcast_multiply_fusion.offsets, ...), custom_call_target="tpu_custom_call" | custom-call | flops 1207959552 | bytes 8388608 | tf_op jit(solution)/shard_map/pallas_call | solution.py:228
  217.0 16.2 %collective-permute-start.27 = (bf16[32,2048]{1,0:T(8,128)(2,1)}, bf16[32,2048]{1,0:T(8,128)(2,1)S(1)}, u32[]{:S(2)}, u32[]{:S(2)}) collective-permute-start(bf16[32,2048]{1,0:T(8,128)(2,1)} %get-tuple-element.167), channel_id=1, source_target_pairs={{0,1},{1,0},{2,3},{3,2},{4,5},{5,4},{6,7},{7,6},{8,9},{9,8},{10,11... | collective-permute-start | bytes 393224 | tf_op jit(solution)/shard_map/ppermute | solution.py:35
  233.2 13.0 %collective-permute-start.29 = (bf16[32,2048]{1,0:T(8,128)(2,1)}, bf16[32,2048]{1,0:T(8,128)(2,1)S(1)}, u32[]{:S(2)}, u32[]{:S(2)}) collective-permute-start(bf16[32,2048]{1,0:T(8,128)(2,1)} %get-tuple-element.169), channel_id=1, source_target_pairs={{0,3},{1,2},{2,1},{3,0},{4,7},{5,6},{6,5},{7,4},{8,11},{9,10},{10,... | collective-permute-start | bytes 393224 | tf_op jit(solution)/shard_map/ppermute | solution.py:35
  246.2 8.0 %shard_map.101 = (bf16[64,2048]{1,0:T(8,128)(2,1)}, bf16[64,2048]{1,0:T(8,128)(2,1)}, bf16[64,2048]{1,0:T(8,128)(2,1)}, bf16[64,2048]{1,0:T(8,128)(2,1)}, bf16[9...) custom-call(s32[8]{0:T(128)} %broadcast_multiply_fusion.offsets, ...), custom_call_target="tpu_custom_call" | custom-call | flops 2013265920 | bytes 8388608 | tf_op jit(solution)/shard_map/pallas_call | solution.py:228
  255.0 3.5 shard_map.102
  260.7 3.1 collective-permute-start.34
  263.8 2.7 collective-permute-done.30.refs_4_
  267.8 2.5 collective-permute-done.33.refs_2_
  270.4 5.8 %collective-permute-done.34.refs_3_ = bf16[64,2048]{1,0:T(8,128)(2,1)} collective-permute-done((bf16[64,2048]{1,0:T(8,128)(2,1)}, bf16[64,2048]{1,0:T(8,128)(2,1)}, u32[]{:S(2)}, u32[]{:S(2)}) %collective-permute-start.34) | collective-permute-done | bytes 262176 | tf_op jit(solution)/shard_map/ppermute | solution.py:35
  276.2 4.1 %shard_map.103 = (bf16[128,2048]{1,0:T(8,128)(2,1)}, bf16[128,2048]{1,0:T(8,128)(2,1)}) custom-call(f32[12,128]{1,0:T(8,128)} %get-tuple-element.135.code, f32[12,128]{1,0:T(8,128)} %get-tuple-element.136.gain, bf16[64,2048]{1,0:T(8,128)(2,1)} %get-tuple-element.183.refs_0_, bf16[64,2048]{1,0:T(8,128)(2,1)} %copy-done.23, bf16[64,2048]{1,0:T(8,128)(2,1)} %copy-done.24, ...), custom_call_target="tpu_custom_call" | custom-call | flops 268435456 | bytes 2097152 | tf_op jit(solution)/shard_map/pallas_call | solution.py:275
  282.6 3.1 collective-permute-start.39
  285.8 6.5 %collective-permute-done.38.refs_2_ = bf16[64,2048]{1,0:T(8,128)(2,1)S(1)} collective-permute-done((bf16[64,2048]{1,0:T(8,128)(2,1)}, bf16[64,2048]{1,0:T(8,128)(2,1)S(1)}, u32[]{:S(2)}, u32[]{:S(2)}) %collective-permute-start.38) | collective-permute-done | bytes 262176 | tf_op jit(solution)/shard_map/ppermute | solution.py:35
  292.3 5.7 %collective-permute-done.39.refs_3_ = bf16[64,2048]{1,0:T(8,128)(2,1)S(1)} collective-permute-done((bf16[64,2048]{1,0:T(8,128)(2,1)}, bf16[64,2048]{1,0:T(8,128)(2,1)S(1)}, u32[]{:S(2)}, u32[]{:S(2)}) %collective-permute-start.39) | collective-permute-done | bytes 262176 | tf_op jit(solution)/shard_map/ppermute | solution.py:35
  299.0 4.2 %shard_map.104 = (bf16[128,2048]{1,0:T(8,128)(2,1)}, bf16[128,2048]{1,0:T(8,128)(2,1)}) custom-call(f32[20,128]{1,0:T(8,128)} %get-tuple-element.123.code, f32[20,128]{1,0:T(8,128)} %get-tuple-element.124.gain, bf16[64,2048]{1,0:T(8,128)(2,1)} %get-tuple-element.212.refs_0_, bf16[64,2048]{1,0:T(8,128)(2,1)} %copy-done.25, bf16[64,2048]{1,0:T(8,128)(2,1)} %copy-done.27, ...), custom_call_target="tpu_custom_call" | custom-call | flops 268435456 | bytes 2097152 | tf_op jit(solution)/shard_map/pallas_call | solution.py:275
  306.2 3.0 collective-permute-start.44
  309.2 9.3 %collective-permute-done.43.refs_2_.a2 = bf16[96,2048]{1,0:T(8,128)(2,1)S(1)} collective-permute-done((bf16[96,2048]{1,0:T(8,128)(2,1)}, bf16[96,2048]{1,0:T(8,128)(2,1)S(1)}, u32[]{:S(2)}, u32[]{:S(2)}) %collective-permute-start.43) | collective-permute-done | bytes 393248 | tf_op jit(solution)/shard_map/ppermute | solution.py:35
  318.5 8.5 %collective-permute-done.44.refs_3_.a3 = bf16[96,2048]{1,0:T(8,128)(2,1)S(1)} collective-permute-done((bf16[96,2048]{1,0:T(8,128)(2,1)}, bf16[96,2048]{1,0:T(8,128)(2,1)S(1)}, u32[]{:S(2)}, u32[]{:S(2)}) %collective-permute-start.44) | collective-permute-done | bytes 393248 | tf_op jit(solution)/shard_map/ppermute | solution.py:35
  327.8 4.3 %shard_map.105 = (bf16[128,2048]{1,0:T(8,128)(2,1)}, bf16[128,2048]{1,0:T(8,128)(2,1)}) custom-call(f32[20,128]{1,0:T(8,128)} %get-tuple-element.123.code, f32[20,128]{1,0:T(8,128)} %get-tuple-element.124.gain, bf16[96,2048]{1,0:T(8,128)(2,1)} %get-tuple-element.211.refs_0_.a0, bf16[96,2048]{1,0:T(8,128)(2,1)} %copy-done.4, bf16[96,2048]{1,0:T(8,128)(2,1)} %copy-done.5, ...), custom_call_target="tpu_custom_call" | custom-call | flops 268435456 | bytes 2097152 | tf_op jit(solution)/shard_map/pallas_call | solution.py:275
  332.1 3.0 collective-permute-start.45
  335.7 10.7 %collective-permute-done.45.left = bf16[128,2048]{1,0:T(8,128)(2,1)S(1)} collective-permute-done((bf16[128,2048]{1,0:T(8,128)(2,1)}, bf16[128,2048]{1,0:T(8,128)(2,1)S(1)}, u32[]{:S(2)}, u32[]{:S(2)}) %collective-permute-start.45) | collective-permute-done | bytes 524320 | tf_op jit(solution)/shard_map/ppermute | solution.py:30
  346.5 3.0 collective-permute-done.46.right
  350.3 8.4 %shard_map.106 = (bf16[128,2048]{1,0:T(8,128)(2,1)}, bf16[128,1536]{1,0:T(8,128)(2,1)}) custom-call(s32[2]{0:T(128)} %add_multiply_fusion.offsets, f32[20,128]{1,0:T(8,128)} %get-tuple-element.123.code, f32[20,128]{1,0:T(8,128)} %get-tuple-element.124.gain, bf16[96,2048]{1,0:T(8,128)(2,1)} %get-tuple-element.211.refs_0_.a0, bf16[96,2048]{1,0:T(8,128)(2,1)} %copy-done.4, ...), custom_call_target="tpu_custom_call" | custom-call | flops 805306368 | bytes 8388608 | tf_op jit(solution)/shard_map/pallas_call | solution.py:322
  (148 shorter events, 42.9 us)
Async XLA Ops:
  7.2 319.9 %all-gather.2.cloned.1.call-start = ((), (), s32[]{:S(2)}) async-start(), calls=%async_computation | async-start | bytes 3538944 | tf_op jit(solution)/shard_map/all_gather | solution.py:374
  60.8 27.5 %collective-permute-start.4 = (bf16[2304,256]{1,0:T(8,128)(2,1)}, bf16[2304,256]{1,0:T(8,128)(2,1)S(1)}, u32[]{:S(2)}, u32[]{:S(2)}) collective-permute-start(bf16[2304,256]{1,0:T(8,128)(2,1)} %get-tuple-element.118.refs_4_.refs_1_), channel_id=1, source_target_pairs={{0,32},{32,64},{64,96},{96,0},{1,33},{33,65},{65,97},{97,1},{2,34}... | collective-permute-start | bytes 3538952 | tf_op jit(solution)/shard_map/ppermute | solution.py:30
  63.0 26.6 %collective-permute-start.5 = (bf16[2304,256]{1,0:T(8,128)(2,1)}, bf16[2304,256]{1,0:T(8,128)(2,1)}, u32[]{:S(2)}, u32[]{:S(2)}) collective-permute-start(bf16[2304,256]{1,0:T(8,128)(2,1)} %get-tuple-element.118.refs_4_.refs_1_), channel_id=1, source_target_pairs={{0,96},{32,0},{64,32},{96,64},{1,97},{33,1},{65,33},{97,65},{2,98}... | collective-permute-start | bytes 3538952 | tf_op jit(solution)/shard_map/ppermute | solution.py:30
  64.5 18.4 %collective-permute-start = (bf16[144,2048]{1,0:T(8,128)(2,1)}, bf16[144,2048]{1,0:T(8,128)(2,1)S(1)}, u32[]{:S(2)}, u32[]{:S(2)}) collective-permute-start(bf16[144,2048]{1,0:T(8,128)(2,1)} %get-tuple-element.117.refs_4_.refs_9_), channel_id=1, source_target_pairs={{0,4},{4,8},{8,12},{12,16},{16,20},{20,24},{24,28},{28,0},{1,5},{5... | collective-permute-start | bytes 1769480 | tf_op jit(solution)/shard_map/ppermute | solution.py:30
  66.2 26.4 %collective-permute-start.6 = (bf16[2304,256]{1,0:T(8,128)(2,1)}, bf16[2304,256]{1,0:T(8,128)(2,1)}, u32[]{:S(2)}, u32[]{:S(2)}) collective-permute-start(bf16[2304,256]{1,0:T(8,128)(2,1)} %get-tuple-element.118.refs_4_.refs_1_), channel_id=1, source_target_pairs={{0,128},{128,0},{1,129},{129,1},{2,130},{130,2},{3,131},{131,3},{4... | collective-permute-start | bytes 3538952 | tf_op jit(solution)/shard_map/ppermute | solution.py:35
  67.4 15.5 %collective-permute-start.1 = (bf16[144,2048]{1,0:T(8,128)(2,1)}, bf16[144,2048]{1,0:T(8,128)(2,1)S(1)}, u32[]{:S(2)}, u32[]{:S(2)}) collective-permute-start(bf16[144,2048]{1,0:T(8,128)(2,1)} %get-tuple-element.117.refs_4_.refs_9_), channel_id=1, source_target_pairs={{0,28},{4,0},{8,4},{12,8},{16,12},{20,16},{24,20},{28,24},{1,29},{... | collective-permute-start | bytes 1769480 | tf_op jit(solution)/shard_map/ppermute | solution.py:30
  82.9 14.4 %collective-permute-start.2 = (bf16[144,2048]{1,0:T(8,128)(2,1)S(1)}, bf16[144,2048]{1,0:T(8,128)(2,1)}, u32[]{:S(2)}, u32[]{:S(2)}) collective-permute-start(bf16[144,2048]{1,0:T(8,128)(2,1)S(1)} %collective-permute-done.refs_2_.refs_7_), channel_id=1, source_target_pairs={{0,4},{4,8},{8,12},{12,16},{16,20},{20,24},{24,28},{28,0},{1,5},{5... | collective-permute-start | bytes 1769480 | tf_op jit(solution)/shard_map/ppermute | solution.py:30
  82.9 14.4 %collective-permute-start.3 = (bf16[144,2048]{1,0:T(8,128)(2,1)S(1)}, bf16[144,2048]{1,0:T(8,128)(2,1)}, u32[]{:S(2)}, u32[]{:S(2)}) collective-permute-start(bf16[144,2048]{1,0:T(8,128)(2,1)S(1)} %collective-permute-done.1.refs_3_.refs_8_), channel_id=1, source_target_pairs={{0,28},{4,0},{8,4},{12,8},{16,12},{20,16},{24,20},{28,24},{1,29},{... | collective-permute-start | bytes 1769480 | tf_op jit(solution)/shard_map/ppermute | solution.py:30
  97.3 13.6 %collective-permute-start.13 = (bf16[144,2048]{1,0:T(8,128)(2,1)}, bf16[144,2048]{1,0:T(8,128)(2,1)}, u32[]{:S(2)}, u32[]{:S(2)}) collective-permute-start(bf16[144,2048]{1,0:T(8,128)(2,1)} %collective-permute-done.3.refs_1_.refs_6_), channel_id=1, source_target_pairs={{0,28},{4,0},{8,4},{12,8},{16,12},{20,16},{24,20},{28,24},{1,29},{... | collective-permute-start | bytes 1769480 | tf_op jit(solution)/shard_map/ppermute | solution.py:30
  100.0 16.2 %collective-permute-start.12 = (bf16[144,2048]{1,0:T(8,128)(2,1)}, bf16[144,2048]{1,0:T(8,128)(2,1)}, u32[]{:S(2)}, u32[]{:S(2)}) collective-permute-start(bf16[144,2048]{1,0:T(8,128)(2,1)} %collective-permute-done.2.refs_0_.refs_5_), channel_id=1, source_target_pairs={{0,4},{4,8},{8,12},{12,16},{16,20},{20,24},{24,28},{28,0},{1,5},{5... | collective-permute-start | bytes 1769480 | tf_op jit(solution)/shard_map/ppermute | solution.py:30
  100.0 51.1 %collective-permute-start.7 = (bf16[2304,256]{1,0:T(8,128)(2,1)}, bf16[2304,256]{1,0:T(8,128)(2,1)}, u32[]{:S(2)}, u32[]{:S(2)}) collective-permute-start(bf16[2304,256]{1,0:T(8,128)(2,1)} %collective-permute-done.6.refs_9_.refs_6_), channel_id=1, source_target_pairs={{0,32},{32,64},{64,96},{96,0},{1,33},{33,65},{65,97},{97,1},{2,34}... | collective-permute-start | bytes 3538952 | tf_op jit(solution)/shard_map/ppermute | solution.py:30
  100.0 51.1 %collective-permute-start.8 = (bf16[2304,256]{1,0:T(8,128)(2,1)}, bf16[2304,256]{1,0:T(8,128)(2,1)}, u32[]{:S(2)}, u32[]{:S(2)}) collective-permute-start(bf16[2304,256]{1,0:T(8,128)(2,1)} %collective-permute-done.6.refs_9_.refs_6_), channel_id=1, source_target_pairs={{0,96},{32,0},{64,32},{96,64},{1,97},{33,1},{65,33},{97,65},{2,98}... | collective-permute-start | bytes 3538952 | tf_op jit(solution)/shard_map/ppermute | solution.py:30
  108.4 14.0 %collective-permute-start.10 = (bf16[160,2048]{1,0:T(8,128)(2,1)}, bf16[160,2048]{1,0:T(8,128)(2,1)S(1)}, u32[]{:S(2)}, u32[]{:S(2)}) collective-permute-start(bf16[160,2048]{1,0:T(8,128)(2,1)} %get-tuple-element.127), channel_id=1, source_target_pairs={{0,2},{1,3},{2,0},{3,1},{4,6},{5,7},{6,4},{7,5},{8,10},{9,11},{10,... | collective-permute-start | bytes 1966088 | tf_op jit(solution)/shard_map/ppermute | solution.py:35
  110.9 29.8 %collective-permute-start.11 = (bf16[160,2048]{1,0:T(8,128)(2,1)}, bf16[160,2048]{1,0:T(8,128)(2,1)S(1)}, u32[]{:S(2)}, u32[]{:S(2)}) collective-permute-start(bf16[160,2048]{1,0:T(8,128)(2,1)} %get-tuple-element.128), channel_id=1, source_target_pairs={{0,3},{1,2},{2,1},{3,0},{4,7},{5,6},{6,5},{7,4},{8,11},{9,10},{10,... | collective-permute-start | bytes 1966088 | tf_op jit(solution)/shard_map/ppermute | solution.py:35
  116.2 29.6 %collective-permute-start.9 = (bf16[160,2048]{1,0:T(8,128)(2,1)}, bf16[160,2048]{1,0:T(8,128)(2,1)S(1)}, u32[]{:S(2)}, u32[]{:S(2)}) collective-permute-start(bf16[160,2048]{1,0:T(8,128)(2,1)} %get-tuple-element.126), channel_id=1, source_target_pairs={{0,1},{1,0},{2,3},{3,2},{4,5},{5,4},{6,7},{7,6},{8,9},{9,8},{10,11... | collective-permute-start | bytes 1966088 | tf_op jit(solution)/shard_map/ppermute | solution.py:35
  123.2 27.2 %collective-permute-start.15 = (bf16[80,2048]{1,0:T(8,128)(2,1)S(1)}, bf16[80,2048]{1,0:T(8,128)(2,1)}, u32[]{:S(2)}, u32[]{:S(2)}) collective-permute-start(bf16[80,2048]{1,0:T(8,128)(2,1)S(1)} %slice.41), channel_id=1, source_target_pairs={{0,28},{4,0},{8,4},{12,8},{16,12},{20,16},{24,20},{28,24},{1,29},{... | collective-permute-start | bytes 983048 | tf_op jit(solution)/shard_map/ppermute | solution.py:30
  140.7 9.8 %collective-permute-start.14 = (bf16[64,2048]{1,0:T(8,128)(2,1)S(1)}, bf16[64,2048]{1,0:T(8,128)(2,1)S(1)}, u32[]{:S(2)}, u32[]{:S(2)}) collective-permute-start(bf16[64,2048]{1,0:T(8,128)(2,1)S(1)} %slice.40), channel_id=1, source_target_pairs={{0,4},{4,8},{8,12},{12,16},{16,20},{20,24},{24,28},{28,0},{1,5},{5... | collective-permute-start | bytes 786440 | tf_op jit(solution)/shard_map/ppermute | solution.py:30
  155.6 10.0 %collective-permute-start.20 = (bf16[96,2048]{1,0:T(8,128)(2,1)}, bf16[96,2048]{1,0:T(8,128)(2,1)S(1)}, u32[]{:S(2)}, u32[]{:S(2)}) collective-permute-start(bf16[96,2048]{1,0:T(8,128)(2,1)} %get-tuple-element.141), channel_id=1, source_target_pairs={{0,1},{1,0},{2,3},{3,2},{4,5},{5,4},{6,7},{7,6},{8,9},{9,8},{10,11... | collective-permute-start | bytes 1179656 | tf_op jit(solution)/shard_map/ppermute | solution.py:35
  156.0 12.4 %collective-permute-start.21 = (bf16[96,2048]{1,0:T(8,128)(2,1)}, bf16[96,2048]{1,0:T(8,128)(2,1)}, u32[]{:S(2)}, u32[]{:S(2)}) collective-permute-start(bf16[96,2048]{1,0:T(8,128)(2,1)} %get-tuple-element.142), channel_id=1, source_target_pairs={{0,2},{1,3},{2,0},{3,1},{4,6},{5,7},{6,4},{7,5},{8,10},{9,11},{10,... | collective-permute-start | bytes 1179656 | tf_op jit(solution)/shard_map/ppermute | solution.py:35
  156.0 21.0 %collective-permute-start.22 = (bf16[96,2048]{1,0:T(8,128)(2,1)}, bf16[96,2048]{1,0:T(8,128)(2,1)S(1)}, u32[]{:S(2)}, u32[]{:S(2)}) collective-permute-start(bf16[96,2048]{1,0:T(8,128)(2,1)} %get-tuple-element.143), channel_id=1, source_target_pairs={{0,3},{1,2},{2,1},{3,0},{4,7},{5,6},{6,5},{7,4},{8,11},{9,10},{10,... | collective-permute-start | bytes 1179656 | tf_op jit(solution)/shard_map/ppermute | solution.py:35
  161.1 15.9 %collective-permute-start.18 = (bf16[768,256]{1,0:T(8,128)(2,1)}, bf16[768,256]{1,0:T(8,128)(2,1)S(1)}, u32[]{:S(2)}, u32[]{:S(2)}) collective-permute-start(bf16[768,256]{1,0:T(8,128)(2,1)} %slice.36), channel_id=1, source_target_pairs={{0,32},{32,64},{64,96},{96,0},{1,33},{33,65},{65,97},{97,1},{2,34}... | collective-permute-start | bytes 1179656 | tf_op jit(solution)/shard_map/ppermute | solution.py:30
  162.9 14.2 %collective-permute-start.19 = (bf16[768,256]{1,0:T(8,128)(2,1)}, bf16[768,256]{1,0:T(8,128)(2,1)S(1)}, u32[]{:S(2)}, u32[]{:S(2)}) collective-permute-start(bf16[768,256]{1,0:T(8,128)(2,1)} %slice.37), channel_id=1, source_target_pairs={{0,96},{32,0},{64,32},{96,64},{1,97},{33,1},{65,33},{97,65},{2,98}... | collective-permute-start | bytes 1179656 | tf_op jit(solution)/shard_map/ppermute | solution.py:30
  165.6 16.0 %collective-permute-start.16 = (bf16[768,256]{1,0:T(8,128)(2,1)}, bf16[768,256]{1,0:T(8,128)(2,1)S(1)}, u32[]{:S(2)}, u32[]{:S(2)}) collective-permute-start(bf16[768,256]{1,0:T(8,128)(2,1)} %slice.32), channel_id=1, source_target_pairs={{0,32},{32,64},{64,96},{96,0},{1,33},{33,65},{65,97},{97,1},{2,34}... | collective-permute-start | bytes 1179656 | tf_op jit(solution)/shard_map/ppermute | solution.py:30
  168.4 14.0 %collective-permute-start.17 = (bf16[768,256]{1,0:T(8,128)(2,1)}, bf16[768,256]{1,0:T(8,128)(2,1)S(1)}, u32[]{:S(2)}, u32[]{:S(2)}) collective-permute-start(bf16[768,256]{1,0:T(8,128)(2,1)} %slice.33), channel_id=1, source_target_pairs={{0,96},{32,0},{64,32},{96,64},{1,97},{33,1},{65,33},{97,65},{2,98}... | collective-permute-start | bytes 1179656 | tf_op jit(solution)/shard_map/ppermute | solution.py:30
  183.8 24.9 %collective-permute-start.23 = (bf16[384,256]{1,0:T(8,128)(2,1)}, bf16[384,256]{1,0:T(8,128)(2,1)S(1)}, u32[]{:S(2)}, u32[]{:S(2)}) collective-permute-start(bf16[384,256]{1,0:T(8,128)(2,1)} %slice.34), channel_id=1, source_target_pairs={{0,32},{32,64},{64,96},{96,0},{1,33},{33,65},{65,97},{97,1},{2,34}... | collective-permute-start | bytes 589832 | tf_op jit(solution)/shard_map/ppermute | solution.py:30
  183.8 25.0 %collective-permute-start.24 = (bf16[384,256]{1,0:T(8,128)(2,1)}, bf16[384,256]{1,0:T(8,128)(2,1)S(1)}, u32[]{:S(2)}, u32[]{:S(2)}) collective-permute-start(bf16[384,256]{1,0:T(8,128)(2,1)} %slice.35), channel_id=1, source_target_pairs={{0,96},{32,0},{64,32},{96,64},{1,97},{33,1},{65,33},{97,65},{2,98}... | collective-permute-start | bytes 589832 | tf_op jit(solution)/shard_map/ppermute | solution.py:30
  187.1 21.7 %collective-permute-start.25 = (bf16[384,256]{1,0:T(8,128)(2,1)}, bf16[384,256]{1,0:T(8,128)(2,1)S(1)}, u32[]{:S(2)}, u32[]{:S(2)}) collective-permute-start(bf16[384,256]{1,0:T(8,128)(2,1)} %slice.38), channel_id=1, source_target_pairs={{0,32},{32,64},{64,96},{96,0},{1,33},{33,65},{65,97},{97,1},{2,34}... | collective-permute-start | bytes 589832 | tf_op jit(solution)/shard_map/ppermute | solution.py:30
  187.1 21.7 %collective-permute-start.26 = (bf16[384,256]{1,0:T(8,128)(2,1)}, bf16[384,256]{1,0:T(8,128)(2,1)S(1)}, u32[]{:S(2)}, u32[]{:S(2)}) collective-permute-start(bf16[384,256]{1,0:T(8,128)(2,1)} %slice.39), channel_id=1, source_target_pairs={{0,96},{32,0},{64,32},{96,64},{1,97},{33,1},{65,33},{97,65},{2,98}... | collective-permute-start | bytes 589832 | tf_op jit(solution)/shard_map/ppermute | solution.py:30
  217.0 37.2 %collective-permute-start.27 = (bf16[32,2048]{1,0:T(8,128)(2,1)}, bf16[32,2048]{1,0:T(8,128)(2,1)S(1)}, u32[]{:S(2)}, u32[]{:S(2)}) collective-permute-start(bf16[32,2048]{1,0:T(8,128)(2,1)} %get-tuple-element.167), channel_id=1, source_target_pairs={{0,1},{1,0},{2,3},{3,2},{4,5},{5,4},{6,7},{7,6},{8,9},{9,8},{10,11... | collective-permute-start | bytes 393224 | tf_op jit(solution)/shard_map/ppermute | solution.py:35
  233.2 21.0 %collective-permute-start.28 = (bf16[32,2048]{1,0:T(8,128)(2,1)}, bf16[32,2048]{1,0:T(8,128)(2,1)S(1)}, u32[]{:S(2)}, u32[]{:S(2)}) collective-permute-start(bf16[32,2048]{1,0:T(8,128)(2,1)} %get-tuple-element.168), channel_id=1, source_target_pairs={{0,2},{1,3},{2,0},{3,1},{4,6},{5,7},{6,4},{7,5},{8,10},{9,11},{10,... | collective-permute-start | bytes 393224 | tf_op jit(solution)/shard_map/ppermute | solution.py:35
  233.2 21.1 %collective-permute-start.29 = (bf16[32,2048]{1,0:T(8,128)(2,1)}, bf16[32,2048]{1,0:T(8,128)(2,1)S(1)}, u32[]{:S(2)}, u32[]{:S(2)}) collective-permute-start(bf16[32,2048]{1,0:T(8,128)(2,1)} %get-tuple-element.169), channel_id=1, source_target_pairs={{0,3},{1,2},{2,1},{3,0},{4,7},{5,6},{6,5},{7,4},{8,11},{9,10},{10,... | collective-permute-start | bytes 393224 | tf_op jit(solution)/shard_map/ppermute | solution.py:35
  258.5 8.0 %collective-permute-start.30 = (bf16[64,2048]{1,0:T(8,128)(2,1)}, bf16[64,2048]{1,0:T(8,128)(2,1)S(1)}, u32[]{:S(2)}, u32[]{:S(2)}) collective-permute-start(bf16[64,2048]{1,0:T(8,128)(2,1)} %get-tuple-element.188), channel_id=1, source_target_pairs={{0,28},{4,0},{8,4},{12,8},{16,12},{20,16},{24,20},{28,24},{1,29},{... | collective-permute-start | bytes 786440 | tf_op jit(solution)/shard_map/ppermute | solution.py:30
  258.5 9.3 %collective-permute-start.31 = (bf16[64,2048]{1,0:T(8,128)(2,1)}, bf16[64,2048]{1,0:T(8,128)(2,1)S(1)}, u32[]{:S(2)}, u32[]{:S(2)}) collective-permute-start(bf16[64,2048]{1,0:T(8,128)(2,1)} %get-tuple-element.189), channel_id=1, source_target_pairs={{0,4},{4,8},{8,12},{12,16},{16,20},{20,24},{24,28},{28,0},{1,5},{5... | collective-permute-start | bytes 786440 | tf_op jit(solution)/shard_map/ppermute | solution.py:30
  260.0 7.8 %collective-permute-start.32 = (bf16[64,2048]{1,0:T(8,128)(2,1)}, bf16[64,2048]{1,0:T(8,128)(2,1)S(1)}, u32[]{:S(2)}, u32[]{:S(2)}) collective-permute-start(bf16[64,2048]{1,0:T(8,128)(2,1)} %get-tuple-element.190), channel_id=1, source_target_pairs={{0,1},{1,0},{2,3},{3,2},{4,5},{5,4},{6,7},{7,6},{8,9},{9,8},{10,11... | collective-permute-start | bytes 786440 | tf_op jit(solution)/shard_map/ppermute | solution.py:35
  260.7 9.7 %collective-permute-start.33 = (bf16[64,2048]{1,0:T(8,128)(2,1)}, bf16[64,2048]{1,0:T(8,128)(2,1)S(1)}, u32[]{:S(2)}, u32[]{:S(2)}) collective-permute-start(bf16[64,2048]{1,0:T(8,128)(2,1)} %get-tuple-element.191), channel_id=1, source_target_pairs={{0,2},{1,3},{2,0},{3,1},{4,6},{5,7},{6,4},{7,5},{8,10},{9,11},{10,... | collective-permute-start | bytes 786440 | tf_op jit(solution)/shard_map/ppermute | solution.py:35
  260.7 15.5 %collective-permute-start.34 = (bf16[64,2048]{1,0:T(8,128)(2,1)}, bf16[64,2048]{1,0:T(8,128)(2,1)}, u32[]{:S(2)}, u32[]{:S(2)}) collective-permute-start(bf16[64,2048]{1,0:T(8,128)(2,1)} %get-tuple-element.192), channel_id=1, source_target_pairs={{0,3},{1,2},{2,1},{3,0},{4,7},{5,6},{6,5},{7,4},{8,11},{9,10},{10,... | collective-permute-start | bytes 786440 | tf_op jit(solution)/shard_map/ppermute | solution.py:35
  280.3 17.7 %collective-permute-start.35 = (bf16[128,2048]{1,0:T(8,128)(2,1)}, bf16[128,2048]{1,0:T(8,128)(2,1)S(1)}, u32[]{:S(2)}, u32[]{:S(2)}) collective-permute-start(bf16[128,2048]{1,0:T(8,128)(2,1)} %get-tuple-element.202), channel_id=1, source_target_pairs={{0,28},{4,0},{8,4},{12,8},{16,12},{20,16},{24,20},{28,24},{1,29},{... | collective-permute-start | bytes 1572872 | tf_op jit(solution)/shard_map/ppermute | solution.py:30
  281.3 16.7 %collective-permute-start.36 = (bf16[128,2048]{1,0:T(8,128)(2,1)}, bf16[128,2048]{1,0:T(8,128)(2,1)S(1)}, u32[]{:S(2)}, u32[]{:S(2)}) collective-permute-start(bf16[128,2048]{1,0:T(8,128)(2,1)} %get-tuple-element.203), channel_id=1, source_target_pairs={{0,4},{4,8},{8,12},{12,16},{16,20},{20,24},{24,28},{28,0},{1,5},{5... | collective-permute-start | bytes 1572872 | tf_op jit(solution)/shard_map/ppermute | solution.py:30
  281.8 4.0 %collective-permute-start.37 = (bf16[64,2048]{1,0:T(8,128)(2,1)}, bf16[64,2048]{1,0:T(8,128)(2,1)S(1)}, u32[]{:S(2)}, u32[]{:S(2)}) collective-permute-start(bf16[64,2048]{1,0:T(8,128)(2,1)} %get-tuple-element.204), channel_id=1, source_target_pairs={{0,1},{1,0},{2,3},{3,2},{4,5},{5,4},{6,7},{7,6},{8,9},{9,8},{10,11... | collective-permute-start | bytes 786440 | tf_op jit(solution)/shard_map/ppermute | solution.py:35
  282.6 9.7 %collective-permute-start.38 = (bf16[64,2048]{1,0:T(8,128)(2,1)}, bf16[64,2048]{1,0:T(8,128)(2,1)S(1)}, u32[]{:S(2)}, u32[]{:S(2)}) collective-permute-start(bf16[64,2048]{1,0:T(8,128)(2,1)} %get-tuple-element.205), channel_id=1, source_target_pairs={{0,2},{1,3},{2,0},{3,1},{4,6},{5,7},{6,4},{7,5},{8,10},{9,11},{10,... | collective-permute-start | bytes 786440 | tf_op jit(solution)/shard_map/ppermute | solution.py:35
  282.6 15.3 %collective-permute-start.39 = (bf16[64,2048]{1,0:T(8,128)(2,1)}, bf16[64,2048]{1,0:T(8,128)(2,1)S(1)}, u32[]{:S(2)}, u32[]{:S(2)}) collective-permute-start(bf16[64,2048]{1,0:T(8,128)(2,1)} %get-tuple-element.206), channel_id=1, source_target_pairs={{0,3},{1,2},{2,1},{3,0},{4,7},{5,6},{6,5},{7,4},{8,11},{9,10},{10,... | collective-permute-start | bytes 786440 | tf_op jit(solution)/shard_map/ppermute | solution.py:35
  303.3 23.8 %collective-permute-start.40 = (bf16[128,2048]{1,0:T(8,128)(2,1)}, bf16[128,2048]{1,0:T(8,128)(2,1)}, u32[]{:S(2)}, u32[]{:S(2)}) collective-permute-start(bf16[128,2048]{1,0:T(8,128)(2,1)} %get-tuple-element.218), channel_id=1, source_target_pairs={{0,28},{4,0},{8,4},{12,8},{16,12},{20,16},{24,20},{28,24},{1,29},{... | collective-permute-start | bytes 1572872 | tf_op jit(solution)/shard_map/ppermute | solution.py:30
  305.5 21.6 %collective-permute-start.41 = (bf16[128,2048]{1,0:T(8,128)(2,1)}, bf16[128,2048]{1,0:T(8,128)(2,1)}, u32[]{:S(2)}, u32[]{:S(2)}) collective-permute-start(bf16[128,2048]{1,0:T(8,128)(2,1)} %get-tuple-element.219), channel_id=1, source_target_pairs={{0,4},{4,8},{8,12},{12,16},{16,20},{20,24},{24,28},{28,0},{1,5},{5... | collective-permute-start | bytes 1572872 | tf_op jit(solution)/shard_map/ppermute | solution.py:30
  306.1 12.5 %collective-permute-start.43 = (bf16[96,2048]{1,0:T(8,128)(2,1)}, bf16[96,2048]{1,0:T(8,128)(2,1)S(1)}, u32[]{:S(2)}, u32[]{:S(2)}) collective-permute-start(bf16[96,2048]{1,0:T(8,128)(2,1)} %get-tuple-element.221), channel_id=1, source_target_pairs={{0,2},{1,3},{2,0},{3,1},{4,6},{5,7},{6,4},{7,5},{8,10},{9,11},{10,... | collective-permute-start | bytes 1179656 | tf_op jit(solution)/shard_map/ppermute | solution.py:35
  306.2 20.9 %collective-permute-start.44 = (bf16[96,2048]{1,0:T(8,128)(2,1)}, bf16[96,2048]{1,0:T(8,128)(2,1)S(1)}, u32[]{:S(2)}, u32[]{:S(2)}) collective-permute-start(bf16[96,2048]{1,0:T(8,128)(2,1)} %get-tuple-element.222), channel_id=1, source_target_pairs={{0,3},{1,2},{2,1},{3,0},{4,7},{5,6},{6,5},{7,4},{8,11},{9,10},{10,... | collective-permute-start | bytes 1179656 | tf_op jit(solution)/shard_map/ppermute | solution.py:35
  327.1 22.4 %collective-permute-start.47 = (bf16[1536,1024]{1,0:T(8,128)(2,1)}, bf16[1536,1024]{1,0:T(8,128)(2,1)}, u32[]{:S(2)}, u32[]{:S(2)}) collective-permute-start(bf16[1536,1024]{1,0:T(8,128)(2,1)} %all-gather.2.cloned.1.call-done.q0), channel_id=1, source_target_pairs={{0,1},{1,0},{2,3},{3,2},{4,5},{5,4},{6,7},{7,6},{8,9},{9,8},{10,11... | collective-permute-start | bytes 9437192 | tf_op jit(solution)/shard_map/ppermute | solution.py:35
  332.1 14.3 %collective-permute-start.45 = (bf16[128,2048]{1,0:T(8,128)(2,1)}, bf16[128,2048]{1,0:T(8,128)(2,1)S(1)}, u32[]{:S(2)}, u32[]{:S(2)}) collective-permute-start(bf16[128,2048]{1,0:T(8,128)(2,1)} %get-tuple-element.229), channel_id=1, source_target_pairs={{0,28},{4,0},{8,4},{12,8},{16,12},{20,16},{24,20},{28,24},{1,29},{... | collective-permute-start | bytes 1572872 | tf_op jit(solution)/shard_map/ppermute | solution.py:30
  335.1 14.3 %collective-permute-start.46 = (bf16[128,2048]{1,0:T(8,128)(2,1)}, bf16[128,2048]{1,0:T(8,128)(2,1)S(1)}, u32[]{:S(2)}, u32[]{:S(2)}) collective-permute-start(bf16[128,2048]{1,0:T(8,128)(2,1)} %get-tuple-element.230), channel_id=1, source_target_pairs={{0,4},{4,8},{8,12},{12,16},{16,20},{20,24},{24,28},{28,0},{1,5},{5... | collective-permute-start | bytes 1572872 | tf_op jit(solution)/shard_map/ppermute | solution.py:30
  (36 other events, 409.5 us)
Sparse Core Ops, SparseCore 0:
  182.6 43.9 all-gather.1

commit v3 on v0

v3 whole, which is shorter than its diff:
```python
import functools

import jax
import jax.numpy as jnp
from jax import lax
from jax.experimental import pallas as pl
from jax.experimental.pallas import tpu as pltpu
from jax.sharding import Mesh, PartitionSpec as P

BF = jnp.bfloat16
F32 = jnp.float32
SLOTS = 32
ANY = pl.BlockSpec(memory_space=pltpu.HBM)
SMEM = pl.BlockSpec(memory_space=pltpu.SMEM)
VMEM = pl.BlockSpec(memory_space=pltpu.VMEM)
GROUPS = ((4,), (3, 5), (2, 6), (1, 7, 0))


def params(mib):
    return pltpu.CompilerParams(vmem_limit_bytes=mib << 20)


def cost(flops, size):
    return pl.CostEstimate(flops=flops, bytes_accessed=size, transcendentals=0)


def shift(x, axis, by):
    n = lax.axis_size(axis)
    return lax.ppermute(x, axis, [(i, (i + by) % n) for i in range(n)])


def swap(x, axes, k):
    n = lax.axis_size(axes)
    return lax.ppermute(x, axes, [(i, i ^ k) for i in range(n)])


def dispatch_kernel(routes, gains, tokens, out, table, onehot):
    experts, rows = 32, tokens.shape[0]

    @pl.when(pl.program_id(0) == 0)
    def _():
        expert = lax.broadcasted_iota(jnp.int32, (experts, rows), 0)
        match = jnp.zeros((experts, rows), F32)
        gain = jnp.zeros((experts, rows), F32)
        for j in range(6):
            hit = routes[j : j + 1, :] == expert
            match = match + jnp.where(hit, 1.0, 0.0)
            gain = gain + jnp.where(hit, gains[j : j + 1, :], 0.0)
        before = lax.broadcasted_iota(jnp.int32, (rows, rows), 0) < lax.broadcasted_iota(jnp.int32, (rows, rows), 1)
        rank = jnp.dot(match.astype(BF), jnp.where(before, 1.0, 0.0).astype(BF), preferred_element_type=F32)
        code = jnp.where(match > 0.5, rank, -1.0)
        table[0:experts] = code
        table[experts : 2 * experts] = gain
        slot = lax.broadcasted_iota(jnp.int32, (SLOTS, rows), 0).astype(F32)
        for e in range(experts):
            onehot[e * SLOTS : (e + 1) * SLOTS] = jnp.where(code[e : e + 1, :] == slot, 1.0, 0.0).astype(BF)

    @pl.loop(0, 4)
    def _(i):
        part = pl.ds(pl.multiple_of(i * 256, 256), 256)
        out[part] = jnp.dot(onehot[part], tokens[...], preferred_element_type=F32).astype(BF)


def dispatch(routes, gains, tokens):
    rows, width = tokens.shape
    step = 512
    return pl.pallas_call(
        dispatch_kernel,
        out_shape=(jax.ShapeDtypeStruct((32 * SLOTS, width), BF), jax.ShapeDtypeStruct((64, rows), F32)),
        grid=(width // step,),
        in_specs=[
            pl.BlockSpec((6, rows), lambda j: (0, 0)),
            pl.BlockSpec((6, rows), lambda j: (0, 0)),
            pl.BlockSpec((rows, step), lambda j: (0, j)),
        ],
        out_specs=(pl.BlockSpec((32 * SLOTS, step), lambda j: (0, j)), pl.BlockSpec((64, rows), lambda j: (0, 0))),
        scratch_shapes=[pltpu.VMEM((32 * SLOTS, rows), BF)],
        compiler_params=params(62),
        cost_estimate=cost(1 << 29, 5 << 20),
    )(routes, gains, tokens)


def mixing_kernel(place, *refs):
    tables, out = refs[:8], refs[8]
    slot = lax.broadcasted_iota(jnp.int32, (SLOTS, 128), 0).astype(F32)
    for s in range(8):
        parts = []
        for k in range(4):
            expert = 4 * place[0] + lax.bitwise_xor(place[1], k)
            code, gain = tables[s][pl.ds(expert, 1), :], tables[s][pl.ds(expert + 32, 1), :]
            parts.append(jnp.where(code == slot, gain, 0.0))
        weight = jnp.concatenate(parts, axis=0).T
        high = weight.astype(BF)
        out[s, :, 0:128] = high
        out[s, :, 128:256] = (weight - high.astype(F32)).astype(BF)


def mixing(place, tables):
    return pl.pallas_call(
        mixing_kernel,
        out_shape=jax.ShapeDtypeStruct((8, 128, 256), BF),
        in_specs=[SMEM] + [VMEM] * 8,
        out_specs=VMEM,
        compiler_params=params(8),
        cost_estimate=cost(1 << 22, 1 << 20),
    )(place, *tables)


def expert_kernel(groups, place, offsets, *refs):
    arrived, gates, ups, downs = refs[0], refs[1:7], refs[7:13], refs[13:19]
    outs, (x, hidden, gate, up, down, sems) = refs[19:-6], refs[-6:]
    copies = []

    def copy(src, dst):
        c = pltpu.make_async_copy(src, dst, sems.at[len(copies)])
        c.start()
        copies.append(c)

    for parts, whole in ((gates, gate), (ups, up)):
        copy(parts[0], whole.at[pl.ds(pl.multiple_of(offsets[0], 1024), 1024)])
        for i in range(3):
            copy(parts[1 + i], whole.at[pl.ds(pl.multiple_of(offsets[1 + i], 256), 256)])
        far = pl.multiple_of(offsets[4], 256)
        copy(parts[4], whole.at[pl.ds(far, 128)])
        copy(parts[5], whole.at[pl.ds(pl.multiple_of(far + 128, 128), 128)])
    at = 0
    for group in groups:
        for k in range(4):
            for s in group:
                source = 4 * lax.rem(place[0] + 8 - s, 8) + lax.bitwise_xor(place[1], k)
                copy(arrived.at[pl.ds(pl.multiple_of(source * SLOTS, SLOTS), SLOTS)], x.at[at : at + SLOTS])
                at += SLOTS
    first = len(copies)
    copy(downs[0], down.at[:, pl.ds(pl.multiple_of(offsets[0], 1024), 1024)])
    for i in range(3):
        copy(downs[1 + i], down.at[:, pl.ds(pl.multiple_of(offsets[1 + i], 256), 256)])
    far = pl.ds(pl.multiple_of(offsets[4], 256), 256)
    copy(downs[4], down.at[0:384, far])
    copy(downs[5], down.at[384:768, far])
    for c in copies[:first]:
        c.wait()

    @pl.loop(0, gate.shape[1] // 256)
    def _(j):
        cols = pl.ds(pl.multiple_of(j * 256, 256), 256)
        g = jnp.dot(x[...], gate[:, cols], preferred_element_type=F32)
        u = jnp.dot(x[...], up[:, cols], preferred_element_type=F32)
        hidden[:, cols] = (g / (1.0 + jnp.exp(-g)) * u).astype(BF)

    for c in copies[first:]:
        c.wait()

    @pl.loop(0, down.shape[1] // 256)
    def _(j):
        cols = pl.ds(pl.multiple_of(j * 256, 256), 256)
        answer = jnp.dot(hidden[...], down[:, cols], preferred_element_type=F32).astype(BF)
        at = 0
        for i, group in enumerate(groups):
            for k in range(4):
                size = len(group) * SLOTS
                outs[4 * i + k][:, cols] = answer[at : at + size]
                at += size


def expert(groups, place, offsets, arrived, gates, ups, downs):
    width, units = arrived.shape[1], gates[0].shape[1]
    shapes = [jax.ShapeDtypeStruct((len(g) * SLOTS, width), BF) for g in groups for _ in range(4)]
    rows = sum(x.shape[0] for x in shapes)
    out = pl.pallas_call(
        functools.partial(expert_kernel, groups),
        out_shape=tuple(shapes),
        in_specs=[SMEM, SMEM] + [ANY] * 19,
        out_specs=(VMEM,) * len(shapes),
        scratch_shapes=[
            pltpu.VMEM((rows, width), BF),
            pltpu.VMEM((rows, units), BF),
            pltpu.VMEM((width, units), BF),
            pltpu.VMEM((width, units), BF),
            pltpu.VMEM((units, width), BF),
            pltpu.SemaphoreType.DMA((18 + rows // SLOTS,)),
        ],
        compiler_params=params(62),
        cost_estimate=cost(6 * rows * width * units, 16 << 20),
    )(place, offsets, arrived, *gates, *ups, *downs)
    return [out[4 * i : 4 * i + 4] for i in range(len(groups))]


def combined(weight, answers):
    rows = jnp.concatenate(list(answers) * 2, axis=0)
    return jnp.dot(weight, rows, preferred_element_type=F32)


def combine_kernel(blocks, n_in, *refs):
    weights, refs = refs[: len(blocks)], refs[len(blocks) :]
    answers, arrived, outs = refs[:4], refs[4 : 4 + n_in], refs[4 + n_in :]
    for i, s in enumerate(blocks):
        rows = slice(i * SLOTS, (i + 1) * SLOTS)
        total = combined(weights[i][...], [a[rows] for a in answers])
        if s == 4:
            outs[0][...] = total[0:64].astype(BF)
            outs[1][...] = total[64:128].astype(BF)
        elif s == 3:
            outs[i][0:64] = (total[0:64] + arrived[i][...].astype(F32)).astype(BF)
            outs[i][64:128] = total[64:128].astype(BF)
        elif s == 5:
            outs[i][0:64] = total[0:64].astype(BF)
            outs[i][64:128] = (total[64:128] + arrived[i][...].astype(F32)).astype(BF)
        else:
            outs[i][...] = (total + arrived[i][...].astype(F32)).astype(BF)


def weight_of(s):
    return pl.BlockSpec((None, 128, 256), lambda *_: (s, 0, 0))


def combine(blocks, weights, answers, arrived):
    width, step = answers[0].shape[1], 1024
    height = 64 if blocks == (4,) else 128
    used = len(blocks) * SLOTS
    return pl.pallas_call(
        functools.partial(combine_kernel, blocks, len(arrived)),
        out_shape=(jax.ShapeDtypeStruct((height, width), BF),) * 2,
        grid=(width // step,),
        in_specs=[weight_of(s) for s in blocks]
        + [pl.BlockSpec((used, step), lambda j: (0, j))] * 4
        + [pl.BlockSpec((x.shape[0], step), lambda j: (0, j)) for x in arrived],
        out_specs=(pl.BlockSpec((height, step), lambda j: (0, j)),) * 2,
        compiler_params=params(8),
        cost_estimate=cost(len(blocks) << 27, 2 << 20),
    )(*[weights] * len(blocks), *answers, *arrived)


def final_kernel(offsets, weight, a0, a1, a2, a3, tokens, left, right, norm, q0, q1, mixed, query, total, normed, held, sems):
    copies = [pltpu.make_async_copy(q, held.at[i], sems.at[i]) for i, q in enumerate((q0, q1))]
    for c in copies:
        c.start()
    width, step = tokens.shape[1], 512
    square = jnp.zeros((128, 1), F32)
    start = 2 * SLOTS
    for j in range(width // step):
        cols = slice(j * step, (j + 1) * step)
        part = combined(weight[...], [a[start : start + SLOTS, cols] for a in (a0, a1, a2, a3)])
        part = part + tokens[:, cols].astype(F32)
        part = part + left[:, cols].astype(F32) + right[:, cols].astype(F32)
        mixed[:, cols] = part.astype(BF)
        total[:, cols] = part
        square = square + jnp.sum(part * part, axis=1, keepdims=True)
    scale = lax.rsqrt(square / width + 1e-06)
    for j in range(width // step):
        cols = slice(j * step, (j + 1) * step)
        normed[:, cols] = (total[:, cols] * scale * norm[:, cols]).astype(BF)
    for c in copies:
        c.wait()
    half = width // 2
    sides = [normed[:, pl.ds(pl.multiple_of(offsets[i], half), half)] for i in range(2)]
    dims = (((1,), (1,)), ((), ()))

    @pl.loop(0, query.shape[1] // 256)
    def _(j):
        cols = pl.ds(pl.multiple_of(j * 256, 256), 256)
        out = lax.dot_general(sides[0], held[0, cols], dims, preferred_element_type=F32)
        out = out + lax.dot_general(sides[1], held[1, cols], dims, preferred_element_type=F32)
        query[:, cols] = out.astype(BF)


def final(offsets, weights, answers, tokens, left, right, norm, q0, q1):
    rows, width = tokens.shape
    features = q0.shape[0]

    def whole(x):
        return pl.BlockSpec(x.shape, lambda i: (0, 0))

    return pl.pallas_call(
        final_kernel,
        out_shape=(jax.ShapeDtypeStruct((rows, width), BF), jax.ShapeDtypeStruct((rows, features), BF)),
        grid=(1,),
        in_specs=[SMEM, weight_of(0)] + [whole(x) for x in (*answers, tokens, left, right, norm)] + [ANY] * 2,
        out_specs=(pl.BlockSpec((rows, width), lambda i: (0, 0)), pl.BlockSpec((rows, features), lambda i: (0, 0))),
        scratch_shapes=[
            pltpu.VMEM((rows, width), F32),
            pltpu.VMEM((rows, width), BF),
            pltpu.VMEM((2, features, width // 2), BF),
            pltpu.SemaphoreType.DMA((2,)),
        ],
        compiler_params=params(24),
        cost_estimate=cost(2 * rows * width * features, 8 << 20),
    )(offsets, weights, *answers, tokens, left, right, norm, q0, q1)


def across_x(x):
    other = swap(x, "xl", 1)
    up, down = shift(other, "y", 1), shift(other, "y", -1)
    half = x.shape[0] // 2
    return [other, up, down, shift(up[:half], "y", 1), shift(down[half:], "y", -1)]


def shards(tokens, routes, route_gain, gate_weight, up_weight, down_weight, norm_gain, query_weight):
    xl, y, z, c = (lax.axis_index(a) for a in ("xl", "y", "z", "c"))
    me = 2 * lax.axis_index("xh") + c
    plane = ("xh", "c")
    across = [1024 * (1 - xl) + 256 * lax.rem(y + d, 4) for d in (0, 3, 1, 2)]
    offsets = jnp.stack([1024 * xl] + across).astype(jnp.int32)
    place = jnp.stack([z, me]).astype(jnp.int32)
    hold = lax.optimization_barrier

    outbound, table = dispatch(routes.T, route_gain.T, tokens)
    arrived = lax.all_to_all(outbound, ("z", "xh", "c"), split_axis=0, concat_axis=0, tiled=True)

    gates = [lax.all_gather(gate_weight[0], "y", axis=0, tiled=True)] + across_x(gate_weight[0])
    ups = [lax.all_gather(up_weight[0], "y", axis=0, tiled=True)] + across_x(up_weight[0])
    downs = [lax.all_gather(down_weight[0], "y", axis=1, tiled=True)] + across_x(down_weight[0])
    weights = mixing(place, [table] + [shift(table, "z", s) for s in range(1, 8)])

    half = query_weight.shape[0] // 2
    share = lax.dynamic_slice(query_weight.T, (0, c * half), (query_weight.shape[1], half))
    share, gates, ups, downs, weights = hold((share, gates, ups, downs, weights))
    q_own = lax.all_gather(share, ("xl", "y"), axis=0, tiled=True)

    def exchange(pieces):
        return tuple(swap(pieces[k], plane, k) for k in (1, 2, 3))

    ans4, ans3 = expert(GROUPS[:2], place, offsets, arrived, gates, ups, downs)
    got4 = exchange(ans4)
    ans2, ans1 = expert(GROUPS[2:], place, offsets, arrived, gates, ups, downs)
    got4, ans3, ans2, ans1 = hold((got4, ans3, ans2, ans1))
    low, high = combine((4,), weights, (ans4[0],) + got4, [])
    low, high, got3 = shift(low, "z", -1), shift(high, "z", 1), exchange(ans3)
    low, high, got3, ans2, q_own = hold((low, high, got3, ans2, q_own))
    low, high = combine((3, 5), weights, (ans3[0],) + got3, [low, high])
    q_other = swap(q_own, "c", 1)
    low, high, got2 = shift(low, "z", -1), shift(high, "z", 1), exchange(ans2)
    low, high, got2, ans1, q_other = hold((low, high, got2, ans1, q_other))
    low, high = combine((2, 6), weights, (ans2[0],) + got2, [low, high])
    low, high, got1 = shift(low, "z", -1), shift(high, "z", 1), exchange(ans1)
    low, high, got1 = hold((low, high, got1))
    got1 = (ans1[0],) + got1
    low, high = combine((1, 7), weights, got1, [low, high])
    low, high = shift(low, "z", -1), shift(high, "z", 1)
    sides = (half * jnp.stack([c, 1 - c])).astype(jnp.int32)
    return final(sides, weights, got1, tokens, low, high, norm_gain[None, :], q_own, q_other)


def solution(mesh):
    fine = Mesh(mesh.devices.reshape(2, 4, 8, 2, 2), ("xl", "y", "z", "xh", "c"))
    grp, ep = ("xl", "y"), ("z", "xh", "c")
    placed = (
        P(grp + ep, None),
        P(grp + ep, None),
        P(grp + ep, None),
        P(ep, grp, None),
        P(ep, grp, None),
        P(ep, None, grp),
        P(),
        P(None, grp),
    )
    return jax.shard_map(
        shards,
        mesh=fine,
        in_specs=placed,
        out_specs=(P(grp + ep, None), P(grp + ep, None)),
        check_vma=False,
    )
```

time: 355 us -> 317 us (0.89)
  waiting for transfers between devices: 245 us -> 167 us
  starting transfers between devices: 25.9 us -> 79.9 us
  Pallas kernels: 0 us -> 43.8 us
  matrix products: 24.7 us -> 0 us
  local copies, waits for them, and re-layouts: 32.4 us -> 11.7 us
  other arithmetic: 10.1 us -> 0.15 us
    all_to_all x2 -> x1, waiting for transfers between devices: 152 us -> 0.01 us  [shards(): lax.all_to_all(outbound, ('z', 'xh', 'c'), split_axis=0, concat_axis=0, t...]
    ppermute x0 -> x43, waiting for transfers between devices: none -> 142 us  [the longest x27 84.4 us: shift(): return lax.ppermute(x, axis, [(i, (i + by) % n) for i in range(n)])]
    all_gather x4, waiting for transfers between devices: 90.8 us -> 23.2 us  [the longest x1 23.2 us: shards(): q_own = lax.all_gather(share, ('xl', 'y'), axis=0, tiled=True)]
    ppermute x0 -> x43, starting transfers between devices: none -> 67 us  [the longest x27 43.8 us: shift(): return lax.ppermute(x, axis, [(i, (i + by) % n) for i in range(n)])]
    pallas_call x0 -> x9, Pallas kernels: none -> 43.8 us  [the longest x2 25 us: expert(): pl.pallas_call(functools.partial(expert_kernel, groups), out_shape=tuple(...]
    dot_general x3 -> x0, matrix products: 24.7 us -> none  [the longest x1 12.8 us: shards(): jnp.dot(hidden, lax.all_gather(down_weight[0], 'grp', axis=1, tiled=True)...]
    all_to_all x2 -> x1, starting transfers between devices: 25.6 us -> 12.8 us  [shards(): lax.all_to_all(outbound, ('z', 'xh', 'c'), split_axis=0, concat_axis=0, t...]
    scatter x1 -> x0, local copies, waits for them, and re-layouts: 9.4 us -> none  [shards(): jnp.zeros((ep_count * capacity, width), jnp.bfloat16).at[slot].set(repeated)]
  transfers between devices with their start and end apart: 6 -> 48, of which waited for: 5 -> 16; matrix products, arithmetic and copies ran while one was open for 17% -> 2% of each run, Pallas kernels for 0% -> 11%
where the time goes in v3:
time: 317 us
  waiting for transfers between devices  167 us (53%)
  starting transfers between devices  79.9 us (25%)
  Pallas kernels  43.8 us (14%)
  between operations  14.2 us (4%)
  local copies, waits for them, and re-layouts  11.7 us (4%)
    ppermute x27, waiting for transfers between devices, shift(): return lax.ppermute(x, axis, [(i, (i + by) % n) for i in range(n)])  84.4 us
    ppermute x16, waiting for transfers between devices, swap(): return lax.ppermute(x, axes, [(i, i ^ k) for i in range(n)])  57.4 us
    ppermute x27, starting transfers between devices, shift(): return lax.ppermute(x, axis, [(i, (i + by) % n) for i in range(n)])  43.8 us
    pallas_call x2, Pallas kernels, expert(): pl.pallas_call(functools.partial(expert_kernel, groups), out_shape=tuple(...  25 us
    all_gather x1, waiting for transfers between devices, shards(): q_own = lax.all_gather(share, ('xl', 'y'), axis=0, tiled=True)  23.2 us
    ppermute x16, starting transfers between devices, swap(): return lax.ppermute(x, axes, [(i, i ^ k) for i in range(n)])  23.2 us
    all_to_all x1, starting transfers between devices, shards(): lax.all_to_all(outbound, ('z', 'xh', 'c'), split_axis=0, concat_axis=0, t...  12.8 us
    unnamed x52, local copies, waits for them, and re-layouts  6.54 us
  transfers between devices with their start and end apart: 48, of which 16 were waited for; matrix products, arithmetic and copies ran while one was open for 2% of the time, Pallas kernels for 11%

profile of v3, /device:TPU:1, one launch (start us, length us, event | category | flops | bytes accessed | tf_op | source)
XLA Modules:
  0.0 316.8 jit_solution(13353183535049635970)
XLA Ops:
  8.7 6.0 %shard_map.95 = (bf16[1024,2048]{1,0:T(8,128)(2,1)}, f32[64,128]{1,0:T(8,128)}) custom-call(s32[6,128]{1,0:T(8,128)} %bitcast.33, f32[6,128]{1,0:T(8,128)} %bitcast.34, bf16[128,2048]{1,0:T(8,128)(2,1)} %tokens.3), custom_call_target="tpu_custom_call" | custom-call | flops 536870912 | bytes 5242880 | tf_op jit(solution)/shard_map/pallas_call | solution.py:67
  14.6 12.8 %all-to-all-start = ((bf16[32,32,2048]{2,1,0:T(8,128)(2,1)}), bf16[32,32,2048]{2,1,0:T(8,128)(2,1)}, u32[]{:S(2)}, u32[]{:S(2)}) async-start(bf16[32,32,2048]{2,1,0:T(8,128)(2,1)} %bitcast.23), calls=%async_computation | async-start | bytes 8388608 | tf_op jit(solution)/shard_map/all_to_all | solution.py:307
  28.6 1.2 collective-permute-start
  30.1 28.1 %collective-permute-done.10.refs_14_ = bf16[768,256]{1,0:T(8,128)(2,1)S(1)} collective-permute-done((bf16[768,256]{1,0:T(8,128)(2,1)S(1)}, bf16[768,256]{1,0:T(8,128)(2,1)S(1)}, u32[]{:S(2)}, u32[]{:S(2)}) %collective-permute-start.10) | collective-permute-done | bytes 393248 | tf_op jit(solution)/shard_map/ppermute | solution.py:34
  58.2 1.3 collective-permute-start.11
  59.5 1.4 collective-permute-start.12
  61.0 55.4 %collective-permute-done.15.refs_1_ = f32[64,128]{1,0:T(8,128)S(1)} collective-permute-done((f32[64,128]{1,0:T(8,128)S(1)}, f32[64,128]{1,0:T(8,128)S(1)}, u32[]{:S(2)}, u32[]{:S(2)}) %collective-permute-start.15) | collective-permute-done | bytes 32800 | tf_op jit(solution)/shard_map/ppermute | solution.py:29
  116.3 4.1 %collective-permute-start.16 = (f32[64,128]{1,0:T(8,128)S(1)}, f32[64,128]{1,0:T(8,128)S(1)}, u32[]{:S(2)}, u32[]{:S(2)}) collective-permute-start(f32[64,128]{1,0:T(8,128)S(1)} %copy-done.9), channel_id=1, source_target_pairs={{0,8},{4,12},{8,16},{12,20},{16,24},{20,28},{24,0},{28,4},{1,9},{5... | collective-permute-start | bytes 98312 | tf_op jit(solution)/shard_map/ppermute | solution.py:29
  120.5 2.9 collective-permute-done.16.refs_2_
  123.4 3.7 %collective-permute-start.17 = (f32[64,128]{1,0:T(8,128)S(1)}, f32[64,128]{1,0:T(8,128)S(1)}, u32[]{:S(2)}, u32[]{:S(2)}) collective-permute-start(f32[64,128]{1,0:T(8,128)S(1)} %copy-done.9), channel_id=1, source_target_pairs={{0,12},{4,16},{8,20},{12,24},{16,28},{20,0},{24,4},{28,8},{1,13},{... | collective-permute-start | bytes 98312 | tf_op jit(solution)/shard_map/ppermute | solution.py:29
  127.1 1.3 collective-permute-start.1
  128.4 3.4 %collective-permute-done.17.refs_3_ = f32[64,128]{1,0:T(8,128)S(1)} collective-permute-done((f32[64,128]{1,0:T(8,128)S(1)}, f32[64,128]{1,0:T(8,128)S(1)}, u32[]{:S(2)}, u32[]{:S(2)}) %collective-permute-start.17) | collective-permute-done | bytes 32800 | tf_op jit(solution)/shard_map/ppermute | solution.py:29
  131.8 2.7 collective-permute-start.2
  134.5 2.7 collective-permute-start.7
  137.3 3.7 %collective-permute-start.18 = (f32[64,128]{1,0:T(8,128)S(1)}, f32[64,128]{1,0:T(8,128)S(1)}, u32[]{:S(2)}, u32[]{:S(2)}) collective-permute-start(f32[64,128]{1,0:T(8,128)S(1)} %copy-done.9), channel_id=1, source_target_pairs={{0,16},{4,20},{8,24},{12,28},{16,0},{20,4},{24,8},{28,12},{1,17},{... | collective-permute-start | bytes 98312 | tf_op jit(solution)/shard_map/ppermute | solution.py:29
  141.0 3.6 %collective-permute-start.19 = (f32[64,128]{1,0:T(8,128)S(1)}, f32[64,128]{1,0:T(8,128)S(1)}, u32[]{:S(2)}, u32[]{:S(2)}) collective-permute-start(f32[64,128]{1,0:T(8,128)S(1)} %copy-done.9), channel_id=1, source_target_pairs={{0,20},{4,24},{8,28},{12,0},{16,4},{20,8},{24,12},{28,16},{1,21},{... | collective-permute-start | bytes 98312 | tf_op jit(solution)/shard_map/ppermute | solution.py:29
  144.6 1.1 collective-permute-done.6.refs_9_
  145.8 3.1 collective-permute-done.7.refs_10_
  152.6 3.6 %collective-permute-start.14 = (bf16[384,256]{1,0:T(8,128)(2,1)}, bf16[384,256]{1,0:T(8,128)(2,1)}, u32[]{:S(2)}, u32[]{:S(2)}) collective-permute-start(bf16[384,256]{1,0:T(8,128)(2,1)} %slice.29), channel_id=1, source_target_pairs={{0,96},{32,0},{64,32},{96,64},{1,97},{33,1},{65,33},{97,65},{2,98}... | collective-permute-start | bytes 589832 | tf_op jit(solution)/shard_map/ppermute | solution.py:29
  156.2 2.7 collective-permute-start.4
  158.9 2.7 collective-permute-start.9
  163.2 2.5 collective-permute-done.8.refs_11_
  167.5 11.0 %shard_map.97 = (bf16[32,2048]{1,0:T(8,128)(2,1)}, bf16[32,2048]{1,0:T(8,128)(2,1)}, bf16[32,2048]{1,0:T(8,128)(2,1)}, bf16[32,2048]{1,0:T(8,128)(2,1)}, bf16[64...) custom-call(s32[2]{0:T(128)} %copy-done.11, ...), custom_call_target="tpu_custom_call" | custom-call | flops 3623878656 | bytes 16777216 | tf_op jit(solution)/shard_map/pallas_call | solution.py:169
  178.5 3.9 %collective-permute-start.22 = (bf16[32,2048]{1,0:T(8,128)(2,1)}, bf16[32,2048]{1,0:T(8,128)(2,1)S(1)}, u32[]{:S(2)}, u32[]{:S(2)}) collective-permute-start(bf16[32,2048]{1,0:T(8,128)(2,1)} %get-tuple-element.109), channel_id=1, source_target_pairs={{0,1},{1,0},{2,3},{3,2},{4,5},{5,4},{6,7},{7,6},{8,9},{9,8},{10,11... | collective-permute-start | bytes 393224 | tf_op jit(solution)/shard_map/ppermute | solution.py:34
  182.4 2.7 collective-permute-start.23
  185.7 14.0 %shard_map.98 = (bf16[64,2048]{1,0:T(8,128)(2,1)}, bf16[64,2048]{1,0:T(8,128)(2,1)}, bf16[64,2048]{1,0:T(8,128)(2,1)}, bf16[64,2048]{1,0:T(8,128)(2,1)}, bf16[96...) custom-call(s32[2]{0:T(128)} %copy-done.11, ...), custom_call_target="tpu_custom_call" | custom-call | flops 6039797760 | bytes 16777216 | tf_op jit(solution)/shard_map/pallas_call | solution.py:169
  199.7 2.0 shard_map.99
  204.0 2.7 collective-permute-start.28
  207.1 23.2 %all-gather.8.cloned.1.call-done.q0 = bf16[1536,1024]{1,0:T(8,128)(2,1)} async-done(((bf16[192,1024]{1,0:T(8,128)(2,1)}), bf16[1536,1024]{1,0:T(8,128)(2,1)}) %all-gather.8.cloned.1.call-update) | async-done | bytes 3145744 | tf_op jit(solution)/shard_map/all_gather | solution.py:317
  230.9 2.8 collective-permute-start.35
  233.8 1.7 shard_map.100
  235.5 3.2 %collective-permute-start.30 = (bf16[128,2048]{1,0:T(8,128)(2,1)S(1)}, bf16[128,2048]{1,0:T(8,128)(2,1)S(1)}, u32[]{:S(2)}, u32[]{:S(2)}) collective-permute-start(bf16[128,2048]{1,0:T(8,128)(2,1)S(1)} %get-tuple-element.144), channel_id=1, source_target_pairs={{0,28},{4,0},{8,4},{12,8},{16,12},{20,16},{24,20},{28,24},{1,29},{... | collective-permute-start | bytes 1572872 | tf_op jit(solution)/shard_map/ppermute | solution.py:29
  239.6 2.9 collective-permute-start.34
  242.5 5.0 %collective-permute-done.33.refs_4_ = bf16[64,2048]{1,0:T(8,128)(2,1)S(1)} collective-permute-done((bf16[64,2048]{1,0:T(8,128)(2,1)}, bf16[64,2048]{1,0:T(8,128)(2,1)S(1)}, u32[]{:S(2)}, u32[]{:S(2)}) %collective-permute-start.33) | collective-permute-done | bytes 262176 | tf_op jit(solution)/shard_map/ppermute | solution.py:34
  247.6 6.5 %collective-permute-done.34.refs_5_ = bf16[64,2048]{1,0:T(8,128)(2,1)S(1)} collective-permute-done((bf16[64,2048]{1,0:T(8,128)(2,1)}, bf16[64,2048]{1,0:T(8,128)(2,1)S(1)}, u32[]{:S(2)}, u32[]{:S(2)}) %collective-permute-start.34) | collective-permute-done | bytes 262176 | tf_op jit(solution)/shard_map/ppermute | solution.py:34
  254.1 1.6 copy-done.2
  256.6 2.8 collective-permute-start.36
  260.4 2.6 collective-permute-start.40
  263.0 8.2 %collective-permute-done.39.refs_4_.a2 = bf16[96,2048]{1,0:T(8,128)(2,1)S(1)} collective-permute-done((bf16[96,2048]{1,0:T(8,128)(2,1)S(1)}, bf16[96,2048]{1,0:T(8,128)(2,1)S(1)}, u32[]{:S(2)}, u32[]{:S(2)}) %collective-permute-start.39) | collective-permute-done | bytes 393248 | tf_op jit(solution)/shard_map/ppermute | solution.py:34
  271.3 9.0 %collective-permute-done.40.refs_5_.a3 = bf16[96,2048]{1,0:T(8,128)(2,1)S(1)} collective-permute-done((bf16[96,2048]{1,0:T(8,128)(2,1)S(1)}, bf16[96,2048]{1,0:T(8,128)(2,1)S(1)}, u32[]{:S(2)}, u32[]{:S(2)}) %collective-permute-start.40) | collective-permute-done | bytes 393248 | tf_op jit(solution)/shard_map/ppermute | solution.py:34
  280.3 1.6 shard_map.102
  281.8 2.7 collective-permute-start.41
  284.6 11.7 %collective-permute-done.41.left = bf16[128,2048]{1,0:T(8,128)(2,1)} collective-permute-done((bf16[128,2048]{1,0:T(8,128)(2,1)}, bf16[128,2048]{1,0:T(8,128)(2,1)}, u32[]{:S(2)}, u32[]{:S(2)}) %collective-permute-start.41) | collective-permute-done | bytes 524320 | tf_op jit(solution)/shard_map/ppermute | solution.py:29
  296.3 3.2 %collective-permute-done.42.right = bf16[128,2048]{1,0:T(8,128)(2,1)} collective-permute-done((bf16[128,2048]{1,0:T(8,128)(2,1)}, bf16[128,2048]{1,0:T(8,128)(2,1)}, u32[]{:S(2)}, u32[]{:S(2)}) %collective-permute-start.42) | collective-permute-done | bytes 524320 | tf_op jit(solution)/shard_map/ppermute | solution.py:29
  299.5 1.9 copy-done.1
  301.4 1.9 copy-done.3
  303.3 1.0 copy-done.5
  304.3 5.9 %shard_map.103 = (bf16[128,2048]{1,0:T(8,128)(2,1)}, bf16[128,1536]{1,0:T(8,128)(2,1)}) custom-call(s32[2]{0:T(128)S(1)} %add_multiply_fusion.offsets, bf16[8,128,256]{2,1,0:T(8,128)(2,1)S(1)} %shard_map.96.refs_0_.refs_1_.weight, bf16[96,2048]{1,0:T(8,128)(2,1)S(1)} %copy-done.4, bf16[96,2048]{1,0:T(8,128)(2,1)S(1)} %collective-permute-done.38.refs_3_.a1, ...), custom_call_target="tpu_custom_call" | custom-call | flops 805306368 | bytes 8388608 | tf_op jit(solution)/shard_map/pallas_call | solution.py:273
  (123 shorter events, 16.8 us)
Async XLA Ops:
  7.2 159.6 %all-gather.10.cloned.1.call-start = ((), (), s32[]{:S(2)}) async-start(), calls=%async_computation.2 | async-start | bytes 1966080 | tf_op jit(solution)/shard_map/all_gather | solution.py:309
  7.9 158.9 %all-gather.12.cloned.1.call-start = ((), (), s32[]{:S(2)}) async-start(), calls=%async_computation.3 | async-start | bytes 1966080 | tf_op jit(solution)/shard_map/all_gather | solution.py:310
  14.6 152.8 %all-to-all-start = ((bf16[32,32,2048]{2,1,0:T(8,128)(2,1)}), bf16[32,32,2048]{2,1,0:T(8,128)(2,1)}, u32[]{:S(2)}, u32[]{:S(2)}) async-start(bf16[32,32,2048]{2,1,0:T(8,128)(2,1)} %bitcast.23), calls=%async_computation | async-start | bytes 8388608 | tf_op jit(solution)/shard_map/all_to_all | solution.py:307
  27.4 139.3 %all-gather.14.cloned.1.call-start = ((), (), s32[]{:S(2)}) async-start(), calls=%async_computation.4 | async-start | bytes 1966080 | tf_op jit(solution)/shard_map/all_gather | solution.py:311
  28.2 202.1 %all-gather.8.cloned.1.call-start = ((), (), s32[]{:S(2)}) async-start(), calls=%async_computation.1 | async-start | bytes 3538944 | tf_op jit(solution)/shard_map/all_gather | solution.py:317
  28.2 30.0 %collective-permute-start.10 = (bf16[768,256]{1,0:T(8,128)(2,1)S(1)}, bf16[768,256]{1,0:T(8,128)(2,1)S(1)}, u32[]{:S(2)}, u32[]{:S(2)}) collective-permute-start(bf16[768,256]{1,0:T(8,128)(2,1)S(1)} %bitcast.32), channel_id=1, source_target_pairs={{0,128},{128,0},{1,129},{129,1},{2,130},{130,2},{3,131},{131,3},{4... | collective-permute-start | bytes 1179656 | tf_op jit(solution)/shard_map/ppermute | solution.py:34
  28.6 98.5 %collective-permute-start = (bf16[256,768]{1,0:T(8,128)(2,1)S(1)}, bf16[256,768]{1,0:T(8,128)(2,1)S(1)}, u32[]{:S(2)}, u32[]{:S(2)}) collective-permute-start(bf16[256,768]{1,0:T(8,128)(2,1)S(1)} %bitcast.30), channel_id=1, source_target_pairs={{0,128},{128,0},{1,129},{129,1},{2,130},{130,2},{3,131},{131,3},{4... | collective-permute-start | bytes 1179656 | tf_op jit(solution)/shard_map/ppermute | solution.py:34
  29.8 104.7 %collective-permute-start.5 = (bf16[256,768]{1,0:T(8,128)(2,1)S(1)}, bf16[256,768]{1,0:T(8,128)(2,1)S(1)}, u32[]{:S(2)}, u32[]{:S(2)}) collective-permute-start(bf16[256,768]{1,0:T(8,128)(2,1)S(1)} %bitcast.31), channel_id=1, source_target_pairs={{0,128},{128,0},{1,129},{129,1},{2,130},{130,2},{3,131},{131,3},{4... | collective-permute-start | bytes 1179656 | tf_op jit(solution)/shard_map/ppermute | solution.py:34
  58.2 76.3 %collective-permute-start.11 = (bf16[768,256]{1,0:T(8,128)(2,1)S(1)}, bf16[768,256]{1,0:T(8,128)(2,1)S(1)}, u32[]{:S(2)}, u32[]{:S(2)}) collective-permute-start(bf16[768,256]{1,0:T(8,128)(2,1)S(1)} %collective-permute-done.10.refs_14_), channel_id=1, source_target_pairs={{0,32},{32,64},{64,96},{96,0},{1,33},{33,65},{65,97},{97,1},{2,34}... | collective-permute-start | bytes 1179656 | tf_op jit(solution)/shard_map/ppermute | solution.py:29
  59.5 77.7 %collective-permute-start.12 = (bf16[768,256]{1,0:T(8,128)(2,1)S(1)}, bf16[768,256]{1,0:T(8,128)(2,1)S(1)}, u32[]{:S(2)}, u32[]{:S(2)}) collective-permute-start(bf16[768,256]{1,0:T(8,128)(2,1)S(1)} %collective-permute-done.10.refs_14_), channel_id=1, source_target_pairs={{0,96},{32,0},{64,32},{96,64},{1,97},{33,1},{65,33},{97,65},{2,98}... | collective-permute-start | bytes 1179656 | tf_op jit(solution)/shard_map/ppermute | solution.py:29
  60.9 55.4 %collective-permute-start.15 = (f32[64,128]{1,0:T(8,128)S(1)}, f32[64,128]{1,0:T(8,128)S(1)}, u32[]{:S(2)}, u32[]{:S(2)}) collective-permute-start(f32[64,128]{1,0:T(8,128)S(1)} %copy-done.9), channel_id=1, source_target_pairs={{0,4},{4,8},{8,12},{12,16},{16,20},{20,24},{24,28},{28,0},{1,5},{5... | collective-permute-start | bytes 98312 | tf_op jit(solution)/shard_map/ppermute | solution.py:29
  116.3 7.0 %collective-permute-start.16 = (f32[64,128]{1,0:T(8,128)S(1)}, f32[64,128]{1,0:T(8,128)S(1)}, u32[]{:S(2)}, u32[]{:S(2)}) collective-permute-start(f32[64,128]{1,0:T(8,128)S(1)} %copy-done.9), channel_id=1, source_target_pairs={{0,8},{4,12},{8,16},{12,20},{16,24},{20,28},{24,0},{28,4},{1,9},{5... | collective-permute-start | bytes 98312 | tf_op jit(solution)/shard_map/ppermute | solution.py:29
  123.4 8.4 %collective-permute-start.17 = (f32[64,128]{1,0:T(8,128)S(1)}, f32[64,128]{1,0:T(8,128)S(1)}, u32[]{:S(2)}, u32[]{:S(2)}) collective-permute-start(f32[64,128]{1,0:T(8,128)S(1)} %copy-done.9), channel_id=1, source_target_pairs={{0,12},{4,16},{8,20},{12,24},{16,28},{20,0},{24,4},{28,8},{1,13},{... | collective-permute-start | bytes 98312 | tf_op jit(solution)/shard_map/ppermute | solution.py:29
  127.1 10.2 %collective-permute-start.1 = (bf16[256,768]{1,0:T(8,128)(2,1)S(1)}, bf16[256,768]{1,0:T(8,128)(2,1)S(1)}, u32[]{:S(2)}, u32[]{:S(2)}) collective-permute-start(bf16[256,768]{1,0:T(8,128)(2,1)S(1)} %collective-permute-done.refs_2_), channel_id=1, source_target_pairs={{0,32},{32,64},{64,96},{96,0},{1,33},{33,65},{65,97},{97,1},{2,34}... | collective-permute-start | bytes 1179656 | tf_op jit(solution)/shard_map/ppermute | solution.py:29
  131.8 9.3 %collective-permute-start.2 = (bf16[256,768]{1,0:T(8,128)(2,1)S(1)}, bf16[256,768]{1,0:T(8,128)(2,1)S(1)}, u32[]{:S(2)}, u32[]{:S(2)}) collective-permute-start(bf16[256,768]{1,0:T(8,128)(2,1)S(1)} %collective-permute-done.refs_2_), channel_id=1, source_target_pairs={{0,96},{32,0},{64,32},{96,64},{1,97},{33,1},{65,33},{97,65},{2,98}... | collective-permute-start | bytes 1179656 | tf_op jit(solution)/shard_map/ppermute | solution.py:29
  134.5 11.3 %collective-permute-start.6 = (bf16[256,768]{1,0:T(8,128)(2,1)S(1)}, bf16[256,768]{1,0:T(8,128)(2,1)S(1)}, u32[]{:S(2)}, u32[]{:S(2)}) collective-permute-start(bf16[256,768]{1,0:T(8,128)(2,1)S(1)} %collective-permute-done.5.refs_8_), channel_id=1, source_target_pairs={{0,32},{32,64},{64,96},{96,0},{1,33},{33,65},{65,97},{97,1},{2,34}... | collective-permute-start | bytes 1179656 | tf_op jit(solution)/shard_map/ppermute | solution.py:29
  134.5 14.3 %collective-permute-start.7 = (bf16[256,768]{1,0:T(8,128)(2,1)S(1)}, bf16[256,768]{1,0:T(8,128)(2,1)}, u32[]{:S(2)}, u32[]{:S(2)}) collective-permute-start(bf16[256,768]{1,0:T(8,128)(2,1)S(1)} %collective-permute-done.5.refs_8_), channel_id=1, source_target_pairs={{0,96},{32,0},{64,32},{96,64},{1,97},{33,1},{65,33},{97,65},{2,98}... | collective-permute-start | bytes 1179656 | tf_op jit(solution)/shard_map/ppermute | solution.py:29
  137.2 21.7 %collective-permute-start.13 = (bf16[384,256]{1,0:T(8,128)(2,1)S(1)}, bf16[384,256]{1,0:T(8,128)(2,1)}, u32[]{:S(2)}, u32[]{:S(2)}) collective-permute-start(bf16[384,256]{1,0:T(8,128)(2,1)S(1)} %slice.28), channel_id=1, source_target_pairs={{0,32},{32,64},{64,96},{96,0},{1,33},{33,65},{65,97},{97,1},{2,34}... | collective-permute-start | bytes 589832 | tf_op jit(solution)/shard_map/ppermute | solution.py:29
  137.3 15.3 %collective-permute-start.18 = (f32[64,128]{1,0:T(8,128)S(1)}, f32[64,128]{1,0:T(8,128)S(1)}, u32[]{:S(2)}, u32[]{:S(2)}) collective-permute-start(f32[64,128]{1,0:T(8,128)S(1)} %copy-done.9), channel_id=1, source_target_pairs={{0,16},{4,20},{8,24},{12,28},{16,0},{20,4},{24,8},{28,12},{1,17},{... | collective-permute-start | bytes 98312 | tf_op jit(solution)/shard_map/ppermute | solution.py:29
  141.0 15.2 %collective-permute-start.19 = (f32[64,128]{1,0:T(8,128)S(1)}, f32[64,128]{1,0:T(8,128)S(1)}, u32[]{:S(2)}, u32[]{:S(2)}) collective-permute-start(f32[64,128]{1,0:T(8,128)S(1)} %copy-done.9), channel_id=1, source_target_pairs={{0,20},{4,24},{8,28},{12,0},{16,4},{20,8},{24,12},{28,16},{1,21},{... | collective-permute-start | bytes 98312 | tf_op jit(solution)/shard_map/ppermute | solution.py:29
  145.7 10.4 %collective-permute-start.20 = (f32[64,128]{1,0:T(8,128)S(1)}, f32[64,128]{1,0:T(8,128)S(1)}, u32[]{:S(2)}, u32[]{:S(2)}) collective-permute-start(f32[64,128]{1,0:T(8,128)S(1)} %copy-done.9), channel_id=1, source_target_pairs={{0,24},{4,28},{8,0},{12,4},{16,8},{20,12},{24,16},{28,20},{1,25},{... | collective-permute-start | bytes 98312 | tf_op jit(solution)/shard_map/ppermute | solution.py:29
  148.8 10.0 %collective-permute-start.21 = (f32[64,128]{1,0:T(8,128)S(1)}, f32[64,128]{1,0:T(8,128)S(1)}, u32[]{:S(2)}, u32[]{:S(2)}) collective-permute-start(f32[64,128]{1,0:T(8,128)S(1)} %copy-done.9), channel_id=1, source_target_pairs={{0,28},{4,0},{8,4},{12,8},{16,12},{20,16},{24,20},{28,24},{1,29},{... | collective-permute-start | bytes 98312 | tf_op jit(solution)/shard_map/ppermute | solution.py:29
  152.6 10.6 %collective-permute-start.14 = (bf16[384,256]{1,0:T(8,128)(2,1)}, bf16[384,256]{1,0:T(8,128)(2,1)}, u32[]{:S(2)}, u32[]{:S(2)}) collective-permute-start(bf16[384,256]{1,0:T(8,128)(2,1)} %slice.29), channel_id=1, source_target_pairs={{0,96},{32,0},{64,32},{96,64},{1,97},{33,1},{65,33},{97,65},{2,98}... | collective-permute-start | bytes 589832 | tf_op jit(solution)/shard_map/ppermute | solution.py:29
  156.2 7.0 %collective-permute-start.3 = (bf16[128,768]{1,0:T(8,128)(2,1)}, bf16[128,768]{1,0:T(8,128)(2,1)}, u32[]{:S(2)}, u32[]{:S(2)}) collective-permute-start(bf16[128,768]{1,0:T(8,128)(2,1)} %slice.24), channel_id=1, source_target_pairs={{0,32},{32,64},{64,96},{96,0},{1,33},{33,65},{65,97},{97,1},{2,34}... | collective-permute-start | bytes 589832 | tf_op jit(solution)/shard_map/ppermute | solution.py:29
  156.2 7.0 %collective-permute-start.4 = (bf16[128,768]{1,0:T(8,128)(2,1)}, bf16[128,768]{1,0:T(8,128)(2,1)}, u32[]{:S(2)}, u32[]{:S(2)}) collective-permute-start(bf16[128,768]{1,0:T(8,128)(2,1)} %slice.25), channel_id=1, source_target_pairs={{0,96},{32,0},{64,32},{96,64},{1,97},{33,1},{65,33},{97,65},{2,98}... | collective-permute-start | bytes 589832 | tf_op jit(solution)/shard_map/ppermute | solution.py:29
  158.9 6.9 %collective-permute-start.8 = (bf16[128,768]{1,0:T(8,128)(2,1)}, bf16[128,768]{1,0:T(8,128)(2,1)}, u32[]{:S(2)}, u32[]{:S(2)}) collective-permute-start(bf16[128,768]{1,0:T(8,128)(2,1)} %slice.26), channel_id=1, source_target_pairs={{0,32},{32,64},{64,96},{96,0},{1,33},{33,65},{65,97},{97,1},{2,34}... | collective-permute-start | bytes 589832 | tf_op jit(solution)/shard_map/ppermute | solution.py:29
  158.9 7.9 %collective-permute-start.9 = (bf16[128,768]{1,0:T(8,128)(2,1)S(1)}, bf16[128,768]{1,0:T(8,128)(2,1)}, u32[]{:S(2)}, u32[]{:S(2)}) collective-permute-start(bf16[128,768]{1,0:T(8,128)(2,1)S(1)} %slice.27), channel_id=1, source_target_pairs={{0,96},{32,0},{64,32},{96,64},{1,97},{33,1},{65,33},{97,65},{2,98}... | collective-permute-start | bytes 589832 | tf_op jit(solution)/shard_map/ppermute | solution.py:29
  178.5 21.2 %collective-permute-start.22 = (bf16[32,2048]{1,0:T(8,128)(2,1)}, bf16[32,2048]{1,0:T(8,128)(2,1)S(1)}, u32[]{:S(2)}, u32[]{:S(2)}) collective-permute-start(bf16[32,2048]{1,0:T(8,128)(2,1)} %get-tuple-element.109), channel_id=1, source_target_pairs={{0,1},{1,0},{2,3},{3,2},{4,5},{5,4},{6,7},{7,6},{8,9},{9,8},{10,11... | collective-permute-start | bytes 393224 | tf_op jit(solution)/shard_map/ppermute | solution.py:34
  182.4 17.3 %collective-permute-start.23 = (bf16[32,2048]{1,0:T(8,128)(2,1)}, bf16[32,2048]{1,0:T(8,128)(2,1)S(1)}, u32[]{:S(2)}, u32[]{:S(2)}) collective-permute-start(bf16[32,2048]{1,0:T(8,128)(2,1)} %get-tuple-element.110), channel_id=1, source_target_pairs={{0,2},{1,3},{2,0},{3,1},{4,6},{5,7},{6,4},{7,5},{8,10},{9,11},{10,... | collective-permute-start | bytes 393224 | tf_op jit(solution)/shard_map/ppermute | solution.py:34
  185.1 14.6 %collective-permute-start.24 = (bf16[32,2048]{1,0:T(8,128)(2,1)}, bf16[32,2048]{1,0:T(8,128)(2,1)}, u32[]{:S(2)}, u32[]{:S(2)}) collective-permute-start(bf16[32,2048]{1,0:T(8,128)(2,1)} %get-tuple-element.111), channel_id=1, source_target_pairs={{0,3},{1,2},{2,1},{3,0},{4,7},{5,6},{6,5},{7,4},{8,11},{9,10},{10,... | collective-permute-start | bytes 393224 | tf_op jit(solution)/shard_map/ppermute | solution.py:34
  201.8 28.6 %collective-permute-start.25 = (bf16[64,2048]{1,0:T(8,128)(2,1)}, bf16[64,2048]{1,0:T(8,128)(2,1)S(1)}, u32[]{:S(2)}, u32[]{:S(2)}) collective-permute-start(bf16[64,2048]{1,0:T(8,128)(2,1)} %get-tuple-element.129), channel_id=1, source_target_pairs={{0,28},{4,0},{8,4},{12,8},{16,12},{20,16},{24,20},{28,24},{1,29},{... | collective-permute-start | bytes 786440 | tf_op jit(solution)/shard_map/ppermute | solution.py:29
  202.3 28.0 %collective-permute-start.26 = (bf16[64,2048]{1,0:T(8,128)(2,1)}, bf16[64,2048]{1,0:T(8,128)(2,1)S(1)}, u32[]{:S(2)}, u32[]{:S(2)}) collective-permute-start(bf16[64,2048]{1,0:T(8,128)(2,1)} %get-tuple-element.130), channel_id=1, source_target_pairs={{0,4},{4,8},{8,12},{12,16},{16,20},{20,24},{24,28},{28,0},{1,5},{5... | collective-permute-start | bytes 786440 | tf_op jit(solution)/shard_map/ppermute | solution.py:29
  203.3 27.0 %collective-permute-start.27 = (bf16[64,2048]{1,0:T(8,128)(2,1)}, bf16[64,2048]{1,0:T(8,128)(2,1)S(1)}, u32[]{:S(2)}, u32[]{:S(2)}) collective-permute-start(bf16[64,2048]{1,0:T(8,128)(2,1)} %get-tuple-element.131), channel_id=1, source_target_pairs={{0,1},{1,0},{2,3},{3,2},{4,5},{5,4},{6,7},{7,6},{8,9},{9,8},{10,11... | collective-permute-start | bytes 786440 | tf_op jit(solution)/shard_map/ppermute | solution.py:34
  204.0 26.4 %collective-permute-start.28 = (bf16[64,2048]{1,0:T(8,128)(2,1)}, bf16[64,2048]{1,0:T(8,128)(2,1)S(1)}, u32[]{:S(2)}, u32[]{:S(2)}) collective-permute-start(bf16[64,2048]{1,0:T(8,128)(2,1)} %get-tuple-element.132), channel_id=1, source_target_pairs={{0,2},{1,3},{2,0},{3,1},{4,6},{5,7},{6,4},{7,5},{8,10},{9,11},{10,... | collective-permute-start | bytes 786440 | tf_op jit(solution)/shard_map/ppermute | solution.py:34
  206.6 24.2 %collective-permute-start.29 = (bf16[64,2048]{1,0:T(8,128)(2,1)}, bf16[64,2048]{1,0:T(8,128)(2,1)}, u32[]{:S(2)}, u32[]{:S(2)}) collective-permute-start(bf16[64,2048]{1,0:T(8,128)(2,1)} %get-tuple-element.133), channel_id=1, source_target_pairs={{0,3},{1,2},{2,1},{3,0},{4,7},{5,6},{6,5},{7,4},{8,11},{9,10},{10,... | collective-permute-start | bytes 786440 | tf_op jit(solution)/shard_map/ppermute | solution.py:34
  230.9 23.2 %collective-permute-start.35 = (bf16[1536,1024]{1,0:T(8,128)(2,1)}, bf16[1536,1024]{1,0:T(8,128)(2,1)S(1)}, u32[]{:S(2)}, u32[]{:S(2)}) collective-permute-start(bf16[1536,1024]{1,0:T(8,128)(2,1)} %all-gather.8.cloned.1.call-done.q0), channel_id=1, source_target_pairs={{0,1},{1,0},{2,3},{3,2},{4,5},{5,4},{6,7},{7,6},{8,9},{9,8},{10,11... | collective-permute-start | bytes 9437192 | tf_op jit(solution)/shard_map/ppermute | solution.py:34
  233.7 5.9 %collective-permute-start.32 = (bf16[64,2048]{1,0:T(8,128)(2,1)}, bf16[64,2048]{1,0:T(8,128)(2,1)S(1)}, u32[]{:S(2)}, u32[]{:S(2)}) collective-permute-start(bf16[64,2048]{1,0:T(8,128)(2,1)} %get-tuple-element.146), channel_id=1, source_target_pairs={{0,1},{1,0},{2,3},{3,2},{4,5},{5,4},{6,7},{7,6},{8,9},{9,8},{10,11... | collective-permute-start | bytes 786440 | tf_op jit(solution)/shard_map/ppermute | solution.py:34
  235.5 18.6 %collective-permute-start.30 = (bf16[128,2048]{1,0:T(8,128)(2,1)S(1)}, bf16[128,2048]{1,0:T(8,128)(2,1)S(1)}, u32[]{:S(2)}, u32[]{:S(2)}) collective-permute-start(bf16[128,2048]{1,0:T(8,128)(2,1)S(1)} %get-tuple-element.144), channel_id=1, source_target_pairs={{0,28},{4,0},{8,4},{12,8},{16,12},{20,16},{24,20},{28,24},{1,29},{... | collective-permute-start | bytes 1572872 | tf_op jit(solution)/shard_map/ppermute | solution.py:29
  238.7 15.4 %collective-permute-start.31 = (bf16[128,2048]{1,0:T(8,128)(2,1)S(1)}, bf16[128,2048]{1,0:T(8,128)(2,1)S(1)}, u32[]{:S(2)}, u32[]{:S(2)}) collective-permute-start(bf16[128,2048]{1,0:T(8,128)(2,1)S(1)} %get-tuple-element.145), channel_id=1, source_target_pairs={{0,4},{4,8},{8,12},{12,16},{16,20},{20,24},{24,28},{28,0},{1,5},{5... | collective-permute-start | bytes 1572872 | tf_op jit(solution)/shard_map/ppermute | solution.py:29
  238.7 8.9 %collective-permute-start.33 = (bf16[64,2048]{1,0:T(8,128)(2,1)}, bf16[64,2048]{1,0:T(8,128)(2,1)S(1)}, u32[]{:S(2)}, u32[]{:S(2)}) collective-permute-start(bf16[64,2048]{1,0:T(8,128)(2,1)} %get-tuple-element.147), channel_id=1, source_target_pairs={{0,2},{1,3},{2,0},{3,1},{4,6},{5,7},{6,4},{7,5},{8,10},{9,11},{10,... | collective-permute-start | bytes 786440 | tf_op jit(solution)/shard_map/ppermute | solution.py:34
  239.6 14.4 %collective-permute-start.34 = (bf16[64,2048]{1,0:T(8,128)(2,1)}, bf16[64,2048]{1,0:T(8,128)(2,1)S(1)}, u32[]{:S(2)}, u32[]{:S(2)}) collective-permute-start(bf16[64,2048]{1,0:T(8,128)(2,1)} %get-tuple-element.148), channel_id=1, source_target_pairs={{0,3},{1,2},{2,1},{3,0},{4,7},{5,6},{6,5},{7,4},{8,11},{9,10},{10,... | collective-permute-start | bytes 786440 | tf_op jit(solution)/shard_map/ppermute | solution.py:34
  256.6 23.6 %collective-permute-start.36 = (bf16[128,2048]{1,0:T(8,128)(2,1)S(1)}, bf16[128,2048]{1,0:T(8,128)(2,1)S(1)}, u32[]{:S(2)}, u32[]{:S(2)}) collective-permute-start(bf16[128,2048]{1,0:T(8,128)(2,1)S(1)} %get-tuple-element.161), channel_id=1, source_target_pairs={{0,28},{4,0},{8,4},{12,8},{16,12},{20,16},{24,20},{28,24},{1,29},{... | collective-permute-start | bytes 1572872 | tf_op jit(solution)/shard_map/ppermute | solution.py:29
  259.4 20.9 %collective-permute-start.37 = (bf16[128,2048]{1,0:T(8,128)(2,1)S(1)}, bf16[128,2048]{1,0:T(8,128)(2,1)S(1)}, u32[]{:S(2)}, u32[]{:S(2)}) collective-permute-start(bf16[128,2048]{1,0:T(8,128)(2,1)S(1)} %get-tuple-element.162), channel_id=1, source_target_pairs={{0,4},{4,8},{8,12},{12,16},{16,20},{20,24},{24,28},{28,0},{1,5},{5... | collective-permute-start | bytes 1572872 | tf_op jit(solution)/shard_map/ppermute | solution.py:29
  259.4 3.7 %collective-permute-start.38 = (bf16[96,2048]{1,0:T(8,128)(2,1)S(1)}, bf16[96,2048]{1,0:T(8,128)(2,1)S(1)}, u32[]{:S(2)}, u32[]{:S(2)}) collective-permute-start(bf16[96,2048]{1,0:T(8,128)(2,1)S(1)} %copy-done.25), channel_id=1, source_target_pairs={{0,1},{1,0},{2,3},{3,2},{4,5},{5,4},{6,7},{7,6},{8,9},{9,8},{10,11... | collective-permute-start | bytes 1179656 | tf_op jit(solution)/shard_map/ppermute | solution.py:34
  259.4 11.9 %collective-permute-start.39 = (bf16[96,2048]{1,0:T(8,128)(2,1)S(1)}, bf16[96,2048]{1,0:T(8,128)(2,1)S(1)}, u32[]{:S(2)}, u32[]{:S(2)}) collective-permute-start(bf16[96,2048]{1,0:T(8,128)(2,1)S(1)} %copy-done.24), channel_id=1, source_target_pairs={{0,2},{1,3},{2,0},{3,1},{4,6},{5,7},{6,4},{7,5},{8,10},{9,11},{10,... | collective-permute-start | bytes 1179656 | tf_op jit(solution)/shard_map/ppermute | solution.py:34
  260.4 19.9 %collective-permute-start.40 = (bf16[96,2048]{1,0:T(8,128)(2,1)S(1)}, bf16[96,2048]{1,0:T(8,128)(2,1)S(1)}, u32[]{:S(2)}, u32[]{:S(2)}) collective-permute-start(bf16[96,2048]{1,0:T(8,128)(2,1)S(1)} %copy-done.23), channel_id=1, source_target_pairs={{0,3},{1,2},{2,1},{3,0},{4,7},{5,6},{6,5},{7,4},{8,11},{9,10},{10,... | collective-permute-start | bytes 1179656 | tf_op jit(solution)/shard_map/ppermute | solution.py:34
  281.8 14.4 %collective-permute-start.41 = (bf16[128,2048]{1,0:T(8,128)(2,1)}, bf16[128,2048]{1,0:T(8,128)(2,1)}, u32[]{:S(2)}, u32[]{:S(2)}) collective-permute-start(bf16[128,2048]{1,0:T(8,128)(2,1)} %get-tuple-element.171), channel_id=1, source_target_pairs={{0,28},{4,0},{8,4},{12,8},{16,12},{20,16},{24,20},{28,24},{1,29},{... | collective-permute-start | bytes 1572872 | tf_op jit(solution)/shard_map/ppermute | solution.py:29
  284.5 15.0 %collective-permute-start.42 = (bf16[128,2048]{1,0:T(8,128)(2,1)}, bf16[128,2048]{1,0:T(8,128)(2,1)}, u32[]{:S(2)}, u32[]{:S(2)}) collective-permute-start(bf16[128,2048]{1,0:T(8,128)(2,1)} %get-tuple-element.172), channel_id=1, source_target_pairs={{0,4},{4,8},{8,12},{12,16},{16,20},{20,24},{24,28},{28,0},{1,5},{5... | collective-permute-start | bytes 1572872 | tf_op jit(solution)/shard_map/ppermute | solution.py:29
  (26 other events, 850.0 us)
Sparse Core Ops, SparseCore 0:
  9.8 32.9 all-gather.9
  44.6 37.5 all-gather.11
  84.0 31.7 all-gather.13
  166.9 63.3 all-gather.7

commit v4 on v3

--- a/solution.py
+++ b/solution.py
@@ -49,8 +49,10 @@
         before = lax.broadcasted_iota(jnp.int32, (rows, rows), 0) < lax.broadcasted_iota(jnp.int32, (rows, rows), 1)
         rank = jnp.dot(match.astype(BF), jnp.where(before, 1.0, 0.0).astype(BF), preferred_element_type=F32)
         code = jnp.where(match > 0.5, rank, -1.0)
-        table[0:experts] = code
-        table[experts : 2 * experts] = gain
+        for d in range(experts // 4):
+            own = slice(4 * d, 4 * d + 4)
+            table[8 * d : 8 * d + 4] = code[own]
+            table[8 * d + 4 : 8 * d + 8] = gain[own]
         slot = lax.broadcasted_iota(jnp.int32, (SLOTS, rows), 0).astype(F32)
         for e in range(experts):
             onehot[e * SLOTS : (e + 1) * SLOTS] = jnp.where(code[e : e + 1, :] == slot, 1.0, 0.0).astype(BF)
@@ -80,14 +82,14 @@
     )(routes, gains, tokens)
 
 
-def mixing_kernel(place, *refs):
-    tables, out = refs[:8], refs[8]
+def mixing_kernel(place, table, out):
     slot = lax.broadcasted_iota(jnp.int32, (SLOTS, 128), 0).astype(F32)
     for s in range(8):
+        source = lax.rem(place[0] + 8 - s, 8)
         parts = []
         for k in range(4):
-            expert = 4 * place[0] + lax.bitwise_xor(place[1], k)
-            code, gain = tables[s][pl.ds(expert, 1), :], tables[s][pl.ds(expert + 32, 1), :]
+            row = 8 * source + lax.bitwise_xor(place[1], k)
+            code, gain = table[pl.ds(row, 1), :], table[pl.ds(row + 4, 1), :]
             parts.append(jnp.where(code == slot, gain, 0.0))
         weight = jnp.concatenate(parts, axis=0).T
         high = weight.astype(BF)
@@ -95,15 +97,15 @@
         out[s, :, 128:256] = (weight - high.astype(F32)).astype(BF)
 
 
-def mixing(place, tables):
+def mixing(place, table):
     return pl.pallas_call(
         mixing_kernel,
         out_shape=jax.ShapeDtypeStruct((8, 128, 256), BF),
-        in_specs=[SMEM] + [VMEM] * 8,
+        in_specs=[SMEM, VMEM],
         out_specs=VMEM,
         compiler_params=params(8),
         cost_estimate=cost(1 << 22, 1 << 20),
-    )(place, *tables)
+    )(place, table)
 
 
 def expert_kernel(groups, place, offsets, *refs):
@@ -282,7 +284,7 @@
             pltpu.VMEM((2, features, width // 2), BF),
             pltpu.SemaphoreType.DMA((2,)),
         ],
-        compiler_params=params(24),
+        compiler_params=params(62),
         cost_estimate=cost(2 * rows * width * features, 8 << 20),
     )(offsets, weights, *answers, tokens, left, right, norm, q0, q1)
 
@@ -309,11 +311,11 @@
     gates = [lax.all_gather(gate_weight[0], "y", axis=0, tiled=True)] + across_x(gate_weight[0])
     ups = [lax.all_gather(up_weight[0], "y", axis=0, tiled=True)] + across_x(up_weight[0])
     downs = [lax.all_gather(down_weight[0], "y", axis=1, tiled=True)] + across_x(down_weight[0])
-    weights = mixing(place, [table] + [shift(table, "z", s) for s in range(1, 8)])
+    tables = lax.all_to_all(table, "z", split_axis=0, concat_axis=0, tiled=True)
+    weights = mixing(place, tables)
 
     half = query_weight.shape[0] // 2
     share = lax.dynamic_slice(query_weight.T, (0, c * half), (query_weight.shape[1], half))
-    share, gates, ups, downs, weights = hold((share, gates, ups, downs, weights))
     q_own = lax.all_gather(share, ("xl", "y"), axis=0, tiled=True)
 
     def exchange(pieces):

time: 317 us -> 269 us (0.85)
  waiting for transfers between devices: 167 us -> 135 us
  starting transfers between devices: 79.9 us -> 51.8 us
  blocking collectives: 0 us -> 15.9 us
  local copies, waits for them, and re-layouts: 11.7 us -> 5.61 us
    ppermute x27 -> x20, waiting for transfers between devices: 84.4 us -> 36.2 us  [shift(): return lax.ppermute(x, axis, [(i, (i + by) % n) for i in range(n)])]
    ppermute x16, waiting for transfers between devices: 57.4 us -> 83.8 us  [swap(): return lax.ppermute(x, axes, [(i, i ^ k) for i in range(n)])]
    ppermute x27 -> x20, starting transfers between devices: 43.8 us -> 24.6 us  [shift(): return lax.ppermute(x, axis, [(i, (i + by) % n) for i in range(n)])]
    all_to_all x0 -> x1, blocking collectives: none -> 15.9 us  [shards(): tables = lax.all_to_all(table, 'z', split_axis=0, concat_axis=0, tiled=True)]
    all_gather x1, waiting for transfers between devices: 23.2 us -> 10.4 us  [shards(): q_own = lax.all_gather(share, ('xl', 'y'), axis=0, tiled=True)]
    all_to_all x1, starting transfers between devices: 12.8 us -> 6.75 us  [shards(): lax.all_to_all(outbound, ('z', 'xh', 'c'), split_axis=0, concat_axis=0, t...]
    unnamed x52 -> x58, local copies, waits for them, and re-layouts: 6.54 us -> 2.02 us
  transfers between devices with their start and end apart: 48 -> 41, of which waited for: 16 -> 18; matrix products, arithmetic and copies ran while one was open for 2% -> 2% of each run, Pallas kernels for 11% -> 13%
where the time goes in v4:
time: 269 us
  waiting for transfers between devices  135 us (50%)
  starting transfers between devices  51.8 us (19%)
  Pallas kernels  45.6 us (17%)
  blocking collectives  15.9 us (6%)
  between operations  14.2 us (5%)
  local copies, waits for them, and re-layouts  5.61 us (2%)
    ppermute x16, waiting for transfers between devices, swap(): return lax.ppermute(x, axes, [(i, i ^ k) for i in range(n)])  83.8 us
    ppermute x20, waiting for transfers between devices, shift(): return lax.ppermute(x, axis, [(i, (i + by) % n) for i in range(n)])  36.2 us
    pallas_call x2, Pallas kernels, expert(): pl.pallas_call(functools.partial(expert_kernel, groups), out_shape=tuple(...  25 us
    ppermute x20, starting transfers between devices, shift(): return lax.ppermute(x, axis, [(i, (i + by) % n) for i in range(n)])  24.6 us
    ppermute x16, starting transfers between devices, swap(): return lax.ppermute(x, axes, [(i, i ^ k) for i in range(n)])  20.3 us
    all_to_all x1, blocking collectives, shards(): tables = lax.all_to_all(table, 'z', split_axis=0, concat_axis=0, tiled=True)  15.9 us
    all_gather x1, waiting for transfers between devices, shards(): q_own = lax.all_gather(share, ('xl', 'y'), axis=0, tiled=True)  10.4 us
    pallas_call x1, Pallas kernels, final(): pl.pallas_call(final_kernel, out_shape=(jax.ShapeDtypeStruct((rows, width...  8.41 us
  transfers between devices with their start and end apart: 41, of which 18 were waited for; matrix products, arithmetic and copies ran while one was open for 2% of the time, Pallas kernels for 13%

profile of v4, /device:TPU:1, one launch (start us, length us, event | category | flops | bytes accessed | tf_op | source)
XLA Modules:
  0.0 268.9 jit_solution(13752032667863441910)
XLA Ops:
  8.7 6.0 %shard_map.95 = (bf16[1024,2048]{1,0:T(8,128)(2,1)}, f32[64,128]{1,0:T(8,128)}) custom-call(s32[6,128]{1,0:T(8,128)} %bitcast.37, f32[6,128]{1,0:T(8,128)} %bitcast.38, bf16[128,2048]{1,0:T(8,128)(2,1)} %tokens.3), custom_call_target="tpu_custom_call" | custom-call | flops 536870912 | bytes 5242880 | tf_op jit(solution)/shard_map/pallas_call | solution.py:69
  14.6 15.9 %all_to_all.22 = f32[8,8,128]{2,1,0:T(8,128)S(1)} all-to-all(f32[8,8,128]{2,1,0:T(8,128)} %bitcast.35), channel_id=1, replica_groups=mesh['xl'=2,'y'=4,'z'=8,'xh'=2,'c'=2] {'z'}, dimensions={0} | all-to-all | bytes 65536 | tf_op jit(solution)/shard_map/all_to_all | solution.py:314
  30.5 6.7 %all-to-all-start.1 = ((bf16[32,32,2048]{2,1,0:T(8,128)(2,1)}), bf16[32,32,2048]{2,1,0:T(8,128)(2,1)}, u32[]{:S(2)}, u32[]{:S(2)}) async-start(bf16[32,32,2048]{2,1,0:T(8,128)(2,1)} %bitcast.25), calls=%async_computation.1 | async-start | bytes 8388608 | tf_op jit(solution)/shard_map/all_to_all | solution.py:309
  38.9 1.2 collective-permute-start.10
  40.5 1.1 collective-permute-start.5
  41.6 27.1 %collective-permute-done.10.refs_14_ = bf16[768,256]{1,0:T(8,128)(2,1)S(1)} collective-permute-done((bf16[768,256]{1,0:T(8,128)(2,1)S(1)}, bf16[768,256]{1,0:T(8,128)(2,1)S(1)}, u32[]{:S(2)}, u32[]{:S(2)}) %collective-permute-start.10) | collective-permute-done | bytes 393248 | tf_op jit(solution)/shard_map/ppermute | solution.py:34
  68.7 1.3 collective-permute-start.11
  70.0 1.4 collective-permute-start.12
  71.5 10.2 %collective-permute-done.refs_2_ = bf16[256,768]{1,0:T(8,128)(2,1)S(1)} collective-permute-done((bf16[256,768]{1,0:T(8,128)(2,1)S(1)}, bf16[256,768]{1,0:T(8,128)(2,1)S(1)}, u32[]{:S(2)}, u32[]{:S(2)}) %collective-permute-start) | collective-permute-done | bytes 393248 | tf_op jit(solution)/shard_map/ppermute | solution.py:34
  81.7 1.3 collective-permute-start.1
  83.0 1.4 collective-permute-start.2
  84.4 8.1 %collective-permute-done.5.refs_8_ = bf16[256,768]{1,0:T(8,128)(2,1)S(1)} collective-permute-done((bf16[256,768]{1,0:T(8,128)(2,1)S(1)}, bf16[256,768]{1,0:T(8,128)(2,1)S(1)}, u32[]{:S(2)}, u32[]{:S(2)}) %collective-permute-start.5) | collective-permute-done | bytes 393248 | tf_op jit(solution)/shard_map/ppermute | solution.py:34
  92.5 1.3 collective-permute-start.6
  93.8 1.5 collective-permute-start.7
  95.5 2.7 %collective-permute-start.14 = (bf16[384,256]{1,0:T(8,128)(2,1)S(1)}, bf16[384,256]{1,0:T(8,128)(2,1)}, u32[]{:S(2)}, u32[]{:S(2)}) collective-permute-start(bf16[384,256]{1,0:T(8,128)(2,1)S(1)} %slice.29), channel_id=1, source_target_pairs={{0,96},{32,0},{64,32},{96,64},{1,97},{33,1},{65,33},{97,65},{2,98}... | collective-permute-start | bytes 589832 | tf_op jit(solution)/shard_map/ppermute | solution.py:29
  99.1 12.4 %collective-permute-done.6.refs_9_ = bf16[256,768]{1,0:T(8,128)(2,1)S(1)} collective-permute-done((bf16[256,768]{1,0:T(8,128)(2,1)S(1)}, bf16[256,768]{1,0:T(8,128)(2,1)S(1)}, u32[]{:S(2)}, u32[]{:S(2)}) %collective-permute-start.6) | collective-permute-done | bytes 393248 | tf_op jit(solution)/shard_map/ppermute | solution.py:29
  111.5 1.2 collective-permute-start.4
  114.8 3.5 %collective-permute-done.13.refs_17_ = bf16[384,256]{1,0:T(8,128)(2,1)S(1)} collective-permute-done((bf16[384,256]{1,0:T(8,128)(2,1)S(1)}, bf16[384,256]{1,0:T(8,128)(2,1)S(1)}, u32[]{:S(2)}, u32[]{:S(2)}) %collective-permute-start.13) | collective-permute-done | bytes 196640 | tf_op jit(solution)/shard_map/ppermute | solution.py:29
  119.0 2.0 collective-permute-start.9
  122.5 2.0 collective-permute-done.3.refs_5_
  124.5 4.2 %collective-permute-done.8.refs_11_ = bf16[128,768]{1,0:T(8,128)(2,1)} collective-permute-done((bf16[128,768]{1,0:T(8,128)(2,1)}, bf16[128,768]{1,0:T(8,128)(2,1)}, u32[]{:S(2)}, u32[]{:S(2)}) %collective-permute-start.8) | collective-permute-done | bytes 196640 | tf_op jit(solution)/shard_map/ppermute | solution.py:29
  128.7 2.6 all-to-all-done.1
  131.3 11.0 %shard_map.97 = (bf16[32,2048]{1,0:T(8,128)(2,1)}, bf16[32,2048]{1,0:T(8,128)(2,1)}, bf16[32,2048]{1,0:T(8,128)(2,1)}, bf16[32,2048]{1,0:T(8,128)(2,1)}, bf16[64...) custom-call(s32[2]{0:T(128)} %copy-done.9, ...), custom_call_target="tpu_custom_call" | custom-call | flops 3623878656 | bytes 16777216 | tf_op jit(solution)/shard_map/pallas_call | solution.py:171
  142.3 3.0 %collective-permute-start.15 = (bf16[32,2048]{1,0:T(8,128)(2,1)}, bf16[32,2048]{1,0:T(8,128)(2,1)S(1)}, u32[]{:S(2)}, u32[]{:S(2)}) collective-permute-start(bf16[32,2048]{1,0:T(8,128)(2,1)} %get-tuple-element.70), channel_id=1, source_target_pairs={{0,1},{1,0},{2,3},{3,2},{4,5},{5,4},{6,7},{7,6},{8,9},{9,8},{10,11... | collective-permute-start | bytes 393224 | tf_op jit(solution)/shard_map/ppermute | solution.py:34
  145.7 2.9 %collective-permute-start.17 = (bf16[32,2048]{1,0:T(8,128)(2,1)}, bf16[32,2048]{1,0:T(8,128)(2,1)}, u32[]{:S(2)}, u32[]{:S(2)}) collective-permute-start(bf16[32,2048]{1,0:T(8,128)(2,1)} %get-tuple-element.72), channel_id=1, source_target_pairs={{0,3},{1,2},{2,1},{3,0},{4,7},{5,6},{6,5},{7,4},{8,11},{9,10},{10,... | collective-permute-start | bytes 393224 | tf_op jit(solution)/shard_map/ppermute | solution.py:34
  148.6 14.0 %shard_map.98 = (bf16[64,2048]{1,0:T(8,128)(2,1)}, bf16[64,2048]{1,0:T(8,128)(2,1)}, bf16[64,2048]{1,0:T(8,128)(2,1)}, bf16[64,2048]{1,0:T(8,128)(2,1)}, bf16[96...) custom-call(s32[2]{0:T(128)} %copy-done.9, ...), custom_call_target="tpu_custom_call" | custom-call | flops 6039797760 | bytes 16777216 | tf_op jit(solution)/shard_map/pallas_call | solution.py:171
  162.7 2.0 shard_map.99
  164.7 1.5 collective-permute-start.19
  166.9 1.1 collective-permute-start.21
  168.0 2.1 collective-permute-start.22
  170.0 10.4 %all-gather.8.cloned.1.call-done.q0 = bf16[1536,1024]{1,0:T(8,128)(2,1)} async-done(((bf16[192,1024]{1,0:T(8,128)(2,1)}), bf16[1536,1024]{1,0:T(8,128)(2,1)}) %all-gather.8.cloned.1.call-update) | async-done | bytes 3145744 | tf_op jit(solution)/shard_map/all_gather | solution.py:319
  180.5 1.8 collective-permute-done.21.refs_4_
  182.3 7.3 %collective-permute-done.22.refs_5_ = bf16[64,2048]{1,0:T(8,128)(2,1)} collective-permute-done((bf16[64,2048]{1,0:T(8,128)(2,1)}, bf16[64,2048]{1,0:T(8,128)(2,1)}, u32[]{:S(2)}, u32[]{:S(2)}) %collective-permute-start.22) | collective-permute-done | bytes 262176 | tf_op jit(solution)/shard_map/ppermute | solution.py:34
  190.1 1.7 shard_map.100
  191.8 3.0 %collective-permute-start.23 = (bf16[128,2048]{1,0:T(8,128)(2,1)S(1)}, bf16[128,2048]{1,0:T(8,128)(2,1)S(1)}, u32[]{:S(2)}, u32[]{:S(2)}) collective-permute-start(bf16[128,2048]{1,0:T(8,128)(2,1)S(1)} %get-tuple-element.104), channel_id=1, source_target_pairs={{0,28},{4,0},{8,4},{12,8},{16,12},{20,16},{24,20},{28,24},{1,29},{... | collective-permute-start | bytes 1572872 | tf_op jit(solution)/shard_map/ppermute | solution.py:29
  195.9 2.7 %collective-permute-start.27 = (bf16[64,2048]{1,0:T(8,128)(2,1)}, bf16[64,2048]{1,0:T(8,128)(2,1)S(1)}, u32[]{:S(2)}, u32[]{:S(2)}) collective-permute-start(bf16[64,2048]{1,0:T(8,128)(2,1)} %get-tuple-element.108), channel_id=1, source_target_pairs={{0,3},{1,2},{2,1},{3,0},{4,7},{5,6},{6,5},{7,4},{8,11},{9,10},{10,... | collective-permute-start | bytes 786440 | tf_op jit(solution)/shard_map/ppermute | solution.py:34
  198.6 5.1 %collective-permute-done.26.refs_4_ = bf16[64,2048]{1,0:T(8,128)(2,1)S(1)} collective-permute-done((bf16[64,2048]{1,0:T(8,128)(2,1)}, bf16[64,2048]{1,0:T(8,128)(2,1)S(1)}, u32[]{:S(2)}, u32[]{:S(2)}) %collective-permute-start.26) | collective-permute-done | bytes 262176 | tf_op jit(solution)/shard_map/ppermute | solution.py:34
  203.6 6.5 %collective-permute-done.27.refs_5_ = bf16[64,2048]{1,0:T(8,128)(2,1)S(1)} collective-permute-done((bf16[64,2048]{1,0:T(8,128)(2,1)}, bf16[64,2048]{1,0:T(8,128)(2,1)S(1)}, u32[]{:S(2)}, u32[]{:S(2)}) %collective-permute-start.27) | collective-permute-done | bytes 262176 | tf_op jit(solution)/shard_map/ppermute | solution.py:34
  210.1 0.9 shard_map.101
  211.1 2.8 %collective-permute-start.29 = (bf16[128,2048]{1,0:T(8,128)(2,1)S(1)}, bf16[128,2048]{1,0:T(8,128)(2,1)S(1)}, u32[]{:S(2)}, u32[]{:S(2)}) collective-permute-start(bf16[128,2048]{1,0:T(8,128)(2,1)S(1)} %get-tuple-element.121), channel_id=1, source_target_pairs={{0,28},{4,0},{8,4},{12,8},{16,12},{20,16},{24,20},{28,24},{1,29},{... | collective-permute-start | bytes 1572872 | tf_op jit(solution)/shard_map/ppermute | solution.py:29
  214.5 2.9 %collective-permute-start.33 = (bf16[96,2048]{1,0:T(8,128)(2,1)S(1)}, bf16[96,2048]{1,0:T(8,128)(2,1)S(1)}, u32[]{:S(2)}, u32[]{:S(2)}) collective-permute-start(bf16[96,2048]{1,0:T(8,128)(2,1)S(1)} %copy-done.26), channel_id=1, source_target_pairs={{0,3},{1,2},{2,1},{3,0},{4,7},{5,6},{6,5},{7,4},{8,11},{9,10},{10,... | collective-permute-start | bytes 1179656 | tf_op jit(solution)/shard_map/ppermute | solution.py:34
  217.5 8.2 %collective-permute-done.32.refs_4_.a2 = bf16[96,2048]{1,0:T(8,128)(2,1)S(1)} collective-permute-done((bf16[96,2048]{1,0:T(8,128)(2,1)S(1)}, bf16[96,2048]{1,0:T(8,128)(2,1)S(1)}, u32[]{:S(2)}, u32[]{:S(2)}) %collective-permute-start.32) | collective-permute-done | bytes 393248 | tf_op jit(solution)/shard_map/ppermute | solution.py:34
  225.7 9.0 %collective-permute-done.33.refs_5_.a3 = bf16[96,2048]{1,0:T(8,128)(2,1)S(1)} collective-permute-done((bf16[96,2048]{1,0:T(8,128)(2,1)S(1)}, bf16[96,2048]{1,0:T(8,128)(2,1)S(1)}, u32[]{:S(2)}, u32[]{:S(2)}) %collective-permute-start.33) | collective-permute-done | bytes 393248 | tf_op jit(solution)/shard_map/ppermute | solution.py:34
  234.7 0.9 shard_map.102
  235.7 2.7 %collective-permute-start.34 = (bf16[128,2048]{1,0:T(8,128)(2,1)S(1)}, bf16[128,2048]{1,0:T(8,128)(2,1)S(1)}, u32[]{:S(2)}, u32[]{:S(2)}) collective-permute-start(bf16[128,2048]{1,0:T(8,128)(2,1)S(1)} %get-tuple-element.131), channel_id=1, source_target_pairs={{0,28},{4,0},{8,4},{12,8},{16,12},{20,16},{24,20},{28,24},{1,29},{... | collective-permute-start | bytes 1572872 | tf_op jit(solution)/shard_map/ppermute | solution.py:29
  239.0 10.9 %collective-permute-done.34.left = bf16[128,2048]{1,0:T(8,128)(2,1)S(1)} collective-permute-done((bf16[128,2048]{1,0:T(8,128)(2,1)S(1)}, bf16[128,2048]{1,0:T(8,128)(2,1)S(1)}, u32[]{:S(2)}, u32[]{:S(2)}) %collective-permute-start.34) | collective-permute-done | bytes 524320 | tf_op jit(solution)/shard_map/ppermute | solution.py:29
  249.9 3.3 %collective-permute-done.35.right = bf16[128,2048]{1,0:T(8,128)(2,1)S(1)} collective-permute-done((bf16[128,2048]{1,0:T(8,128)(2,1)S(1)}, bf16[128,2048]{1,0:T(8,128)(2,1)S(1)}, u32[]{:S(2)}, u32[]{:S(2)}) %collective-permute-start.35) | collective-permute-done | bytes 524320 | tf_op jit(solution)/shard_map/ppermute | solution.py:29
  253.9 8.4 %shard_map.103 = (bf16[128,2048]{1,0:T(8,128)(2,1)}, bf16[128,1536]{1,0:T(8,128)(2,1)}) custom-call(s32[2]{0:T(128)} %add_multiply_fusion.offsets, bf16[8,128,256]{2,1,0:T(8,128)(2,1)} %copy-done.1, bf16[96,2048]{1,0:T(8,128)(2,1)} %get-tuple-element.114.refs_2_.a0, bf16[96,2048]{1,0:T(8,128)(2,1)} %copy-done.3, bf16[96,2048]{1,0:T(8,128)(2,1)} %copy-done.4, ...), custom_call_target="tpu_custom_call" | custom-call | flops 805306368 | bytes 8388608 | tf_op jit(solution)/shard_map/pallas_call | solution.py:275
  (116 shorter events, 13.6 us)
Async XLA Ops:
  7.2 121.5 %all-gather.10.cloned.1.call-start = ((), (), s32[]{:S(2)}) async-start(), calls=%async_computation.3 | async-start | bytes 1966080 | tf_op jit(solution)/shard_map/all_gather | solution.py:311
  7.9 120.8 %all-gather.12.cloned.1.call-start = ((), (), s32[]{:S(2)}) async-start(), calls=%async_computation.4 | async-start | bytes 1966080 | tf_op jit(solution)/shard_map/all_gather | solution.py:312
  30.5 100.8 %all-to-all-start.1 = ((bf16[32,32,2048]{2,1,0:T(8,128)(2,1)}), bf16[32,32,2048]{2,1,0:T(8,128)(2,1)}, u32[]{:S(2)}, u32[]{:S(2)}) async-start(bf16[32,32,2048]{2,1,0:T(8,128)(2,1)} %bitcast.25), calls=%async_computation.1 | async-start | bytes 8388608 | tf_op jit(solution)/shard_map/all_to_all | solution.py:309
  37.3 91.5 %all-gather.14.cloned.1.call-start = ((), (), s32[]{:S(2)}) async-start(), calls=%async_computation.5 | async-start | bytes 1966080 | tf_op jit(solution)/shard_map/all_gather | solution.py:313
  38.0 142.5 %all-gather.8.cloned.1.call-start = ((), (), s32[]{:S(2)}) async-start(), calls=%async_computation.2 | async-start | bytes 3538944 | tf_op jit(solution)/shard_map/all_gather | solution.py:319
  38.9 29.8 %collective-permute-start.10 = (bf16[768,256]{1,0:T(8,128)(2,1)S(1)}, bf16[768,256]{1,0:T(8,128)(2,1)S(1)}, u32[]{:S(2)}, u32[]{:S(2)}) collective-permute-start(bf16[768,256]{1,0:T(8,128)(2,1)S(1)} %bitcast.34), channel_id=1, source_target_pairs={{0,128},{128,0},{1,129},{129,1},{2,130},{130,2},{3,131},{131,3},{4... | collective-permute-start | bytes 1179656 | tf_op jit(solution)/shard_map/ppermute | solution.py:34
  40.1 41.5 %collective-permute-start = (bf16[256,768]{1,0:T(8,128)(2,1)S(1)}, bf16[256,768]{1,0:T(8,128)(2,1)S(1)}, u32[]{:S(2)}, u32[]{:S(2)}) collective-permute-start(bf16[256,768]{1,0:T(8,128)(2,1)S(1)} %bitcast.32), channel_id=1, source_target_pairs={{0,128},{128,0},{1,129},{129,1},{2,130},{130,2},{3,131},{131,3},{4... | collective-permute-start | bytes 1179656 | tf_op jit(solution)/shard_map/ppermute | solution.py:34
  40.5 52.1 %collective-permute-start.5 = (bf16[256,768]{1,0:T(8,128)(2,1)S(1)}, bf16[256,768]{1,0:T(8,128)(2,1)S(1)}, u32[]{:S(2)}, u32[]{:S(2)}) collective-permute-start(bf16[256,768]{1,0:T(8,128)(2,1)S(1)} %bitcast.33), channel_id=1, source_target_pairs={{0,128},{128,0},{1,129},{129,1},{2,130},{130,2},{3,131},{131,3},{4... | collective-permute-start | bytes 1179656 | tf_op jit(solution)/shard_map/ppermute | solution.py:34
  68.7 46.1 %copy-start.19 = (bf16[768,256]{1,0:T(8,128)(2,1)}, bf16[768,256]{1,0:T(8,128)(2,1)S(1)}, u32[]{:S(2)}) copy-start(bf16[768,256]{1,0:T(8,128)(2,1)S(1)} %collective-permute-done.10.refs_14_) | copy-start | bytes 1179652
  68.7 25.1 %collective-permute-start.11 = (bf16[768,256]{1,0:T(8,128)(2,1)S(1)}, bf16[768,256]{1,0:T(8,128)(2,1)S(1)}, u32[]{:S(2)}, u32[]{:S(2)}) collective-permute-start(bf16[768,256]{1,0:T(8,128)(2,1)S(1)} %collective-permute-done.10.refs_14_), channel_id=1, source_target_pairs={{0,32},{32,64},{64,96},{96,0},{1,33},{33,65},{65,97},{97,1},{2,34}... | collective-permute-start | bytes 1179656 | tf_op jit(solution)/shard_map/ppermute | solution.py:29
  70.0 25.3 %collective-permute-start.12 = (bf16[768,256]{1,0:T(8,128)(2,1)S(1)}, bf16[768,256]{1,0:T(8,128)(2,1)S(1)}, u32[]{:S(2)}, u32[]{:S(2)}) collective-permute-start(bf16[768,256]{1,0:T(8,128)(2,1)S(1)} %collective-permute-done.10.refs_14_), channel_id=1, source_target_pairs={{0,96},{32,0},{64,32},{96,64},{1,97},{33,1},{65,33},{97,65},{2,98}... | collective-permute-start | bytes 1179656 | tf_op jit(solution)/shard_map/ppermute | solution.py:29
  81.7 36.6 %copy-start.20 = (bf16[256,768]{1,0:T(8,128)(2,1)}, bf16[256,768]{1,0:T(8,128)(2,1)S(1)}, u32[]{:S(2)}) copy-start(bf16[256,768]{1,0:T(8,128)(2,1)S(1)} %collective-permute-done.refs_2_) | copy-start | bytes 1179652
  81.7 13.8 %collective-permute-start.1 = (bf16[256,768]{1,0:T(8,128)(2,1)S(1)}, bf16[256,768]{1,0:T(8,128)(2,1)S(1)}, u32[]{:S(2)}, u32[]{:S(2)}) collective-permute-start(bf16[256,768]{1,0:T(8,128)(2,1)S(1)} %collective-permute-done.refs_2_), channel_id=1, source_target_pairs={{0,32},{32,64},{64,96},{96,0},{1,33},{33,65},{65,97},{97,1},{2,34}... | collective-permute-start | bytes 1179656 | tf_op jit(solution)/shard_map/ppermute | solution.py:29
  83.0 15.3 %collective-permute-start.2 = (bf16[256,768]{1,0:T(8,128)(2,1)S(1)}, bf16[256,768]{1,0:T(8,128)(2,1)S(1)}, u32[]{:S(2)}, u32[]{:S(2)}) collective-permute-start(bf16[256,768]{1,0:T(8,128)(2,1)S(1)} %collective-permute-done.refs_2_), channel_id=1, source_target_pairs={{0,96},{32,0},{64,32},{96,64},{1,97},{33,1},{65,33},{97,65},{2,98}... | collective-permute-start | bytes 1179656 | tf_op jit(solution)/shard_map/ppermute | solution.py:29
  92.5 19.0 %collective-permute-start.6 = (bf16[256,768]{1,0:T(8,128)(2,1)S(1)}, bf16[256,768]{1,0:T(8,128)(2,1)S(1)}, u32[]{:S(2)}, u32[]{:S(2)}) collective-permute-start(bf16[256,768]{1,0:T(8,128)(2,1)S(1)} %collective-permute-done.5.refs_8_), channel_id=1, source_target_pairs={{0,32},{32,64},{64,96},{96,0},{1,33},{33,65},{65,97},{97,1},{2,34}... | collective-permute-start | bytes 1179656 | tf_op jit(solution)/shard_map/ppermute | solution.py:29
  93.8 37.5 %copy-start.11 = (bf16[768,256]{1,0:T(8,128)(2,1)}, bf16[768,256]{1,0:T(8,128)(2,1)S(1)}, u32[]{:S(2)}) copy-start(bf16[768,256]{1,0:T(8,128)(2,1)S(1)} %collective-permute-done.11.refs_15_) | copy-start | bytes 1179652
  93.8 19.6 %collective-permute-start.7 = (bf16[256,768]{1,0:T(8,128)(2,1)S(1)}, bf16[256,768]{1,0:T(8,128)(2,1)S(1)}, u32[]{:S(2)}, u32[]{:S(2)}) collective-permute-start(bf16[256,768]{1,0:T(8,128)(2,1)S(1)} %collective-permute-done.5.refs_8_), channel_id=1, source_target_pairs={{0,96},{32,0},{64,32},{96,64},{1,97},{33,1},{65,33},{97,65},{2,98}... | collective-permute-start | bytes 1179656 | tf_op jit(solution)/shard_map/ppermute | solution.py:29
  95.4 22.9 %collective-permute-start.13 = (bf16[384,256]{1,0:T(8,128)(2,1)S(1)}, bf16[384,256]{1,0:T(8,128)(2,1)S(1)}, u32[]{:S(2)}, u32[]{:S(2)}) collective-permute-start(bf16[384,256]{1,0:T(8,128)(2,1)S(1)} %slice.28), channel_id=1, source_target_pairs={{0,32},{32,64},{64,96},{96,0},{1,33},{33,65},{65,97},{97,1},{2,34}... | collective-permute-start | bytes 589832 | tf_op jit(solution)/shard_map/ppermute | solution.py:29
  95.5 27.0 %collective-permute-start.14 = (bf16[384,256]{1,0:T(8,128)(2,1)S(1)}, bf16[384,256]{1,0:T(8,128)(2,1)}, u32[]{:S(2)}, u32[]{:S(2)}) collective-permute-start(bf16[384,256]{1,0:T(8,128)(2,1)S(1)} %slice.29), channel_id=1, source_target_pairs={{0,96},{32,0},{64,32},{96,64},{1,97},{33,1},{65,33},{97,65},{2,98}... | collective-permute-start | bytes 589832 | tf_op jit(solution)/shard_map/ppermute | solution.py:29
  98.3 26.2 %collective-permute-start.3 = (bf16[128,768]{1,0:T(8,128)(2,1)S(1)}, bf16[128,768]{1,0:T(8,128)(2,1)}, u32[]{:S(2)}, u32[]{:S(2)}) collective-permute-start(bf16[128,768]{1,0:T(8,128)(2,1)S(1)} %slice.24), channel_id=1, source_target_pairs={{0,32},{32,64},{64,96},{96,0},{1,33},{33,65},{65,97},{97,1},{2,34}... | collective-permute-start | bytes 589832 | tf_op jit(solution)/shard_map/ppermute | solution.py:29
  111.5 12.9 %collective-permute-start.4 = (bf16[128,768]{1,0:T(8,128)(2,1)}, bf16[128,768]{1,0:T(8,128)(2,1)}, u32[]{:S(2)}, u32[]{:S(2)}) collective-permute-start(bf16[128,768]{1,0:T(8,128)(2,1)} %slice.25), channel_id=1, source_target_pairs={{0,96},{32,0},{64,32},{96,64},{1,97},{33,1},{65,33},{97,65},{2,98}... | collective-permute-start | bytes 589832 | tf_op jit(solution)/shard_map/ppermute | solution.py:29
  113.4 15.3 %collective-permute-start.8 = (bf16[128,768]{1,0:T(8,128)(2,1)}, bf16[128,768]{1,0:T(8,128)(2,1)}, u32[]{:S(2)}, u32[]{:S(2)}) collective-permute-start(bf16[128,768]{1,0:T(8,128)(2,1)} %slice.26), channel_id=1, source_target_pairs={{0,32},{32,64},{64,96},{96,0},{1,33},{33,65},{65,97},{97,1},{2,34}... | collective-permute-start | bytes 589832 | tf_op jit(solution)/shard_map/ppermute | solution.py:29
  119.0 9.7 %collective-permute-start.9 = (bf16[128,768]{1,0:T(8,128)(2,1)}, bf16[128,768]{1,0:T(8,128)(2,1)}, u32[]{:S(2)}, u32[]{:S(2)}) collective-permute-start(bf16[128,768]{1,0:T(8,128)(2,1)} %slice.27), channel_id=1, source_target_pairs={{0,96},{32,0},{64,32},{96,64},{1,97},{33,1},{65,33},{97,65},{2,98}... | collective-permute-start | bytes 589832 | tf_op jit(solution)/shard_map/ppermute | solution.py:29
  122.5 112.2 %copy-start.1 = (bf16[8,128,256]{2,1,0:T(8,128)(2,1)}, bf16[8,128,256]{2,1,0:T(8,128)(2,1)S(1)}, u32[]{:S(2)}) copy-start(bf16[8,128,256]{2,1,0:T(8,128)(2,1)S(1)} %shard_map.96.refs_0_.refs_1_.weight) | copy-start | bytes 1572868
  142.3 20.3 %collective-permute-start.15 = (bf16[32,2048]{1,0:T(8,128)(2,1)}, bf16[32,2048]{1,0:T(8,128)(2,1)S(1)}, u32[]{:S(2)}, u32[]{:S(2)}) collective-permute-start(bf16[32,2048]{1,0:T(8,128)(2,1)} %get-tuple-element.70), channel_id=1, source_target_pairs={{0,1},{1,0},{2,3},{3,2},{4,5},{5,4},{6,7},{7,6},{8,9},{9,8},{10,11... | collective-permute-start | bytes 393224 | tf_op jit(solution)/shard_map/ppermute | solution.py:34
  145.3 17.3 %collective-permute-start.16 = (bf16[32,2048]{1,0:T(8,128)(2,1)}, bf16[32,2048]{1,0:T(8,128)(2,1)S(1)}, u32[]{:S(2)}, u32[]{:S(2)}) collective-permute-start(bf16[32,2048]{1,0:T(8,128)(2,1)} %get-tuple-element.71), channel_id=1, source_target_pairs={{0,2},{1,3},{2,0},{3,1},{4,6},{5,7},{6,4},{7,5},{8,10},{9,11},{10,... | collective-permute-start | bytes 393224 | tf_op jit(solution)/shard_map/ppermute | solution.py:34
  145.7 44.4 %copy-start.7 = (bf16[64,2048]{1,0:T(8,128)(2,1)S(1)}, bf16[64,2048]{1,0:T(8,128)(2,1)}, u32[]{:S(2)}) copy-start(bf16[64,2048]{1,0:T(8,128)(2,1)} %get-tuple-element.85.refs_2_) | copy-start | bytes 786436
  145.7 16.9 %collective-permute-start.17 = (bf16[32,2048]{1,0:T(8,128)(2,1)}, bf16[32,2048]{1,0:T(8,128)(2,1)}, u32[]{:S(2)}, u32[]{:S(2)}) collective-permute-start(bf16[32,2048]{1,0:T(8,128)(2,1)} %get-tuple-element.72), channel_id=1, source_target_pairs={{0,3},{1,2},{2,1},{3,0},{4,7},{5,6},{6,5},{7,4},{8,11},{9,10},{10,... | collective-permute-start | bytes 393224 | tf_op jit(solution)/shard_map/ppermute | solution.py:34
  162.6 47.5 %copy-start.6 = (bf16[64,2048]{1,0:T(8,128)(2,1)S(1)}, bf16[64,2048]{1,0:T(8,128)(2,1)}, u32[]{:S(2)}) copy-start(bf16[64,2048]{1,0:T(8,128)(2,1)} %get-tuple-element.115.refs_2_) | copy-start | bytes 786436
  164.7 70.0 %copy-start.2 = (bf16[96,2048]{1,0:T(8,128)(2,1)S(1)}, bf16[96,2048]{1,0:T(8,128)(2,1)}, u32[]{:S(2)}) copy-start(bf16[96,2048]{1,0:T(8,128)(2,1)} %get-tuple-element.114.refs_2_.a0) | copy-start | bytes 1179652
  164.7 15.8 %collective-permute-start.18 = (bf16[64,2048]{1,0:T(8,128)(2,1)}, bf16[64,2048]{1,0:T(8,128)(2,1)S(1)}, u32[]{:S(2)}, u32[]{:S(2)}) collective-permute-start(bf16[64,2048]{1,0:T(8,128)(2,1)} %get-tuple-element.90), channel_id=1, source_target_pairs={{0,28},{4,0},{8,4},{12,8},{16,12},{20,16},{24,20},{28,24},{1,29},{... | collective-permute-start | bytes 786440 | tf_op jit(solution)/shard_map/ppermute | solution.py:29
  164.7 15.8 %collective-permute-start.19 = (bf16[64,2048]{1,0:T(8,128)(2,1)}, bf16[64,2048]{1,0:T(8,128)(2,1)S(1)}, u32[]{:S(2)}, u32[]{:S(2)}) collective-permute-start(bf16[64,2048]{1,0:T(8,128)(2,1)} %get-tuple-element.91), channel_id=1, source_target_pairs={{0,4},{4,8},{8,12},{12,16},{16,20},{20,24},{24,28},{28,0},{1,5},{5... | collective-permute-start | bytes 786440 | tf_op jit(solution)/shard_map/ppermute | solution.py:29
  166.2 14.3 %collective-permute-start.20 = (bf16[64,2048]{1,0:T(8,128)(2,1)}, bf16[64,2048]{1,0:T(8,128)(2,1)S(1)}, u32[]{:S(2)}, u32[]{:S(2)}) collective-permute-start(bf16[64,2048]{1,0:T(8,128)(2,1)} %get-tuple-element.92), channel_id=1, source_target_pairs={{0,1},{1,0},{2,3},{3,2},{4,5},{5,4},{6,7},{7,6},{8,9},{9,8},{10,11... | collective-permute-start | bytes 786440 | tf_op jit(solution)/shard_map/ppermute | solution.py:34
  166.9 15.4 %collective-permute-start.21 = (bf16[64,2048]{1,0:T(8,128)(2,1)}, bf16[64,2048]{1,0:T(8,128)(2,1)S(1)}, u32[]{:S(2)}, u32[]{:S(2)}) collective-permute-start(bf16[64,2048]{1,0:T(8,128)(2,1)} %get-tuple-element.93), channel_id=1, source_target_pairs={{0,2},{1,3},{2,0},{3,1},{4,6},{5,7},{6,4},{7,5},{8,10},{9,11},{10,... | collective-permute-start | bytes 786440 | tf_op jit(solution)/shard_map/ppermute | solution.py:34
  168.0 21.6 %collective-permute-start.22 = (bf16[64,2048]{1,0:T(8,128)(2,1)}, bf16[64,2048]{1,0:T(8,128)(2,1)}, u32[]{:S(2)}, u32[]{:S(2)}) collective-permute-start(bf16[64,2048]{1,0:T(8,128)(2,1)} %get-tuple-element.94), channel_id=1, source_target_pairs={{0,3},{1,2},{2,1},{3,0},{4,7},{5,6},{6,5},{7,4},{8,11},{9,10},{10,... | collective-permute-start | bytes 786440 | tf_op jit(solution)/shard_map/ppermute | solution.py:34
  189.6 20.5 %collective-permute-start.28 = (bf16[1536,1024]{1,0:T(8,128)(2,1)}, bf16[1536,1024]{1,0:T(8,128)(2,1)S(1)}, u32[]{:S(2)}, u32[]{:S(2)}) collective-permute-start(bf16[1536,1024]{1,0:T(8,128)(2,1)} %all-gather.8.cloned.1.call-done.q0), channel_id=1, source_target_pairs={{0,1},{1,0},{2,3},{3,2},{4,5},{5,4},{6,7},{7,6},{8,9},{9,8},{10,11... | collective-permute-start | bytes 9437192 | tf_op jit(solution)/shard_map/ppermute | solution.py:34
  190.0 5.9 %collective-permute-start.25 = (bf16[64,2048]{1,0:T(8,128)(2,1)}, bf16[64,2048]{1,0:T(8,128)(2,1)S(1)}, u32[]{:S(2)}, u32[]{:S(2)}) collective-permute-start(bf16[64,2048]{1,0:T(8,128)(2,1)} %get-tuple-element.106), channel_id=1, source_target_pairs={{0,1},{1,0},{2,3},{3,2},{4,5},{5,4},{6,7},{7,6},{8,9},{9,8},{10,11... | collective-permute-start | bytes 786440 | tf_op jit(solution)/shard_map/ppermute | solution.py:34
  191.8 18.3 %collective-permute-start.23 = (bf16[128,2048]{1,0:T(8,128)(2,1)S(1)}, bf16[128,2048]{1,0:T(8,128)(2,1)S(1)}, u32[]{:S(2)}, u32[]{:S(2)}) collective-permute-start(bf16[128,2048]{1,0:T(8,128)(2,1)S(1)} %get-tuple-element.104), channel_id=1, source_target_pairs={{0,28},{4,0},{8,4},{12,8},{16,12},{20,16},{24,20},{28,24},{1,29},{... | collective-permute-start | bytes 1572872 | tf_op jit(solution)/shard_map/ppermute | solution.py:29
  194.7 15.4 %collective-permute-start.24 = (bf16[128,2048]{1,0:T(8,128)(2,1)S(1)}, bf16[128,2048]{1,0:T(8,128)(2,1)S(1)}, u32[]{:S(2)}, u32[]{:S(2)}) collective-permute-start(bf16[128,2048]{1,0:T(8,128)(2,1)S(1)} %get-tuple-element.105), channel_id=1, source_target_pairs={{0,4},{4,8},{8,12},{12,16},{16,20},{20,24},{24,28},{28,0},{1,5},{5... | collective-permute-start | bytes 1572872 | tf_op jit(solution)/shard_map/ppermute | solution.py:29
  194.7 8.9 %collective-permute-start.26 = (bf16[64,2048]{1,0:T(8,128)(2,1)}, bf16[64,2048]{1,0:T(8,128)(2,1)S(1)}, u32[]{:S(2)}, u32[]{:S(2)}) collective-permute-start(bf16[64,2048]{1,0:T(8,128)(2,1)} %get-tuple-element.107), channel_id=1, source_target_pairs={{0,2},{1,3},{2,0},{3,1},{4,6},{5,7},{6,4},{7,5},{8,10},{9,11},{10,... | collective-permute-start | bytes 786440 | tf_op jit(solution)/shard_map/ppermute | solution.py:34
  195.9 14.3 %collective-permute-start.27 = (bf16[64,2048]{1,0:T(8,128)(2,1)}, bf16[64,2048]{1,0:T(8,128)(2,1)S(1)}, u32[]{:S(2)}, u32[]{:S(2)}) collective-permute-start(bf16[64,2048]{1,0:T(8,128)(2,1)} %get-tuple-element.108), channel_id=1, source_target_pairs={{0,3},{1,2},{2,1},{3,0},{4,7},{5,6},{6,5},{7,4},{8,11},{9,10},{10,... | collective-permute-start | bytes 786440 | tf_op jit(solution)/shard_map/ppermute | solution.py:34
  211.1 23.6 %collective-permute-start.29 = (bf16[128,2048]{1,0:T(8,128)(2,1)S(1)}, bf16[128,2048]{1,0:T(8,128)(2,1)S(1)}, u32[]{:S(2)}, u32[]{:S(2)}) collective-permute-start(bf16[128,2048]{1,0:T(8,128)(2,1)S(1)} %get-tuple-element.121), channel_id=1, source_target_pairs={{0,28},{4,0},{8,4},{12,8},{16,12},{20,16},{24,20},{28,24},{1,29},{... | collective-permute-start | bytes 1572872 | tf_op jit(solution)/shard_map/ppermute | solution.py:29
  213.8 20.9 %collective-permute-start.30 = (bf16[128,2048]{1,0:T(8,128)(2,1)S(1)}, bf16[128,2048]{1,0:T(8,128)(2,1)S(1)}, u32[]{:S(2)}, u32[]{:S(2)}) collective-permute-start(bf16[128,2048]{1,0:T(8,128)(2,1)S(1)} %get-tuple-element.122), channel_id=1, source_target_pairs={{0,4},{4,8},{8,12},{12,16},{16,20},{20,24},{24,28},{28,0},{1,5},{5... | collective-permute-start | bytes 1572872 | tf_op jit(solution)/shard_map/ppermute | solution.py:29
  213.8 3.7 %collective-permute-start.31 = (bf16[96,2048]{1,0:T(8,128)(2,1)S(1)}, bf16[96,2048]{1,0:T(8,128)(2,1)S(1)}, u32[]{:S(2)}, u32[]{:S(2)}) collective-permute-start(bf16[96,2048]{1,0:T(8,128)(2,1)S(1)} %copy-done.28), channel_id=1, source_target_pairs={{0,1},{1,0},{2,3},{3,2},{4,5},{5,4},{6,7},{7,6},{8,9},{9,8},{10,11... | collective-permute-start | bytes 1179656 | tf_op jit(solution)/shard_map/ppermute | solution.py:34
  213.8 11.9 %collective-permute-start.32 = (bf16[96,2048]{1,0:T(8,128)(2,1)S(1)}, bf16[96,2048]{1,0:T(8,128)(2,1)S(1)}, u32[]{:S(2)}, u32[]{:S(2)}) collective-permute-start(bf16[96,2048]{1,0:T(8,128)(2,1)S(1)} %copy-done.27), channel_id=1, source_target_pairs={{0,2},{1,3},{2,0},{3,1},{4,6},{5,7},{6,4},{7,5},{8,10},{9,11},{10,... | collective-permute-start | bytes 1179656 | tf_op jit(solution)/shard_map/ppermute | solution.py:34
  214.5 20.2 %collective-permute-start.33 = (bf16[96,2048]{1,0:T(8,128)(2,1)S(1)}, bf16[96,2048]{1,0:T(8,128)(2,1)S(1)}, u32[]{:S(2)}, u32[]{:S(2)}) collective-permute-start(bf16[96,2048]{1,0:T(8,128)(2,1)S(1)} %copy-done.26), channel_id=1, source_target_pairs={{0,3},{1,2},{2,1},{3,0},{4,7},{5,6},{6,5},{7,4},{8,11},{9,10},{10,... | collective-permute-start | bytes 1179656 | tf_op jit(solution)/shard_map/ppermute | solution.py:34
  235.7 14.2 %collective-permute-start.34 = (bf16[128,2048]{1,0:T(8,128)(2,1)S(1)}, bf16[128,2048]{1,0:T(8,128)(2,1)S(1)}, u32[]{:S(2)}, u32[]{:S(2)}) collective-permute-start(bf16[128,2048]{1,0:T(8,128)(2,1)S(1)} %get-tuple-element.131), channel_id=1, source_target_pairs={{0,28},{4,0},{8,4},{12,8},{16,12},{20,16},{24,20},{28,24},{1,29},{... | collective-permute-start | bytes 1572872 | tf_op jit(solution)/shard_map/ppermute | solution.py:29
  238.4 14.7 %collective-permute-start.35 = (bf16[128,2048]{1,0:T(8,128)(2,1)S(1)}, bf16[128,2048]{1,0:T(8,128)(2,1)S(1)}, u32[]{:S(2)}, u32[]{:S(2)}) collective-permute-start(bf16[128,2048]{1,0:T(8,128)(2,1)S(1)} %get-tuple-element.132), channel_id=1, source_target_pairs={{0,4},{4,8},{8,12},{12,16},{16,20},{20,24},{24,28},{28,0},{1,5},{5... | collective-permute-start | bytes 1572872 | tf_op jit(solution)/shard_map/ppermute | solution.py:29
  (22 other events, 365.3 us)
Sparse Core Ops, SparseCore 0:
  9.8 32.9 all-gather.9
  44.6 29.5 all-gather.11
  76.0 47.5 all-gather.13
  125.2 55.2 all-gather.7

commit v5 on v4

--- a/solution.py
+++ b/solution.py
@@ -13,7 +13,7 @@
 ANY = pl.BlockSpec(memory_space=pltpu.HBM)
 SMEM = pl.BlockSpec(memory_space=pltpu.SMEM)
 VMEM = pl.BlockSpec(memory_space=pltpu.VMEM)
-GROUPS = ((4,), (3, 5), (2, 6), (1, 7, 0))
+GROUPS = ((4,), (3, 5), (2, 6), (1, 7), (0,))
 
 
 def params(mib):
@@ -238,10 +238,9 @@
         c.start()
     width, step = tokens.shape[1], 512
     square = jnp.zeros((128, 1), F32)
-    start = 2 * SLOTS
     for j in range(width // step):
         cols = slice(j * step, (j + 1) * step)
-        part = combined(weight[...], [a[start : start + SLOTS, cols] for a in (a0, a1, a2, a3)])
+        part = combined(weight[...], [a[:, cols] for a in (a0, a1, a2, a3)])
         part = part + tokens[:, cols].astype(F32)
         part = part + left[:, cols].astype(F32) + right[:, cols].astype(F32)
         mixed[:, cols] = part.astype(BF)
@@ -322,24 +321,24 @@
         return tuple(swap(pieces[k], plane, k) for k in (1, 2, 3))
 
     ans4, ans3 = expert(GROUPS[:2], place, offsets, arrived, gates, ups, downs)
-    got4 = exchange(ans4)
-    ans2, ans1 = expert(GROUPS[2:], place, offsets, arrived, gates, ups, downs)
-    got4, ans3, ans2, ans1 = hold((got4, ans3, ans2, ans1))
+    got4, got3 = exchange(ans4), exchange(ans3)
+    ans2, ans1, ans0 = expert(GROUPS[2:], place, offsets, arrived, gates, ups, downs)
+    got4, ans2, ans1, ans0 = hold((got4, ans2, ans1, ans0))
     low, high = combine((4,), weights, (ans4[0],) + got4, [])
-    low, high, got3 = shift(low, "z", -1), shift(high, "z", 1), exchange(ans3)
-    low, high, got3, ans2, q_own = hold((low, high, got3, ans2, q_own))
+    low, high, got0 = shift(low, "z", -1), shift(high, "z", 1), exchange(ans0)
+    low, high, got3, got0, ans2 = hold((low, high, got3, got0, ans2))
     low, high = combine((3, 5), weights, (ans3[0],) + got3, [low, high])
+    low, high, got2 = shift(low, "z", -1), shift(high, "z", 1), exchange(ans2)
+    low, high, got2, ans1, q_own = hold((low, high, got2, ans1, q_own))
+    low, high = combine((2, 6), weights, (ans2[0],) + got2, [low, high])
     q_other = swap(q_own, "c", 1)
-    low, high, got2 = shift(low, "z", -1), shift(high, "z", 1), exchange(ans2)
-    low, high, got2, ans1, q_other = hold((low, high, got2, ans1, q_other))
-    low, high = combine((2, 6), weights, (ans2[0],) + got2, [low, high])
     low, high, got1 = shift(low, "z", -1), shift(high, "z", 1), exchange(ans1)
-    low, high, got1 = hold((low, high, got1))
-    got1 = (ans1[0],) + got1
-    low, high = combine((1, 7), weights, got1, [low, high])
+    low, high, got1, q_other = hold((low, high, got1, q_other))
+    low, high = combine((1, 7), weights, (ans1[0],) + got1, [low, high])
     low, high = shift(low, "z", -1), shift(high, "z", 1)
+    got0 = (ans0[0],) + got0
     sides = (half * jnp.stack([c, 1 - c])).astype(jnp.int32)
-    return final(sides, weights, got1, tokens, low, high, norm_gain[None, :], q_own, q_other)
+    return final(sides, weights, got0, tokens, low, high, norm_gain[None, :], q_own, q_other)
 
 
 def solution(mesh):

time: 269 us -> 272 us (1.011)
  starting transfers between devices: 51.8 us -> 56.9 us
    all_gather x1, waiting for transfers between devices: 10.4 us -> 0.01 us  [shards(): q_own = lax.all_gather(share, ('xl', 'y'), axis=0, tiled=True)]
    all_gather x1, waiting for transfers between devices: 0.01 us -> 9.01 us  [shards(): lax.all_gather(down_weight[0], 'y', axis=1, tiled=True)]
    all_to_all x1, starting transfers between devices: 6.75 us -> 12.8 us  [shards(): lax.all_to_all(outbound, ('z', 'xh', 'c'), split_axis=0, concat_axis=0, t...]
    unnamed x58 -> x74, local copies, waits for them, and re-layouts: 2.02 us -> 6.38 us
    ppermute x20, waiting for transfers between devices: 36.2 us -> 40.5 us  [shift(): return lax.ppermute(x, axis, [(i, (i + by) % n) for i in range(n)])]
    ppermute x16 -> x19, waiting for transfers between devices: 83.8 us -> 81.4 us  [swap(): return lax.ppermute(x, axes, [(i, i ^ k) for i in range(n)])]
    ppermute x16 -> x19, starting transfers between devices: 20.3 us -> 21.8 us  [swap(): return lax.ppermute(x, axes, [(i, i ^ k) for i in range(n)])]
  transfers between devices with their start and end apart: 41 -> 44, of which waited for: 18 -> 18; matrix products, arithmetic and copies ran while one was open for 2% -> 1% of each run, Pallas kernels for 13% -> 13%
where the time goes in v5:
time: 272 us; the launch traced here: 271 us
  waiting for transfers between devices  133 us (49%)
  starting transfers between devices  56.9 us (21%)
  Pallas kernels  44.7 us (16%)
  between operations  14.2 us (5%)
  blocking collectives  13.3 us (5%)
  local copies, waits for them, and re-layouts  7.92 us (3%)
    ppermute x19, waiting for transfers between devices, swap(): return lax.ppermute(x, axes, [(i, i ^ k) for i in range(n)])  81.4 us
    ppermute x20, waiting for transfers between devices, shift(): return lax.ppermute(x, axis, [(i, (i + by) % n) for i in range(n)])  40.5 us
    pallas_call x2, Pallas kernels, expert(): pl.pallas_call(functools.partial(expert_kernel, groups), out_shape=tuple(...  25.2 us
    ppermute x20, starting transfers between devices, shift(): return lax.ppermute(x, axis, [(i, (i + by) % n) for i in range(n)])  22.2 us
    ppermute x19, starting transfers between devices, swap(): return lax.ppermute(x, axes, [(i, i ^ k) for i in range(n)])  21.8 us
    all_to_all x1, blocking collectives, shards(): tables = lax.all_to_all(table, 'z', split_axis=0, concat_axis=0, tiled=True)  13.3 us
    all_to_all x1, starting transfers between devices, shards(): lax.all_to_all(outbound, ('z', 'xh', 'c'), split_axis=0, concat_axis=0, t...  12.8 us
    all_gather x1, waiting for transfers between devices, shards(): lax.all_gather(down_weight[0], 'y', axis=1, tiled=True)  9.01 us
  transfers between devices with their start and end apart: 44, of which 18 were waited for; matrix products, arithmetic and copies ran while one was open for 1% of the time, Pallas kernels for 13%

profile of v5, /device:TPU:1, one launch (start us, length us, event | category | flops | bytes accessed | tf_op | source)
XLA Modules:
  0.0 271.3 jit_solution(17229343878502174608)
XLA Ops:
  8.7 6.0 %shard_map.95 = (bf16[1024,2048]{1,0:T(8,128)(2,1)}, f32[64,128]{1,0:T(8,128)}) custom-call(s32[6,128]{1,0:T(8,128)} %bitcast.37, f32[6,128]{1,0:T(8,128)} %bitcast.38, bf16[128,2048]{1,0:T(8,128)(2,1)} %tokens.3), custom_call_target="tpu_custom_call" | custom-call | flops 536870912 | bytes 5242880 | tf_op jit(solution)/shard_map/pallas_call | solution.py:69
  14.6 12.8 %all-to-all-start.1 = ((bf16[32,32,2048]{2,1,0:T(8,128)(2,1)}), bf16[32,32,2048]{2,1,0:T(8,128)(2,1)}, u32[]{:S(2)}, u32[]{:S(2)}) async-start(bf16[32,32,2048]{2,1,0:T(8,128)(2,1)} %bitcast.25), calls=%async_computation.1 | async-start | bytes 8388608 | tf_op jit(solution)/shard_map/all_to_all | solution.py:308
  29.5 1.2 collective-permute-start
  31.0 27.3 %collective-permute-done.10.refs_14_ = bf16[768,256]{1,0:T(8,128)(2,1)S(1)} collective-permute-done((bf16[768,256]{1,0:T(8,128)(2,1)S(1)}, bf16[768,256]{1,0:T(8,128)(2,1)S(1)}, u32[]{:S(2)}, u32[]{:S(2)}) %collective-permute-start.10) | collective-permute-done | bytes 393248 | tf_op jit(solution)/shard_map/ppermute | solution.py:34
  58.2 1.3 collective-permute-start.11
  59.5 1.4 collective-permute-start.12
  61.0 10.2 %collective-permute-done.refs_2_ = bf16[256,768]{1,0:T(8,128)(2,1)S(1)} collective-permute-done((bf16[256,768]{1,0:T(8,128)(2,1)S(1)}, bf16[256,768]{1,0:T(8,128)(2,1)S(1)}, u32[]{:S(2)}, u32[]{:S(2)}) %collective-permute-start) | collective-permute-done | bytes 393248 | tf_op jit(solution)/shard_map/ppermute | solution.py:34
  71.2 1.3 collective-permute-start.1
  72.5 1.4 collective-permute-start.2
  73.9 8.2 %collective-permute-done.5.refs_8_ = bf16[256,768]{1,0:T(8,128)(2,1)S(1)} collective-permute-done((bf16[256,768]{1,0:T(8,128)(2,1)S(1)}, bf16[256,768]{1,0:T(8,128)(2,1)S(1)}, u32[]{:S(2)}, u32[]{:S(2)}) %collective-permute-start.5) | collective-permute-done | bytes 393248 | tf_op jit(solution)/shard_map/ppermute | solution.py:34
  82.1 1.3 collective-permute-start.6
  83.5 1.5 collective-permute-start.7
  85.1 4.9 %collective-permute-done.1.refs_3_ = bf16[256,768]{1,0:T(8,128)(2,1)S(1)} collective-permute-done((bf16[256,768]{1,0:T(8,128)(2,1)S(1)}, bf16[256,768]{1,0:T(8,128)(2,1)S(1)}, u32[]{:S(2)}, u32[]{:S(2)}) %collective-permute-start.1) | collective-permute-done | bytes 393248 | tf_op jit(solution)/shard_map/ppermute | solution.py:29
  90.7 0.9 collective-permute-start.3
  91.6 6.8 %collective-permute-done.6.refs_9_ = bf16[256,768]{1,0:T(8,128)(2,1)S(1)} collective-permute-done((bf16[256,768]{1,0:T(8,128)(2,1)S(1)}, bf16[256,768]{1,0:T(8,128)(2,1)S(1)}, u32[]{:S(2)}, u32[]{:S(2)}) %collective-permute-start.6) | collective-permute-done | bytes 393248 | tf_op jit(solution)/shard_map/ppermute | solution.py:29
  100.1 2.6 collective-permute-done.13.refs_17_
  104.8 5.5 %collective-permute-done.3.refs_5_ = bf16[128,768]{1,0:T(8,128)(2,1)} collective-permute-done((bf16[128,768]{1,0:T(8,128)(2,1)S(1)}, bf16[128,768]{1,0:T(8,128)(2,1)}, u32[]{:S(2)}, u32[]{:S(2)}) %collective-permute-start.3) | collective-permute-done | bytes 196640 | tf_op jit(solution)/shard_map/ppermute | solution.py:29
  110.3 6.2 %collective-permute-done.8.refs_11_ = bf16[128,768]{1,0:T(8,128)(2,1)} collective-permute-done((bf16[128,768]{1,0:T(8,128)(2,1)S(1)}, bf16[128,768]{1,0:T(8,128)(2,1)}, u32[]{:S(2)}, u32[]{:S(2)}) %collective-permute-start.8) | collective-permute-done | bytes 196640 | tf_op jit(solution)/shard_map/ppermute | solution.py:29
  117.2 9.0 %all-gather.14.cloned.1.call-done = bf16[1,768,1024]{2,1,0:T(8,128)(2,1)} async-done(((bf16[1,768,256]{2,1,0:T(8,128)(2,1)}), bf16[1,768,1024]{2,1,0:T(8,128)(2,1)}) %all-gather.14.cloned.1.call-update) | async-done | bytes 1572880 | tf_op jit(solution)/shard_map/all_gather | solution.py:312
  126.2 11.0 %shard_map.97 = (bf16[32,2048]{1,0:T(8,128)(2,1)}, bf16[32,2048]{1,0:T(8,128)(2,1)}, bf16[32,2048]{1,0:T(8,128)(2,1)}, bf16[32,2048]{1,0:T(8,128)(2,1)}, bf16[64...) custom-call(s32[2]{0:T(128)} %pad_add_fusion.place, ...), custom_call_target="tpu_custom_call" | custom-call | flops 3623878656 | bytes 16777216 | tf_op jit(solution)/shard_map/pallas_call | solution.py:171
  137.2 0.9 collective-permute-start.15
  138.3 3.1 %collective-permute-start.17 = (bf16[32,2048]{1,0:T(8,128)(2,1)}, bf16[32,2048]{1,0:T(8,128)(2,1)S(1)}, u32[]{:S(2)}, u32[]{:S(2)}) collective-permute-start(bf16[32,2048]{1,0:T(8,128)(2,1)} %get-tuple-element.79), channel_id=1, source_target_pairs={{0,3},{1,2},{2,1},{3,0},{4,7},{5,6},{6,5},{7,4},{8,11},{9,10},{10,... | collective-permute-start | bytes 393224 | tf_op jit(solution)/shard_map/ppermute | solution.py:34
  141.5 14.2 %shard_map.98 = (bf16[64,2048]{1,0:T(8,128)(2,1)}, bf16[64,2048]{1,0:T(8,128)(2,1)}, bf16[64,2048]{1,0:T(8,128)(2,1)}, bf16[64,2048]{1,0:T(8,128)(2,1)}, bf16[64...) custom-call(s32[2]{0:T(128)} %pad_add_fusion.place, ...), custom_call_target="tpu_custom_call" | custom-call | flops 6039797760 | bytes 16777216 | tf_op jit(solution)/shard_map/pallas_call | solution.py:171
  158.1 3.2 %collective-permute-start.25 = (bf16[32,2048]{1,0:T(8,128)(2,1)}, bf16[32,2048]{1,0:T(8,128)(2,1)S(1)}, u32[]{:S(2)}, u32[]{:S(2)}) collective-permute-start(bf16[32,2048]{1,0:T(8,128)(2,1)} %get-tuple-element.104), channel_id=1, source_target_pairs={{0,3},{1,2},{2,1},{3,0},{4,7},{5,6},{6,5},{7,4},{8,11},{9,10},{10,... | collective-permute-start | bytes 393224 | tf_op jit(solution)/shard_map/ppermute | solution.py:34
  161.3 13.3 %all_to_all.22 = f32[8,8,128]{2,1,0:T(8,128)S(1)} all-to-all(f32[8,8,128]{2,1,0:T(8,128)S(1)} %bitcast.35), channel_id=1, replica_groups=mesh['xl'=2,'y'=4,'z'=8,'xh'=2,'c'=2] {'z'}, dimensions={0} | all-to-all | bytes 65536 | tf_op jit(solution)/shard_map/all_to_all | solution.py:313
  175.4 1.4 collective-permute-start.20
  176.8 2.3 collective-permute-start.21
  182.4 1.1 collective-permute-start.22
  183.6 1.4 collective-permute-start.19
  185.0 5.3 %collective-permute-done.21.refs_4_ = bf16[64,2048]{1,0:T(8,128)(2,1)S(1)} collective-permute-done((bf16[64,2048]{1,0:T(8,128)(2,1)}, bf16[64,2048]{1,0:T(8,128)(2,1)S(1)}, u32[]{:S(2)}, u32[]{:S(2)}) %collective-permute-start.21) | collective-permute-done | bytes 262176 | tf_op jit(solution)/shard_map/ppermute | solution.py:34
  190.2 5.6 %collective-permute-done.22.refs_5_ = bf16[64,2048]{1,0:T(8,128)(2,1)S(1)} collective-permute-done((bf16[64,2048]{1,0:T(8,128)(2,1)S(1)}, bf16[64,2048]{1,0:T(8,128)(2,1)S(1)}, u32[]{:S(2)}, u32[]{:S(2)}) %collective-permute-start.22) | collective-permute-done | bytes 262176 | tf_op jit(solution)/shard_map/ppermute | solution.py:34
  195.9 1.5 shard_map.100
  197.4 3.0 %collective-permute-start.26 = (bf16[128,2048]{1,0:T(8,128)(2,1)}, bf16[128,2048]{1,0:T(8,128)(2,1)S(1)}, u32[]{:S(2)}, u32[]{:S(2)}) collective-permute-start(bf16[128,2048]{1,0:T(8,128)(2,1)} %get-tuple-element.118), channel_id=1, source_target_pairs={{0,28},{4,0},{8,4},{12,8},{16,12},{20,16},{24,20},{28,24},{1,29},{... | collective-permute-start | bytes 1572872 | tf_op jit(solution)/shard_map/ppermute | solution.py:29
  200.4 1.0 collective-permute-start.28
  201.6 3.1 %collective-permute-start.30 = (bf16[64,2048]{1,0:T(8,128)(2,1)}, bf16[64,2048]{1,0:T(8,128)(2,1)}, u32[]{:S(2)}, u32[]{:S(2)}) collective-permute-start(bf16[64,2048]{1,0:T(8,128)(2,1)} %get-tuple-element.122), channel_id=1, source_target_pairs={{0,3},{1,2},{2,1},{3,0},{4,7},{5,6},{6,5},{7,4},{8,11},{9,10},{10,... | collective-permute-start | bytes 786440 | tf_op jit(solution)/shard_map/ppermute | solution.py:34
  204.7 6.4 %collective-permute-done.29.refs_4_ = bf16[64,2048]{1,0:T(8,128)(2,1)} collective-permute-done((bf16[64,2048]{1,0:T(8,128)(2,1)}, bf16[64,2048]{1,0:T(8,128)(2,1)}, u32[]{:S(2)}, u32[]{:S(2)}) %collective-permute-start.29) | collective-permute-done | bytes 262176 | tf_op jit(solution)/shard_map/ppermute | solution.py:34
  211.1 5.8 %collective-permute-done.30.refs_5_ = bf16[64,2048]{1,0:T(8,128)(2,1)} collective-permute-done((bf16[64,2048]{1,0:T(8,128)(2,1)}, bf16[64,2048]{1,0:T(8,128)(2,1)}, u32[]{:S(2)}, u32[]{:S(2)}) %collective-permute-start.30) | collective-permute-done | bytes 262176 | tf_op jit(solution)/shard_map/ppermute | solution.py:34
  217.4 1.7 shard_map.101
  219.2 2.7 collective-permute-start.31
  222.0 1.1 collective-permute-done.33.refs_3_
  223.2 2.4 collective-permute-start.35
  225.6 5.1 %collective-permute-done.34.refs_4_ = bf16[64,2048]{1,0:T(8,128)(2,1)S(1)} collective-permute-done((bf16[64,2048]{1,0:T(8,128)(2,1)S(1)}, bf16[64,2048]{1,0:T(8,128)(2,1)S(1)}, u32[]{:S(2)}, u32[]{:S(2)}) %collective-permute-start.34) | collective-permute-done | bytes 262176 | tf_op jit(solution)/shard_map/ppermute | solution.py:34
  230.6 6.4 %collective-permute-done.35.refs_5_ = bf16[64,2048]{1,0:T(8,128)(2,1)S(1)} collective-permute-done((bf16[64,2048]{1,0:T(8,128)(2,1)S(1)}, bf16[64,2048]{1,0:T(8,128)(2,1)S(1)}, u32[]{:S(2)}, u32[]{:S(2)}) %collective-permute-start.35) | collective-permute-done | bytes 262176 | tf_op jit(solution)/shard_map/ppermute | solution.py:34
  237.1 0.9 shard_map.102
  238.0 2.7 %collective-permute-start.37 = (bf16[128,2048]{1,0:T(8,128)(2,1)S(1)}, bf16[128,2048]{1,0:T(8,128)(2,1)S(1)}, u32[]{:S(2)}, u32[]{:S(2)}) collective-permute-start(bf16[128,2048]{1,0:T(8,128)(2,1)S(1)} %get-tuple-element.145), channel_id=1, source_target_pairs={{0,28},{4,0},{8,4},{12,8},{16,12},{20,16},{24,20},{28,24},{1,29},{... | collective-permute-start | bytes 1572872 | tf_op jit(solution)/shard_map/ppermute | solution.py:29
  241.3 10.9 %collective-permute-done.37.left = bf16[128,2048]{1,0:T(8,128)(2,1)S(1)} collective-permute-done((bf16[128,2048]{1,0:T(8,128)(2,1)S(1)}, bf16[128,2048]{1,0:T(8,128)(2,1)S(1)}, u32[]{:S(2)}, u32[]{:S(2)}) %collective-permute-start.37) | collective-permute-done | bytes 524320 | tf_op jit(solution)/shard_map/ppermute | solution.py:29
  252.3 3.6 %collective-permute-done.38.right = bf16[128,2048]{1,0:T(8,128)(2,1)S(1)} collective-permute-done((bf16[128,2048]{1,0:T(8,128)(2,1)S(1)}, bf16[128,2048]{1,0:T(8,128)(2,1)S(1)}, u32[]{:S(2)}, u32[]{:S(2)}) %collective-permute-start.38) | collective-permute-done | bytes 524320 | tf_op jit(solution)/shard_map/ppermute | solution.py:29
  256.6 8.1 %shard_map.103 = (bf16[128,2048]{1,0:T(8,128)(2,1)}, bf16[128,1536]{1,0:T(8,128)(2,1)}) custom-call(s32[2]{0:T(128)} %add_multiply_fusion.offsets, bf16[8,128,256]{2,1,0:T(8,128)(2,1)} %copy-done.1, bf16[32,2048]{1,0:T(8,128)(2,1)} %get-tuple-element.92.a0, bf16[32,2048]{1,0:T(8,128)(2,1)} %copy-done.30, bf16[32,2048]{1,0:T(8,128)(2,1)} %copy-done.31, ...), custom_call_target="tpu_custom_call" | custom-call | flops 805306368 | bytes 8388608 | tf_op jit(solution)/shard_map/pallas_call | solution.py:274
  (138 shorter events, 18.0 us)
Async XLA Ops:
  7.2 109.3 %all-gather.10.cloned.1.call-start = ((), (), s32[]{:S(2)}) async-start(), calls=%async_computation.3 | async-start | bytes 1966080 | tf_op jit(solution)/shard_map/all_gather | solution.py:310
  7.9 109.2 %all-gather.12.cloned.1.call-start = ((), (), s32[]{:S(2)}) async-start(), calls=%async_computation.4 | async-start | bytes 1966080 | tf_op jit(solution)/shard_map/all_gather | solution.py:311
  14.6 111.5 %all-to-all-start.1 = ((bf16[32,32,2048]{2,1,0:T(8,128)(2,1)}), bf16[32,32,2048]{2,1,0:T(8,128)(2,1)}, u32[]{:S(2)}, u32[]{:S(2)}) async-start(bf16[32,32,2048]{2,1,0:T(8,128)(2,1)} %bitcast.25), calls=%async_computation.1 | async-start | bytes 8388608 | tf_op jit(solution)/shard_map/all_to_all | solution.py:308
  27.4 98.7 %all-gather.14.cloned.1.call-start = ((), (), s32[]{:S(2)}) async-start(), calls=%async_computation.5 | async-start | bytes 1966080 | tf_op jit(solution)/shard_map/all_gather | solution.py:312
  28.2 176.5 %all-gather.8.cloned.1.call-start = ((), (), s32[]{:S(2)}) async-start(), calls=%async_computation.2 | async-start | bytes 3538944 | tf_op jit(solution)/shard_map/all_gather | solution.py:318
  29.1 29.1 %collective-permute-start.10 = (bf16[768,256]{1,0:T(8,128)(2,1)S(1)}, bf16[768,256]{1,0:T(8,128)(2,1)S(1)}, u32[]{:S(2)}, u32[]{:S(2)}) collective-permute-start(bf16[768,256]{1,0:T(8,128)(2,1)S(1)} %bitcast.34), channel_id=1, source_target_pairs={{0,128},{128,0},{1,129},{129,1},{2,130},{130,2},{3,131},{131,3},{4... | collective-permute-start | bytes 1179656 | tf_op jit(solution)/shard_map/ppermute | solution.py:34
  29.5 41.7 %collective-permute-start = (bf16[256,768]{1,0:T(8,128)(2,1)S(1)}, bf16[256,768]{1,0:T(8,128)(2,1)S(1)}, u32[]{:S(2)}, u32[]{:S(2)}) collective-permute-start(bf16[256,768]{1,0:T(8,128)(2,1)S(1)} %bitcast.32), channel_id=1, source_target_pairs={{0,128},{128,0},{1,129},{129,1},{2,130},{130,2},{3,131},{131,3},{4... | collective-permute-start | bytes 1179656 | tf_op jit(solution)/shard_map/ppermute | solution.py:34
  30.6 51.5 %collective-permute-start.5 = (bf16[256,768]{1,0:T(8,128)(2,1)S(1)}, bf16[256,768]{1,0:T(8,128)(2,1)S(1)}, u32[]{:S(2)}, u32[]{:S(2)}) collective-permute-start(bf16[256,768]{1,0:T(8,128)(2,1)S(1)} %bitcast.33), channel_id=1, source_target_pairs={{0,128},{128,0},{1,129},{129,1},{2,130},{130,2},{3,131},{131,3},{4... | collective-permute-start | bytes 1179656 | tf_op jit(solution)/shard_map/ppermute | solution.py:34
  58.2 25.2 %collective-permute-start.11 = (bf16[768,256]{1,0:T(8,128)(2,1)S(1)}, bf16[768,256]{1,0:T(8,128)(2,1)S(1)}, u32[]{:S(2)}, u32[]{:S(2)}) collective-permute-start(bf16[768,256]{1,0:T(8,128)(2,1)S(1)} %collective-permute-done.10.refs_14_), channel_id=1, source_target_pairs={{0,32},{32,64},{64,96},{96,0},{1,33},{33,65},{65,97},{97,1},{2,34}... | collective-permute-start | bytes 1179656 | tf_op jit(solution)/shard_map/ppermute | solution.py:29
  59.5 25.5 %collective-permute-start.12 = (bf16[768,256]{1,0:T(8,128)(2,1)S(1)}, bf16[768,256]{1,0:T(8,128)(2,1)S(1)}, u32[]{:S(2)}, u32[]{:S(2)}) collective-permute-start(bf16[768,256]{1,0:T(8,128)(2,1)S(1)} %collective-permute-done.10.refs_14_), channel_id=1, source_target_pairs={{0,96},{32,0},{64,32},{96,64},{1,97},{33,1},{65,33},{97,65},{2,98}... | collective-permute-start | bytes 1179656 | tf_op jit(solution)/shard_map/ppermute | solution.py:29
  71.2 18.8 %collective-permute-start.1 = (bf16[256,768]{1,0:T(8,128)(2,1)S(1)}, bf16[256,768]{1,0:T(8,128)(2,1)S(1)}, u32[]{:S(2)}, u32[]{:S(2)}) collective-permute-start(bf16[256,768]{1,0:T(8,128)(2,1)S(1)} %collective-permute-done.refs_2_), channel_id=1, source_target_pairs={{0,32},{32,64},{64,96},{96,0},{1,33},{33,65},{65,97},{97,1},{2,34}... | collective-permute-start | bytes 1179656 | tf_op jit(solution)/shard_map/ppermute | solution.py:29
  72.5 18.2 %collective-permute-start.2 = (bf16[256,768]{1,0:T(8,128)(2,1)S(1)}, bf16[256,768]{1,0:T(8,128)(2,1)S(1)}, u32[]{:S(2)}, u32[]{:S(2)}) collective-permute-start(bf16[256,768]{1,0:T(8,128)(2,1)S(1)} %collective-permute-done.refs_2_), channel_id=1, source_target_pairs={{0,96},{32,0},{64,32},{96,64},{1,97},{33,1},{65,33},{97,65},{2,98}... | collective-permute-start | bytes 1179656 | tf_op jit(solution)/shard_map/ppermute | solution.py:29
  82.1 16.3 %collective-permute-start.6 = (bf16[256,768]{1,0:T(8,128)(2,1)S(1)}, bf16[256,768]{1,0:T(8,128)(2,1)S(1)}, u32[]{:S(2)}, u32[]{:S(2)}) collective-permute-start(bf16[256,768]{1,0:T(8,128)(2,1)S(1)} %collective-permute-done.5.refs_8_), channel_id=1, source_target_pairs={{0,32},{32,64},{64,96},{96,0},{1,33},{33,65},{65,97},{97,1},{2,34}... | collective-permute-start | bytes 1179656 | tf_op jit(solution)/shard_map/ppermute | solution.py:29
  83.5 15.8 %collective-permute-start.7 = (bf16[256,768]{1,0:T(8,128)(2,1)S(1)}, bf16[256,768]{1,0:T(8,128)(2,1)S(1)}, u32[]{:S(2)}, u32[]{:S(2)}) collective-permute-start(bf16[256,768]{1,0:T(8,128)(2,1)S(1)} %collective-permute-done.5.refs_8_), channel_id=1, source_target_pairs={{0,96},{32,0},{64,32},{96,64},{1,97},{33,1},{65,33},{97,65},{2,98}... | collective-permute-start | bytes 1179656 | tf_op jit(solution)/shard_map/ppermute | solution.py:29
  85.0 17.7 %collective-permute-start.13 = (bf16[384,256]{1,0:T(8,128)(2,1)S(1)}, bf16[384,256]{1,0:T(8,128)(2,1)S(1)}, u32[]{:S(2)}, u32[]{:S(2)}) collective-permute-start(bf16[384,256]{1,0:T(8,128)(2,1)S(1)} %slice.28), channel_id=1, source_target_pairs={{0,32},{32,64},{64,96},{96,0},{1,33},{33,65},{65,97},{97,1},{2,34}... | collective-permute-start | bytes 589832 | tf_op jit(solution)/shard_map/ppermute | solution.py:29
  90.0 14.8 %collective-permute-start.14 = (bf16[384,256]{1,0:T(8,128)(2,1)S(1)}, bf16[384,256]{1,0:T(8,128)(2,1)}, u32[]{:S(2)}, u32[]{:S(2)}) collective-permute-start(bf16[384,256]{1,0:T(8,128)(2,1)S(1)} %slice.29), channel_id=1, source_target_pairs={{0,96},{32,0},{64,32},{96,64},{1,97},{33,1},{65,33},{97,65},{2,98}... | collective-permute-start | bytes 589832 | tf_op jit(solution)/shard_map/ppermute | solution.py:29
  90.7 19.6 %collective-permute-start.3 = (bf16[128,768]{1,0:T(8,128)(2,1)S(1)}, bf16[128,768]{1,0:T(8,128)(2,1)}, u32[]{:S(2)}, u32[]{:S(2)}) collective-permute-start(bf16[128,768]{1,0:T(8,128)(2,1)S(1)} %slice.24), channel_id=1, source_target_pairs={{0,32},{32,64},{64,96},{96,0},{1,33},{33,65},{65,97},{97,1},{2,34}... | collective-permute-start | bytes 589832 | tf_op jit(solution)/shard_map/ppermute | solution.py:29
  98.5 11.8 %collective-permute-start.4 = (bf16[128,768]{1,0:T(8,128)(2,1)S(1)}, bf16[128,768]{1,0:T(8,128)(2,1)}, u32[]{:S(2)}, u32[]{:S(2)}) collective-permute-start(bf16[128,768]{1,0:T(8,128)(2,1)S(1)} %slice.25), channel_id=1, source_target_pairs={{0,96},{32,0},{64,32},{96,64},{1,97},{33,1},{65,33},{97,65},{2,98}... | collective-permute-start | bytes 589832 | tf_op jit(solution)/shard_map/ppermute | solution.py:29
  99.3 17.2 %collective-permute-start.8 = (bf16[128,768]{1,0:T(8,128)(2,1)S(1)}, bf16[128,768]{1,0:T(8,128)(2,1)}, u32[]{:S(2)}, u32[]{:S(2)}) collective-permute-start(bf16[128,768]{1,0:T(8,128)(2,1)S(1)} %slice.26), channel_id=1, source_target_pairs={{0,32},{32,64},{64,96},{96,0},{1,33},{33,65},{65,97},{97,1},{2,34}... | collective-permute-start | bytes 589832 | tf_op jit(solution)/shard_map/ppermute | solution.py:29
  102.7 13.8 %collective-permute-start.9 = (bf16[128,768]{1,0:T(8,128)(2,1)S(1)}, bf16[128,768]{1,0:T(8,128)(2,1)S(1)}, u32[]{:S(2)}, u32[]{:S(2)}) collective-permute-start(bf16[128,768]{1,0:T(8,128)(2,1)S(1)} %slice.27), channel_id=1, source_target_pairs={{0,96},{32,0},{64,32},{96,64},{1,97},{33,1},{65,33},{97,65},{2,98}... | collective-permute-start | bytes 589832 | tf_op jit(solution)/shard_map/ppermute | solution.py:29
  137.2 18.4 %collective-permute-start.15 = (bf16[32,2048]{1,0:T(8,128)(2,1)}, bf16[32,2048]{1,0:T(8,128)(2,1)S(1)}, u32[]{:S(2)}, u32[]{:S(2)}) collective-permute-start(bf16[32,2048]{1,0:T(8,128)(2,1)} %get-tuple-element.77), channel_id=1, source_target_pairs={{0,1},{1,0},{2,3},{3,2},{4,5},{5,4},{6,7},{7,6},{8,9},{9,8},{10,11... | collective-permute-start | bytes 393224 | tf_op jit(solution)/shard_map/ppermute | solution.py:34
  138.1 18.2 %collective-permute-start.16 = (bf16[32,2048]{1,0:T(8,128)(2,1)}, bf16[32,2048]{1,0:T(8,128)(2,1)S(1)}, u32[]{:S(2)}, u32[]{:S(2)}) collective-permute-start(bf16[32,2048]{1,0:T(8,128)(2,1)} %get-tuple-element.78), channel_id=1, source_target_pairs={{0,2},{1,3},{2,0},{3,1},{4,6},{5,7},{6,4},{7,5},{8,10},{9,11},{10,... | collective-permute-start | bytes 393224 | tf_op jit(solution)/shard_map/ppermute | solution.py:34
  138.3 57.6 %copy-start.4 = (bf16[64,2048]{1,0:T(8,128)(2,1)S(1)}, bf16[64,2048]{1,0:T(8,128)(2,1)}, u32[]{:S(2)}) copy-start(bf16[64,2048]{1,0:T(8,128)(2,1)} %get-tuple-element.112.refs_2_) | copy-start | bytes 786436
  138.3 18.6 %collective-permute-start.17 = (bf16[32,2048]{1,0:T(8,128)(2,1)}, bf16[32,2048]{1,0:T(8,128)(2,1)S(1)}, u32[]{:S(2)}, u32[]{:S(2)}) collective-permute-start(bf16[32,2048]{1,0:T(8,128)(2,1)} %get-tuple-element.79), channel_id=1, source_target_pairs={{0,3},{1,2},{2,1},{3,0},{4,7},{5,6},{6,5},{7,4},{8,11},{9,10},{10,... | collective-permute-start | bytes 393224 | tf_op jit(solution)/shard_map/ppermute | solution.py:34
  155.6 61.8 %copy-start.3 = (bf16[64,2048]{1,0:T(8,128)(2,1)S(1)}, bf16[64,2048]{1,0:T(8,128)(2,1)}, u32[]{:S(2)}) copy-start(bf16[64,2048]{1,0:T(8,128)(2,1)} %get-tuple-element.128.refs_2_) | copy-start | bytes 786436
  157.6 24.8 %collective-permute-start.23 = (bf16[32,2048]{1,0:T(8,128)(2,1)}, bf16[32,2048]{1,0:T(8,128)(2,1)S(1)}, u32[]{:S(2)}, u32[]{:S(2)}) collective-permute-start(bf16[32,2048]{1,0:T(8,128)(2,1)} %get-tuple-element.102), channel_id=1, source_target_pairs={{0,1},{1,0},{2,3},{3,2},{4,5},{5,4},{6,7},{7,6},{8,9},{9,8},{10,11... | collective-permute-start | bytes 393224 | tf_op jit(solution)/shard_map/ppermute | solution.py:34
  157.7 25.7 %collective-permute-start.24 = (bf16[32,2048]{1,0:T(8,128)(2,1)}, bf16[32,2048]{1,0:T(8,128)(2,1)S(1)}, u32[]{:S(2)}, u32[]{:S(2)}) collective-permute-start(bf16[32,2048]{1,0:T(8,128)(2,1)} %get-tuple-element.103), channel_id=1, source_target_pairs={{0,2},{1,3},{2,0},{3,1},{4,6},{5,7},{6,4},{7,5},{8,10},{9,11},{10,... | collective-permute-start | bytes 393224 | tf_op jit(solution)/shard_map/ppermute | solution.py:34
  158.1 25.5 %collective-permute-start.25 = (bf16[32,2048]{1,0:T(8,128)(2,1)}, bf16[32,2048]{1,0:T(8,128)(2,1)S(1)}, u32[]{:S(2)}, u32[]{:S(2)}) collective-permute-start(bf16[32,2048]{1,0:T(8,128)(2,1)} %get-tuple-element.104), channel_id=1, source_target_pairs={{0,3},{1,2},{2,1},{3,0},{4,7},{5,6},{6,5},{7,4},{8,11},{9,10},{10,... | collective-permute-start | bytes 393224 | tf_op jit(solution)/shard_map/ppermute | solution.py:34
  175.3 61.7 %copy-start.1 = (bf16[8,128,256]{2,1,0:T(8,128)(2,1)}, bf16[8,128,256]{2,1,0:T(8,128)(2,1)S(1)}, u32[]{:S(2)}) copy-start(bf16[8,128,256]{2,1,0:T(8,128)(2,1)S(1)} %shard_map.96.refs_0_.refs_1_.weight) | copy-start | bytes 1572868
  175.4 9.6 %collective-permute-start.20 = (bf16[64,2048]{1,0:T(8,128)(2,1)}, bf16[64,2048]{1,0:T(8,128)(2,1)S(1)}, u32[]{:S(2)}, u32[]{:S(2)}) collective-permute-start(bf16[64,2048]{1,0:T(8,128)(2,1)} %get-tuple-element.99), channel_id=1, source_target_pairs={{0,1},{1,0},{2,3},{3,2},{4,5},{5,4},{6,7},{7,6},{8,9},{9,8},{10,11... | collective-permute-start | bytes 786440 | tf_op jit(solution)/shard_map/ppermute | solution.py:34
  176.8 13.4 %collective-permute-start.21 = (bf16[64,2048]{1,0:T(8,128)(2,1)}, bf16[64,2048]{1,0:T(8,128)(2,1)S(1)}, u32[]{:S(2)}, u32[]{:S(2)}) collective-permute-start(bf16[64,2048]{1,0:T(8,128)(2,1)} %get-tuple-element.100), channel_id=1, source_target_pairs={{0,2},{1,3},{2,0},{3,1},{4,6},{5,7},{6,4},{7,5},{8,10},{9,11},{10,... | collective-permute-start | bytes 786440 | tf_op jit(solution)/shard_map/ppermute | solution.py:34
  182.4 55.6 %copy-start.30 = (bf16[32,2048]{1,0:T(8,128)(2,1)}, bf16[32,2048]{1,0:T(8,128)(2,1)S(1)}, u32[]{:S(2)}) copy-start(bf16[32,2048]{1,0:T(8,128)(2,1)S(1)} %collective-permute-done.23.a1) | copy-start | bytes 393220
  182.4 13.4 %collective-permute-start.22 = (bf16[64,2048]{1,0:T(8,128)(2,1)S(1)}, bf16[64,2048]{1,0:T(8,128)(2,1)S(1)}, u32[]{:S(2)}, u32[]{:S(2)}) collective-permute-start(bf16[64,2048]{1,0:T(8,128)(2,1)S(1)} %copy-done.36), channel_id=1, source_target_pairs={{0,3},{1,2},{2,1},{3,0},{4,7},{5,6},{6,5},{7,4},{8,11},{9,10},{10,... | collective-permute-start | bytes 786440 | tf_op jit(solution)/shard_map/ppermute | solution.py:34
  183.5 12.4 %collective-permute-start.18 = (bf16[64,2048]{1,0:T(8,128)(2,1)S(1)}, bf16[64,2048]{1,0:T(8,128)(2,1)S(1)}, u32[]{:S(2)}, u32[]{:S(2)}) collective-permute-start(bf16[64,2048]{1,0:T(8,128)(2,1)S(1)} %get-tuple-element.97), channel_id=1, source_target_pairs={{0,28},{4,0},{8,4},{12,8},{16,12},{20,16},{24,20},{28,24},{1,29},{... | collective-permute-start | bytes 786440 | tf_op jit(solution)/shard_map/ppermute | solution.py:29
  183.6 12.3 %collective-permute-start.19 = (bf16[64,2048]{1,0:T(8,128)(2,1)S(1)}, bf16[64,2048]{1,0:T(8,128)(2,1)S(1)}, u32[]{:S(2)}, u32[]{:S(2)}) collective-permute-start(bf16[64,2048]{1,0:T(8,128)(2,1)S(1)} %get-tuple-element.98), channel_id=1, source_target_pairs={{0,4},{4,8},{8,12},{12,16},{16,20},{20,24},{24,28},{28,0},{1,5},{5... | collective-permute-start | bytes 786440 | tf_op jit(solution)/shard_map/ppermute | solution.py:29
  197.4 19.5 %collective-permute-start.26 = (bf16[128,2048]{1,0:T(8,128)(2,1)}, bf16[128,2048]{1,0:T(8,128)(2,1)S(1)}, u32[]{:S(2)}, u32[]{:S(2)}) collective-permute-start(bf16[128,2048]{1,0:T(8,128)(2,1)} %get-tuple-element.118), channel_id=1, source_target_pairs={{0,28},{4,0},{8,4},{12,8},{16,12},{20,16},{24,20},{28,24},{1,29},{... | collective-permute-start | bytes 1572872 | tf_op jit(solution)/shard_map/ppermute | solution.py:29
  200.4 16.5 %collective-permute-start.27 = (bf16[128,2048]{1,0:T(8,128)(2,1)}, bf16[128,2048]{1,0:T(8,128)(2,1)S(1)}, u32[]{:S(2)}, u32[]{:S(2)}) collective-permute-start(bf16[128,2048]{1,0:T(8,128)(2,1)} %get-tuple-element.119), channel_id=1, source_target_pairs={{0,4},{4,8},{8,12},{12,16},{16,20},{20,24},{24,28},{28,0},{1,5},{5... | collective-permute-start | bytes 1572872 | tf_op jit(solution)/shard_map/ppermute | solution.py:29
  200.4 4.2 %collective-permute-start.28 = (bf16[64,2048]{1,0:T(8,128)(2,1)}, bf16[64,2048]{1,0:T(8,128)(2,1)S(1)}, u32[]{:S(2)}, u32[]{:S(2)}) collective-permute-start(bf16[64,2048]{1,0:T(8,128)(2,1)} %get-tuple-element.120), channel_id=1, source_target_pairs={{0,1},{1,0},{2,3},{3,2},{4,5},{5,4},{6,7},{7,6},{8,9},{9,8},{10,11... | collective-permute-start | bytes 786440 | tf_op jit(solution)/shard_map/ppermute | solution.py:34
  201.4 9.7 %collective-permute-start.29 = (bf16[64,2048]{1,0:T(8,128)(2,1)}, bf16[64,2048]{1,0:T(8,128)(2,1)}, u32[]{:S(2)}, u32[]{:S(2)}) collective-permute-start(bf16[64,2048]{1,0:T(8,128)(2,1)} %get-tuple-element.121), channel_id=1, source_target_pairs={{0,2},{1,3},{2,0},{3,1},{4,6},{5,7},{6,4},{7,5},{8,10},{9,11},{10,... | collective-permute-start | bytes 786440 | tf_op jit(solution)/shard_map/ppermute | solution.py:34
  201.6 15.3 %collective-permute-start.30 = (bf16[64,2048]{1,0:T(8,128)(2,1)}, bf16[64,2048]{1,0:T(8,128)(2,1)}, u32[]{:S(2)}, u32[]{:S(2)}) collective-permute-start(bf16[64,2048]{1,0:T(8,128)(2,1)} %get-tuple-element.122), channel_id=1, source_target_pairs={{0,3},{1,2},{2,1},{3,0},{4,7},{5,6},{6,5},{7,4},{8,11},{9,10},{10,... | collective-permute-start | bytes 786440 | tf_op jit(solution)/shard_map/ppermute | solution.py:34
  216.9 20.1 %collective-permute-start.36 = (bf16[1536,1024]{1,0:T(8,128)(2,1)}, bf16[1536,1024]{1,0:T(8,128)(2,1)S(1)}, u32[]{:S(2)}, u32[]{:S(2)}) collective-permute-start(bf16[1536,1024]{1,0:T(8,128)(2,1)} %all-gather.8.cloned.1.call-done.q0), channel_id=1, source_target_pairs={{0,1},{1,0},{2,3},{3,2},{4,5},{5,4},{6,7},{7,6},{8,9},{9,8},{10,11... | collective-permute-start | bytes 9437192 | tf_op jit(solution)/shard_map/ppermute | solution.py:34
  217.1 6.0 %collective-permute-start.33 = (bf16[64,2048]{1,0:T(8,128)(2,1)}, bf16[64,2048]{1,0:T(8,128)(2,1)S(1)}, u32[]{:S(2)}, u32[]{:S(2)}) collective-permute-start(bf16[64,2048]{1,0:T(8,128)(2,1)} %get-tuple-element.136), channel_id=1, source_target_pairs={{0,1},{1,0},{2,3},{3,2},{4,5},{5,4},{6,7},{7,6},{8,9},{9,8},{10,11... | collective-permute-start | bytes 786440 | tf_op jit(solution)/shard_map/ppermute | solution.py:34
  219.2 17.9 %collective-permute-start.31 = (bf16[128,2048]{1,0:T(8,128)(2,1)S(1)}, bf16[128,2048]{1,0:T(8,128)(2,1)S(1)}, u32[]{:S(2)}, u32[]{:S(2)}) collective-permute-start(bf16[128,2048]{1,0:T(8,128)(2,1)S(1)} %get-tuple-element.134), channel_id=1, source_target_pairs={{0,28},{4,0},{8,4},{12,8},{16,12},{20,16},{24,20},{28,24},{1,29},{... | collective-permute-start | bytes 1572872 | tf_op jit(solution)/shard_map/ppermute | solution.py:29
  221.9 15.2 %collective-permute-start.32 = (bf16[128,2048]{1,0:T(8,128)(2,1)S(1)}, bf16[128,2048]{1,0:T(8,128)(2,1)S(1)}, u32[]{:S(2)}, u32[]{:S(2)}) collective-permute-start(bf16[128,2048]{1,0:T(8,128)(2,1)S(1)} %get-tuple-element.135), channel_id=1, source_target_pairs={{0,4},{4,8},{8,12},{12,16},{16,20},{20,24},{24,28},{28,0},{1,5},{5... | collective-permute-start | bytes 1572872 | tf_op jit(solution)/shard_map/ppermute | solution.py:29
  221.9 8.8 %collective-permute-start.34 = (bf16[64,2048]{1,0:T(8,128)(2,1)S(1)}, bf16[64,2048]{1,0:T(8,128)(2,1)S(1)}, u32[]{:S(2)}, u32[]{:S(2)}) collective-permute-start(bf16[64,2048]{1,0:T(8,128)(2,1)S(1)} %copy-done.35), channel_id=1, source_target_pairs={{0,2},{1,3},{2,0},{3,1},{4,6},{5,7},{6,4},{7,5},{8,10},{9,11},{10,... | collective-permute-start | bytes 786440 | tf_op jit(solution)/shard_map/ppermute | solution.py:34
  223.2 13.9 %collective-permute-start.35 = (bf16[64,2048]{1,0:T(8,128)(2,1)S(1)}, bf16[64,2048]{1,0:T(8,128)(2,1)S(1)}, u32[]{:S(2)}, u32[]{:S(2)}) collective-permute-start(bf16[64,2048]{1,0:T(8,128)(2,1)S(1)} %copy-done.34), channel_id=1, source_target_pairs={{0,3},{1,2},{2,1},{3,0},{4,7},{5,6},{6,5},{7,4},{8,11},{9,10},{10,... | collective-permute-start | bytes 786440 | tf_op jit(solution)/shard_map/ppermute | solution.py:34
  238.0 14.3 %collective-permute-start.37 = (bf16[128,2048]{1,0:T(8,128)(2,1)S(1)}, bf16[128,2048]{1,0:T(8,128)(2,1)S(1)}, u32[]{:S(2)}, u32[]{:S(2)}) collective-permute-start(bf16[128,2048]{1,0:T(8,128)(2,1)S(1)} %get-tuple-element.145), channel_id=1, source_target_pairs={{0,28},{4,0},{8,4},{12,8},{16,12},{20,16},{24,20},{28,24},{1,29},{... | collective-permute-start | bytes 1572872 | tf_op jit(solution)/shard_map/ppermute | solution.py:29
  240.7 15.1 %collective-permute-start.38 = (bf16[128,2048]{1,0:T(8,128)(2,1)S(1)}, bf16[128,2048]{1,0:T(8,128)(2,1)S(1)}, u32[]{:S(2)}, u32[]{:S(2)}) collective-permute-start(bf16[128,2048]{1,0:T(8,128)(2,1)S(1)} %get-tuple-element.146), channel_id=1, source_target_pairs={{0,4},{4,8},{8,12},{12,16},{16,20},{20,24},{24,28},{28,0},{1,5},{5... | collective-permute-start | bytes 1572872 | tf_op jit(solution)/shard_map/ppermute | solution.py:29
  (33 other events, 601.4 us)
Sparse Core Ops, SparseCore 0:
  9.8 32.9 all-gather.9
  44.6 40.0 all-gather.11
  86.5 39.6 all-gather.13
  127.8 57.5 all-gather.7

commit v6 on v5

--- a/solution.py
+++ b/solution.py
@@ -305,12 +305,13 @@
     hold = lax.optimization_barrier
 
     outbound, table = dispatch(routes.T, route_gain.T, tokens)
+    tables = lax.all_to_all(table, "z", split_axis=0, concat_axis=0, tiled=True)
+    outbound, tables = hold((outbound, tables))
     arrived = lax.all_to_all(outbound, ("z", "xh", "c"), split_axis=0, concat_axis=0, tiled=True)
 
     gates = [lax.all_gather(gate_weight[0], "y", axis=0, tiled=True)] + across_x(gate_weight[0])
     ups = [lax.all_gather(up_weight[0], "y", axis=0, tiled=True)] + across_x(up_weight[0])
     downs = [lax.all_gather(down_weight[0], "y", axis=1, tiled=True)] + across_x(down_weight[0])
-    tables = lax.all_to_all(table, "z", split_axis=0, concat_axis=0, tiled=True)
     weights = mixing(place, tables)
 
     half = query_weight.shape[0] // 2
@@ -323,10 +324,10 @@
     ans4, ans3 = expert(GROUPS[:2], place, offsets, arrived, gates, ups, downs)
     got4, got3 = exchange(ans4), exchange(ans3)
     ans2, ans1, ans0 = expert(GROUPS[2:], place, offsets, arrived, gates, ups, downs)
-    got4, ans2, ans1, ans0 = hold((got4, ans2, ans1, ans0))
+    got4, got3, ans2, ans1, ans0 = hold((got4, got3, ans2, ans1, ans0))
     low, high = combine((4,), weights, (ans4[0],) + got4, [])
     low, high, got0 = shift(low, "z", -1), shift(high, "z", 1), exchange(ans0)
-    low, high, got3, got0, ans2 = hold((low, high, got3, got0, ans2))
+    low, high, got0, ans2 = hold((low, high, got0, ans2))
     low, high = combine((3, 5), weights, (ans3[0],) + got3, [low, high])
     low, high, got2 = shift(low, "z", -1), shift(high, "z", 1), exchange(ans2)
     low, high, got2, ans1, q_own = hold((low, high, got2, ans1, q_own))

time: 272 us -> 274 us (level)
  waiting for transfers between devices: 133 us -> 136 us
  local copies, waits for them, and re-layouts: 7.92 us -> 4.96 us
    ppermute x19, waiting for transfers between devices: 81.4 us -> 92.7 us  [swap(): return lax.ppermute(x, axes, [(i, i ^ k) for i in range(n)])]
    all_gather x1, waiting for transfers between devices: 9.01 us -> 0.02 us  [shards(): lax.all_gather(down_weight[0], 'y', axis=1, tiled=True)]
    all_to_all x1, starting transfers between devices: 12.8 us -> 6.75 us  [shards(): lax.all_to_all(outbound, ('z', 'xh', 'c'), split_axis=0, concat_axis=0, t...]
    unnamed x74 -> x64, local copies, waits for them, and re-layouts: 6.38 us -> 3.48 us
  transfers between devices with their start and end apart: 44 -> 44, of which waited for: 18 -> 18; matrix products, arithmetic and copies ran while one was open for 1% -> 1% of each run, Pallas kernels for 13% -> 14%
where the time goes in v6:
time: 274 us; the launch traced here: 273 us
  waiting for transfers between devices  136 us (50%)
  starting transfers between devices  54.3 us (20%)
  Pallas kernels  46.5 us (17%)
  blocking collectives  15.9 us (6%)
  between operations  14.2 us (5%)
  local copies, waits for them, and re-layouts  4.96 us (2%)
    ppermute x19, waiting for transfers between devices, swap(): return lax.ppermute(x, axes, [(i, i ^ k) for i in range(n)])  92.7 us
    ppermute x20, waiting for transfers between devices, shift(): return lax.ppermute(x, axis, [(i, (i + by) % n) for i in range(n)])  38.7 us
    pallas_call x2, Pallas kernels, expert(): pl.pallas_call(functools.partial(expert_kernel, groups), out_shape=tuple(...  25.1 us
    ppermute x19, starting transfers between devices, swap(): return lax.ppermute(x, axes, [(i, i ^ k) for i in range(n)])  23.9 us
    ppermute x20, starting transfers between devices, shift(): return lax.ppermute(x, axis, [(i, (i + by) % n) for i in range(n)])  23.5 us
    all_to_all x1, blocking collectives, shards(): tables = lax.all_to_all(table, 'z', split_axis=0, concat_axis=0, tiled=True)  15.9 us
    pallas_call x1, Pallas kernels, final(): pl.pallas_call(final_kernel, out_shape=(jax.ShapeDtypeStruct((rows, width...  8.15 us
    all_to_all x1, starting transfers between devices, shards(): lax.all_to_all(outbound, ('z', 'xh', 'c'), split_axis=0, concat_axis=0, t...  6.75 us
  transfers between devices with their start and end apart: 44, of which 18 were waited for; matrix products, arithmetic and copies ran while one was open for 1% of the time, Pallas kernels for 14%

profile of v6, /device:TPU:1, one launch (start us, length us, event | category | flops | bytes accessed | tf_op | source)
XLA Modules:
  0.0 273.1 jit_solution(14381172965286190560)
XLA Ops:
  8.7 6.0 %shard_map.95 = (bf16[1024,2048]{1,0:T(8,128)(2,1)}, f32[64,128]{1,0:T(8,128)}) custom-call(s32[6,128]{1,0:T(8,128)} %bitcast.37, f32[6,128]{1,0:T(8,128)} %bitcast.38, bf16[128,2048]{1,0:T(8,128)(2,1)} %tokens.3), custom_call_target="tpu_custom_call" | custom-call | flops 536870912 | bytes 5242880 | tf_op jit(solution)/shard_map/pallas_call | solution.py:69
  14.6 15.9 %all_to_all.23 = f32[8,8,128]{2,1,0:T(8,128)S(1)} all-to-all(f32[8,8,128]{2,1,0:T(8,128)} %bitcast.35), channel_id=1, replica_groups=mesh['xl'=2,'y'=4,'z'=8,'xh'=2,'c'=2] {'z'}, dimensions={0} | all-to-all | bytes 65536 | tf_op jit(solution)/shard_map/all_to_all | solution.py:308
  30.6 6.7 %all-to-all-start.1 = ((bf16[32,32,2048]{2,1,0:T(8,128)(2,1)}), bf16[32,32,2048]{2,1,0:T(8,128)(2,1)}, u32[]{:S(2)}, u32[]{:S(2)}) async-start(bf16[32,32,2048]{2,1,0:T(8,128)(2,1)} %bitcast.25), calls=%async_computation.1 | async-start | bytes 8388608 | tf_op jit(solution)/shard_map/all_to_all | solution.py:310
  41.6 27.1 %collective-permute-done.10.refs_14_ = bf16[768,256]{1,0:T(8,128)(2,1)S(1)} collective-permute-done((bf16[768,256]{1,0:T(8,128)(2,1)S(1)}, bf16[768,256]{1,0:T(8,128)(2,1)S(1)}, u32[]{:S(2)}, u32[]{:S(2)}) %collective-permute-start.10) | collective-permute-done | bytes 393248 | tf_op jit(solution)/shard_map/ppermute | solution.py:34
  68.8 1.3 collective-permute-start.11
  70.1 1.4 collective-permute-start.12
  71.5 10.2 %collective-permute-done.refs_2_ = bf16[256,768]{1,0:T(8,128)(2,1)S(1)} collective-permute-done((bf16[256,768]{1,0:T(8,128)(2,1)S(1)}, bf16[256,768]{1,0:T(8,128)(2,1)S(1)}, u32[]{:S(2)}, u32[]{:S(2)}) %collective-permute-start) | collective-permute-done | bytes 393248 | tf_op jit(solution)/shard_map/ppermute | solution.py:34
  81.7 1.3 collective-permute-start.1
  83.0 1.4 collective-permute-start.2
  84.5 8.1 %collective-permute-done.5.refs_8_ = bf16[256,768]{1,0:T(8,128)(2,1)S(1)} collective-permute-done((bf16[256,768]{1,0:T(8,128)(2,1)S(1)}, bf16[256,768]{1,0:T(8,128)(2,1)S(1)}, u32[]{:S(2)}, u32[]{:S(2)}) %collective-permute-start.5) | collective-permute-done | bytes 393248 | tf_op jit(solution)/shard_map/ppermute | solution.py:34
  92.6 1.3 collective-permute-start.6
  93.9 1.5 collective-permute-start.7
  95.6 2.7 %collective-permute-start.14 = (bf16[384,256]{1,0:T(8,128)(2,1)S(1)}, bf16[384,256]{1,0:T(8,128)(2,1)S(1)}, u32[]{:S(2)}, u32[]{:S(2)}) collective-permute-start(bf16[384,256]{1,0:T(8,128)(2,1)S(1)} %slice.29), channel_id=1, source_target_pairs={{0,96},{32,0},{64,32},{96,64},{1,97},{33,1},{65,33},{97,65},{2,98}... | collective-permute-start | bytes 589832 | tf_op jit(solution)/shard_map/ppermute | solution.py:29
  99.1 12.5 %collective-permute-done.6.refs_9_ = bf16[256,768]{1,0:T(8,128)(2,1)S(1)} collective-permute-done((bf16[256,768]{1,0:T(8,128)(2,1)S(1)}, bf16[256,768]{1,0:T(8,128)(2,1)S(1)}, u32[]{:S(2)}, u32[]{:S(2)}) %collective-permute-start.6) | collective-permute-done | bytes 393248 | tf_op jit(solution)/shard_map/ppermute | solution.py:29
  113.6 4.8 %collective-permute-done.13.refs_17_ = bf16[384,256]{1,0:T(8,128)(2,1)S(1)} collective-permute-done((bf16[384,256]{1,0:T(8,128)(2,1)S(1)}, bf16[384,256]{1,0:T(8,128)(2,1)S(1)}, u32[]{:S(2)}, u32[]{:S(2)}) %collective-permute-start.13) | collective-permute-done | bytes 196640 | tf_op jit(solution)/shard_map/ppermute | solution.py:29
  118.4 2.2 collective-permute-start.9
  121.8 2.7 collective-permute-done.3.refs_5_
  124.5 4.2 %collective-permute-done.8.refs_11_ = bf16[128,768]{1,0:T(8,128)(2,1)} collective-permute-done((bf16[128,768]{1,0:T(8,128)(2,1)S(1)}, bf16[128,768]{1,0:T(8,128)(2,1)}, u32[]{:S(2)}, u32[]{:S(2)}) %collective-permute-start.8) | collective-permute-done | bytes 196640 | tf_op jit(solution)/shard_map/ppermute | solution.py:29
  128.7 2.6 all-to-all-done.1
  131.4 11.0 %shard_map.97 = (bf16[32,2048]{1,0:T(8,128)(2,1)}, bf16[32,2048]{1,0:T(8,128)(2,1)}, bf16[32,2048]{1,0:T(8,128)(2,1)}, bf16[32,2048]{1,0:T(8,128)(2,1)}, bf16[64...) custom-call(s32[2]{0:T(128)} %pad_add_fusion.place, ...), custom_call_target="tpu_custom_call" | custom-call | flops 3623878656 | bytes 16777216 | tf_op jit(solution)/shard_map/pallas_call | solution.py:171
  142.4 3.0 %collective-permute-start.15 = (bf16[32,2048]{1,0:T(8,128)(2,1)}, bf16[32,2048]{1,0:T(8,128)(2,1)S(1)}, u32[]{:S(2)}, u32[]{:S(2)}) collective-permute-start(bf16[32,2048]{1,0:T(8,128)(2,1)} %get-tuple-element.81), channel_id=1, source_target_pairs={{0,1},{1,0},{2,3},{3,2},{4,5},{5,4},{6,7},{7,6},{8,9},{9,8},{10,11... | collective-permute-start | bytes 393224 | tf_op jit(solution)/shard_map/ppermute | solution.py:34
  146.8 3.2 %collective-permute-start.20 = (bf16[64,2048]{1,0:T(8,128)(2,1)}, bf16[64,2048]{1,0:T(8,128)(2,1)}, u32[]{:S(2)}, u32[]{:S(2)}) collective-permute-start(bf16[64,2048]{1,0:T(8,128)(2,1)} %get-tuple-element.86), channel_id=1, source_target_pairs={{0,3},{1,2},{2,1},{3,0},{4,7},{5,6},{6,5},{7,4},{8,11},{9,10},{10,... | collective-permute-start | bytes 786440 | tf_op jit(solution)/shard_map/ppermute | solution.py:34
  151.0 2.6 collective-permute-start.17
  153.5 14.1 %shard_map.98 = (bf16[64,2048]{1,0:T(8,128)(2,1)}, bf16[64,2048]{1,0:T(8,128)(2,1)}, bf16[64,2048]{1,0:T(8,128)(2,1)}, bf16[64,2048]{1,0:T(8,128)(2,1)}, bf16[64...) custom-call(s32[2]{0:T(128)} %pad_add_fusion.place, ...), custom_call_target="tpu_custom_call" | custom-call | flops 6039797760 | bytes 16777216 | tf_op jit(solution)/shard_map/pallas_call | solution.py:171
  167.7 10.7 %collective-permute-done.16.refs_3_ = bf16[32,2048]{1,0:T(8,128)(2,1)} collective-permute-done((bf16[32,2048]{1,0:T(8,128)(2,1)}, bf16[32,2048]{1,0:T(8,128)(2,1)}, u32[]{:S(2)}, u32[]{:S(2)}) %collective-permute-start.16) | collective-permute-done | bytes 131104 | tf_op jit(solution)/shard_map/ppermute | solution.py:34
  178.4 6.7 %collective-permute-done.17.refs_4_ = bf16[32,2048]{1,0:T(8,128)(2,1)} collective-permute-done((bf16[32,2048]{1,0:T(8,128)(2,1)}, bf16[32,2048]{1,0:T(8,128)(2,1)}, u32[]{:S(2)}, u32[]{:S(2)}) %collective-permute-start.17) | collective-permute-done | bytes 131104 | tf_op jit(solution)/shard_map/ppermute | solution.py:34
  186.0 1.4 shard_map.99
  187.5 1.5 collective-permute-start.22
  189.0 1.3 collective-permute-start.24
  190.3 2.3 collective-permute-start.25
  192.6 2.6 collective-permute-done.24.a2
  195.2 3.5 %collective-permute-done.25.a3 = bf16[32,2048]{1,0:T(8,128)(2,1)S(1)} collective-permute-done((bf16[32,2048]{1,0:T(8,128)(2,1)}, bf16[32,2048]{1,0:T(8,128)(2,1)S(1)}, u32[]{:S(2)}, u32[]{:S(2)}) %collective-permute-start.25) | collective-permute-done | bytes 131104 | tf_op jit(solution)/shard_map/ppermute | solution.py:34
  198.7 2.5 shard_map.100
  201.2 1.3 collective-permute-start.26
  203.1 1.9 collective-permute-start.29
  205.0 1.3 collective-permute-start.30
  206.3 6.5 %collective-permute-done.29.refs_4_ = bf16[64,2048]{1,0:T(8,128)(2,1)} collective-permute-done((bf16[64,2048]{1,0:T(8,128)(2,1)}, bf16[64,2048]{1,0:T(8,128)(2,1)}, u32[]{:S(2)}, u32[]{:S(2)}) %collective-permute-start.29) | collective-permute-done | bytes 262176 | tf_op jit(solution)/shard_map/ppermute | solution.py:34
  212.8 5.8 %collective-permute-done.30.refs_5_ = bf16[64,2048]{1,0:T(8,128)(2,1)} collective-permute-done((bf16[64,2048]{1,0:T(8,128)(2,1)}, bf16[64,2048]{1,0:T(8,128)(2,1)}, u32[]{:S(2)}, u32[]{:S(2)}) %collective-permute-start.30) | collective-permute-done | bytes 262176 | tf_op jit(solution)/shard_map/ppermute | solution.py:34
  219.1 1.7 shard_map.101
  220.8 2.8 %collective-permute-start.31 = (bf16[128,2048]{1,0:T(8,128)(2,1)S(1)}, bf16[128,2048]{1,0:T(8,128)(2,1)S(1)}, u32[]{:S(2)}, u32[]{:S(2)}) collective-permute-start(bf16[128,2048]{1,0:T(8,128)(2,1)S(1)} %get-tuple-element.138), channel_id=1, source_target_pairs={{0,28},{4,0},{8,4},{12,8},{16,12},{20,16},{24,20},{28,24},{1,29},{... | collective-permute-start | bytes 1572872 | tf_op jit(solution)/shard_map/ppermute | solution.py:29
  223.6 2.1 collective-permute-start.34
  225.7 1.6 collective-permute-start.35
  227.4 5.1 %collective-permute-done.34.refs_4_ = bf16[64,2048]{1,0:T(8,128)(2,1)S(1)} collective-permute-done((bf16[64,2048]{1,0:T(8,128)(2,1)S(1)}, bf16[64,2048]{1,0:T(8,128)(2,1)S(1)}, u32[]{:S(2)}, u32[]{:S(2)}) %collective-permute-start.34) | collective-permute-done | bytes 262176 | tf_op jit(solution)/shard_map/ppermute | solution.py:34
  232.4 6.4 %collective-permute-done.35.refs_5_ = bf16[64,2048]{1,0:T(8,128)(2,1)S(1)} collective-permute-done((bf16[64,2048]{1,0:T(8,128)(2,1)S(1)}, bf16[64,2048]{1,0:T(8,128)(2,1)S(1)}, u32[]{:S(2)}, u32[]{:S(2)}) %collective-permute-start.35) | collective-permute-done | bytes 262176 | tf_op jit(solution)/shard_map/ppermute | solution.py:34
  239.8 2.7 %collective-permute-start.37 = (bf16[128,2048]{1,0:T(8,128)(2,1)S(1)}, bf16[128,2048]{1,0:T(8,128)(2,1)S(1)}, u32[]{:S(2)}, u32[]{:S(2)}) collective-permute-start(bf16[128,2048]{1,0:T(8,128)(2,1)S(1)} %get-tuple-element.149), channel_id=1, source_target_pairs={{0,28},{4,0},{8,4},{12,8},{16,12},{20,16},{24,20},{28,24},{1,29},{... | collective-permute-start | bytes 1572872 | tf_op jit(solution)/shard_map/ppermute | solution.py:29
  243.1 10.9 %collective-permute-done.37.left = bf16[128,2048]{1,0:T(8,128)(2,1)S(1)} collective-permute-done((bf16[128,2048]{1,0:T(8,128)(2,1)S(1)}, bf16[128,2048]{1,0:T(8,128)(2,1)S(1)}, u32[]{:S(2)}, u32[]{:S(2)}) %collective-permute-start.37) | collective-permute-done | bytes 524320 | tf_op jit(solution)/shard_map/ppermute | solution.py:29
  254.0 3.6 %collective-permute-done.38.right = bf16[128,2048]{1,0:T(8,128)(2,1)S(1)} collective-permute-done((bf16[128,2048]{1,0:T(8,128)(2,1)S(1)}, bf16[128,2048]{1,0:T(8,128)(2,1)S(1)}, u32[]{:S(2)}, u32[]{:S(2)}) %collective-permute-start.38) | collective-permute-done | bytes 524320 | tf_op jit(solution)/shard_map/ppermute | solution.py:29
  258.4 8.1 %shard_map.103 = (bf16[128,2048]{1,0:T(8,128)(2,1)}, bf16[128,1536]{1,0:T(8,128)(2,1)}) custom-call(s32[2]{0:T(128)} %add_multiply_fusion.offsets, bf16[8,128,256]{2,1,0:T(8,128)(2,1)} %copy-done.1, bf16[32,2048]{1,0:T(8,128)(2,1)} %get-tuple-element.99.a0, bf16[32,2048]{1,0:T(8,128)(2,1)} %copy-done.27, bf16[32,2048]{1,0:T(8,128)(2,1)} %copy-done.28, ...), custom_call_target="tpu_custom_call" | custom-call | flops 805306368 | bytes 8388608 | tf_op jit(solution)/shard_map/pallas_call | solution.py:274
  (128 shorter events, 16.7 us)
Async XLA Ops:
  7.2 121.5 %all-gather.10.cloned.1.call-start = ((), (), s32[]{:S(2)}) async-start(), calls=%async_computation.3 | async-start | bytes 1966080 | tf_op jit(solution)/shard_map/all_gather | solution.py:312
  7.9 120.8 %all-gather.12.cloned.1.call-start = ((), (), s32[]{:S(2)}) async-start(), calls=%async_computation.4 | async-start | bytes 1966080 | tf_op jit(solution)/shard_map/all_gather | solution.py:313
  30.6 100.8 %all-to-all-start.1 = ((bf16[32,32,2048]{2,1,0:T(8,128)(2,1)}), bf16[32,32,2048]{2,1,0:T(8,128)(2,1)}, u32[]{:S(2)}, u32[]{:S(2)}) async-start(bf16[32,32,2048]{2,1,0:T(8,128)(2,1)} %bitcast.25), calls=%async_computation.1 | async-start | bytes 8388608 | tf_op jit(solution)/shard_map/all_to_all | solution.py:310
  37.3 91.4 %all-gather.14.cloned.1.call-start = ((), (), s32[]{:S(2)}) async-start(), calls=%async_computation.5 | async-start | bytes 1966080 | tf_op jit(solution)/shard_map/all_gather | solution.py:314
  38.0 168.3 %all-gather.8.cloned.1.call-start = ((), (), s32[]{:S(2)}) async-start(), calls=%async_computation.2 | async-start | bytes 3538944 | tf_op jit(solution)/shard_map/all_gather | solution.py:319
  38.9 29.8 %collective-permute-start.10 = (bf16[768,256]{1,0:T(8,128)(2,1)S(1)}, bf16[768,256]{1,0:T(8,128)(2,1)S(1)}, u32[]{:S(2)}, u32[]{:S(2)}) collective-permute-start(bf16[768,256]{1,0:T(8,128)(2,1)S(1)} %bitcast.34), channel_id=1, source_target_pairs={{0,128},{128,0},{1,129},{129,1},{2,130},{130,2},{3,131},{131,3},{4... | collective-permute-start | bytes 1179656 | tf_op jit(solution)/shard_map/ppermute | solution.py:34
  40.2 41.6 %collective-permute-start = (bf16[256,768]{1,0:T(8,128)(2,1)S(1)}, bf16[256,768]{1,0:T(8,128)(2,1)S(1)}, u32[]{:S(2)}, u32[]{:S(2)}) collective-permute-start(bf16[256,768]{1,0:T(8,128)(2,1)S(1)} %bitcast.32), channel_id=1, source_target_pairs={{0,128},{128,0},{1,129},{129,1},{2,130},{130,2},{3,131},{131,3},{4... | collective-permute-start | bytes 1179656 | tf_op jit(solution)/shard_map/ppermute | solution.py:34
  40.5 52.1 %collective-permute-start.5 = (bf16[256,768]{1,0:T(8,128)(2,1)S(1)}, bf16[256,768]{1,0:T(8,128)(2,1)S(1)}, u32[]{:S(2)}, u32[]{:S(2)}) collective-permute-start(bf16[256,768]{1,0:T(8,128)(2,1)S(1)} %bitcast.33), channel_id=1, source_target_pairs={{0,128},{128,0},{1,129},{129,1},{2,130},{130,2},{3,131},{131,3},{4... | collective-permute-start | bytes 1179656 | tf_op jit(solution)/shard_map/ppermute | solution.py:34
  68.8 25.1 %collective-permute-start.11 = (bf16[768,256]{1,0:T(8,128)(2,1)S(1)}, bf16[768,256]{1,0:T(8,128)(2,1)S(1)}, u32[]{:S(2)}, u32[]{:S(2)}) collective-permute-start(bf16[768,256]{1,0:T(8,128)(2,1)S(1)} %collective-permute-done.10.refs_14_), channel_id=1, source_target_pairs={{0,32},{32,64},{64,96},{96,0},{1,33},{33,65},{65,97},{97,1},{2,34}... | collective-permute-start | bytes 1179656 | tf_op jit(solution)/shard_map/ppermute | solution.py:29
  70.1 25.3 %collective-permute-start.12 = (bf16[768,256]{1,0:T(8,128)(2,1)S(1)}, bf16[768,256]{1,0:T(8,128)(2,1)S(1)}, u32[]{:S(2)}, u32[]{:S(2)}) collective-permute-start(bf16[768,256]{1,0:T(8,128)(2,1)S(1)} %collective-permute-done.10.refs_14_), channel_id=1, source_target_pairs={{0,96},{32,0},{64,32},{96,64},{1,97},{33,1},{65,33},{97,65},{2,98}... | collective-permute-start | bytes 1179656 | tf_op jit(solution)/shard_map/ppermute | solution.py:29
  81.7 13.8 %collective-permute-start.1 = (bf16[256,768]{1,0:T(8,128)(2,1)S(1)}, bf16[256,768]{1,0:T(8,128)(2,1)S(1)}, u32[]{:S(2)}, u32[]{:S(2)}) collective-permute-start(bf16[256,768]{1,0:T(8,128)(2,1)S(1)} %collective-permute-done.refs_2_), channel_id=1, source_target_pairs={{0,32},{32,64},{64,96},{96,0},{1,33},{33,65},{65,97},{97,1},{2,34}... | collective-permute-start | bytes 1179656 | tf_op jit(solution)/shard_map/ppermute | solution.py:29
  83.0 15.3 %collective-permute-start.2 = (bf16[256,768]{1,0:T(8,128)(2,1)S(1)}, bf16[256,768]{1,0:T(8,128)(2,1)S(1)}, u32[]{:S(2)}, u32[]{:S(2)}) collective-permute-start(bf16[256,768]{1,0:T(8,128)(2,1)S(1)} %collective-permute-done.refs_2_), channel_id=1, source_target_pairs={{0,96},{32,0},{64,32},{96,64},{1,97},{33,1},{65,33},{97,65},{2,98}... | collective-permute-start | bytes 1179656 | tf_op jit(solution)/shard_map/ppermute | solution.py:29
  92.6 19.0 %collective-permute-start.6 = (bf16[256,768]{1,0:T(8,128)(2,1)S(1)}, bf16[256,768]{1,0:T(8,128)(2,1)S(1)}, u32[]{:S(2)}, u32[]{:S(2)}) collective-permute-start(bf16[256,768]{1,0:T(8,128)(2,1)S(1)} %collective-permute-done.5.refs_8_), channel_id=1, source_target_pairs={{0,32},{32,64},{64,96},{96,0},{1,33},{33,65},{65,97},{97,1},{2,34}... | collective-permute-start | bytes 1179656 | tf_op jit(solution)/shard_map/ppermute | solution.py:29
  93.9 18.9 %collective-permute-start.7 = (bf16[256,768]{1,0:T(8,128)(2,1)S(1)}, bf16[256,768]{1,0:T(8,128)(2,1)S(1)}, u32[]{:S(2)}, u32[]{:S(2)}) collective-permute-start(bf16[256,768]{1,0:T(8,128)(2,1)S(1)} %collective-permute-done.5.refs_8_), channel_id=1, source_target_pairs={{0,96},{32,0},{64,32},{96,64},{1,97},{33,1},{65,33},{97,65},{2,98}... | collective-permute-start | bytes 1179656 | tf_op jit(solution)/shard_map/ppermute | solution.py:29
  95.4 22.9 %collective-permute-start.13 = (bf16[384,256]{1,0:T(8,128)(2,1)S(1)}, bf16[384,256]{1,0:T(8,128)(2,1)S(1)}, u32[]{:S(2)}, u32[]{:S(2)}) collective-permute-start(bf16[384,256]{1,0:T(8,128)(2,1)S(1)} %slice.28), channel_id=1, source_target_pairs={{0,32},{32,64},{64,96},{96,0},{1,33},{33,65},{65,97},{97,1},{2,34}... | collective-permute-start | bytes 589832 | tf_op jit(solution)/shard_map/ppermute | solution.py:29
  95.6 26.2 %collective-permute-start.14 = (bf16[384,256]{1,0:T(8,128)(2,1)S(1)}, bf16[384,256]{1,0:T(8,128)(2,1)S(1)}, u32[]{:S(2)}, u32[]{:S(2)}) collective-permute-start(bf16[384,256]{1,0:T(8,128)(2,1)S(1)} %slice.29), channel_id=1, source_target_pairs={{0,96},{32,0},{64,32},{96,64},{1,97},{33,1},{65,33},{97,65},{2,98}... | collective-permute-start | bytes 589832 | tf_op jit(solution)/shard_map/ppermute | solution.py:29
  98.3 26.1 %collective-permute-start.3 = (bf16[128,768]{1,0:T(8,128)(2,1)S(1)}, bf16[128,768]{1,0:T(8,128)(2,1)}, u32[]{:S(2)}, u32[]{:S(2)}) collective-permute-start(bf16[128,768]{1,0:T(8,128)(2,1)S(1)} %slice.24), channel_id=1, source_target_pairs={{0,32},{32,64},{64,96},{96,0},{1,33},{33,65},{65,97},{97,1},{2,34}... | collective-permute-start | bytes 589832 | tf_op jit(solution)/shard_map/ppermute | solution.py:29
  111.6 12.9 %collective-permute-start.4 = (bf16[128,768]{1,0:T(8,128)(2,1)S(1)}, bf16[128,768]{1,0:T(8,128)(2,1)}, u32[]{:S(2)}, u32[]{:S(2)}) collective-permute-start(bf16[128,768]{1,0:T(8,128)(2,1)S(1)} %slice.25), channel_id=1, source_target_pairs={{0,96},{32,0},{64,32},{96,64},{1,97},{33,1},{65,33},{97,65},{2,98}... | collective-permute-start | bytes 589832 | tf_op jit(solution)/shard_map/ppermute | solution.py:29
  112.8 15.9 %collective-permute-start.8 = (bf16[128,768]{1,0:T(8,128)(2,1)S(1)}, bf16[128,768]{1,0:T(8,128)(2,1)}, u32[]{:S(2)}, u32[]{:S(2)}) collective-permute-start(bf16[128,768]{1,0:T(8,128)(2,1)S(1)} %slice.26), channel_id=1, source_target_pairs={{0,32},{32,64},{64,96},{96,0},{1,33},{33,65},{65,97},{97,1},{2,34}... | collective-permute-start | bytes 589832 | tf_op jit(solution)/shard_map/ppermute | solution.py:29
  118.4 10.3 %collective-permute-start.9 = (bf16[128,768]{1,0:T(8,128)(2,1)S(1)}, bf16[128,768]{1,0:T(8,128)(2,1)S(1)}, u32[]{:S(2)}, u32[]{:S(2)}) collective-permute-start(bf16[128,768]{1,0:T(8,128)(2,1)S(1)} %slice.27), channel_id=1, source_target_pairs={{0,96},{32,0},{64,32},{96,64},{1,97},{33,1},{65,33},{97,65},{2,98}... | collective-permute-start | bytes 589832 | tf_op jit(solution)/shard_map/ppermute | solution.py:29
  142.4 7.9 %collective-permute-start.15 = (bf16[32,2048]{1,0:T(8,128)(2,1)}, bf16[32,2048]{1,0:T(8,128)(2,1)S(1)}, u32[]{:S(2)}, u32[]{:S(2)}) collective-permute-start(bf16[32,2048]{1,0:T(8,128)(2,1)} %get-tuple-element.81), channel_id=1, source_target_pairs={{0,1},{1,0},{2,3},{3,2},{4,5},{5,4},{6,7},{7,6},{8,9},{9,8},{10,11... | collective-permute-start | bytes 393224 | tf_op jit(solution)/shard_map/ppermute | solution.py:34
  146.2 92.6 %copy-start.1 = (bf16[8,128,256]{2,1,0:T(8,128)(2,1)}, bf16[8,128,256]{2,1,0:T(8,128)(2,1)S(1)}, u32[]{:S(2)}) copy-start(bf16[8,128,256]{2,1,0:T(8,128)(2,1)S(1)} %shard_map.96.refs_0_.refs_1_.weight) | copy-start | bytes 1572868
  146.2 38.9 %collective-permute-start.18 = (bf16[64,2048]{1,0:T(8,128)(2,1)}, bf16[64,2048]{1,0:T(8,128)(2,1)}, u32[]{:S(2)}, u32[]{:S(2)}) collective-permute-start(bf16[64,2048]{1,0:T(8,128)(2,1)} %get-tuple-element.84), channel_id=1, source_target_pairs={{0,1},{1,0},{2,3},{3,2},{4,5},{5,4},{6,7},{7,6},{8,9},{9,8},{10,11... | collective-permute-start | bytes 786440 | tf_op jit(solution)/shard_map/ppermute | solution.py:34
  146.3 38.8 %collective-permute-start.19 = (bf16[64,2048]{1,0:T(8,128)(2,1)}, bf16[64,2048]{1,0:T(8,128)(2,1)}, u32[]{:S(2)}, u32[]{:S(2)}) collective-permute-start(bf16[64,2048]{1,0:T(8,128)(2,1)} %get-tuple-element.85), channel_id=1, source_target_pairs={{0,2},{1,3},{2,0},{3,1},{4,6},{5,7},{6,4},{7,5},{8,10},{9,11},{10,... | collective-permute-start | bytes 786440 | tf_op jit(solution)/shard_map/ppermute | solution.py:34
  146.8 38.3 %collective-permute-start.20 = (bf16[64,2048]{1,0:T(8,128)(2,1)}, bf16[64,2048]{1,0:T(8,128)(2,1)}, u32[]{:S(2)}, u32[]{:S(2)}) collective-permute-start(bf16[64,2048]{1,0:T(8,128)(2,1)} %get-tuple-element.86), channel_id=1, source_target_pairs={{0,3},{1,2},{2,1},{3,0},{4,7},{5,6},{6,5},{7,4},{8,11},{9,10},{10,... | collective-permute-start | bytes 786440 | tf_op jit(solution)/shard_map/ppermute | solution.py:34
  149.9 28.4 %collective-permute-start.16 = (bf16[32,2048]{1,0:T(8,128)(2,1)}, bf16[32,2048]{1,0:T(8,128)(2,1)}, u32[]{:S(2)}, u32[]{:S(2)}) collective-permute-start(bf16[32,2048]{1,0:T(8,128)(2,1)} %get-tuple-element.82), channel_id=1, source_target_pairs={{0,2},{1,3},{2,0},{3,1},{4,6},{5,7},{6,4},{7,5},{8,10},{9,11},{10,... | collective-permute-start | bytes 393224 | tf_op jit(solution)/shard_map/ppermute | solution.py:34
  151.0 47.8 %copy-start.4 = (bf16[64,2048]{1,0:T(8,128)(2,1)S(1)}, bf16[64,2048]{1,0:T(8,128)(2,1)}, u32[]{:S(2)}) copy-start(bf16[64,2048]{1,0:T(8,128)(2,1)} %get-tuple-element.116.refs_2_) | copy-start | bytes 786436
  151.0 34.1 %collective-permute-start.17 = (bf16[32,2048]{1,0:T(8,128)(2,1)}, bf16[32,2048]{1,0:T(8,128)(2,1)}, u32[]{:S(2)}, u32[]{:S(2)}) collective-permute-start(bf16[32,2048]{1,0:T(8,128)(2,1)} %get-tuple-element.83), channel_id=1, source_target_pairs={{0,3},{1,2},{2,1},{3,0},{4,7},{5,6},{6,5},{7,4},{8,11},{9,10},{10,... | collective-permute-start | bytes 393224 | tf_op jit(solution)/shard_map/ppermute | solution.py:34
  167.7 51.5 %copy-start.3 = (bf16[64,2048]{1,0:T(8,128)(2,1)S(1)}, bf16[64,2048]{1,0:T(8,128)(2,1)}, u32[]{:S(2)}) copy-start(bf16[64,2048]{1,0:T(8,128)(2,1)} %get-tuple-element.132.refs_2_) | copy-start | bytes 786436
  187.4 51.4 %copy-start.2 = (bf16[64,2048]{1,0:T(8,128)(2,1)S(1)}, bf16[64,2048]{1,0:T(8,128)(2,1)}, u32[]{:S(2)}) copy-start(bf16[64,2048]{1,0:T(8,128)(2,1)} %get-tuple-element.131.refs_2_) | copy-start | bytes 786436
  187.4 11.3 %collective-permute-start.21 = (bf16[64,2048]{1,0:T(8,128)(2,1)S(1)}, bf16[64,2048]{1,0:T(8,128)(2,1)S(1)}, u32[]{:S(2)}, u32[]{:S(2)}) collective-permute-start(bf16[64,2048]{1,0:T(8,128)(2,1)S(1)} %get-tuple-element.104), channel_id=1, source_target_pairs={{0,28},{4,0},{8,4},{12,8},{16,12},{20,16},{24,20},{28,24},{1,29},{... | collective-permute-start | bytes 786440 | tf_op jit(solution)/shard_map/ppermute | solution.py:29
  187.5 11.2 %collective-permute-start.22 = (bf16[64,2048]{1,0:T(8,128)(2,1)S(1)}, bf16[64,2048]{1,0:T(8,128)(2,1)S(1)}, u32[]{:S(2)}, u32[]{:S(2)}) collective-permute-start(bf16[64,2048]{1,0:T(8,128)(2,1)S(1)} %get-tuple-element.105), channel_id=1, source_target_pairs={{0,4},{4,8},{8,12},{12,16},{16,20},{20,24},{24,28},{28,0},{1,5},{5... | collective-permute-start | bytes 786440 | tf_op jit(solution)/shard_map/ppermute | solution.py:29
  189.0 3.6 %collective-permute-start.23 = (bf16[32,2048]{1,0:T(8,128)(2,1)}, bf16[32,2048]{1,0:T(8,128)(2,1)S(1)}, u32[]{:S(2)}, u32[]{:S(2)}) collective-permute-start(bf16[32,2048]{1,0:T(8,128)(2,1)} %get-tuple-element.106), channel_id=1, source_target_pairs={{0,1},{1,0},{2,3},{3,2},{4,5},{5,4},{6,7},{7,6},{8,9},{9,8},{10,11... | collective-permute-start | bytes 393224 | tf_op jit(solution)/shard_map/ppermute | solution.py:34
  189.0 6.3 %collective-permute-start.24 = (bf16[32,2048]{1,0:T(8,128)(2,1)}, bf16[32,2048]{1,0:T(8,128)(2,1)S(1)}, u32[]{:S(2)}, u32[]{:S(2)}) collective-permute-start(bf16[32,2048]{1,0:T(8,128)(2,1)} %get-tuple-element.107), channel_id=1, source_target_pairs={{0,2},{1,3},{2,0},{3,1},{4,6},{5,7},{6,4},{7,5},{8,10},{9,11},{10,... | collective-permute-start | bytes 393224 | tf_op jit(solution)/shard_map/ppermute | solution.py:34
  190.3 8.4 %collective-permute-start.25 = (bf16[32,2048]{1,0:T(8,128)(2,1)}, bf16[32,2048]{1,0:T(8,128)(2,1)S(1)}, u32[]{:S(2)}, u32[]{:S(2)}) collective-permute-start(bf16[32,2048]{1,0:T(8,128)(2,1)} %get-tuple-element.108), channel_id=1, source_target_pairs={{0,3},{1,2},{2,1},{3,0},{4,7},{5,6},{6,5},{7,4},{8,11},{9,10},{10,... | collective-permute-start | bytes 393224 | tf_op jit(solution)/shard_map/ppermute | solution.py:34
  201.2 17.4 %collective-permute-start.26 = (bf16[128,2048]{1,0:T(8,128)(2,1)}, bf16[128,2048]{1,0:T(8,128)(2,1)S(1)}, u32[]{:S(2)}, u32[]{:S(2)}) collective-permute-start(bf16[128,2048]{1,0:T(8,128)(2,1)} %get-tuple-element.122), channel_id=1, source_target_pairs={{0,28},{4,0},{8,4},{12,8},{16,12},{20,16},{24,20},{28,24},{1,29},{... | collective-permute-start | bytes 1572872 | tf_op jit(solution)/shard_map/ppermute | solution.py:29
  202.5 16.1 %collective-permute-start.27 = (bf16[128,2048]{1,0:T(8,128)(2,1)}, bf16[128,2048]{1,0:T(8,128)(2,1)S(1)}, u32[]{:S(2)}, u32[]{:S(2)}) collective-permute-start(bf16[128,2048]{1,0:T(8,128)(2,1)} %get-tuple-element.123), channel_id=1, source_target_pairs={{0,4},{4,8},{8,12},{12,16},{16,20},{20,24},{24,28},{28,0},{1,5},{5... | collective-permute-start | bytes 1572872 | tf_op jit(solution)/shard_map/ppermute | solution.py:29
  202.7 3.7 %collective-permute-start.28 = (bf16[64,2048]{1,0:T(8,128)(2,1)}, bf16[64,2048]{1,0:T(8,128)(2,1)S(1)}, u32[]{:S(2)}, u32[]{:S(2)}) collective-permute-start(bf16[64,2048]{1,0:T(8,128)(2,1)} %get-tuple-element.124), channel_id=1, source_target_pairs={{0,1},{1,0},{2,3},{3,2},{4,5},{5,4},{6,7},{7,6},{8,9},{9,8},{10,11... | collective-permute-start | bytes 786440 | tf_op jit(solution)/shard_map/ppermute | solution.py:34
  203.1 9.7 %collective-permute-start.29 = (bf16[64,2048]{1,0:T(8,128)(2,1)}, bf16[64,2048]{1,0:T(8,128)(2,1)}, u32[]{:S(2)}, u32[]{:S(2)}) collective-permute-start(bf16[64,2048]{1,0:T(8,128)(2,1)} %get-tuple-element.125), channel_id=1, source_target_pairs={{0,2},{1,3},{2,0},{3,1},{4,6},{5,7},{6,4},{7,5},{8,10},{9,11},{10,... | collective-permute-start | bytes 786440 | tf_op jit(solution)/shard_map/ppermute | solution.py:34
  205.0 13.6 %collective-permute-start.30 = (bf16[64,2048]{1,0:T(8,128)(2,1)}, bf16[64,2048]{1,0:T(8,128)(2,1)}, u32[]{:S(2)}, u32[]{:S(2)}) collective-permute-start(bf16[64,2048]{1,0:T(8,128)(2,1)} %get-tuple-element.126), channel_id=1, source_target_pairs={{0,3},{1,2},{2,1},{3,0},{4,7},{5,6},{6,5},{7,4},{8,11},{9,10},{10,... | collective-permute-start | bytes 786440 | tf_op jit(solution)/shard_map/ppermute | solution.py:34
  218.6 20.2 %collective-permute-start.36 = (bf16[1536,1024]{1,0:T(8,128)(2,1)}, bf16[1536,1024]{1,0:T(8,128)(2,1)S(1)}, u32[]{:S(2)}, u32[]{:S(2)}) collective-permute-start(bf16[1536,1024]{1,0:T(8,128)(2,1)} %all-gather.8.cloned.1.call-done.q0), channel_id=1, source_target_pairs={{0,1},{1,0},{2,3},{3,2},{4,5},{5,4},{6,7},{7,6},{8,9},{9,8},{10,11... | collective-permute-start | bytes 9437192 | tf_op jit(solution)/shard_map/ppermute | solution.py:34
  218.8 6.9 %collective-permute-start.33 = (bf16[64,2048]{1,0:T(8,128)(2,1)}, bf16[64,2048]{1,0:T(8,128)(2,1)S(1)}, u32[]{:S(2)}, u32[]{:S(2)}) collective-permute-start(bf16[64,2048]{1,0:T(8,128)(2,1)} %get-tuple-element.140), channel_id=1, source_target_pairs={{0,1},{1,0},{2,3},{3,2},{4,5},{5,4},{6,7},{7,6},{8,9},{9,8},{10,11... | collective-permute-start | bytes 786440 | tf_op jit(solution)/shard_map/ppermute | solution.py:34
  220.8 17.9 %collective-permute-start.31 = (bf16[128,2048]{1,0:T(8,128)(2,1)S(1)}, bf16[128,2048]{1,0:T(8,128)(2,1)S(1)}, u32[]{:S(2)}, u32[]{:S(2)}) collective-permute-start(bf16[128,2048]{1,0:T(8,128)(2,1)S(1)} %get-tuple-element.138), channel_id=1, source_target_pairs={{0,28},{4,0},{8,4},{12,8},{16,12},{20,16},{24,20},{28,24},{1,29},{... | collective-permute-start | bytes 1572872 | tf_op jit(solution)/shard_map/ppermute | solution.py:29
  223.6 15.2 %collective-permute-start.32 = (bf16[128,2048]{1,0:T(8,128)(2,1)S(1)}, bf16[128,2048]{1,0:T(8,128)(2,1)S(1)}, u32[]{:S(2)}, u32[]{:S(2)}) collective-permute-start(bf16[128,2048]{1,0:T(8,128)(2,1)S(1)} %get-tuple-element.139), channel_id=1, source_target_pairs={{0,4},{4,8},{8,12},{12,16},{16,20},{20,24},{24,28},{28,0},{1,5},{5... | collective-permute-start | bytes 1572872 | tf_op jit(solution)/shard_map/ppermute | solution.py:29
  223.6 8.8 %collective-permute-start.34 = (bf16[64,2048]{1,0:T(8,128)(2,1)S(1)}, bf16[64,2048]{1,0:T(8,128)(2,1)S(1)}, u32[]{:S(2)}, u32[]{:S(2)}) collective-permute-start(bf16[64,2048]{1,0:T(8,128)(2,1)S(1)} %copy-done.31), channel_id=1, source_target_pairs={{0,2},{1,3},{2,0},{3,1},{4,6},{5,7},{6,4},{7,5},{8,10},{9,11},{10,... | collective-permute-start | bytes 786440 | tf_op jit(solution)/shard_map/ppermute | solution.py:34
  225.7 13.0 %collective-permute-start.35 = (bf16[64,2048]{1,0:T(8,128)(2,1)S(1)}, bf16[64,2048]{1,0:T(8,128)(2,1)S(1)}, u32[]{:S(2)}, u32[]{:S(2)}) collective-permute-start(bf16[64,2048]{1,0:T(8,128)(2,1)S(1)} %copy-done.30), channel_id=1, source_target_pairs={{0,3},{1,2},{2,1},{3,0},{4,7},{5,6},{6,5},{7,4},{8,11},{9,10},{10,... | collective-permute-start | bytes 786440 | tf_op jit(solution)/shard_map/ppermute | solution.py:34
  239.8 14.3 %collective-permute-start.37 = (bf16[128,2048]{1,0:T(8,128)(2,1)S(1)}, bf16[128,2048]{1,0:T(8,128)(2,1)S(1)}, u32[]{:S(2)}, u32[]{:S(2)}) collective-permute-start(bf16[128,2048]{1,0:T(8,128)(2,1)S(1)} %get-tuple-element.149), channel_id=1, source_target_pairs={{0,28},{4,0},{8,4},{12,8},{16,12},{20,16},{24,20},{28,24},{1,29},{... | collective-permute-start | bytes 1572872 | tf_op jit(solution)/shard_map/ppermute | solution.py:29
  242.5 15.1 %collective-permute-start.38 = (bf16[128,2048]{1,0:T(8,128)(2,1)S(1)}, bf16[128,2048]{1,0:T(8,128)(2,1)S(1)}, u32[]{:S(2)}, u32[]{:S(2)}) collective-permute-start(bf16[128,2048]{1,0:T(8,128)(2,1)S(1)} %get-tuple-element.150), channel_id=1, source_target_pairs={{0,4},{4,8},{8,12},{12,16},{16,20},{20,24},{24,28},{28,0},{1,5},{5... | collective-permute-start | bytes 1572872 | tf_op jit(solution)/shard_map/ppermute | solution.py:29
  (28 other events, 460.2 us)
Sparse Core Ops, SparseCore 0:
  9.8 32.9 all-gather.9
  44.6 29.5 all-gather.11
  75.9 47.3 all-gather.13
  124.9 63.3 all-gather.7

commit v7 on v6

--- a/solution.py
+++ b/solution.py
@@ -232,8 +232,11 @@
     )(*[weights] * len(blocks), *answers, *arrived)
 
 
-def final_kernel(offsets, weight, a0, a1, a2, a3, tokens, left, right, norm, q0, q1, mixed, query, total, normed, held, sems):
-    copies = [pltpu.make_async_copy(q, held.at[i], sems.at[i]) for i, q in enumerate((q0, q1))]
+def final_kernel(offsets, weight, a0, a1, a2, a3, tokens, left, right, norm, q0, q1, q2, q3, mixed, query, total, normed, held, sems):
+    copies = []
+    for i, q in enumerate((q0, q1, q2, q3)):
+        rows = pl.ds(pl.multiple_of(offsets[2 + i % 2], 768), 768)
+        copies.append(pltpu.make_async_copy(q, held.at[i // 2, rows], sems.at[i]))
     for c in copies:
         c.start()
     width, step = tokens.shape[1], 512
@@ -264,9 +267,9 @@
         query[:, cols] = out.astype(BF)
 
 
-def final(offsets, weights, answers, tokens, left, right, norm, q0, q1):
+def final(offsets, weights, answers, tokens, left, right, norm, parts):
     rows, width = tokens.shape
-    features = q0.shape[0]
+    features = 2 * parts[0].shape[0]
 
     def whole(x):
         return pl.BlockSpec(x.shape, lambda i: (0, 0))
@@ -275,17 +278,17 @@
         final_kernel,
         out_shape=(jax.ShapeDtypeStruct((rows, width), BF), jax.ShapeDtypeStruct((rows, features), BF)),
         grid=(1,),
-        in_specs=[SMEM, weight_of(0)] + [whole(x) for x in (*answers, tokens, left, right, norm)] + [ANY] * 2,
+        in_specs=[SMEM, weight_of(0)] + [whole(x) for x in (*answers, tokens, left, right, norm)] + [ANY] * 4,
         out_specs=(pl.BlockSpec((rows, width), lambda i: (0, 0)), pl.BlockSpec((rows, features), lambda i: (0, 0))),
         scratch_shapes=[
             pltpu.VMEM((rows, width), F32),
             pltpu.VMEM((rows, width), BF),
             pltpu.VMEM((2, features, width // 2), BF),
-            pltpu.SemaphoreType.DMA((2,)),
+            pltpu.SemaphoreType.DMA((4,)),
         ],
         compiler_params=params(62),
         cost_estimate=cost(2 * rows * width * features, 8 << 20),
-    )(offsets, weights, *answers, tokens, left, right, norm, q0, q1)
+    )(offsets, weights, *answers, tokens, left, right, norm, *parts)
 
 
 def across_x(x):
@@ -316,7 +319,7 @@
 
     half = query_weight.shape[0] // 2
     share = lax.dynamic_slice(query_weight.T, (0, c * half), (query_weight.shape[1], half))
-    q_own = lax.all_gather(share, ("xl", "y"), axis=0, tiled=True)
+    q_own = tuple(lax.all_gather(x, "y", axis=0, tiled=True) for x in (share, swap(share, "xl", 1)))
 
     def exchange(pieces):
         return tuple(swap(pieces[k], plane, k) for k in (1, 2, 3))
@@ -332,14 +335,14 @@
     low, high, got2 = shift(low, "z", -1), shift(high, "z", 1), exchange(ans2)
     low, high, got2, ans1, q_own = hold((low, high, got2, ans1, q_own))
     low, high = combine((2, 6), weights, (ans2[0],) + got2, [low, high])
-    q_other = swap(q_own, "c", 1)
+    q_other = tuple(swap(x, "c", 1) for x in q_own)
     low, high, got1 = shift(low, "z", -1), shift(high, "z", 1), exchange(ans1)
     low, high, got1, q_other = hold((low, high, got1, q_other))
     low, high = combine((1, 7), weights, (ans1[0],) + got1, [low, high])
     low, high = shift(low, "z", -1), shift(high, "z", 1)
     got0 = (ans0[0],) + got0
-    sides = (half * jnp.stack([c, 1 - c])).astype(jnp.int32)
-    return final(sides, weights, got0, tokens, low, high, norm_gain[None, :], q_own, q_other)
+    sides = jnp.stack([half * c, half * (1 - c), 768 * xl, 768 * (1 - xl)]).astype(jnp.int32)
+    return final(sides, weights, got0, tokens, low, high, norm_gain[None, :], q_own + q_other)
 
 
 def solution(mesh):

time: 274 us -> 275 us (level)
  waiting for transfers between devices: 136 us -> 122 us
  starting transfers between devices: 54.3 us -> 63.1 us
  local copies, waits for them, and re-layouts: 4.96 us -> 10.8 us
    ppermute x20, waiting for transfers between devices: 38.7 us -> 23.7 us  [shift(): return lax.ppermute(x, axis, [(i, (i + by) % n) for i in range(n)])]
    ppermute x20, starting transfers between devices: 23.5 us -> 30.4 us  [shift(): return lax.ppermute(x, axis, [(i, (i + by) % n) for i in range(n)])]
    ppermute x19 -> x21, waiting for transfers between devices: 92.7 us -> 96.2 us  [swap(): return lax.ppermute(x, axes, [(i, i ^ k) for i in range(n)])]
    unnamed x64 -> x56, local copies, waits for them, and re-layouts: 3.48 us -> 6.27 us
    ppermute x19 -> x21, starting transfers between devices: 23.9 us -> 25.9 us  [swap(): return lax.ppermute(x, axes, [(i, i ^ k) for i in range(n)])]
  transfers between devices with their start and end apart: 44 -> 47, of which waited for: 18 -> 19; matrix products, arithmetic and copies ran while one was open for 1% -> 2% of each run, Pallas kernels for 14% -> 14%
where the time goes in v7:
time: 275 us; the launch traced here: 274 us
  waiting for transfers between devices  122 us (44%)
  starting transfers between devices  63.1 us (23%)
  Pallas kernels  46.4 us (17%)
  blocking collectives  15.9 us (6%)
  between operations  14.2 us (5%)
  local copies, waits for them, and re-layouts  10.8 us (4%)
    ppermute x21, waiting for transfers between devices, swap(): return lax.ppermute(x, axes, [(i, i ^ k) for i in range(n)])  96.2 us
    ppermute x20, starting transfers between devices, shift(): return lax.ppermute(x, axis, [(i, (i + by) % n) for i in range(n)])  30.4 us
    ppermute x21, starting transfers between devices, swap(): return lax.ppermute(x, axes, [(i, i ^ k) for i in range(n)])  25.9 us
    pallas_call x2, Pallas kernels, expert(): pl.pallas_call(functools.partial(expert_kernel, groups), out_shape=tuple(...  25.1 us
    ppermute x20, waiting for transfers between devices, shift(): return lax.ppermute(x, axis, [(i, (i + by) % n) for i in range(n)])  23.7 us
    all_to_all x1, blocking collectives, shards(): tables = lax.all_to_all(table, 'z', split_axis=0, concat_axis=0, tiled=True)  15.9 us
    pallas_call x1, Pallas kernels, final(): pl.pallas_call(final_kernel, out_shape=(jax.ShapeDtypeStruct((rows, width...  8.15 us
    all_to_all x1, starting transfers between devices, shards(): lax.all_to_all(outbound, ('z', 'xh', 'c'), split_axis=0, concat_axis=0, t...  6.62 us
  transfers between devices with their start and end apart: 47, of which 19 were waited for; matrix products, arithmetic and copies ran while one was open for 2% of the time, Pallas kernels for 14%

profile of v7, /device:TPU:1, one launch (start us, length us, event | category | flops | bytes accessed | tf_op | source)
XLA Modules:
  0.0 273.6 jit_solution(3948312772529521937)
XLA Ops:
  7.9 6.0 %shard_map.95 = (bf16[1024,2048]{1,0:T(8,128)(2,1)}, f32[64,128]{1,0:T(8,128)}) custom-call(s32[6,128]{1,0:T(8,128)} %bitcast.39, f32[6,128]{1,0:T(8,128)} %bitcast.40, bf16[128,2048]{1,0:T(8,128)(2,1)} %tokens.3), custom_call_target="tpu_custom_call" | custom-call | flops 536870912 | bytes 5242880 | tf_op jit(solution)/shard_map/pallas_call | solution.py:69
  13.9 15.9 %all_to_all.23 = f32[8,8,128]{2,1,0:T(8,128)S(1)} all-to-all(f32[8,8,128]{2,1,0:T(8,128)} %bitcast.37), channel_id=1, replica_groups=mesh['xl'=2,'y'=4,'z'=8,'xh'=2,'c'=2] {'z'}, dimensions={0} | all-to-all | bytes 65536 | tf_op jit(solution)/shard_map/all_to_all | solution.py:311
  29.8 6.6 %all-to-all-start.1 = ((bf16[32,32,2048]{2,1,0:T(8,128)(2,1)}), bf16[32,32,2048]{2,1,0:T(8,128)(2,1)}, u32[]{:S(2)}, u32[]{:S(2)}) async-start(bf16[32,32,2048]{2,1,0:T(8,128)(2,1)} %bitcast.27), calls=%async_computation.1 | async-start | bytes 8388608 | tf_op jit(solution)/shard_map/all_to_all | solution.py:313
  38.9 1.2 collective-permute-start.10
  40.4 1.1 collective-permute-start.5
  41.9 26.0 %collective-permute-done.10.refs_14_ = bf16[768,256]{1,0:T(8,128)(2,1)} collective-permute-done((bf16[768,256]{1,0:T(8,128)(2,1)S(1)}, bf16[768,256]{1,0:T(8,128)(2,1)}, u32[]{:S(2)}, u32[]{:S(2)}) %collective-permute-start.10) | collective-permute-done | bytes 393248 | tf_op jit(solution)/shard_map/ppermute | solution.py:34
  67.9 1.3 collective-permute-start.11
  69.2 1.4 collective-permute-start.12
  70.6 10.2 %collective-permute-done.refs_2_ = bf16[256,768]{1,0:T(8,128)(2,1)} collective-permute-done((bf16[256,768]{1,0:T(8,128)(2,1)S(1)}, bf16[256,768]{1,0:T(8,128)(2,1)}, u32[]{:S(2)}, u32[]{:S(2)}) %collective-permute-start) | collective-permute-done | bytes 393248 | tf_op jit(solution)/shard_map/ppermute | solution.py:34
  80.8 1.3 collective-permute-start.1
  82.1 9.6 %collective-permute-done.5.refs_8_ = bf16[256,768]{1,0:T(8,128)(2,1)} collective-permute-done((bf16[256,768]{1,0:T(8,128)(2,1)S(1)}, bf16[256,768]{1,0:T(8,128)(2,1)}, u32[]{:S(2)}, u32[]{:S(2)}) %collective-permute-start.5) | collective-permute-done | bytes 393248 | tf_op jit(solution)/shard_map/ppermute | solution.py:34
  91.7 2.7 collective-permute-start.2
  94.4 18.3 %collective-permute-done.31 = bf16[192,1024]{1,0:T(8,128)(2,1)S(1)} collective-permute-done((bf16[192,1024]{1,0:T(8,128)(2,1)}, bf16[192,1024]{1,0:T(8,128)(2,1)S(1)}, u32[]{:S(2)}, u32[]{:S(2)}) %collective-permute-start.31) | collective-permute-done | bytes 393248 | tf_op jit(solution)/shard_map/ppermute | solution.py:34
  113.5 1.3 collective-permute-start.6
  114.8 1.5 collective-permute-start.7
  116.5 2.7 collective-permute-start.14
  120.1 4.3 %collective-permute-done.6.refs_9_ = bf16[256,768]{1,0:T(8,128)(2,1)S(1)} collective-permute-done((bf16[256,768]{1,0:T(8,128)(2,1)}, bf16[256,768]{1,0:T(8,128)(2,1)S(1)}, u32[]{:S(2)}, u32[]{:S(2)}) %collective-permute-start.6) | collective-permute-done | bytes 393248 | tf_op jit(solution)/shard_map/ppermute | solution.py:29
  124.4 1.4 collective-permute-start.4
  126.5 1.6 slice.27
  129.3 2.2 collective-permute-start.9
  132.8 1.3 collective-permute-done.4.refs_6_
  134.1 2.9 %collective-permute-done.8.refs_11_ = bf16[128,768]{1,0:T(8,128)(2,1)} collective-permute-done((bf16[128,768]{1,0:T(8,128)(2,1)}, bf16[128,768]{1,0:T(8,128)(2,1)}, u32[]{:S(2)}, u32[]{:S(2)}) %collective-permute-start.8) | collective-permute-done | bytes 196640 | tf_op jit(solution)/shard_map/ppermute | solution.py:29
  137.0 1.2 collective-permute-done.9.refs_12_
  138.3 11.0 %shard_map.97 = (bf16[32,2048]{1,0:T(8,128)(2,1)}, bf16[32,2048]{1,0:T(8,128)(2,1)}, bf16[32,2048]{1,0:T(8,128)(2,1)}, bf16[32,2048]{1,0:T(8,128)(2,1)}, bf16[64...) custom-call(s32[2]{0:T(128)} %pad_add_fusion.1.place, ...), custom_call_target="tpu_custom_call" | custom-call | flops 3623878656 | bytes 16777216 | tf_op jit(solution)/shard_map/pallas_call | solution.py:171
  149.3 5.7 %collective-permute-start.15 = (bf16[32,2048]{1,0:T(8,128)(2,1)}, bf16[32,2048]{1,0:T(8,128)(2,1)S(1)}, u32[]{:S(2)}, u32[]{:S(2)}) collective-permute-start(bf16[32,2048]{1,0:T(8,128)(2,1)} %get-tuple-element.83), channel_id=1, source_target_pairs={{0,1},{1,0},{2,3},{3,2},{4,5},{5,4},{6,7},{7,6},{8,9},{9,8},{10,11... | collective-permute-start | bytes 393224 | tf_op jit(solution)/shard_map/ppermute | solution.py:34
  156.0 3.5 %collective-permute-start.20 = (bf16[64,2048]{1,0:T(8,128)(2,1)}, bf16[64,2048]{1,0:T(8,128)(2,1)}, u32[]{:S(2)}, u32[]{:S(2)}) collective-permute-start(bf16[64,2048]{1,0:T(8,128)(2,1)} %get-tuple-element.88), channel_id=1, source_target_pairs={{0,3},{1,2},{2,1},{3,0},{4,7},{5,6},{6,5},{7,4},{8,11},{9,10},{10,... | collective-permute-start | bytes 786440 | tf_op jit(solution)/shard_map/ppermute | solution.py:34
  160.2 3.0 %collective-permute-start.17 = (bf16[32,2048]{1,0:T(8,128)(2,1)}, bf16[32,2048]{1,0:T(8,128)(2,1)}, u32[]{:S(2)}, u32[]{:S(2)}) collective-permute-start(bf16[32,2048]{1,0:T(8,128)(2,1)} %get-tuple-element.85), channel_id=1, source_target_pairs={{0,3},{1,2},{2,1},{3,0},{4,7},{5,6},{6,5},{7,4},{8,11},{9,10},{10,... | collective-permute-start | bytes 393224 | tf_op jit(solution)/shard_map/ppermute | solution.py:34
  163.2 14.1 %shard_map.98 = (bf16[64,2048]{1,0:T(8,128)(2,1)}, bf16[64,2048]{1,0:T(8,128)(2,1)}, bf16[64,2048]{1,0:T(8,128)(2,1)}, bf16[64,2048]{1,0:T(8,128)(2,1)}, bf16[64...) custom-call(s32[2]{0:T(128)} %pad_add_fusion.1.place, ...), custom_call_target="tpu_custom_call" | custom-call | flops 6039797760 | bytes 16777216 | tf_op jit(solution)/shard_map/pallas_call | solution.py:171
  178.9 1.4 shard_map.99
  180.4 6.1 %collective-permute-start.21 = (bf16[64,2048]{1,0:T(8,128)(2,1)S(1)}, bf16[64,2048]{1,0:T(8,128)(2,1)S(1)}, u32[]{:S(2)}, u32[]{:S(2)}) collective-permute-start(bf16[64,2048]{1,0:T(8,128)(2,1)S(1)} %get-tuple-element.106), channel_id=1, source_target_pairs={{0,28},{4,0},{8,4},{12,8},{16,12},{20,16},{24,20},{28,24},{1,29},{... | collective-permute-start | bytes 786440 | tf_op jit(solution)/shard_map/ppermute | solution.py:29
  187.2 3.1 %collective-permute-start.25 = (bf16[32,2048]{1,0:T(8,128)(2,1)}, bf16[32,2048]{1,0:T(8,128)(2,1)S(1)}, u32[]{:S(2)}, u32[]{:S(2)}) collective-permute-start(bf16[32,2048]{1,0:T(8,128)(2,1)} %get-tuple-element.110), channel_id=1, source_target_pairs={{0,3},{1,2},{2,1},{3,0},{4,7},{5,6},{6,5},{7,4},{8,11},{9,10},{10,... | collective-permute-start | bytes 393224 | tf_op jit(solution)/shard_map/ppermute | solution.py:34
  190.4 3.7 %collective-permute-done.24.a2 = bf16[32,2048]{1,0:T(8,128)(2,1)S(1)} collective-permute-done((bf16[32,2048]{1,0:T(8,128)(2,1)}, bf16[32,2048]{1,0:T(8,128)(2,1)S(1)}, u32[]{:S(2)}, u32[]{:S(2)}) %collective-permute-start.24) | collective-permute-done | bytes 131104 | tf_op jit(solution)/shard_map/ppermute | solution.py:34
  194.1 2.9 %collective-permute-done.25.a3 = bf16[32,2048]{1,0:T(8,128)(2,1)S(1)} collective-permute-done((bf16[32,2048]{1,0:T(8,128)(2,1)}, bf16[32,2048]{1,0:T(8,128)(2,1)S(1)}, u32[]{:S(2)}, u32[]{:S(2)}) %collective-permute-start.25) | collective-permute-done | bytes 131104 | tf_op jit(solution)/shard_map/ppermute | solution.py:34
  197.0 1.0 copy-done.6
  198.0 2.4 shard_map.100
  200.4 3.0 %collective-permute-start.26 = (bf16[128,2048]{1,0:T(8,128)(2,1)}, bf16[128,2048]{1,0:T(8,128)(2,1)S(1)}, u32[]{:S(2)}, u32[]{:S(2)}) collective-permute-start(bf16[128,2048]{1,0:T(8,128)(2,1)} %get-tuple-element.124), channel_id=1, source_target_pairs={{0,28},{4,0},{8,4},{12,8},{16,12},{20,16},{24,20},{28,24},{1,29},{... | collective-permute-start | bytes 1572872 | tf_op jit(solution)/shard_map/ppermute | solution.py:29
  204.7 2.8 %collective-permute-start.30 = (bf16[64,2048]{1,0:T(8,128)(2,1)}, bf16[64,2048]{1,0:T(8,128)(2,1)}, u32[]{:S(2)}, u32[]{:S(2)}) collective-permute-start(bf16[64,2048]{1,0:T(8,128)(2,1)} %get-tuple-element.128), channel_id=1, source_target_pairs={{0,3},{1,2},{2,1},{3,0},{4,7},{5,6},{6,5},{7,4},{8,11},{9,10},{10,... | collective-permute-start | bytes 786440 | tf_op jit(solution)/shard_map/ppermute | solution.py:34
  207.5 6.4 %collective-permute-done.29.refs_4_ = bf16[64,2048]{1,0:T(8,128)(2,1)} collective-permute-done((bf16[64,2048]{1,0:T(8,128)(2,1)}, bf16[64,2048]{1,0:T(8,128)(2,1)}, u32[]{:S(2)}, u32[]{:S(2)}) %collective-permute-start.29) | collective-permute-done | bytes 262176 | tf_op jit(solution)/shard_map/ppermute | solution.py:34
  213.9 5.8 %collective-permute-done.30.refs_5_ = bf16[64,2048]{1,0:T(8,128)(2,1)} collective-permute-done((bf16[64,2048]{1,0:T(8,128)(2,1)}, bf16[64,2048]{1,0:T(8,128)(2,1)}, u32[]{:S(2)}, u32[]{:S(2)}) %collective-permute-start.30) | collective-permute-done | bytes 262176 | tf_op jit(solution)/shard_map/ppermute | solution.py:34
  220.9 1.7 shard_map.101
  222.6 2.8 %collective-permute-start.32 = (bf16[128,2048]{1,0:T(8,128)(2,1)S(1)}, bf16[128,2048]{1,0:T(8,128)(2,1)S(1)}, u32[]{:S(2)}, u32[]{:S(2)}) collective-permute-start(bf16[128,2048]{1,0:T(8,128)(2,1)S(1)} %get-tuple-element.140), channel_id=1, source_target_pairs={{0,28},{4,0},{8,4},{12,8},{16,12},{20,16},{24,20},{28,24},{1,29},{... | collective-permute-start | bytes 1572872 | tf_op jit(solution)/shard_map/ppermute | solution.py:29
  226.0 3.8 %collective-permute-done.35.refs_4_ = bf16[64,2048]{1,0:T(8,128)(2,1)S(1)} collective-permute-done((bf16[64,2048]{1,0:T(8,128)(2,1)}, bf16[64,2048]{1,0:T(8,128)(2,1)S(1)}, u32[]{:S(2)}, u32[]{:S(2)}) %collective-permute-start.35) | collective-permute-done | bytes 262176 | tf_op jit(solution)/shard_map/ppermute | solution.py:34
  229.8 1.4 collective-permute-start.36
  231.2 8.9 %collective-permute-done.36.refs_5_ = bf16[64,2048]{1,0:T(8,128)(2,1)S(1)} collective-permute-done((bf16[64,2048]{1,0:T(8,128)(2,1)}, bf16[64,2048]{1,0:T(8,128)(2,1)S(1)}, u32[]{:S(2)}, u32[]{:S(2)}) %collective-permute-start.36) | collective-permute-done | bytes 262176 | tf_op jit(solution)/shard_map/ppermute | solution.py:34
  242.2 2.4 collective-permute-start.39
  245.1 9.9 %collective-permute-done.39.left = bf16[128,2048]{1,0:T(8,128)(2,1)S(1)} collective-permute-done((bf16[128,2048]{1,0:T(8,128)(2,1)S(1)}, bf16[128,2048]{1,0:T(8,128)(2,1)S(1)}, u32[]{:S(2)}, u32[]{:S(2)}) %collective-permute-start.39) | collective-permute-done | bytes 524320 | tf_op jit(solution)/shard_map/ppermute | solution.py:29
  255.1 3.1 %collective-permute-done.40.right = bf16[128,2048]{1,0:T(8,128)(2,1)S(1)} collective-permute-done((bf16[128,2048]{1,0:T(8,128)(2,1)S(1)}, bf16[128,2048]{1,0:T(8,128)(2,1)S(1)}, u32[]{:S(2)}, u32[]{:S(2)}) %collective-permute-start.40) | collective-permute-done | bytes 524320 | tf_op jit(solution)/shard_map/ppermute | solution.py:29
  258.9 8.1 %shard_map.103 = (bf16[128,2048]{1,0:T(8,128)(2,1)}, bf16[128,1536]{1,0:T(8,128)(2,1)}) custom-call(s32[4]{0:T(128)} %pad_add_fusion.offsets, bf16[8,128,256]{2,1,0:T(8,128)(2,1)} %copy-done.1, bf16[32,2048]{1,0:T(8,128)(2,1)} %get-tuple-element.101.a0, bf16[32,2048]{1,0:T(8,128)(2,1)} %copy-done.25, bf16[32,2048]{1,0:T(8,128)(2,1)} %copy-done.26, ...), custom_call_target="tpu_custom_call" | custom-call | flops 805306368 | bytes 8388608 | tf_op jit(solution)/shard_map/pallas_call | solution.py:277
  (127 shorter events, 19.2 us)
Async XLA Ops:
  7.2 131.1 %all-gather.13.cloned.1.call-start = ((), (), s32[]{:S(2)}) async-start(), calls=%async_computation.4 | async-start | bytes 1966080 | tf_op jit(solution)/shard_map/all_gather | solution.py:315
  29.8 108.5 %all-to-all-start.1 = ((bf16[32,32,2048]{2,1,0:T(8,128)(2,1)}), bf16[32,32,2048]{2,1,0:T(8,128)(2,1)}, u32[]{:S(2)}, u32[]{:S(2)}) async-start(bf16[32,32,2048]{2,1,0:T(8,128)(2,1)} %bitcast.27), calls=%async_computation.1 | async-start | bytes 8388608 | tf_op jit(solution)/shard_map/all_to_all | solution.py:313
  36.4 101.8 %all-gather.15.cloned.1.call-start = ((), (), s32[]{:S(2)}) async-start(), calls=%async_computation.5 | async-start | bytes 1966080 | tf_op jit(solution)/shard_map/all_gather | solution.py:316
  37.2 101.1 %all-gather.17.cloned.1.call-start = ((), (), s32[]{:S(2)}) async-start(), calls=%async_computation.6 | async-start | bytes 1966080 | tf_op jit(solution)/shard_map/all_gather | solution.py:317
  37.9 169.6 %all-gather.9.cloned.1.call-start = ((), (), s32[]{:S(2)}) async-start(), calls=%async_computation.2 | async-start | bytes 1966080 | tf_op jit(solution)/shard_map/all_gather | solution.py:322
  38.8 168.7 %all-gather.11.cloned.1.call-start = ((), (), s32[]{:S(2)}) async-start(), calls=%async_computation.3 | async-start | bytes 1966080 | tf_op jit(solution)/shard_map/all_gather | solution.py:322
  38.9 29.0 %collective-permute-start.10 = (bf16[768,256]{1,0:T(8,128)(2,1)S(1)}, bf16[768,256]{1,0:T(8,128)(2,1)}, u32[]{:S(2)}, u32[]{:S(2)}) collective-permute-start(bf16[768,256]{1,0:T(8,128)(2,1)S(1)} %bitcast.36), channel_id=1, source_target_pairs={{0,128},{128,0},{1,129},{129,1},{2,130},{130,2},{3,131},{131,3},{4... | collective-permute-start | bytes 1179656 | tf_op jit(solution)/shard_map/ppermute | solution.py:34
  40.1 40.7 %collective-permute-start = (bf16[256,768]{1,0:T(8,128)(2,1)S(1)}, bf16[256,768]{1,0:T(8,128)(2,1)}, u32[]{:S(2)}, u32[]{:S(2)}) collective-permute-start(bf16[256,768]{1,0:T(8,128)(2,1)S(1)} %bitcast.34), channel_id=1, source_target_pairs={{0,128},{128,0},{1,129},{129,1},{2,130},{130,2},{3,131},{131,3},{4... | collective-permute-start | bytes 1179656 | tf_op jit(solution)/shard_map/ppermute | solution.py:34
  40.4 51.2 %collective-permute-start.5 = (bf16[256,768]{1,0:T(8,128)(2,1)S(1)}, bf16[256,768]{1,0:T(8,128)(2,1)}, u32[]{:S(2)}, u32[]{:S(2)}) collective-permute-start(bf16[256,768]{1,0:T(8,128)(2,1)S(1)} %bitcast.35), channel_id=1, source_target_pairs={{0,128},{128,0},{1,129},{129,1},{2,130},{130,2},{3,131},{131,3},{4... | collective-permute-start | bytes 1179656 | tf_op jit(solution)/shard_map/ppermute | solution.py:34
  41.6 71.1 %collective-permute-start.31 = (bf16[192,1024]{1,0:T(8,128)(2,1)}, bf16[192,1024]{1,0:T(8,128)(2,1)S(1)}, u32[]{:S(2)}, u32[]{:S(2)}) collective-permute-start(bf16[192,1024]{1,0:T(8,128)(2,1)} %dynamic-slice_bitcast_fusion), channel_id=1, source_target_pairs={{0,128},{128,0},{1,129},{129,1},{2,130},{130,2},{3,131},{131,3},{4... | collective-permute-start | bytes 1179656 | tf_op jit(solution)/shard_map/ppermute | solution.py:34
  67.9 46.9 %collective-permute-start.11 = (bf16[768,256]{1,0:T(8,128)(2,1)}, bf16[768,256]{1,0:T(8,128)(2,1)S(1)}, u32[]{:S(2)}, u32[]{:S(2)}) collective-permute-start(bf16[768,256]{1,0:T(8,128)(2,1)} %collective-permute-done.10.refs_14_), channel_id=1, source_target_pairs={{0,32},{32,64},{64,96},{96,0},{1,33},{33,65},{65,97},{97,1},{2,34}... | collective-permute-start | bytes 1179656 | tf_op jit(solution)/shard_map/ppermute | solution.py:29
  69.2 47.2 %collective-permute-start.12 = (bf16[768,256]{1,0:T(8,128)(2,1)}, bf16[768,256]{1,0:T(8,128)(2,1)S(1)}, u32[]{:S(2)}, u32[]{:S(2)}) collective-permute-start(bf16[768,256]{1,0:T(8,128)(2,1)} %collective-permute-done.10.refs_14_), channel_id=1, source_target_pairs={{0,96},{32,0},{64,32},{96,64},{1,97},{33,1},{65,33},{97,65},{2,98}... | collective-permute-start | bytes 1179656 | tf_op jit(solution)/shard_map/ppermute | solution.py:29
  80.8 35.7 %collective-permute-start.1 = (bf16[256,768]{1,0:T(8,128)(2,1)}, bf16[256,768]{1,0:T(8,128)(2,1)S(1)}, u32[]{:S(2)}, u32[]{:S(2)}) collective-permute-start(bf16[256,768]{1,0:T(8,128)(2,1)} %collective-permute-done.refs_2_), channel_id=1, source_target_pairs={{0,32},{32,64},{64,96},{96,0},{1,33},{33,65},{65,97},{97,1},{2,34}... | collective-permute-start | bytes 1179656 | tf_op jit(solution)/shard_map/ppermute | solution.py:29
  91.7 27.6 %collective-permute-start.2 = (bf16[256,768]{1,0:T(8,128)(2,1)}, bf16[256,768]{1,0:T(8,128)(2,1)S(1)}, u32[]{:S(2)}, u32[]{:S(2)}) collective-permute-start(bf16[256,768]{1,0:T(8,128)(2,1)} %collective-permute-done.refs_2_), channel_id=1, source_target_pairs={{0,96},{32,0},{64,32},{96,64},{1,97},{33,1},{65,33},{97,65},{2,98}... | collective-permute-start | bytes 1179656 | tf_op jit(solution)/shard_map/ppermute | solution.py:29
  113.5 10.9 %collective-permute-start.6 = (bf16[256,768]{1,0:T(8,128)(2,1)}, bf16[256,768]{1,0:T(8,128)(2,1)S(1)}, u32[]{:S(2)}, u32[]{:S(2)}) collective-permute-start(bf16[256,768]{1,0:T(8,128)(2,1)} %collective-permute-done.5.refs_8_), channel_id=1, source_target_pairs={{0,32},{32,64},{64,96},{96,0},{1,33},{33,65},{65,97},{97,1},{2,34}... | collective-permute-start | bytes 1179656 | tf_op jit(solution)/shard_map/ppermute | solution.py:29
  114.8 11.7 %collective-permute-start.7 = (bf16[256,768]{1,0:T(8,128)(2,1)}, bf16[256,768]{1,0:T(8,128)(2,1)}, u32[]{:S(2)}, u32[]{:S(2)}) collective-permute-start(bf16[256,768]{1,0:T(8,128)(2,1)} %collective-permute-done.5.refs_8_), channel_id=1, source_target_pairs={{0,96},{32,0},{64,32},{96,64},{1,97},{33,1},{65,33},{97,65},{2,98}... | collective-permute-start | bytes 1179656 | tf_op jit(solution)/shard_map/ppermute | solution.py:29
  116.3 12.2 %collective-permute-start.13 = (bf16[384,256]{1,0:T(8,128)(2,1)S(1)}, bf16[384,256]{1,0:T(8,128)(2,1)S(1)}, u32[]{:S(2)}, u32[]{:S(2)}) collective-permute-start(bf16[384,256]{1,0:T(8,128)(2,1)S(1)} %slice.28), channel_id=1, source_target_pairs={{0,32},{32,64},{64,96},{96,0},{1,33},{33,65},{65,97},{97,1},{2,34}... | collective-permute-start | bytes 589832 | tf_op jit(solution)/shard_map/ppermute | solution.py:29
  116.5 16.3 %collective-permute-start.14 = (bf16[384,256]{1,0:T(8,128)(2,1)S(1)}, bf16[384,256]{1,0:T(8,128)(2,1)}, u32[]{:S(2)}, u32[]{:S(2)}) collective-permute-start(bf16[384,256]{1,0:T(8,128)(2,1)S(1)} %slice.29), channel_id=1, source_target_pairs={{0,96},{32,0},{64,32},{96,64},{1,97},{33,1},{65,33},{97,65},{2,98}... | collective-permute-start | bytes 589832 | tf_op jit(solution)/shard_map/ppermute | solution.py:29
  119.3 13.6 %collective-permute-start.3 = (bf16[128,768]{1,0:T(8,128)(2,1)S(1)}, bf16[128,768]{1,0:T(8,128)(2,1)}, u32[]{:S(2)}, u32[]{:S(2)}) collective-permute-start(bf16[128,768]{1,0:T(8,128)(2,1)S(1)} %slice.24), channel_id=1, source_target_pairs={{0,32},{32,64},{64,96},{96,0},{1,33},{33,65},{65,97},{97,1},{2,34}... | collective-permute-start | bytes 589832 | tf_op jit(solution)/shard_map/ppermute | solution.py:29
  124.4 9.8 %collective-permute-start.4 = (bf16[128,768]{1,0:T(8,128)(2,1)}, bf16[128,768]{1,0:T(8,128)(2,1)}, u32[]{:S(2)}, u32[]{:S(2)}) collective-permute-start(bf16[128,768]{1,0:T(8,128)(2,1)} %slice.25), channel_id=1, source_target_pairs={{0,96},{32,0},{64,32},{96,64},{1,97},{33,1},{65,33},{97,65},{2,98}... | collective-permute-start | bytes 589832 | tf_op jit(solution)/shard_map/ppermute | solution.py:29
  126.5 10.5 %collective-permute-start.8 = (bf16[128,768]{1,0:T(8,128)(2,1)}, bf16[128,768]{1,0:T(8,128)(2,1)}, u32[]{:S(2)}, u32[]{:S(2)}) collective-permute-start(bf16[128,768]{1,0:T(8,128)(2,1)} %slice.26), channel_id=1, source_target_pairs={{0,32},{32,64},{64,96},{96,0},{1,33},{33,65},{65,97},{97,1},{2,34}... | collective-permute-start | bytes 589832 | tf_op jit(solution)/shard_map/ppermute | solution.py:29
  129.3 9.0 %collective-permute-start.9 = (bf16[128,768]{1,0:T(8,128)(2,1)}, bf16[128,768]{1,0:T(8,128)(2,1)}, u32[]{:S(2)}, u32[]{:S(2)}) collective-permute-start(bf16[128,768]{1,0:T(8,128)(2,1)} %slice.27), channel_id=1, source_target_pairs={{0,96},{32,0},{64,32},{96,64},{1,97},{33,1},{65,33},{97,65},{2,98}... | collective-permute-start | bytes 589832 | tf_op jit(solution)/shard_map/ppermute | solution.py:29
  149.3 10.2 %collective-permute-start.15 = (bf16[32,2048]{1,0:T(8,128)(2,1)}, bf16[32,2048]{1,0:T(8,128)(2,1)S(1)}, u32[]{:S(2)}, u32[]{:S(2)}) collective-permute-start(bf16[32,2048]{1,0:T(8,128)(2,1)} %get-tuple-element.83), channel_id=1, source_target_pairs={{0,1},{1,0},{2,3},{3,2},{4,5},{5,4},{6,7},{7,6},{8,9},{9,8},{10,11... | collective-permute-start | bytes 393224 | tf_op jit(solution)/shard_map/ppermute | solution.py:34
  155.8 84.7 %copy-start.1 = (bf16[8,128,256]{2,1,0:T(8,128)(2,1)}, bf16[8,128,256]{2,1,0:T(8,128)(2,1)S(1)}, u32[]{:S(2)}) copy-start(bf16[8,128,256]{2,1,0:T(8,128)(2,1)S(1)} %shard_map.96.refs_0_.refs_1_.weight) | copy-start | bytes 1572868
  155.8 21.5 %collective-permute-start.18 = (bf16[64,2048]{1,0:T(8,128)(2,1)}, bf16[64,2048]{1,0:T(8,128)(2,1)S(1)}, u32[]{:S(2)}, u32[]{:S(2)}) collective-permute-start(bf16[64,2048]{1,0:T(8,128)(2,1)} %get-tuple-element.86), channel_id=1, source_target_pairs={{0,1},{1,0},{2,3},{3,2},{4,5},{5,4},{6,7},{7,6},{8,9},{9,8},{10,11... | collective-permute-start | bytes 786440 | tf_op jit(solution)/shard_map/ppermute | solution.py:34
  155.9 22.1 %collective-permute-start.19 = (bf16[64,2048]{1,0:T(8,128)(2,1)}, bf16[64,2048]{1,0:T(8,128)(2,1)}, u32[]{:S(2)}, u32[]{:S(2)}) collective-permute-start(bf16[64,2048]{1,0:T(8,128)(2,1)} %get-tuple-element.87), channel_id=1, source_target_pairs={{0,2},{1,3},{2,0},{3,1},{4,6},{5,7},{6,4},{7,5},{8,10},{9,11},{10,... | collective-permute-start | bytes 786440 | tf_op jit(solution)/shard_map/ppermute | solution.py:34
  156.0 22.0 %collective-permute-start.20 = (bf16[64,2048]{1,0:T(8,128)(2,1)}, bf16[64,2048]{1,0:T(8,128)(2,1)}, u32[]{:S(2)}, u32[]{:S(2)}) collective-permute-start(bf16[64,2048]{1,0:T(8,128)(2,1)} %get-tuple-element.88), channel_id=1, source_target_pairs={{0,3},{1,2},{2,1},{3,0},{4,7},{5,6},{6,5},{7,4},{8,11},{9,10},{10,... | collective-permute-start | bytes 786440 | tf_op jit(solution)/shard_map/ppermute | solution.py:34
  159.6 17.7 %collective-permute-start.16 = (bf16[32,2048]{1,0:T(8,128)(2,1)}, bf16[32,2048]{1,0:T(8,128)(2,1)}, u32[]{:S(2)}, u32[]{:S(2)}) collective-permute-start(bf16[32,2048]{1,0:T(8,128)(2,1)} %get-tuple-element.84), channel_id=1, source_target_pairs={{0,2},{1,3},{2,0},{3,1},{4,6},{5,7},{6,4},{7,5},{8,10},{9,11},{10,... | collective-permute-start | bytes 393224 | tf_op jit(solution)/shard_map/ppermute | solution.py:34
  160.2 17.1 %collective-permute-start.17 = (bf16[32,2048]{1,0:T(8,128)(2,1)}, bf16[32,2048]{1,0:T(8,128)(2,1)}, u32[]{:S(2)}, u32[]{:S(2)}) collective-permute-start(bf16[32,2048]{1,0:T(8,128)(2,1)} %get-tuple-element.85), channel_id=1, source_target_pairs={{0,3},{1,2},{2,1},{3,0},{4,7},{5,6},{6,5},{7,4},{8,11},{9,10},{10,... | collective-permute-start | bytes 393224 | tf_op jit(solution)/shard_map/ppermute | solution.py:34
  180.4 16.6 %collective-permute-start.21 = (bf16[64,2048]{1,0:T(8,128)(2,1)S(1)}, bf16[64,2048]{1,0:T(8,128)(2,1)S(1)}, u32[]{:S(2)}, u32[]{:S(2)}) collective-permute-start(bf16[64,2048]{1,0:T(8,128)(2,1)S(1)} %get-tuple-element.106), channel_id=1, source_target_pairs={{0,28},{4,0},{8,4},{12,8},{16,12},{20,16},{24,20},{28,24},{1,29},{... | collective-permute-start | bytes 786440 | tf_op jit(solution)/shard_map/ppermute | solution.py:29
  186.5 10.5 %collective-permute-start.22 = (bf16[64,2048]{1,0:T(8,128)(2,1)S(1)}, bf16[64,2048]{1,0:T(8,128)(2,1)S(1)}, u32[]{:S(2)}, u32[]{:S(2)}) collective-permute-start(bf16[64,2048]{1,0:T(8,128)(2,1)S(1)} %get-tuple-element.107), channel_id=1, source_target_pairs={{0,4},{4,8},{8,12},{12,16},{16,20},{20,24},{24,28},{28,0},{1,5},{5... | collective-permute-start | bytes 786440 | tf_op jit(solution)/shard_map/ppermute | solution.py:29
  186.5 3.9 %collective-permute-start.23 = (bf16[32,2048]{1,0:T(8,128)(2,1)}, bf16[32,2048]{1,0:T(8,128)(2,1)S(1)}, u32[]{:S(2)}, u32[]{:S(2)}) collective-permute-start(bf16[32,2048]{1,0:T(8,128)(2,1)} %get-tuple-element.108), channel_id=1, source_target_pairs={{0,1},{1,0},{2,3},{3,2},{4,5},{5,4},{6,7},{7,6},{8,9},{9,8},{10,11... | collective-permute-start | bytes 393224 | tf_op jit(solution)/shard_map/ppermute | solution.py:34
  187.2 6.8 %collective-permute-start.24 = (bf16[32,2048]{1,0:T(8,128)(2,1)}, bf16[32,2048]{1,0:T(8,128)(2,1)S(1)}, u32[]{:S(2)}, u32[]{:S(2)}) collective-permute-start(bf16[32,2048]{1,0:T(8,128)(2,1)} %get-tuple-element.109), channel_id=1, source_target_pairs={{0,2},{1,3},{2,0},{3,1},{4,6},{5,7},{6,4},{7,5},{8,10},{9,11},{10,... | collective-permute-start | bytes 393224 | tf_op jit(solution)/shard_map/ppermute | solution.py:34
  187.2 9.7 %collective-permute-start.25 = (bf16[32,2048]{1,0:T(8,128)(2,1)}, bf16[32,2048]{1,0:T(8,128)(2,1)S(1)}, u32[]{:S(2)}, u32[]{:S(2)}) collective-permute-start(bf16[32,2048]{1,0:T(8,128)(2,1)} %get-tuple-element.110), channel_id=1, source_target_pairs={{0,3},{1,2},{2,1},{3,0},{4,7},{5,6},{6,5},{7,4},{8,11},{9,10},{10,... | collective-permute-start | bytes 393224 | tf_op jit(solution)/shard_map/ppermute | solution.py:34
  200.4 19.3 %collective-permute-start.26 = (bf16[128,2048]{1,0:T(8,128)(2,1)}, bf16[128,2048]{1,0:T(8,128)(2,1)S(1)}, u32[]{:S(2)}, u32[]{:S(2)}) collective-permute-start(bf16[128,2048]{1,0:T(8,128)(2,1)} %get-tuple-element.124), channel_id=1, source_target_pairs={{0,28},{4,0},{8,4},{12,8},{16,12},{20,16},{24,20},{28,24},{1,29},{... | collective-permute-start | bytes 1572872 | tf_op jit(solution)/shard_map/ppermute | solution.py:29
  203.3 16.4 %collective-permute-start.27 = (bf16[128,2048]{1,0:T(8,128)(2,1)}, bf16[128,2048]{1,0:T(8,128)(2,1)S(1)}, u32[]{:S(2)}, u32[]{:S(2)}) collective-permute-start(bf16[128,2048]{1,0:T(8,128)(2,1)} %get-tuple-element.125), channel_id=1, source_target_pairs={{0,4},{4,8},{8,12},{12,16},{16,20},{20,24},{24,28},{28,0},{1,5},{5... | collective-permute-start | bytes 1572872 | tf_op jit(solution)/shard_map/ppermute | solution.py:29
  203.4 4.1 %collective-permute-start.28 = (bf16[64,2048]{1,0:T(8,128)(2,1)}, bf16[64,2048]{1,0:T(8,128)(2,1)S(1)}, u32[]{:S(2)}, u32[]{:S(2)}) collective-permute-start(bf16[64,2048]{1,0:T(8,128)(2,1)} %get-tuple-element.126), channel_id=1, source_target_pairs={{0,1},{1,0},{2,3},{3,2},{4,5},{5,4},{6,7},{7,6},{8,9},{9,8},{10,11... | collective-permute-start | bytes 786440 | tf_op jit(solution)/shard_map/ppermute | solution.py:34
  204.2 9.7 %collective-permute-start.29 = (bf16[64,2048]{1,0:T(8,128)(2,1)}, bf16[64,2048]{1,0:T(8,128)(2,1)}, u32[]{:S(2)}, u32[]{:S(2)}) collective-permute-start(bf16[64,2048]{1,0:T(8,128)(2,1)} %get-tuple-element.127), channel_id=1, source_target_pairs={{0,2},{1,3},{2,0},{3,1},{4,6},{5,7},{6,4},{7,5},{8,10},{9,11},{10,... | collective-permute-start | bytes 786440 | tf_op jit(solution)/shard_map/ppermute | solution.py:34
  204.7 15.1 %collective-permute-start.30 = (bf16[64,2048]{1,0:T(8,128)(2,1)}, bf16[64,2048]{1,0:T(8,128)(2,1)}, u32[]{:S(2)}, u32[]{:S(2)}) collective-permute-start(bf16[64,2048]{1,0:T(8,128)(2,1)} %get-tuple-element.128), channel_id=1, source_target_pairs={{0,3},{1,2},{2,1},{3,0},{4,7},{5,6},{6,5},{7,4},{8,11},{9,10},{10,... | collective-permute-start | bytes 786440 | tf_op jit(solution)/shard_map/ppermute | solution.py:34
  219.7 20.8 %collective-permute-start.37 = (bf16[768,1024]{1,0:T(8,128)(2,1)}, bf16[768,1024]{1,0:T(8,128)(2,1)S(1)}, u32[]{:S(2)}, u32[]{:S(2)}) collective-permute-start(bf16[768,1024]{1,0:T(8,128)(2,1)} %all-gather.9.cloned.1.call-done.q0), channel_id=1, source_target_pairs={{0,1},{1,0},{2,3},{3,2},{4,5},{5,4},{6,7},{7,6},{8,9},{9,8},{10,11... | collective-permute-start | bytes 4718600 | tf_op jit(solution)/shard_map/ppermute | solution.py:34
  219.9 20.6 %collective-permute-start.38 = (bf16[768,1024]{1,0:T(8,128)(2,1)}, bf16[768,1024]{1,0:T(8,128)(2,1)S(1)}, u32[]{:S(2)}, u32[]{:S(2)}) collective-permute-start(bf16[768,1024]{1,0:T(8,128)(2,1)} %all-gather.11.cloned.1.call-done.q1), channel_id=1, source_target_pairs={{0,1},{1,0},{2,3},{3,2},{4,5},{5,4},{6,7},{7,6},{8,9},{9,8},{10,11... | collective-permute-start | bytes 4718600 | tf_op jit(solution)/shard_map/ppermute | solution.py:34
  220.2 5.7 %collective-permute-start.34 = (bf16[64,2048]{1,0:T(8,128)(2,1)}, bf16[64,2048]{1,0:T(8,128)(2,1)S(1)}, u32[]{:S(2)}, u32[]{:S(2)}) collective-permute-start(bf16[64,2048]{1,0:T(8,128)(2,1)} %get-tuple-element.142), channel_id=1, source_target_pairs={{0,1},{1,0},{2,3},{3,2},{4,5},{5,4},{6,7},{7,6},{8,9},{9,8},{10,11... | collective-permute-start | bytes 786440 | tf_op jit(solution)/shard_map/ppermute | solution.py:34
  220.5 9.3 %collective-permute-start.35 = (bf16[64,2048]{1,0:T(8,128)(2,1)}, bf16[64,2048]{1,0:T(8,128)(2,1)S(1)}, u32[]{:S(2)}, u32[]{:S(2)}) collective-permute-start(bf16[64,2048]{1,0:T(8,128)(2,1)} %get-tuple-element.143), channel_id=1, source_target_pairs={{0,2},{1,3},{2,0},{3,1},{4,6},{5,7},{6,4},{7,5},{8,10},{9,11},{10,... | collective-permute-start | bytes 786440 | tf_op jit(solution)/shard_map/ppermute | solution.py:34
  222.6 17.4 %collective-permute-start.32 = (bf16[128,2048]{1,0:T(8,128)(2,1)S(1)}, bf16[128,2048]{1,0:T(8,128)(2,1)S(1)}, u32[]{:S(2)}, u32[]{:S(2)}) collective-permute-start(bf16[128,2048]{1,0:T(8,128)(2,1)S(1)} %get-tuple-element.140), channel_id=1, source_target_pairs={{0,28},{4,0},{8,4},{12,8},{16,12},{20,16},{24,20},{28,24},{1,29},{... | collective-permute-start | bytes 1572872 | tf_op jit(solution)/shard_map/ppermute | solution.py:29
  226.0 14.5 %collective-permute-start.33 = (bf16[128,2048]{1,0:T(8,128)(2,1)S(1)}, bf16[128,2048]{1,0:T(8,128)(2,1)S(1)}, u32[]{:S(2)}, u32[]{:S(2)}) collective-permute-start(bf16[128,2048]{1,0:T(8,128)(2,1)S(1)} %get-tuple-element.141), channel_id=1, source_target_pairs={{0,4},{4,8},{8,12},{12,16},{16,20},{20,24},{24,28},{28,0},{1,5},{5... | collective-permute-start | bytes 1572872 | tf_op jit(solution)/shard_map/ppermute | solution.py:29
  229.8 10.3 %collective-permute-start.36 = (bf16[64,2048]{1,0:T(8,128)(2,1)}, bf16[64,2048]{1,0:T(8,128)(2,1)S(1)}, u32[]{:S(2)}, u32[]{:S(2)}) collective-permute-start(bf16[64,2048]{1,0:T(8,128)(2,1)} %get-tuple-element.144), channel_id=1, source_target_pairs={{0,3},{1,2},{2,1},{3,0},{4,7},{5,6},{6,5},{7,4},{8,11},{9,10},{10,... | collective-permute-start | bytes 786440 | tf_op jit(solution)/shard_map/ppermute | solution.py:34
  242.2 12.9 %collective-permute-start.39 = (bf16[128,2048]{1,0:T(8,128)(2,1)S(1)}, bf16[128,2048]{1,0:T(8,128)(2,1)S(1)}, u32[]{:S(2)}, u32[]{:S(2)}) collective-permute-start(bf16[128,2048]{1,0:T(8,128)(2,1)S(1)} %get-tuple-element.152), channel_id=1, source_target_pairs={{0,28},{4,0},{8,4},{12,8},{16,12},{20,16},{24,20},{28,24},{1,29},{... | collective-permute-start | bytes 1572872 | tf_op jit(solution)/shard_map/ppermute | solution.py:29
  244.5 13.6 %collective-permute-start.40 = (bf16[128,2048]{1,0:T(8,128)(2,1)S(1)}, bf16[128,2048]{1,0:T(8,128)(2,1)S(1)}, u32[]{:S(2)}, u32[]{:S(2)}) collective-permute-start(bf16[128,2048]{1,0:T(8,128)(2,1)S(1)} %get-tuple-element.153), channel_id=1, source_target_pairs={{0,4},{4,8},{8,12},{12,16},{16,20},{20,24},{24,28},{28,0},{1,5},{5... | collective-permute-start | bytes 1572872 | tf_op jit(solution)/shard_map/ppermute | solution.py:29
  (27 other events, 349.4 us)
Sparse Core Ops, SparseCore 0:
  9.8 32.8 all-gather.12
  44.6 29.9 all-gather.14
  76.4 42.1 all-gather.16
  120.2 32.2 all-gather.8
  154.2 30.4 all-gather.10

commit v8 on v7

--- a/solution.py
+++ b/solution.py
@@ -319,12 +319,12 @@
 
     half = query_weight.shape[0] // 2
     share = lax.dynamic_slice(query_weight.T, (0, c * half), (query_weight.shape[1], half))
-    q_own = tuple(lax.all_gather(x, "y", axis=0, tiled=True) for x in (share, swap(share, "xl", 1)))
-
     def exchange(pieces):
         return tuple(swap(pieces[k], plane, k) for k in (1, 2, 3))
 
     ans4, ans3 = expert(GROUPS[:2], place, offsets, arrived, gates, ups, downs)
+    across, _ = hold((swap(share, "xl", 1), ans4[0]))
+    q_own = tuple(lax.all_gather(x, "y", axis=0, tiled=True) for x in (share, across))
     got4, got3 = exchange(ans4), exchange(ans3)
     ans2, ans1, ans0 = expert(GROUPS[2:], place, offsets, arrived, gates, ups, downs)
     got4, got3, ans2, ans1, ans0 = hold((got4, got3, ans2, ans1, ans0))

time: 275 us -> 259 us (0.942)
  waiting for transfers between devices: 122 us -> 113 us
  starting transfers between devices: 63.1 us -> 59.3 us
    ppermute x21, waiting for transfers between devices: 96.2 us -> 72.7 us  [swap(): return lax.ppermute(x, axes, [(i, i ^ k) for i in range(n)])]
    ppermute x20, waiting for transfers between devices: 23.7 us -> 36.6 us  [shift(): return lax.ppermute(x, axis, [(i, (i + by) % n) for i in range(n)])]
    ppermute x20, starting transfers between devices: 30.4 us -> 25.2 us  [shift(): return lax.ppermute(x, axis, [(i, (i + by) % n) for i in range(n)])]
    unnamed x56 -> x68, local copies, waits for them, and re-layouts: 6.27 us -> 6.93 us
  transfers between devices with their start and end apart: 47 -> 47, of which waited for: 19 -> 17; matrix products, arithmetic and copies ran while one was open for 2% -> 1% of each run, Pallas kernels for 14% -> 14%
where the time goes in v8:
time: 259 us
  waiting for transfers between devices  113 us (44%)
  starting transfers between devices  59.3 us (23%)
  Pallas kernels  46.3 us (18%)
  blocking collectives  15.9 us (6%)
  between operations  14.3 us (6%)
  local copies, waits for them, and re-layouts  8.48 us (3%)
    ppermute x21, waiting for transfers between devices, swap(): return lax.ppermute(x, axes, [(i, i ^ k) for i in range(n)])  72.7 us
    ppermute x20, waiting for transfers between devices, shift(): return lax.ppermute(x, axis, [(i, (i + by) % n) for i in range(n)])  36.6 us
    ppermute x21, starting transfers between devices, swap(): return lax.ppermute(x, axes, [(i, i ^ k) for i in range(n)])  27.3 us
    ppermute x20, starting transfers between devices, shift(): return lax.ppermute(x, axis, [(i, (i + by) % n) for i in range(n)])  25.2 us
    pallas_call x2, Pallas kernels, expert(): pl.pallas_call(functools.partial(expert_kernel, groups), out_shape=tuple(...  25 us
    all_to_all x1, blocking collectives, shards(): tables = lax.all_to_all(table, 'z', split_axis=0, concat_axis=0, tiled=True)  15.9 us
    pallas_call x1, Pallas kernels, final(): pl.pallas_call(final_kernel, out_shape=(jax.ShapeDtypeStruct((rows, width...  8.15 us
    unnamed x68, local copies, waits for them, and re-layouts  6.93 us
  transfers between devices with their start and end apart: 47, of which 17 were waited for; matrix products, arithmetic and copies ran while one was open for 1% of the time, Pallas kernels for 14%

profile of v8, /device:TPU:1, one launch (start us, length us, event | category | flops | bytes accessed | tf_op | source)
XLA Modules:
  0.0 258.7 jit_solution(1109722437466999970)
XLA Ops:
  7.9 6.0 %shard_map.95 = (bf16[1024,2048]{1,0:T(8,128)(2,1)}, f32[64,128]{1,0:T(8,128)}) custom-call(s32[6,128]{1,0:T(8,128)} %bitcast.39, f32[6,128]{1,0:T(8,128)} %bitcast.40, bf16[128,2048]{1,0:T(8,128)(2,1)} %tokens.3), custom_call_target="tpu_custom_call" | custom-call | flops 536870912 | bytes 5242880 | tf_op jit(solution)/shard_map/pallas_call | solution.py:69
  13.9 15.9 %all_to_all.23 = f32[8,8,128]{2,1,0:T(8,128)S(1)} all-to-all(f32[8,8,128]{2,1,0:T(8,128)} %bitcast.37), channel_id=1, replica_groups=mesh['xl'=2,'y'=4,'z'=8,'xh'=2,'c'=2] {'z'}, dimensions={0} | all-to-all | bytes 65536 | tf_op jit(solution)/shard_map/all_to_all | solution.py:311
  29.8 6.6 %all-to-all-start.1 = ((bf16[32,32,2048]{2,1,0:T(8,128)(2,1)}), bf16[32,32,2048]{2,1,0:T(8,128)(2,1)}, u32[]{:S(2)}, u32[]{:S(2)}) async-start(bf16[32,32,2048]{2,1,0:T(8,128)(2,1)} %bitcast.27), calls=%async_computation.1 | async-start | bytes 8388608 | tf_op jit(solution)/shard_map/all_to_all | solution.py:313
  38.9 1.2 collective-permute-start.10
  40.4 1.1 collective-permute-start.5
  41.6 26.3 %collective-permute-done.10.refs_14_ = bf16[768,256]{1,0:T(8,128)(2,1)S(1)} collective-permute-done((bf16[768,256]{1,0:T(8,128)(2,1)S(1)}, bf16[768,256]{1,0:T(8,128)(2,1)S(1)}, u32[]{:S(2)}, u32[]{:S(2)}) %collective-permute-start.10) | collective-permute-done | bytes 393248 | tf_op jit(solution)/shard_map/ppermute | solution.py:34
  67.9 1.3 collective-permute-start.11
  69.2 1.4 collective-permute-start.12
  70.6 10.2 %collective-permute-done.refs_2_ = bf16[256,768]{1,0:T(8,128)(2,1)S(1)} collective-permute-done((bf16[256,768]{1,0:T(8,128)(2,1)S(1)}, bf16[256,768]{1,0:T(8,128)(2,1)S(1)}, u32[]{:S(2)}, u32[]{:S(2)}) %collective-permute-start) | collective-permute-done | bytes 393248 | tf_op jit(solution)/shard_map/ppermute | solution.py:34
  80.8 1.3 collective-permute-start.1
  82.1 1.4 collective-permute-start.2
  83.5 8.1 %collective-permute-done.5.refs_8_ = bf16[256,768]{1,0:T(8,128)(2,1)S(1)} collective-permute-done((bf16[256,768]{1,0:T(8,128)(2,1)S(1)}, bf16[256,768]{1,0:T(8,128)(2,1)S(1)}, u32[]{:S(2)}, u32[]{:S(2)}) %collective-permute-start.5) | collective-permute-done | bytes 393248 | tf_op jit(solution)/shard_map/ppermute | solution.py:34
  91.7 1.3 collective-permute-start.6
  93.0 1.5 collective-permute-start.7
  95.3 2.1 collective-permute-start.14
  98.2 10.8 %collective-permute-done.6.refs_9_ = bf16[256,768]{1,0:T(8,128)(2,1)S(1)} collective-permute-done((bf16[256,768]{1,0:T(8,128)(2,1)S(1)}, bf16[256,768]{1,0:T(8,128)(2,1)S(1)}, u32[]{:S(2)}, u32[]{:S(2)}) %collective-permute-start.6) | collective-permute-done | bytes 393248 | tf_op jit(solution)/shard_map/ppermute | solution.py:29
  109.0 2.7 %collective-permute-start.4 = (bf16[128,768]{1,0:T(8,128)(2,1)S(1)}, bf16[128,768]{1,0:T(8,128)(2,1)}, u32[]{:S(2)}, u32[]{:S(2)}) collective-permute-start(bf16[128,768]{1,0:T(8,128)(2,1)S(1)} %slice.25), channel_id=1, source_target_pairs={{0,96},{32,0},{64,32},{96,64},{1,97},{33,1},{65,33},{97,65},{2,98}... | collective-permute-start | bytes 589832 | tf_op jit(solution)/shard_map/ppermute | solution.py:29
  112.5 3.7 %collective-permute-done.13.refs_17_ = bf16[384,256]{1,0:T(8,128)(2,1)S(1)} collective-permute-done((bf16[384,256]{1,0:T(8,128)(2,1)S(1)}, bf16[384,256]{1,0:T(8,128)(2,1)S(1)}, u32[]{:S(2)}, u32[]{:S(2)}) %collective-permute-start.13) | collective-permute-done | bytes 196640 | tf_op jit(solution)/shard_map/ppermute | solution.py:29
  116.2 3.4 %collective-permute-start.9 = (bf16[128,768]{1,0:T(8,128)(2,1)S(1)}, bf16[128,768]{1,0:T(8,128)(2,1)S(1)}, u32[]{:S(2)}, u32[]{:S(2)}) collective-permute-start(bf16[128,768]{1,0:T(8,128)(2,1)S(1)} %slice.27), channel_id=1, source_target_pairs={{0,96},{32,0},{64,32},{96,64},{1,97},{33,1},{65,33},{97,65},{2,98}... | collective-permute-start | bytes 589832 | tf_op jit(solution)/shard_map/ppermute | solution.py:29
  121.1 3.1 %collective-permute-done.3.refs_5_ = bf16[128,768]{1,0:T(8,128)(2,1)} collective-permute-done((bf16[128,768]{1,0:T(8,128)(2,1)S(1)}, bf16[128,768]{1,0:T(8,128)(2,1)}, u32[]{:S(2)}, u32[]{:S(2)}) %collective-permute-start.3) | collective-permute-done | bytes 196640 | tf_op jit(solution)/shard_map/ppermute | solution.py:29
  124.1 4.6 %collective-permute-done.8.refs_11_ = bf16[128,768]{1,0:T(8,128)(2,1)} collective-permute-done((bf16[128,768]{1,0:T(8,128)(2,1)S(1)}, bf16[128,768]{1,0:T(8,128)(2,1)}, u32[]{:S(2)}, u32[]{:S(2)}) %collective-permute-start.8) | collective-permute-done | bytes 196640 | tf_op jit(solution)/shard_map/ppermute | solution.py:29
  128.8 1.7 all-to-all-done.1
  130.5 10.9 %shard_map.97 = (bf16[32,2048]{1,0:T(8,128)(2,1)}, bf16[32,2048]{1,0:T(8,128)(2,1)}, bf16[32,2048]{1,0:T(8,128)(2,1)}, bf16[32,2048]{1,0:T(8,128)(2,1)}, bf16[64...) custom-call(s32[2]{0:T(128)} %pad_add_fusion.1.place, ...), custom_call_target="tpu_custom_call" | custom-call | flops 3623878656 | bytes 16777216 | tf_op jit(solution)/shard_map/pallas_call | solution.py:171
  141.5 3.0 %collective-permute-start.15 = (bf16[32,2048]{1,0:T(8,128)(2,1)}, bf16[32,2048]{1,0:T(8,128)(2,1)S(1)}, u32[]{:S(2)}, u32[]{:S(2)}) collective-permute-start(bf16[32,2048]{1,0:T(8,128)(2,1)} %get-tuple-element.84), channel_id=1, source_target_pairs={{0,1},{1,0},{2,3},{3,2},{4,5},{5,4},{6,7},{7,6},{8,9},{9,8},{10,11... | collective-permute-start | bytes 393224 | tf_op jit(solution)/shard_map/ppermute | solution.py:34
  145.8 3.2 %collective-permute-start.20 = (bf16[64,2048]{1,0:T(8,128)(2,1)}, bf16[64,2048]{1,0:T(8,128)(2,1)}, u32[]{:S(2)}, u32[]{:S(2)}) collective-permute-start(bf16[64,2048]{1,0:T(8,128)(2,1)} %get-tuple-element.89), channel_id=1, source_target_pairs={{0,3},{1,2},{2,1},{3,0},{4,7},{5,6},{6,5},{7,4},{8,11},{9,10},{10,... | collective-permute-start | bytes 786440 | tf_op jit(solution)/shard_map/ppermute | solution.py:34
  150.0 2.6 %collective-permute-start.17 = (bf16[32,2048]{1,0:T(8,128)(2,1)}, bf16[32,2048]{1,0:T(8,128)(2,1)}, u32[]{:S(2)}, u32[]{:S(2)}) collective-permute-start(bf16[32,2048]{1,0:T(8,128)(2,1)} %get-tuple-element.86), channel_id=1, source_target_pairs={{0,3},{1,2},{2,1},{3,0},{4,7},{5,6},{6,5},{7,4},{8,11},{9,10},{10,... | collective-permute-start | bytes 393224 | tf_op jit(solution)/shard_map/ppermute | solution.py:34
  152.6 14.1 %shard_map.98 = (bf16[64,2048]{1,0:T(8,128)(2,1)}, bf16[64,2048]{1,0:T(8,128)(2,1)}, bf16[64,2048]{1,0:T(8,128)(2,1)}, bf16[64,2048]{1,0:T(8,128)(2,1)}, bf16[64...) custom-call(s32[2]{0:T(128)} %pad_add_fusion.1.place, ...), custom_call_target="tpu_custom_call" | custom-call | flops 6039797760 | bytes 16777216 | tf_op jit(solution)/shard_map/pallas_call | solution.py:171
  168.4 1.4 shard_map.99
  172.3 1.7 collective-permute-start.24
  174.0 1.5 collective-permute-start.25
  175.5 3.7 %collective-permute-done.24.a2 = bf16[32,2048]{1,0:T(8,128)(2,1)S(1)} collective-permute-done((bf16[32,2048]{1,0:T(8,128)(2,1)}, bf16[32,2048]{1,0:T(8,128)(2,1)S(1)}, u32[]{:S(2)}, u32[]{:S(2)}) %collective-permute-start.24) | collective-permute-done | bytes 131104 | tf_op jit(solution)/shard_map/ppermute | solution.py:34
  179.2 2.9 %collective-permute-done.25.a3 = bf16[32,2048]{1,0:T(8,128)(2,1)S(1)} collective-permute-done((bf16[32,2048]{1,0:T(8,128)(2,1)}, bf16[32,2048]{1,0:T(8,128)(2,1)S(1)}, u32[]{:S(2)}, u32[]{:S(2)}) %collective-permute-start.25) | collective-permute-done | bytes 131104 | tf_op jit(solution)/shard_map/ppermute | solution.py:34
  183.1 2.4 shard_map.100
  185.5 1.9 collective-permute-start.26
  188.2 2.6 %collective-permute-start.29 = (bf16[64,2048]{1,0:T(8,128)(2,1)}, bf16[64,2048]{1,0:T(8,128)(2,1)}, u32[]{:S(2)}, u32[]{:S(2)}) collective-permute-start(bf16[64,2048]{1,0:T(8,128)(2,1)} %get-tuple-element.128), channel_id=1, source_target_pairs={{0,2},{1,3},{2,0},{3,1},{4,6},{5,7},{6,4},{7,5},{8,10},{9,11},{10,... | collective-permute-start | bytes 786440 | tf_op jit(solution)/shard_map/ppermute | solution.py:34
  191.5 6.4 %collective-permute-done.29.refs_4_ = bf16[64,2048]{1,0:T(8,128)(2,1)} collective-permute-done((bf16[64,2048]{1,0:T(8,128)(2,1)}, bf16[64,2048]{1,0:T(8,128)(2,1)}, u32[]{:S(2)}, u32[]{:S(2)}) %collective-permute-start.29) | collective-permute-done | bytes 262176 | tf_op jit(solution)/shard_map/ppermute | solution.py:34
  197.9 5.8 %collective-permute-done.30.refs_5_ = bf16[64,2048]{1,0:T(8,128)(2,1)} collective-permute-done((bf16[64,2048]{1,0:T(8,128)(2,1)}, bf16[64,2048]{1,0:T(8,128)(2,1)}, u32[]{:S(2)}, u32[]{:S(2)}) %collective-permute-start.30) | collective-permute-done | bytes 262176 | tf_op jit(solution)/shard_map/ppermute | solution.py:34
  204.5 2.5 collective-permute-start.35
  207.0 1.7 shard_map.101
  208.7 3.1 %collective-permute-start.32 = (bf16[128,2048]{1,0:T(8,128)(2,1)S(1)}, bf16[128,2048]{1,0:T(8,128)(2,1)S(1)}, u32[]{:S(2)}, u32[]{:S(2)}) collective-permute-start(bf16[128,2048]{1,0:T(8,128)(2,1)S(1)} %get-tuple-element.142), channel_id=1, source_target_pairs={{0,28},{4,0},{8,4},{12,8},{16,12},{20,16},{24,20},{28,24},{1,29},{... | collective-permute-start | bytes 1572872 | tf_op jit(solution)/shard_map/ppermute | solution.py:29
  211.8 2.0 collective-permute-done.35.refs_4_
  213.9 3.5 %collective-permute-start.36 = (bf16[64,2048]{1,0:T(8,128)(2,1)}, bf16[64,2048]{1,0:T(8,128)(2,1)S(1)}, u32[]{:S(2)}, u32[]{:S(2)}) collective-permute-start(bf16[64,2048]{1,0:T(8,128)(2,1)} %get-tuple-element.146), channel_id=1, source_target_pairs={{0,3},{1,2},{2,1},{3,0},{4,7},{5,6},{6,5},{7,4},{8,11},{9,10},{10,... | collective-permute-start | bytes 786440 | tf_op jit(solution)/shard_map/ppermute | solution.py:34
  217.3 7.1 %collective-permute-done.36.refs_5_ = bf16[64,2048]{1,0:T(8,128)(2,1)S(1)} collective-permute-done((bf16[64,2048]{1,0:T(8,128)(2,1)}, bf16[64,2048]{1,0:T(8,128)(2,1)S(1)}, u32[]{:S(2)}, u32[]{:S(2)}) %collective-permute-start.36) | collective-permute-done | bytes 262176 | tf_op jit(solution)/shard_map/ppermute | solution.py:34
  224.5 1.2 collective-permute-done.33.refs_7_
  227.4 1.9 collective-permute-start.39
  229.9 10.2 %collective-permute-done.39.left = bf16[128,2048]{1,0:T(8,128)(2,1)S(1)} collective-permute-done((bf16[128,2048]{1,0:T(8,128)(2,1)S(1)}, bf16[128,2048]{1,0:T(8,128)(2,1)S(1)}, u32[]{:S(2)}, u32[]{:S(2)}) %collective-permute-start.39) | collective-permute-done | bytes 524320 | tf_op jit(solution)/shard_map/ppermute | solution.py:29
  240.1 3.1 %collective-permute-done.40.right = bf16[128,2048]{1,0:T(8,128)(2,1)S(1)} collective-permute-done((bf16[128,2048]{1,0:T(8,128)(2,1)S(1)}, bf16[128,2048]{1,0:T(8,128)(2,1)S(1)}, u32[]{:S(2)}, u32[]{:S(2)}) %collective-permute-start.40) | collective-permute-done | bytes 524320 | tf_op jit(solution)/shard_map/ppermute | solution.py:29
  244.0 8.1 %shard_map.103 = (bf16[128,2048]{1,0:T(8,128)(2,1)}, bf16[128,1536]{1,0:T(8,128)(2,1)}) custom-call(s32[4]{0:T(128)} %pad_add_fusion.offsets, bf16[8,128,256]{2,1,0:T(8,128)(2,1)} %copy-done.1, bf16[32,2048]{1,0:T(8,128)(2,1)} %get-tuple-element.102.a0, bf16[32,2048]{1,0:T(8,128)(2,1)} %copy-done.31, bf16[32,2048]{1,0:T(8,128)(2,1)} %copy-done.32, ...), custom_call_target="tpu_custom_call" | custom-call | flops 805306368 | bytes 8388608 | tf_op jit(solution)/shard_map/pallas_call | solution.py:277
  (139 shorter events, 20.0 us)
Async XLA Ops:
  7.2 121.5 %all-gather.13.cloned.1.call-start = ((), (), s32[]{:S(2)}) async-start(), calls=%async_computation.4 | async-start | bytes 1966080 | tf_op jit(solution)/shard_map/all_gather | solution.py:315
  29.8 100.7 %all-to-all-start.1 = ((bf16[32,32,2048]{2,1,0:T(8,128)(2,1)}), bf16[32,32,2048]{2,1,0:T(8,128)(2,1)}, u32[]{:S(2)}, u32[]{:S(2)}) async-start(bf16[32,32,2048]{2,1,0:T(8,128)(2,1)} %bitcast.27), calls=%async_computation.1 | async-start | bytes 8388608 | tf_op jit(solution)/shard_map/all_to_all | solution.py:313
  36.4 92.3 %all-gather.15.cloned.1.call-start = ((), (), s32[]{:S(2)}) async-start(), calls=%async_computation.5 | async-start | bytes 1966080 | tf_op jit(solution)/shard_map/all_gather | solution.py:316
  37.2 91.6 %all-gather.17.cloned.1.call-start = ((), (), s32[]{:S(2)}) async-start(), calls=%async_computation.6 | async-start | bytes 1966080 | tf_op jit(solution)/shard_map/all_gather | solution.py:317
  37.9 153.5 %all-gather.9.cloned.1.call-start = ((), (), s32[]{:S(2)}) async-start(), calls=%async_computation.2 | async-start | bytes 1966080 | tf_op jit(solution)/shard_map/all_gather | solution.py:327
  38.8 80.9 %copy-start.11 = (bf16[192,1024]{1,0:T(8,128)(2,1)S(1)}, bf16[192,1024]{1,0:T(8,128)(2,1)}, u32[]{:S(2)}) copy-start(bf16[192,1024]{1,0:T(8,128)(2,1)} %dynamic-slice_bitcast_fusion) | copy-start | bytes 1179652
  38.8 164.9 %all-gather.11.cloned.1.call-start = ((), (), s32[]{:S(2)}) async-start(), calls=%async_computation.3 | async-start | bytes 1966080 | tf_op jit(solution)/shard_map/all_gather | solution.py:327
  38.9 29.0 %collective-permute-start.10 = (bf16[768,256]{1,0:T(8,128)(2,1)S(1)}, bf16[768,256]{1,0:T(8,128)(2,1)S(1)}, u32[]{:S(2)}, u32[]{:S(2)}) collective-permute-start(bf16[768,256]{1,0:T(8,128)(2,1)S(1)} %bitcast.36), channel_id=1, source_target_pairs={{0,128},{128,0},{1,129},{129,1},{2,130},{130,2},{3,131},{131,3},{4... | collective-permute-start | bytes 1179656 | tf_op jit(solution)/shard_map/ppermute | solution.py:34
  40.1 40.7 %collective-permute-start = (bf16[256,768]{1,0:T(8,128)(2,1)S(1)}, bf16[256,768]{1,0:T(8,128)(2,1)S(1)}, u32[]{:S(2)}, u32[]{:S(2)}) collective-permute-start(bf16[256,768]{1,0:T(8,128)(2,1)S(1)} %bitcast.34), channel_id=1, source_target_pairs={{0,128},{128,0},{1,129},{129,1},{2,130},{130,2},{3,131},{131,3},{4... | collective-permute-start | bytes 1179656 | tf_op jit(solution)/shard_map/ppermute | solution.py:34
  40.4 51.2 %collective-permute-start.5 = (bf16[256,768]{1,0:T(8,128)(2,1)S(1)}, bf16[256,768]{1,0:T(8,128)(2,1)S(1)}, u32[]{:S(2)}, u32[]{:S(2)}) collective-permute-start(bf16[256,768]{1,0:T(8,128)(2,1)S(1)} %bitcast.35), channel_id=1, source_target_pairs={{0,128},{128,0},{1,129},{129,1},{2,130},{130,2},{3,131},{131,3},{4... | collective-permute-start | bytes 1179656 | tf_op jit(solution)/shard_map/ppermute | solution.py:34
  67.9 25.1 %collective-permute-start.11 = (bf16[768,256]{1,0:T(8,128)(2,1)S(1)}, bf16[768,256]{1,0:T(8,128)(2,1)S(1)}, u32[]{:S(2)}, u32[]{:S(2)}) collective-permute-start(bf16[768,256]{1,0:T(8,128)(2,1)S(1)} %collective-permute-done.10.refs_14_), channel_id=1, source_target_pairs={{0,32},{32,64},{64,96},{96,0},{1,33},{33,65},{65,97},{97,1},{2,34}... | collective-permute-start | bytes 1179656 | tf_op jit(solution)/shard_map/ppermute | solution.py:29
  69.2 25.3 %collective-permute-start.12 = (bf16[768,256]{1,0:T(8,128)(2,1)S(1)}, bf16[768,256]{1,0:T(8,128)(2,1)S(1)}, u32[]{:S(2)}, u32[]{:S(2)}) collective-permute-start(bf16[768,256]{1,0:T(8,128)(2,1)S(1)} %collective-permute-done.10.refs_14_), channel_id=1, source_target_pairs={{0,96},{32,0},{64,32},{96,64},{1,97},{33,1},{65,33},{97,65},{2,98}... | collective-permute-start | bytes 1179656 | tf_op jit(solution)/shard_map/ppermute | solution.py:29
  80.8 14.5 %collective-permute-start.1 = (bf16[256,768]{1,0:T(8,128)(2,1)S(1)}, bf16[256,768]{1,0:T(8,128)(2,1)S(1)}, u32[]{:S(2)}, u32[]{:S(2)}) collective-permute-start(bf16[256,768]{1,0:T(8,128)(2,1)S(1)} %collective-permute-done.refs_2_), channel_id=1, source_target_pairs={{0,32},{32,64},{64,96},{96,0},{1,33},{33,65},{65,97},{97,1},{2,34}... | collective-permute-start | bytes 1179656 | tf_op jit(solution)/shard_map/ppermute | solution.py:29
  82.1 15.3 %collective-permute-start.2 = (bf16[256,768]{1,0:T(8,128)(2,1)S(1)}, bf16[256,768]{1,0:T(8,128)(2,1)S(1)}, u32[]{:S(2)}, u32[]{:S(2)}) collective-permute-start(bf16[256,768]{1,0:T(8,128)(2,1)S(1)} %collective-permute-done.refs_2_), channel_id=1, source_target_pairs={{0,96},{32,0},{64,32},{96,64},{1,97},{33,1},{65,33},{97,65},{2,98}... | collective-permute-start | bytes 1179656 | tf_op jit(solution)/shard_map/ppermute | solution.py:29
  91.7 17.3 %collective-permute-start.6 = (bf16[256,768]{1,0:T(8,128)(2,1)S(1)}, bf16[256,768]{1,0:T(8,128)(2,1)S(1)}, u32[]{:S(2)}, u32[]{:S(2)}) collective-permute-start(bf16[256,768]{1,0:T(8,128)(2,1)S(1)} %collective-permute-done.5.refs_8_), channel_id=1, source_target_pairs={{0,32},{32,64},{64,96},{96,0},{1,33},{33,65},{65,97},{97,1},{2,34}... | collective-permute-start | bytes 1179656 | tf_op jit(solution)/shard_map/ppermute | solution.py:29
  93.0 18.7 %collective-permute-start.7 = (bf16[256,768]{1,0:T(8,128)(2,1)S(1)}, bf16[256,768]{1,0:T(8,128)(2,1)S(1)}, u32[]{:S(2)}, u32[]{:S(2)}) collective-permute-start(bf16[256,768]{1,0:T(8,128)(2,1)S(1)} %collective-permute-done.5.refs_8_), channel_id=1, source_target_pairs={{0,96},{32,0},{64,32},{96,64},{1,97},{33,1},{65,33},{97,65},{2,98}... | collective-permute-start | bytes 1179656 | tf_op jit(solution)/shard_map/ppermute | solution.py:29
  94.5 21.7 %collective-permute-start.13 = (bf16[384,256]{1,0:T(8,128)(2,1)S(1)}, bf16[384,256]{1,0:T(8,128)(2,1)S(1)}, u32[]{:S(2)}, u32[]{:S(2)}) collective-permute-start(bf16[384,256]{1,0:T(8,128)(2,1)S(1)} %slice.28), channel_id=1, source_target_pairs={{0,32},{32,64},{64,96},{96,0},{1,33},{33,65},{65,97},{97,1},{2,34}... | collective-permute-start | bytes 589832 | tf_op jit(solution)/shard_map/ppermute | solution.py:29
  95.3 24.3 %collective-permute-start.14 = (bf16[384,256]{1,0:T(8,128)(2,1)S(1)}, bf16[384,256]{1,0:T(8,128)(2,1)S(1)}, u32[]{:S(2)}, u32[]{:S(2)}) collective-permute-start(bf16[384,256]{1,0:T(8,128)(2,1)S(1)} %slice.29), channel_id=1, source_target_pairs={{0,96},{32,0},{64,32},{96,64},{1,97},{33,1},{65,33},{97,65},{2,98}... | collective-permute-start | bytes 589832 | tf_op jit(solution)/shard_map/ppermute | solution.py:29
  97.4 26.7 %collective-permute-start.3 = (bf16[128,768]{1,0:T(8,128)(2,1)S(1)}, bf16[128,768]{1,0:T(8,128)(2,1)}, u32[]{:S(2)}, u32[]{:S(2)}) collective-permute-start(bf16[128,768]{1,0:T(8,128)(2,1)S(1)} %slice.24), channel_id=1, source_target_pairs={{0,32},{32,64},{64,96},{96,0},{1,33},{33,65},{65,97},{97,1},{2,34}... | collective-permute-start | bytes 589832 | tf_op jit(solution)/shard_map/ppermute | solution.py:29
  109.0 15.1 %collective-permute-start.4 = (bf16[128,768]{1,0:T(8,128)(2,1)S(1)}, bf16[128,768]{1,0:T(8,128)(2,1)}, u32[]{:S(2)}, u32[]{:S(2)}) collective-permute-start(bf16[128,768]{1,0:T(8,128)(2,1)S(1)} %slice.25), channel_id=1, source_target_pairs={{0,96},{32,0},{64,32},{96,64},{1,97},{33,1},{65,33},{97,65},{2,98}... | collective-permute-start | bytes 589832 | tf_op jit(solution)/shard_map/ppermute | solution.py:29
  111.7 17.0 %collective-permute-start.8 = (bf16[128,768]{1,0:T(8,128)(2,1)S(1)}, bf16[128,768]{1,0:T(8,128)(2,1)}, u32[]{:S(2)}, u32[]{:S(2)}) collective-permute-start(bf16[128,768]{1,0:T(8,128)(2,1)S(1)} %slice.26), channel_id=1, source_target_pairs={{0,32},{32,64},{64,96},{96,0},{1,33},{33,65},{65,97},{97,1},{2,34}... | collective-permute-start | bytes 589832 | tf_op jit(solution)/shard_map/ppermute | solution.py:29
  116.2 12.5 %collective-permute-start.9 = (bf16[128,768]{1,0:T(8,128)(2,1)S(1)}, bf16[128,768]{1,0:T(8,128)(2,1)S(1)}, u32[]{:S(2)}, u32[]{:S(2)}) collective-permute-start(bf16[128,768]{1,0:T(8,128)(2,1)S(1)} %slice.27), channel_id=1, source_target_pairs={{0,96},{32,0},{64,32},{96,64},{1,97},{33,1},{65,33},{97,65},{2,98}... | collective-permute-start | bytes 589832 | tf_op jit(solution)/shard_map/ppermute | solution.py:29
  119.6 21.8 %collective-permute-start.31 = (bf16[192,1024]{1,0:T(8,128)(2,1)S(1)}, bf16[192,1024]{1,0:T(8,128)(2,1)}, u32[]{:S(2)}, u32[]{:S(2)}) collective-permute-start(bf16[192,1024]{1,0:T(8,128)(2,1)S(1)} %copy-done.11), channel_id=1, source_target_pairs={{0,128},{128,0},{1,129},{129,1},{2,130},{130,2},{3,131},{131,3},{4... | collective-permute-start | bytes 1179656 | tf_op jit(solution)/shard_map/ppermute | solution.py:34
  141.5 7.9 %collective-permute-start.15 = (bf16[32,2048]{1,0:T(8,128)(2,1)}, bf16[32,2048]{1,0:T(8,128)(2,1)S(1)}, u32[]{:S(2)}, u32[]{:S(2)}) collective-permute-start(bf16[32,2048]{1,0:T(8,128)(2,1)} %get-tuple-element.84), channel_id=1, source_target_pairs={{0,1},{1,0},{2,3},{3,2},{4,5},{5,4},{6,7},{7,6},{8,9},{9,8},{10,11... | collective-permute-start | bytes 393224 | tf_op jit(solution)/shard_map/ppermute | solution.py:34
  145.3 21.5 %collective-permute-start.18 = (bf16[64,2048]{1,0:T(8,128)(2,1)}, bf16[64,2048]{1,0:T(8,128)(2,1)S(1)}, u32[]{:S(2)}, u32[]{:S(2)}) collective-permute-start(bf16[64,2048]{1,0:T(8,128)(2,1)} %get-tuple-element.87), channel_id=1, source_target_pairs={{0,1},{1,0},{2,3},{3,2},{4,5},{5,4},{6,7},{7,6},{8,9},{9,8},{10,11... | collective-permute-start | bytes 786440 | tf_op jit(solution)/shard_map/ppermute | solution.py:34
  145.4 22.1 %collective-permute-start.19 = (bf16[64,2048]{1,0:T(8,128)(2,1)}, bf16[64,2048]{1,0:T(8,128)(2,1)}, u32[]{:S(2)}, u32[]{:S(2)}) collective-permute-start(bf16[64,2048]{1,0:T(8,128)(2,1)} %get-tuple-element.88), channel_id=1, source_target_pairs={{0,2},{1,3},{2,0},{3,1},{4,6},{5,7},{6,4},{7,5},{8,10},{9,11},{10,... | collective-permute-start | bytes 786440 | tf_op jit(solution)/shard_map/ppermute | solution.py:34
  145.8 21.7 %collective-permute-start.20 = (bf16[64,2048]{1,0:T(8,128)(2,1)}, bf16[64,2048]{1,0:T(8,128)(2,1)}, u32[]{:S(2)}, u32[]{:S(2)}) collective-permute-start(bf16[64,2048]{1,0:T(8,128)(2,1)} %get-tuple-element.89), channel_id=1, source_target_pairs={{0,3},{1,2},{2,1},{3,0},{4,7},{5,6},{6,5},{7,4},{8,11},{9,10},{10,... | collective-permute-start | bytes 786440 | tf_op jit(solution)/shard_map/ppermute | solution.py:34
  149.0 17.7 %collective-permute-start.16 = (bf16[32,2048]{1,0:T(8,128)(2,1)}, bf16[32,2048]{1,0:T(8,128)(2,1)}, u32[]{:S(2)}, u32[]{:S(2)}) collective-permute-start(bf16[32,2048]{1,0:T(8,128)(2,1)} %get-tuple-element.85), channel_id=1, source_target_pairs={{0,2},{1,3},{2,0},{3,1},{4,6},{5,7},{6,4},{7,5},{8,10},{9,11},{10,... | collective-permute-start | bytes 393224 | tf_op jit(solution)/shard_map/ppermute | solution.py:34
  150.0 16.7 %collective-permute-start.17 = (bf16[32,2048]{1,0:T(8,128)(2,1)}, bf16[32,2048]{1,0:T(8,128)(2,1)}, u32[]{:S(2)}, u32[]{:S(2)}) collective-permute-start(bf16[32,2048]{1,0:T(8,128)(2,1)} %get-tuple-element.86), channel_id=1, source_target_pairs={{0,3},{1,2},{2,1},{3,0},{4,7},{5,6},{6,5},{7,4},{8,11},{9,10},{10,... | collective-permute-start | bytes 393224 | tf_op jit(solution)/shard_map/ppermute | solution.py:34
  169.8 12.3 %collective-permute-start.21 = (bf16[64,2048]{1,0:T(8,128)(2,1)S(1)}, bf16[64,2048]{1,0:T(8,128)(2,1)S(1)}, u32[]{:S(2)}, u32[]{:S(2)}) collective-permute-start(bf16[64,2048]{1,0:T(8,128)(2,1)S(1)} %get-tuple-element.107), channel_id=1, source_target_pairs={{0,28},{4,0},{8,4},{12,8},{16,12},{20,16},{24,20},{28,24},{1,29},{... | collective-permute-start | bytes 786440 | tf_op jit(solution)/shard_map/ppermute | solution.py:29
  170.6 11.5 %collective-permute-start.22 = (bf16[64,2048]{1,0:T(8,128)(2,1)S(1)}, bf16[64,2048]{1,0:T(8,128)(2,1)S(1)}, u32[]{:S(2)}, u32[]{:S(2)}) collective-permute-start(bf16[64,2048]{1,0:T(8,128)(2,1)S(1)} %get-tuple-element.108), channel_id=1, source_target_pairs={{0,4},{4,8},{8,12},{12,16},{16,20},{20,24},{24,28},{28,0},{1,5},{5... | collective-permute-start | bytes 786440 | tf_op jit(solution)/shard_map/ppermute | solution.py:29
  171.3 4.1 %collective-permute-start.23 = (bf16[32,2048]{1,0:T(8,128)(2,1)}, bf16[32,2048]{1,0:T(8,128)(2,1)S(1)}, u32[]{:S(2)}, u32[]{:S(2)}) collective-permute-start(bf16[32,2048]{1,0:T(8,128)(2,1)} %get-tuple-element.109), channel_id=1, source_target_pairs={{0,1},{1,0},{2,3},{3,2},{4,5},{5,4},{6,7},{7,6},{8,9},{9,8},{10,11... | collective-permute-start | bytes 393224 | tf_op jit(solution)/shard_map/ppermute | solution.py:34
  172.3 6.8 %collective-permute-start.24 = (bf16[32,2048]{1,0:T(8,128)(2,1)}, bf16[32,2048]{1,0:T(8,128)(2,1)S(1)}, u32[]{:S(2)}, u32[]{:S(2)}) collective-permute-start(bf16[32,2048]{1,0:T(8,128)(2,1)} %get-tuple-element.110), channel_id=1, source_target_pairs={{0,2},{1,3},{2,0},{3,1},{4,6},{5,7},{6,4},{7,5},{8,10},{9,11},{10,... | collective-permute-start | bytes 393224 | tf_op jit(solution)/shard_map/ppermute | solution.py:34
  174.0 8.1 %collective-permute-start.25 = (bf16[32,2048]{1,0:T(8,128)(2,1)}, bf16[32,2048]{1,0:T(8,128)(2,1)S(1)}, u32[]{:S(2)}, u32[]{:S(2)}) collective-permute-start(bf16[32,2048]{1,0:T(8,128)(2,1)} %get-tuple-element.111), channel_id=1, source_target_pairs={{0,3},{1,2},{2,1},{3,0},{4,7},{5,6},{6,5},{7,4},{8,11},{9,10},{10,... | collective-permute-start | bytes 393224 | tf_op jit(solution)/shard_map/ppermute | solution.py:34
  185.5 18.2 %collective-permute-start.26 = (bf16[128,2048]{1,0:T(8,128)(2,1)}, bf16[128,2048]{1,0:T(8,128)(2,1)S(1)}, u32[]{:S(2)}, u32[]{:S(2)}) collective-permute-start(bf16[128,2048]{1,0:T(8,128)(2,1)} %get-tuple-element.125), channel_id=1, source_target_pairs={{0,28},{4,0},{8,4},{12,8},{16,12},{20,16},{24,20},{28,24},{1,29},{... | collective-permute-start | bytes 1572872 | tf_op jit(solution)/shard_map/ppermute | solution.py:29
  187.5 16.2 %collective-permute-start.27 = (bf16[128,2048]{1,0:T(8,128)(2,1)}, bf16[128,2048]{1,0:T(8,128)(2,1)S(1)}, u32[]{:S(2)}, u32[]{:S(2)}) collective-permute-start(bf16[128,2048]{1,0:T(8,128)(2,1)} %get-tuple-element.126), channel_id=1, source_target_pairs={{0,4},{4,8},{8,12},{12,16},{16,20},{20,24},{24,28},{28,0},{1,5},{5... | collective-permute-start | bytes 1572872 | tf_op jit(solution)/shard_map/ppermute | solution.py:29
  187.5 4.0 %collective-permute-start.28 = (bf16[64,2048]{1,0:T(8,128)(2,1)}, bf16[64,2048]{1,0:T(8,128)(2,1)S(1)}, u32[]{:S(2)}, u32[]{:S(2)}) collective-permute-start(bf16[64,2048]{1,0:T(8,128)(2,1)} %get-tuple-element.127), channel_id=1, source_target_pairs={{0,1},{1,0},{2,3},{3,2},{4,5},{5,4},{6,7},{7,6},{8,9},{9,8},{10,11... | collective-permute-start | bytes 786440 | tf_op jit(solution)/shard_map/ppermute | solution.py:34
  188.2 9.7 %collective-permute-start.29 = (bf16[64,2048]{1,0:T(8,128)(2,1)}, bf16[64,2048]{1,0:T(8,128)(2,1)}, u32[]{:S(2)}, u32[]{:S(2)}) collective-permute-start(bf16[64,2048]{1,0:T(8,128)(2,1)} %get-tuple-element.128), channel_id=1, source_target_pairs={{0,2},{1,3},{2,0},{3,1},{4,6},{5,7},{6,4},{7,5},{8,10},{9,11},{10,... | collective-permute-start | bytes 786440 | tf_op jit(solution)/shard_map/ppermute | solution.py:34
  190.8 12.9 %collective-permute-start.30 = (bf16[64,2048]{1,0:T(8,128)(2,1)}, bf16[64,2048]{1,0:T(8,128)(2,1)}, u32[]{:S(2)}, u32[]{:S(2)}) collective-permute-start(bf16[64,2048]{1,0:T(8,128)(2,1)} %get-tuple-element.129), channel_id=1, source_target_pairs={{0,3},{1,2},{2,1},{3,0},{4,7},{5,6},{6,5},{7,4},{8,11},{9,10},{10,... | collective-permute-start | bytes 786440 | tf_op jit(solution)/shard_map/ppermute | solution.py:34
  203.7 21.9 %collective-permute-start.37 = (bf16[768,1024]{1,0:T(8,128)(2,1)}, bf16[768,1024]{1,0:T(8,128)(2,1)S(1)}, u32[]{:S(2)}, u32[]{:S(2)}) collective-permute-start(bf16[768,1024]{1,0:T(8,128)(2,1)} %all-gather.9.cloned.1.call-done.q0), channel_id=1, source_target_pairs={{0,1},{1,0},{2,3},{3,2},{4,5},{5,4},{6,7},{7,6},{8,9},{9,8},{10,11... | collective-permute-start | bytes 4718600 | tf_op jit(solution)/shard_map/ppermute | solution.py:34
  204.0 21.6 %collective-permute-start.38 = (bf16[768,1024]{1,0:T(8,128)(2,1)}, bf16[768,1024]{1,0:T(8,128)(2,1)S(1)}, u32[]{:S(2)}, u32[]{:S(2)}) collective-permute-start(bf16[768,1024]{1,0:T(8,128)(2,1)} %all-gather.11.cloned.1.call-done.q1), channel_id=1, source_target_pairs={{0,1},{1,0},{2,3},{3,2},{4,5},{5,4},{6,7},{7,6},{8,9},{9,8},{10,11... | collective-permute-start | bytes 4718600 | tf_op jit(solution)/shard_map/ppermute | solution.py:34
  204.3 7.5 %collective-permute-start.34 = (bf16[64,2048]{1,0:T(8,128)(2,1)}, bf16[64,2048]{1,0:T(8,128)(2,1)S(1)}, u32[]{:S(2)}, u32[]{:S(2)}) collective-permute-start(bf16[64,2048]{1,0:T(8,128)(2,1)} %get-tuple-element.144), channel_id=1, source_target_pairs={{0,1},{1,0},{2,3},{3,2},{4,5},{5,4},{6,7},{7,6},{8,9},{9,8},{10,11... | collective-permute-start | bytes 786440 | tf_op jit(solution)/shard_map/ppermute | solution.py:34
  204.5 9.3 %collective-permute-start.35 = (bf16[64,2048]{1,0:T(8,128)(2,1)}, bf16[64,2048]{1,0:T(8,128)(2,1)S(1)}, u32[]{:S(2)}, u32[]{:S(2)}) collective-permute-start(bf16[64,2048]{1,0:T(8,128)(2,1)} %get-tuple-element.145), channel_id=1, source_target_pairs={{0,2},{1,3},{2,0},{3,1},{4,6},{5,7},{6,4},{7,5},{8,10},{9,11},{10,... | collective-permute-start | bytes 786440 | tf_op jit(solution)/shard_map/ppermute | solution.py:34
  208.7 15.7 %collective-permute-start.32 = (bf16[128,2048]{1,0:T(8,128)(2,1)S(1)}, bf16[128,2048]{1,0:T(8,128)(2,1)S(1)}, u32[]{:S(2)}, u32[]{:S(2)}) collective-permute-start(bf16[128,2048]{1,0:T(8,128)(2,1)S(1)} %get-tuple-element.142), channel_id=1, source_target_pairs={{0,28},{4,0},{8,4},{12,8},{16,12},{20,16},{24,20},{28,24},{1,29},{... | collective-permute-start | bytes 1572872 | tf_op jit(solution)/shard_map/ppermute | solution.py:29
  211.8 13.8 %collective-permute-start.33 = (bf16[128,2048]{1,0:T(8,128)(2,1)S(1)}, bf16[128,2048]{1,0:T(8,128)(2,1)S(1)}, u32[]{:S(2)}, u32[]{:S(2)}) collective-permute-start(bf16[128,2048]{1,0:T(8,128)(2,1)S(1)} %get-tuple-element.143), channel_id=1, source_target_pairs={{0,4},{4,8},{8,12},{12,16},{16,20},{20,24},{24,28},{28,0},{1,5},{5... | collective-permute-start | bytes 1572872 | tf_op jit(solution)/shard_map/ppermute | solution.py:29
  213.9 10.6 %collective-permute-start.36 = (bf16[64,2048]{1,0:T(8,128)(2,1)}, bf16[64,2048]{1,0:T(8,128)(2,1)S(1)}, u32[]{:S(2)}, u32[]{:S(2)}) collective-permute-start(bf16[64,2048]{1,0:T(8,128)(2,1)} %get-tuple-element.146), channel_id=1, source_target_pairs={{0,3},{1,2},{2,1},{3,0},{4,7},{5,6},{6,5},{7,4},{8,11},{9,10},{10,... | collective-permute-start | bytes 786440 | tf_op jit(solution)/shard_map/ppermute | solution.py:34
  227.4 12.6 %collective-permute-start.39 = (bf16[128,2048]{1,0:T(8,128)(2,1)S(1)}, bf16[128,2048]{1,0:T(8,128)(2,1)S(1)}, u32[]{:S(2)}, u32[]{:S(2)}) collective-permute-start(bf16[128,2048]{1,0:T(8,128)(2,1)S(1)} %get-tuple-element.154), channel_id=1, source_target_pairs={{0,28},{4,0},{8,4},{12,8},{16,12},{20,16},{24,20},{28,24},{1,29},{... | collective-permute-start | bytes 1572872 | tf_op jit(solution)/shard_map/ppermute | solution.py:29
  229.3 13.8 %collective-permute-start.40 = (bf16[128,2048]{1,0:T(8,128)(2,1)S(1)}, bf16[128,2048]{1,0:T(8,128)(2,1)S(1)}, u32[]{:S(2)}, u32[]{:S(2)}) collective-permute-start(bf16[128,2048]{1,0:T(8,128)(2,1)S(1)} %get-tuple-element.155), channel_id=1, source_target_pairs={{0,4},{4,8},{8,12},{12,16},{16,20},{20,24},{24,28},{28,0},{1,5},{5... | collective-permute-start | bytes 1572872 | tf_op jit(solution)/shard_map/ppermute | solution.py:29
  (33 other events, 493.4 us)
Sparse Core Ops, SparseCore 0:
  9.8 32.8 all-gather.12
  44.6 30.1 all-gather.14
  76.6 49.6 all-gather.16
  128.0 29.5 all-gather.8
  159.2 29.1 all-gather.10

commit v9 on v8

--- a/solution.py
+++ b/solution.py
@@ -329,15 +329,15 @@
     ans2, ans1, ans0 = expert(GROUPS[2:], place, offsets, arrived, gates, ups, downs)
     got4, got3, ans2, ans1, ans0 = hold((got4, got3, ans2, ans1, ans0))
     low, high = combine((4,), weights, (ans4[0],) + got4, [])
-    low, high, got0 = shift(low, "z", -1), shift(high, "z", 1), exchange(ans0)
-    low, high, got0, ans2 = hold((low, high, got0, ans2))
+    low, high, got2 = shift(low, "z", -1), shift(high, "z", 1), exchange(ans2)
+    low, high, got2, ans1 = hold((low, high, got2, ans1))
     low, high = combine((3, 5), weights, (ans3[0],) + got3, [low, high])
-    low, high, got2 = shift(low, "z", -1), shift(high, "z", 1), exchange(ans2)
-    low, high, got2, ans1, q_own = hold((low, high, got2, ans1, q_own))
+    low, high, got1 = shift(low, "z", -1), shift(high, "z", 1), exchange(ans1)
+    low, high, got1, ans0, q_own = hold((low, high, got1, ans0, q_own))
     low, high = combine((2, 6), weights, (ans2[0],) + got2, [low, high])
     q_other = tuple(swap(x, "c", 1) for x in q_own)
-    low, high, got1 = shift(low, "z", -1), shift(high, "z", 1), exchange(ans1)
-    low, high, got1, q_other = hold((low, high, got1, q_other))
+    low, high, got0 = shift(low, "z", -1), shift(high, "z", 1), exchange(ans0)
+    low, high, got0, q_other = hold((low, high, got0, q_other))
     low, high = combine((1, 7), weights, (ans1[0],) + got1, [low, high])
     low, high = shift(low, "z", -1), shift(high, "z", 1)
     got0 = (ans0[0],) + got0

time: 259 us -> 269 us (1.039)
  local copies, waits for them, and re-layouts: 8.48 us -> 13.2 us
  waiting for transfers between devices: 113 us -> 116 us
    unnamed x68 -> x84, local copies, waits for them, and re-layouts: 6.93 us -> 11.7 us
    ppermute x20, waiting for transfers between devices: 36.6 us -> 39.5 us  [shift(): return lax.ppermute(x, axis, [(i, (i + by) % n) for i in range(n)])]
  transfers between devices with their start and end apart: 47 -> 47, of which waited for: 17 -> 19; matrix products, arithmetic and copies ran while one was open for 1% -> 1% of each run, Pallas kernels for 14% -> 14%
where the time goes in v9:
time: 269 us
  waiting for transfers between devices  116 us (43%)
  starting transfers between devices  61.3 us (23%)
  Pallas kernels  46.9 us (17%)
  blocking collectives  15.9 us (6%)
  between operations  14.2 us (5%)
  local copies, waits for them, and re-layouts  13.2 us (5%)
    ppermute x21, waiting for transfers between devices, swap(): return lax.ppermute(x, axes, [(i, i ^ k) for i in range(n)])  72.6 us
    ppermute x20, waiting for transfers between devices, shift(): return lax.ppermute(x, axis, [(i, (i + by) % n) for i in range(n)])  39.5 us
    ppermute x21, starting transfers between devices, swap(): return lax.ppermute(x, axes, [(i, i ^ k) for i in range(n)])  28.2 us
    ppermute x20, starting transfers between devices, shift(): return lax.ppermute(x, axis, [(i, (i + by) % n) for i in range(n)])  26.2 us
    pallas_call x2, Pallas kernels, expert(): pl.pallas_call(functools.partial(expert_kernel, groups), out_shape=tuple(...  25.1 us
    all_to_all x1, blocking collectives, shards(): tables = lax.all_to_all(table, 'z', split_axis=0, concat_axis=0, tiled=True)  15.9 us
    unnamed x84, local copies, waits for them, and re-layouts  11.7 us
    pallas_call x1, Pallas kernels, final(): pl.pallas_call(final_kernel, out_shape=(jax.ShapeDtypeStruct((rows, width...  8.15 us
  transfers between devices with their start and end apart: 47, of which 19 were waited for; matrix products, arithmetic and copies ran while one was open for 1% of the time, Pallas kernels for 14%

profile of v9, /device:TPU:1, one launch (start us, length us, event | category | flops | bytes accessed | tf_op | source)
XLA Modules:
  0.0 268.6 jit_solution(12016929173733212518)
XLA Ops:
  7.9 6.0 %shard_map.95 = (bf16[1024,2048]{1,0:T(8,128)(2,1)}, f32[64,128]{1,0:T(8,128)}) custom-call(s32[6,128]{1,0:T(8,128)} %bitcast.39, f32[6,128]{1,0:T(8,128)} %bitcast.40, bf16[128,2048]{1,0:T(8,128)(2,1)} %tokens.3), custom_call_target="tpu_custom_call" | custom-call | flops 536870912 | bytes 5242880 | tf_op jit(solution)/shard_map/pallas_call | solution.py:69
  13.9 15.9 %all_to_all.23 = f32[8,8,128]{2,1,0:T(8,128)S(1)} all-to-all(f32[8,8,128]{2,1,0:T(8,128)} %bitcast.37), channel_id=1, replica_groups=mesh['xl'=2,'y'=4,'z'=8,'xh'=2,'c'=2] {'z'}, dimensions={0} | all-to-all | bytes 65536 | tf_op jit(solution)/shard_map/all_to_all | solution.py:311
  29.8 6.6 %all-to-all-start.1 = ((bf16[32,32,2048]{2,1,0:T(8,128)(2,1)}), bf16[32,32,2048]{2,1,0:T(8,128)(2,1)}, u32[]{:S(2)}, u32[]{:S(2)}) async-start(bf16[32,32,2048]{2,1,0:T(8,128)(2,1)} %bitcast.27), calls=%async_computation.1 | async-start | bytes 8388608 | tf_op jit(solution)/shard_map/all_to_all | solution.py:313
  38.9 1.2 collective-permute-start.10
  41.6 26.3 %collective-permute-done.10.refs_14_ = bf16[768,256]{1,0:T(8,128)(2,1)S(1)} collective-permute-done((bf16[768,256]{1,0:T(8,128)(2,1)S(1)}, bf16[768,256]{1,0:T(8,128)(2,1)S(1)}, u32[]{:S(2)}, u32[]{:S(2)}) %collective-permute-start.10) | collective-permute-done | bytes 393248 | tf_op jit(solution)/shard_map/ppermute | solution.py:34
  67.9 1.3 collective-permute-start.11
  69.2 1.4 collective-permute-start.12
  70.6 10.2 %collective-permute-done.refs_2_ = bf16[256,768]{1,0:T(8,128)(2,1)S(1)} collective-permute-done((bf16[256,768]{1,0:T(8,128)(2,1)S(1)}, bf16[256,768]{1,0:T(8,128)(2,1)S(1)}, u32[]{:S(2)}, u32[]{:S(2)}) %collective-permute-start) | collective-permute-done | bytes 393248 | tf_op jit(solution)/shard_map/ppermute | solution.py:34
  80.8 1.3 collective-permute-start.1
  82.1 1.4 collective-permute-start.2
  83.5 8.1 %collective-permute-done.5.refs_8_ = bf16[256,768]{1,0:T(8,128)(2,1)S(1)} collective-permute-done((bf16[256,768]{1,0:T(8,128)(2,1)S(1)}, bf16[256,768]{1,0:T(8,128)(2,1)S(1)}, u32[]{:S(2)}, u32[]{:S(2)}) %collective-permute-start.5) | collective-permute-done | bytes 393248 | tf_op jit(solution)/shard_map/ppermute | solution.py:34
  91.7 1.3 collective-permute-start.6
  93.0 1.5 collective-permute-start.7
  95.3 2.1 collective-permute-start.14
  98.2 10.7 %collective-permute-done.6.refs_9_ = bf16[256,768]{1,0:T(8,128)(2,1)S(1)} collective-permute-done((bf16[256,768]{1,0:T(8,128)(2,1)S(1)}, bf16[256,768]{1,0:T(8,128)(2,1)S(1)}, u32[]{:S(2)}, u32[]{:S(2)}) %collective-permute-start.6) | collective-permute-done | bytes 393248 | tf_op jit(solution)/shard_map/ppermute | solution.py:29
  108.9 2.8 %collective-permute-start.4 = (bf16[128,768]{1,0:T(8,128)(2,1)S(1)}, bf16[128,768]{1,0:T(8,128)(2,1)}, u32[]{:S(2)}, u32[]{:S(2)}) collective-permute-start(bf16[128,768]{1,0:T(8,128)(2,1)S(1)} %slice.25), channel_id=1, source_target_pairs={{0,96},{32,0},{64,32},{96,64},{1,97},{33,1},{65,33},{97,65},{2,98}... | collective-permute-start | bytes 589832 | tf_op jit(solution)/shard_map/ppermute | solution.py:29
  112.5 3.6 %collective-permute-done.13.refs_17_ = bf16[384,256]{1,0:T(8,128)(2,1)S(1)} collective-permute-done((bf16[384,256]{1,0:T(8,128)(2,1)S(1)}, bf16[384,256]{1,0:T(8,128)(2,1)S(1)}, u32[]{:S(2)}, u32[]{:S(2)}) %collective-permute-start.13) | collective-permute-done | bytes 196640 | tf_op jit(solution)/shard_map/ppermute | solution.py:29
  116.2 3.4 %collective-permute-start.9 = (bf16[128,768]{1,0:T(8,128)(2,1)S(1)}, bf16[128,768]{1,0:T(8,128)(2,1)S(1)}, u32[]{:S(2)}, u32[]{:S(2)}) collective-permute-start(bf16[128,768]{1,0:T(8,128)(2,1)S(1)} %slice.27), channel_id=1, source_target_pairs={{0,96},{32,0},{64,32},{96,64},{1,97},{33,1},{65,33},{97,65},{2,98}... | collective-permute-start | bytes 589832 | tf_op jit(solution)/shard_map/ppermute | solution.py:29
  120.9 3.2 %collective-permute-done.3.refs_5_ = bf16[128,768]{1,0:T(8,128)(2,1)} collective-permute-done((bf16[128,768]{1,0:T(8,128)(2,1)S(1)}, bf16[128,768]{1,0:T(8,128)(2,1)}, u32[]{:S(2)}, u32[]{:S(2)}) %collective-permute-start.3) | collective-permute-done | bytes 196640 | tf_op jit(solution)/shard_map/ppermute | solution.py:29
  124.1 4.6 %collective-permute-done.8.refs_11_ = bf16[128,768]{1,0:T(8,128)(2,1)} collective-permute-done((bf16[128,768]{1,0:T(8,128)(2,1)S(1)}, bf16[128,768]{1,0:T(8,128)(2,1)}, u32[]{:S(2)}, u32[]{:S(2)}) %collective-permute-start.8) | collective-permute-done | bytes 196640 | tf_op jit(solution)/shard_map/ppermute | solution.py:29
  128.8 1.7 all-to-all-done.1
  130.5 11.0 %shard_map.97 = (bf16[32,2048]{1,0:T(8,128)(2,1)}, bf16[32,2048]{1,0:T(8,128)(2,1)}, bf16[32,2048]{1,0:T(8,128)(2,1)}, bf16[32,2048]{1,0:T(8,128)(2,1)}, bf16[64...) custom-call(s32[2]{0:T(128)} %pad_add_fusion.1.place, ...), custom_call_target="tpu_custom_call" | custom-call | flops 3623878656 | bytes 16777216 | tf_op jit(solution)/shard_map/pallas_call | solution.py:171
  141.5 3.0 %collective-permute-start.15 = (bf16[32,2048]{1,0:T(8,128)(2,1)}, bf16[32,2048]{1,0:T(8,128)(2,1)S(1)}, u32[]{:S(2)}, u32[]{:S(2)}) collective-permute-start(bf16[32,2048]{1,0:T(8,128)(2,1)} %get-tuple-element.85), channel_id=1, source_target_pairs={{0,1},{1,0},{2,3},{3,2},{4,5},{5,4},{6,7},{7,6},{8,9},{9,8},{10,11... | collective-permute-start | bytes 393224 | tf_op jit(solution)/shard_map/ppermute | solution.py:34
  145.8 3.2 %collective-permute-start.20 = (bf16[64,2048]{1,0:T(8,128)(2,1)}, bf16[64,2048]{1,0:T(8,128)(2,1)}, u32[]{:S(2)}, u32[]{:S(2)}) collective-permute-start(bf16[64,2048]{1,0:T(8,128)(2,1)} %get-tuple-element.90), channel_id=1, source_target_pairs={{0,3},{1,2},{2,1},{3,0},{4,7},{5,6},{6,5},{7,4},{8,11},{9,10},{10,... | collective-permute-start | bytes 786440 | tf_op jit(solution)/shard_map/ppermute | solution.py:34
  150.1 2.6 collective-permute-start.17
  152.7 14.1 %shard_map.98 = (bf16[64,2048]{1,0:T(8,128)(2,1)}, bf16[64,2048]{1,0:T(8,128)(2,1)}, bf16[64,2048]{1,0:T(8,128)(2,1)}, bf16[64,2048]{1,0:T(8,128)(2,1)}, bf16[64...) custom-call(s32[2]{0:T(128)} %pad_add_fusion.1.place, ...), custom_call_target="tpu_custom_call" | custom-call | flops 6039797760 | bytes 16777216 | tf_op jit(solution)/shard_map/pallas_call | solution.py:171
  168.5 1.4 shard_map.99
  172.4 1.7 collective-permute-start.24
  174.1 1.5 collective-permute-start.25
  175.6 2.0 collective-permute-done.21.refs_6_
  177.5 1.9 collective-permute-done.22.refs_7_
  180.2 1.9 collective-permute-done.24.refs_4_
  182.8 5.0 %collective-permute-done.25.refs_5_ = bf16[64,2048]{1,0:T(8,128)(2,1)S(1)} collective-permute-done((bf16[64,2048]{1,0:T(8,128)(2,1)}, bf16[64,2048]{1,0:T(8,128)(2,1)S(1)}, u32[]{:S(2)}, u32[]{:S(2)}) %collective-permute-start.25) | collective-permute-done | bytes 262176 | tf_op jit(solution)/shard_map/ppermute | solution.py:34
  189.5 2.5 shard_map.100
  192.0 1.8 collective-permute-start.26
  194.3 2.8 %collective-permute-start.29 = (bf16[64,2048]{1,0:T(8,128)(2,1)}, bf16[64,2048]{1,0:T(8,128)(2,1)}, u32[]{:S(2)}, u32[]{:S(2)}) collective-permute-start(bf16[64,2048]{1,0:T(8,128)(2,1)} %get-tuple-element.124), channel_id=1, source_target_pairs={{0,2},{1,3},{2,0},{3,1},{4,6},{5,7},{6,4},{7,5},{8,10},{9,11},{10,... | collective-permute-start | bytes 786440 | tf_op jit(solution)/shard_map/ppermute | solution.py:34
  197.6 6.4 %collective-permute-done.29.refs_4_ = bf16[64,2048]{1,0:T(8,128)(2,1)} collective-permute-done((bf16[64,2048]{1,0:T(8,128)(2,1)}, bf16[64,2048]{1,0:T(8,128)(2,1)}, u32[]{:S(2)}, u32[]{:S(2)}) %collective-permute-start.29) | collective-permute-done | bytes 262176 | tf_op jit(solution)/shard_map/ppermute | solution.py:34
  204.0 5.8 %collective-permute-done.30.refs_5_ = bf16[64,2048]{1,0:T(8,128)(2,1)} collective-permute-done((bf16[64,2048]{1,0:T(8,128)(2,1)}, bf16[64,2048]{1,0:T(8,128)(2,1)}, u32[]{:S(2)}, u32[]{:S(2)}) %collective-permute-start.30) | collective-permute-done | bytes 262176 | tf_op jit(solution)/shard_map/ppermute | solution.py:34
  214.2 3.0 %collective-permute-start.32 = (bf16[128,2048]{1,0:T(8,128)(2,1)S(1)}, bf16[128,2048]{1,0:T(8,128)(2,1)S(1)}, u32[]{:S(2)}, u32[]{:S(2)}) collective-permute-start(bf16[128,2048]{1,0:T(8,128)(2,1)S(1)} %get-tuple-element.138), channel_id=1, source_target_pairs={{0,28},{4,0},{8,4},{12,8},{16,12},{20,16},{24,20},{28,24},{1,29},{... | collective-permute-start | bytes 1572872 | tf_op jit(solution)/shard_map/ppermute | solution.py:29
  219.0 2.8 %collective-permute-start.35 = (bf16[32,2048]{1,0:T(8,128)(2,1)S(1)}, bf16[32,2048]{1,0:T(8,128)(2,1)S(1)}, u32[]{:S(2)}, u32[]{:S(2)}) collective-permute-start(bf16[32,2048]{1,0:T(8,128)(2,1)S(1)} %copy-done.41), channel_id=1, source_target_pairs={{0,2},{1,3},{2,0},{3,1},{4,6},{5,7},{6,4},{7,5},{8,10},{9,11},{10,... | collective-permute-start | bytes 393224 | tf_op jit(solution)/shard_map/ppermute | solution.py:34
  221.8 3.4 %collective-permute-done.35.a2 = bf16[32,2048]{1,0:T(8,128)(2,1)S(1)} collective-permute-done((bf16[32,2048]{1,0:T(8,128)(2,1)S(1)}, bf16[32,2048]{1,0:T(8,128)(2,1)S(1)}, u32[]{:S(2)}, u32[]{:S(2)}) %collective-permute-start.35) | collective-permute-done | bytes 131104 | tf_op jit(solution)/shard_map/ppermute | solution.py:34
  225.2 3.9 %collective-permute-start.36 = (bf16[32,2048]{1,0:T(8,128)(2,1)S(1)}, bf16[32,2048]{1,0:T(8,128)(2,1)S(1)}, u32[]{:S(2)}, u32[]{:S(2)}) collective-permute-start(bf16[32,2048]{1,0:T(8,128)(2,1)S(1)} %copy-done.40), channel_id=1, source_target_pairs={{0,3},{1,2},{2,1},{3,0},{4,7},{5,6},{6,5},{7,4},{8,11},{9,10},{10,... | collective-permute-start | bytes 393224 | tf_op jit(solution)/shard_map/ppermute | solution.py:34
  229.1 4.1 %collective-permute-done.36.a3 = bf16[32,2048]{1,0:T(8,128)(2,1)S(1)} collective-permute-done((bf16[32,2048]{1,0:T(8,128)(2,1)S(1)}, bf16[32,2048]{1,0:T(8,128)(2,1)S(1)}, u32[]{:S(2)}, u32[]{:S(2)}) %collective-permute-start.36) | collective-permute-done | bytes 131104 | tf_op jit(solution)/shard_map/ppermute | solution.py:34
  233.9 2.1 shard_map.102
  236.0 3.0 %collective-permute-start.39 = (bf16[128,2048]{1,0:T(8,128)(2,1)S(1)}, bf16[128,2048]{1,0:T(8,128)(2,1)S(1)}, u32[]{:S(2)}, u32[]{:S(2)}) collective-permute-start(bf16[128,2048]{1,0:T(8,128)(2,1)S(1)} %get-tuple-element.154), channel_id=1, source_target_pairs={{0,28},{4,0},{8,4},{12,8},{16,12},{20,16},{24,20},{28,24},{1,29},{... | collective-permute-start | bytes 1572872 | tf_op jit(solution)/shard_map/ppermute | solution.py:29
  239.7 10.3 %collective-permute-done.39.left = bf16[128,2048]{1,0:T(8,128)(2,1)S(1)} collective-permute-done((bf16[128,2048]{1,0:T(8,128)(2,1)S(1)}, bf16[128,2048]{1,0:T(8,128)(2,1)S(1)}, u32[]{:S(2)}, u32[]{:S(2)}) %collective-permute-start.39) | collective-permute-done | bytes 524320 | tf_op jit(solution)/shard_map/ppermute | solution.py:29
  250.0 3.1 %collective-permute-done.40.right = bf16[128,2048]{1,0:T(8,128)(2,1)S(1)} collective-permute-done((bf16[128,2048]{1,0:T(8,128)(2,1)S(1)}, bf16[128,2048]{1,0:T(8,128)(2,1)S(1)}, u32[]{:S(2)}, u32[]{:S(2)}) %collective-permute-start.40) | collective-permute-done | bytes 524320 | tf_op jit(solution)/shard_map/ppermute | solution.py:29
  253.9 8.2 %shard_map.103 = (bf16[128,2048]{1,0:T(8,128)(2,1)}, bf16[128,1536]{1,0:T(8,128)(2,1)}) custom-call(s32[4]{0:T(128)} %pad_add_fusion.offsets, bf16[8,128,256]{2,1,0:T(8,128)(2,1)} %copy-done.1, bf16[32,2048]{1,0:T(8,128)(2,1)} %get-tuple-element.131.a0, bf16[32,2048]{1,0:T(8,128)(2,1)} %copy-done.37, bf16[32,2048]{1,0:T(8,128)(2,1)} %copy-done.38, ...), custom_call_target="tpu_custom_call" | custom-call | flops 805306368 | bytes 8388608 | tf_op jit(solution)/shard_map/pallas_call | solution.py:277
  (155 shorter events, 26.9 us)
Async XLA Ops:
  7.2 121.5 %all-gather.13.cloned.1.call-start = ((), (), s32[]{:S(2)}) async-start(), calls=%async_computation.4 | async-start | bytes 1966080 | tf_op jit(solution)/shard_map/all_gather | solution.py:315
  29.8 100.7 %all-to-all-start.1 = ((bf16[32,32,2048]{2,1,0:T(8,128)(2,1)}), bf16[32,32,2048]{2,1,0:T(8,128)(2,1)}, u32[]{:S(2)}, u32[]{:S(2)}) async-start(bf16[32,32,2048]{2,1,0:T(8,128)(2,1)} %bitcast.27), calls=%async_computation.1 | async-start | bytes 8388608 | tf_op jit(solution)/shard_map/all_to_all | solution.py:313
  36.4 92.3 %all-gather.15.cloned.1.call-start = ((), (), s32[]{:S(2)}) async-start(), calls=%async_computation.5 | async-start | bytes 1966080 | tf_op jit(solution)/shard_map/all_gather | solution.py:316
  37.2 91.6 %all-gather.17.cloned.1.call-start = ((), (), s32[]{:S(2)}) async-start(), calls=%async_computation.6 | async-start | bytes 1966080 | tf_op jit(solution)/shard_map/all_gather | solution.py:317
  37.9 159.6 %all-gather.9.cloned.1.call-start = ((), (), s32[]{:S(2)}) async-start(), calls=%async_computation.2 | async-start | bytes 1966080 | tf_op jit(solution)/shard_map/all_gather | solution.py:327
  38.8 171.0 %all-gather.11.cloned.1.call-start = ((), (), s32[]{:S(2)}) async-start(), calls=%async_computation.3 | async-start | bytes 1966080 | tf_op jit(solution)/shard_map/all_gather | solution.py:327
  38.9 29.0 %collective-permute-start.10 = (bf16[768,256]{1,0:T(8,128)(2,1)S(1)}, bf16[768,256]{1,0:T(8,128)(2,1)S(1)}, u32[]{:S(2)}, u32[]{:S(2)}) collective-permute-start(bf16[768,256]{1,0:T(8,128)(2,1)S(1)} %bitcast.36), channel_id=1, source_target_pairs={{0,128},{128,0},{1,129},{129,1},{2,130},{130,2},{3,131},{131,3},{4... | collective-permute-start | bytes 1179656 | tf_op jit(solution)/shard_map/ppermute | solution.py:34
  40.1 40.7 %collective-permute-start = (bf16[256,768]{1,0:T(8,128)(2,1)S(1)}, bf16[256,768]{1,0:T(8,128)(2,1)S(1)}, u32[]{:S(2)}, u32[]{:S(2)}) collective-permute-start(bf16[256,768]{1,0:T(8,128)(2,1)S(1)} %bitcast.34), channel_id=1, source_target_pairs={{0,128},{128,0},{1,129},{129,1},{2,130},{130,2},{3,131},{131,3},{4... | collective-permute-start | bytes 1179656 | tf_op jit(solution)/shard_map/ppermute | solution.py:34
  40.5 51.2 %collective-permute-start.5 = (bf16[256,768]{1,0:T(8,128)(2,1)S(1)}, bf16[256,768]{1,0:T(8,128)(2,1)S(1)}, u32[]{:S(2)}, u32[]{:S(2)}) collective-permute-start(bf16[256,768]{1,0:T(8,128)(2,1)S(1)} %bitcast.35), channel_id=1, source_target_pairs={{0,128},{128,0},{1,129},{129,1},{2,130},{130,2},{3,131},{131,3},{4... | collective-permute-start | bytes 1179656 | tf_op jit(solution)/shard_map/ppermute | solution.py:34
  67.9 25.1 %collective-permute-start.11 = (bf16[768,256]{1,0:T(8,128)(2,1)S(1)}, bf16[768,256]{1,0:T(8,128)(2,1)S(1)}, u32[]{:S(2)}, u32[]{:S(2)}) collective-permute-start(bf16[768,256]{1,0:T(8,128)(2,1)S(1)} %collective-permute-done.10.refs_14_), channel_id=1, source_target_pairs={{0,32},{32,64},{64,96},{96,0},{1,33},{33,65},{65,97},{97,1},{2,34}... | collective-permute-start | bytes 1179656 | tf_op jit(solution)/shard_map/ppermute | solution.py:29
  69.2 25.3 %collective-permute-start.12 = (bf16[768,256]{1,0:T(8,128)(2,1)S(1)}, bf16[768,256]{1,0:T(8,128)(2,1)S(1)}, u32[]{:S(2)}, u32[]{:S(2)}) collective-permute-start(bf16[768,256]{1,0:T(8,128)(2,1)S(1)} %collective-permute-done.10.refs_14_), channel_id=1, source_target_pairs={{0,96},{32,0},{64,32},{96,64},{1,97},{33,1},{65,33},{97,65},{2,98}... | collective-permute-start | bytes 1179656 | tf_op jit(solution)/shard_map/ppermute | solution.py:29
  80.8 14.5 %collective-permute-start.1 = (bf16[256,768]{1,0:T(8,128)(2,1)S(1)}, bf16[256,768]{1,0:T(8,128)(2,1)S(1)}, u32[]{:S(2)}, u32[]{:S(2)}) collective-permute-start(bf16[256,768]{1,0:T(8,128)(2,1)S(1)} %collective-permute-done.refs_2_), channel_id=1, source_target_pairs={{0,32},{32,64},{64,96},{96,0},{1,33},{33,65},{65,97},{97,1},{2,34}... | collective-permute-start | bytes 1179656 | tf_op jit(solution)/shard_map/ppermute | solution.py:29
  82.1 15.3 %collective-permute-start.2 = (bf16[256,768]{1,0:T(8,128)(2,1)S(1)}, bf16[256,768]{1,0:T(8,128)(2,1)S(1)}, u32[]{:S(2)}, u32[]{:S(2)}) collective-permute-start(bf16[256,768]{1,0:T(8,128)(2,1)S(1)} %collective-permute-done.refs_2_), channel_id=1, source_target_pairs={{0,96},{32,0},{64,32},{96,64},{1,97},{33,1},{65,33},{97,65},{2,98}... | collective-permute-start | bytes 1179656 | tf_op jit(solution)/shard_map/ppermute | solution.py:29
  91.7 17.3 %collective-permute-start.6 = (bf16[256,768]{1,0:T(8,128)(2,1)S(1)}, bf16[256,768]{1,0:T(8,128)(2,1)S(1)}, u32[]{:S(2)}, u32[]{:S(2)}) collective-permute-start(bf16[256,768]{1,0:T(8,128)(2,1)S(1)} %collective-permute-done.5.refs_8_), channel_id=1, source_target_pairs={{0,32},{32,64},{64,96},{96,0},{1,33},{33,65},{65,97},{97,1},{2,34}... | collective-permute-start | bytes 1179656 | tf_op jit(solution)/shard_map/ppermute | solution.py:29
  93.0 18.8 %collective-permute-start.7 = (bf16[256,768]{1,0:T(8,128)(2,1)S(1)}, bf16[256,768]{1,0:T(8,128)(2,1)S(1)}, u32[]{:S(2)}, u32[]{:S(2)}) collective-permute-start(bf16[256,768]{1,0:T(8,128)(2,1)S(1)} %collective-permute-done.5.refs_8_), channel_id=1, source_target_pairs={{0,96},{32,0},{64,32},{96,64},{1,97},{33,1},{65,33},{97,65},{2,98}... | collective-permute-start | bytes 1179656 | tf_op jit(solution)/shard_map/ppermute | solution.py:29
  94.5 21.6 %collective-permute-start.13 = (bf16[384,256]{1,0:T(8,128)(2,1)S(1)}, bf16[384,256]{1,0:T(8,128)(2,1)S(1)}, u32[]{:S(2)}, u32[]{:S(2)}) collective-permute-start(bf16[384,256]{1,0:T(8,128)(2,1)S(1)} %slice.28), channel_id=1, source_target_pairs={{0,32},{32,64},{64,96},{96,0},{1,33},{33,65},{65,97},{97,1},{2,34}... | collective-permute-start | bytes 589832 | tf_op jit(solution)/shard_map/ppermute | solution.py:29
  95.3 24.3 %collective-permute-start.14 = (bf16[384,256]{1,0:T(8,128)(2,1)S(1)}, bf16[384,256]{1,0:T(8,128)(2,1)S(1)}, u32[]{:S(2)}, u32[]{:S(2)}) collective-permute-start(bf16[384,256]{1,0:T(8,128)(2,1)S(1)} %slice.29), channel_id=1, source_target_pairs={{0,96},{32,0},{64,32},{96,64},{1,97},{33,1},{65,33},{97,65},{2,98}... | collective-permute-start | bytes 589832 | tf_op jit(solution)/shard_map/ppermute | solution.py:29
  97.4 26.7 %collective-permute-start.3 = (bf16[128,768]{1,0:T(8,128)(2,1)S(1)}, bf16[128,768]{1,0:T(8,128)(2,1)}, u32[]{:S(2)}, u32[]{:S(2)}) collective-permute-start(bf16[128,768]{1,0:T(8,128)(2,1)S(1)} %slice.24), channel_id=1, source_target_pairs={{0,32},{32,64},{64,96},{96,0},{1,33},{33,65},{65,97},{97,1},{2,34}... | collective-permute-start | bytes 589832 | tf_op jit(solution)/shard_map/ppermute | solution.py:29
  108.9 15.2 %collective-permute-start.4 = (bf16[128,768]{1,0:T(8,128)(2,1)S(1)}, bf16[128,768]{1,0:T(8,128)(2,1)}, u32[]{:S(2)}, u32[]{:S(2)}) collective-permute-start(bf16[128,768]{1,0:T(8,128)(2,1)S(1)} %slice.25), channel_id=1, source_target_pairs={{0,96},{32,0},{64,32},{96,64},{1,97},{33,1},{65,33},{97,65},{2,98}... | collective-permute-start | bytes 589832 | tf_op jit(solution)/shard_map/ppermute | solution.py:29
  111.7 17.0 %collective-permute-start.8 = (bf16[128,768]{1,0:T(8,128)(2,1)S(1)}, bf16[128,768]{1,0:T(8,128)(2,1)}, u32[]{:S(2)}, u32[]{:S(2)}) collective-permute-start(bf16[128,768]{1,0:T(8,128)(2,1)S(1)} %slice.26), channel_id=1, source_target_pairs={{0,32},{32,64},{64,96},{96,0},{1,33},{33,65},{65,97},{97,1},{2,34}... | collective-permute-start | bytes 589832 | tf_op jit(solution)/shard_map/ppermute | solution.py:29
  116.2 12.5 %collective-permute-start.9 = (bf16[128,768]{1,0:T(8,128)(2,1)S(1)}, bf16[128,768]{1,0:T(8,128)(2,1)S(1)}, u32[]{:S(2)}, u32[]{:S(2)}) collective-permute-start(bf16[128,768]{1,0:T(8,128)(2,1)S(1)} %slice.27), channel_id=1, source_target_pairs={{0,96},{32,0},{64,32},{96,64},{1,97},{33,1},{65,33},{97,65},{2,98}... | collective-permute-start | bytes 589832 | tf_op jit(solution)/shard_map/ppermute | solution.py:29
  119.6 21.8 %collective-permute-start.31 = (bf16[192,1024]{1,0:T(8,128)(2,1)S(1)}, bf16[192,1024]{1,0:T(8,128)(2,1)}, u32[]{:S(2)}, u32[]{:S(2)}) collective-permute-start(bf16[192,1024]{1,0:T(8,128)(2,1)S(1)} %copy-done.17), channel_id=1, source_target_pairs={{0,128},{128,0},{1,129},{129,1},{2,130},{130,2},{3,131},{131,3},{4... | collective-permute-start | bytes 1179656 | tf_op jit(solution)/shard_map/ppermute | solution.py:34
  141.5 7.9 %collective-permute-start.15 = (bf16[32,2048]{1,0:T(8,128)(2,1)}, bf16[32,2048]{1,0:T(8,128)(2,1)S(1)}, u32[]{:S(2)}, u32[]{:S(2)}) collective-permute-start(bf16[32,2048]{1,0:T(8,128)(2,1)} %get-tuple-element.85), channel_id=1, source_target_pairs={{0,1},{1,0},{2,3},{3,2},{4,5},{5,4},{6,7},{7,6},{8,9},{9,8},{10,11... | collective-permute-start | bytes 393224 | tf_op jit(solution)/shard_map/ppermute | solution.py:34
  145.3 88.6 %copy-start.1 = (bf16[8,128,256]{2,1,0:T(8,128)(2,1)}, bf16[8,128,256]{2,1,0:T(8,128)(2,1)S(1)}, u32[]{:S(2)}) copy-start(bf16[8,128,256]{2,1,0:T(8,128)(2,1)S(1)} %shard_map.96.refs_0_.refs_1_.weight) | copy-start | bytes 1572868
  145.3 21.5 %collective-permute-start.18 = (bf16[64,2048]{1,0:T(8,128)(2,1)}, bf16[64,2048]{1,0:T(8,128)(2,1)S(1)}, u32[]{:S(2)}, u32[]{:S(2)}) collective-permute-start(bf16[64,2048]{1,0:T(8,128)(2,1)} %get-tuple-element.88), channel_id=1, source_target_pairs={{0,1},{1,0},{2,3},{3,2},{4,5},{5,4},{6,7},{7,6},{8,9},{9,8},{10,11... | collective-permute-start | bytes 786440 | tf_op jit(solution)/shard_map/ppermute | solution.py:34
  145.4 22.1 %collective-permute-start.19 = (bf16[64,2048]{1,0:T(8,128)(2,1)}, bf16[64,2048]{1,0:T(8,128)(2,1)}, u32[]{:S(2)}, u32[]{:S(2)}) collective-permute-start(bf16[64,2048]{1,0:T(8,128)(2,1)} %get-tuple-element.89), channel_id=1, source_target_pairs={{0,2},{1,3},{2,0},{3,1},{4,6},{5,7},{6,4},{7,5},{8,10},{9,11},{10,... | collective-permute-start | bytes 786440 | tf_op jit(solution)/shard_map/ppermute | solution.py:34
  145.8 21.7 %collective-permute-start.20 = (bf16[64,2048]{1,0:T(8,128)(2,1)}, bf16[64,2048]{1,0:T(8,128)(2,1)}, u32[]{:S(2)}, u32[]{:S(2)}) collective-permute-start(bf16[64,2048]{1,0:T(8,128)(2,1)} %get-tuple-element.90), channel_id=1, source_target_pairs={{0,3},{1,2},{2,1},{3,0},{4,7},{5,6},{6,5},{7,4},{8,11},{9,10},{10,... | collective-permute-start | bytes 786440 | tf_op jit(solution)/shard_map/ppermute | solution.py:34
  149.0 17.8 %collective-permute-start.16 = (bf16[32,2048]{1,0:T(8,128)(2,1)}, bf16[32,2048]{1,0:T(8,128)(2,1)}, u32[]{:S(2)}, u32[]{:S(2)}) collective-permute-start(bf16[32,2048]{1,0:T(8,128)(2,1)} %get-tuple-element.86), channel_id=1, source_target_pairs={{0,2},{1,3},{2,0},{3,1},{4,6},{5,7},{6,4},{7,5},{8,10},{9,11},{10,... | collective-permute-start | bytes 393224 | tf_op jit(solution)/shard_map/ppermute | solution.py:34
  150.1 16.8 %collective-permute-start.17 = (bf16[32,2048]{1,0:T(8,128)(2,1)}, bf16[32,2048]{1,0:T(8,128)(2,1)}, u32[]{:S(2)}, u32[]{:S(2)}) collective-permute-start(bf16[32,2048]{1,0:T(8,128)(2,1)} %get-tuple-element.87), channel_id=1, source_target_pairs={{0,3},{1,2},{2,1},{3,0},{4,7},{5,6},{6,5},{7,4},{8,11},{9,10},{10,... | collective-permute-start | bytes 393224 | tf_op jit(solution)/shard_map/ppermute | solution.py:34
  169.9 7.6 %collective-permute-start.21 = (bf16[64,2048]{1,0:T(8,128)(2,1)S(1)}, bf16[64,2048]{1,0:T(8,128)(2,1)S(1)}, u32[]{:S(2)}, u32[]{:S(2)}) collective-permute-start(bf16[64,2048]{1,0:T(8,128)(2,1)S(1)} %get-tuple-element.110), channel_id=1, source_target_pairs={{0,28},{4,0},{8,4},{12,8},{16,12},{20,16},{24,20},{28,24},{1,29},{... | collective-permute-start | bytes 786440 | tf_op jit(solution)/shard_map/ppermute | solution.py:29
  170.8 8.7 %collective-permute-start.22 = (bf16[64,2048]{1,0:T(8,128)(2,1)S(1)}, bf16[64,2048]{1,0:T(8,128)(2,1)S(1)}, u32[]{:S(2)}, u32[]{:S(2)}) collective-permute-start(bf16[64,2048]{1,0:T(8,128)(2,1)S(1)} %get-tuple-element.111), channel_id=1, source_target_pairs={{0,4},{4,8},{8,12},{12,16},{16,20},{20,24},{24,28},{28,0},{1,5},{5... | collective-permute-start | bytes 786440 | tf_op jit(solution)/shard_map/ppermute | solution.py:29
  171.4 8.0 %collective-permute-start.23 = (bf16[64,2048]{1,0:T(8,128)(2,1)}, bf16[64,2048]{1,0:T(8,128)(2,1)S(1)}, u32[]{:S(2)}, u32[]{:S(2)}) collective-permute-start(bf16[64,2048]{1,0:T(8,128)(2,1)} %get-tuple-element.112), channel_id=1, source_target_pairs={{0,1},{1,0},{2,3},{3,2},{4,5},{5,4},{6,7},{7,6},{8,9},{9,8},{10,11... | collective-permute-start | bytes 786440 | tf_op jit(solution)/shard_map/ppermute | solution.py:34
  172.4 9.7 %collective-permute-start.24 = (bf16[64,2048]{1,0:T(8,128)(2,1)}, bf16[64,2048]{1,0:T(8,128)(2,1)S(1)}, u32[]{:S(2)}, u32[]{:S(2)}) collective-permute-start(bf16[64,2048]{1,0:T(8,128)(2,1)} %get-tuple-element.113), channel_id=1, source_target_pairs={{0,2},{1,3},{2,0},{3,1},{4,6},{5,7},{6,4},{7,5},{8,10},{9,11},{10,... | collective-permute-start | bytes 786440 | tf_op jit(solution)/shard_map/ppermute | solution.py:34
  174.1 13.7 %collective-permute-start.25 = (bf16[64,2048]{1,0:T(8,128)(2,1)}, bf16[64,2048]{1,0:T(8,128)(2,1)S(1)}, u32[]{:S(2)}, u32[]{:S(2)}) collective-permute-start(bf16[64,2048]{1,0:T(8,128)(2,1)} %get-tuple-element.114), channel_id=1, source_target_pairs={{0,3},{1,2},{2,1},{3,0},{4,7},{5,6},{6,5},{7,4},{8,11},{9,10},{10,... | collective-permute-start | bytes 786440 | tf_op jit(solution)/shard_map/ppermute | solution.py:34
  192.0 17.8 %collective-permute-start.26 = (bf16[128,2048]{1,0:T(8,128)(2,1)}, bf16[128,2048]{1,0:T(8,128)(2,1)S(1)}, u32[]{:S(2)}, u32[]{:S(2)}) collective-permute-start(bf16[128,2048]{1,0:T(8,128)(2,1)} %get-tuple-element.121), channel_id=1, source_target_pairs={{0,28},{4,0},{8,4},{12,8},{16,12},{20,16},{24,20},{28,24},{1,29},{... | collective-permute-start | bytes 1572872 | tf_op jit(solution)/shard_map/ppermute | solution.py:29
  193.8 16.0 %collective-permute-start.27 = (bf16[128,2048]{1,0:T(8,128)(2,1)}, bf16[128,2048]{1,0:T(8,128)(2,1)S(1)}, u32[]{:S(2)}, u32[]{:S(2)}) collective-permute-start(bf16[128,2048]{1,0:T(8,128)(2,1)} %get-tuple-element.122), channel_id=1, source_target_pairs={{0,4},{4,8},{8,12},{12,16},{16,20},{20,24},{24,28},{28,0},{1,5},{5... | collective-permute-start | bytes 1572872 | tf_op jit(solution)/shard_map/ppermute | solution.py:29
  193.8 3.8 %collective-permute-start.28 = (bf16[64,2048]{1,0:T(8,128)(2,1)}, bf16[64,2048]{1,0:T(8,128)(2,1)S(1)}, u32[]{:S(2)}, u32[]{:S(2)}) collective-permute-start(bf16[64,2048]{1,0:T(8,128)(2,1)} %get-tuple-element.123), channel_id=1, source_target_pairs={{0,1},{1,0},{2,3},{3,2},{4,5},{5,4},{6,7},{7,6},{8,9},{9,8},{10,11... | collective-permute-start | bytes 786440 | tf_op jit(solution)/shard_map/ppermute | solution.py:34
  194.3 9.7 %collective-permute-start.29 = (bf16[64,2048]{1,0:T(8,128)(2,1)}, bf16[64,2048]{1,0:T(8,128)(2,1)}, u32[]{:S(2)}, u32[]{:S(2)}) collective-permute-start(bf16[64,2048]{1,0:T(8,128)(2,1)} %get-tuple-element.124), channel_id=1, source_target_pairs={{0,2},{1,3},{2,0},{3,1},{4,6},{5,7},{6,4},{7,5},{8,10},{9,11},{10,... | collective-permute-start | bytes 786440 | tf_op jit(solution)/shard_map/ppermute | solution.py:34
  197.2 12.6 %collective-permute-start.30 = (bf16[64,2048]{1,0:T(8,128)(2,1)}, bf16[64,2048]{1,0:T(8,128)(2,1)}, u32[]{:S(2)}, u32[]{:S(2)}) collective-permute-start(bf16[64,2048]{1,0:T(8,128)(2,1)} %get-tuple-element.125), channel_id=1, source_target_pairs={{0,3},{1,2},{2,1},{3,0},{4,7},{5,6},{6,5},{7,4},{8,11},{9,10},{10,... | collective-permute-start | bytes 786440 | tf_op jit(solution)/shard_map/ppermute | solution.py:34
  209.8 23.4 %collective-permute-start.37 = (bf16[768,1024]{1,0:T(8,128)(2,1)}, bf16[768,1024]{1,0:T(8,128)(2,1)S(1)}, u32[]{:S(2)}, u32[]{:S(2)}) collective-permute-start(bf16[768,1024]{1,0:T(8,128)(2,1)} %all-gather.9.cloned.1.call-done.q0), channel_id=1, source_target_pairs={{0,1},{1,0},{2,3},{3,2},{4,5},{5,4},{6,7},{7,6},{8,9},{9,8},{10,11... | collective-permute-start | bytes 4718600 | tf_op jit(solution)/shard_map/ppermute | solution.py:34
  210.1 23.7 %collective-permute-start.38 = (bf16[768,1024]{1,0:T(8,128)(2,1)}, bf16[768,1024]{1,0:T(8,128)(2,1)S(1)}, u32[]{:S(2)}, u32[]{:S(2)}) collective-permute-start(bf16[768,1024]{1,0:T(8,128)(2,1)} %all-gather.11.cloned.1.call-done.q1), channel_id=1, source_target_pairs={{0,1},{1,0},{2,3},{3,2},{4,5},{5,4},{6,7},{7,6},{8,9},{9,8},{10,11... | collective-permute-start | bytes 4718600 | tf_op jit(solution)/shard_map/ppermute | solution.py:34
  214.2 19.0 %collective-permute-start.32 = (bf16[128,2048]{1,0:T(8,128)(2,1)S(1)}, bf16[128,2048]{1,0:T(8,128)(2,1)S(1)}, u32[]{:S(2)}, u32[]{:S(2)}) collective-permute-start(bf16[128,2048]{1,0:T(8,128)(2,1)S(1)} %get-tuple-element.138), channel_id=1, source_target_pairs={{0,28},{4,0},{8,4},{12,8},{16,12},{20,16},{24,20},{28,24},{1,29},{... | collective-permute-start | bytes 1572872 | tf_op jit(solution)/shard_map/ppermute | solution.py:29
  217.2 16.0 %collective-permute-start.33 = (bf16[128,2048]{1,0:T(8,128)(2,1)S(1)}, bf16[128,2048]{1,0:T(8,128)(2,1)S(1)}, u32[]{:S(2)}, u32[]{:S(2)}) collective-permute-start(bf16[128,2048]{1,0:T(8,128)(2,1)S(1)} %get-tuple-element.139), channel_id=1, source_target_pairs={{0,4},{4,8},{8,12},{12,16},{16,20},{20,24},{24,28},{28,0},{1,5},{5... | collective-permute-start | bytes 1572872 | tf_op jit(solution)/shard_map/ppermute | solution.py:29
  217.2 1.8 collective-permute-start.34
  219.0 6.2 %collective-permute-start.35 = (bf16[32,2048]{1,0:T(8,128)(2,1)S(1)}, bf16[32,2048]{1,0:T(8,128)(2,1)S(1)}, u32[]{:S(2)}, u32[]{:S(2)}) collective-permute-start(bf16[32,2048]{1,0:T(8,128)(2,1)S(1)} %copy-done.41), channel_id=1, source_target_pairs={{0,2},{1,3},{2,0},{3,1},{4,6},{5,7},{6,4},{7,5},{8,10},{9,11},{10,... | collective-permute-start | bytes 393224 | tf_op jit(solution)/shard_map/ppermute | solution.py:34
  225.2 8.0 %collective-permute-start.36 = (bf16[32,2048]{1,0:T(8,128)(2,1)S(1)}, bf16[32,2048]{1,0:T(8,128)(2,1)S(1)}, u32[]{:S(2)}, u32[]{:S(2)}) collective-permute-start(bf16[32,2048]{1,0:T(8,128)(2,1)S(1)} %copy-done.40), channel_id=1, source_target_pairs={{0,3},{1,2},{2,1},{3,0},{4,7},{5,6},{6,5},{7,4},{8,11},{9,10},{10,... | collective-permute-start | bytes 393224 | tf_op jit(solution)/shard_map/ppermute | solution.py:34
  236.0 13.9 %collective-permute-start.39 = (bf16[128,2048]{1,0:T(8,128)(2,1)S(1)}, bf16[128,2048]{1,0:T(8,128)(2,1)S(1)}, u32[]{:S(2)}, u32[]{:S(2)}) collective-permute-start(bf16[128,2048]{1,0:T(8,128)(2,1)S(1)} %get-tuple-element.154), channel_id=1, source_target_pairs={{0,28},{4,0},{8,4},{12,8},{16,12},{20,16},{24,20},{28,24},{1,29},{... | collective-permute-start | bytes 1572872 | tf_op jit(solution)/shard_map/ppermute | solution.py:29
  239.1 14.0 %collective-permute-start.40 = (bf16[128,2048]{1,0:T(8,128)(2,1)S(1)}, bf16[128,2048]{1,0:T(8,128)(2,1)S(1)}, u32[]{:S(2)}, u32[]{:S(2)}) collective-permute-start(bf16[128,2048]{1,0:T(8,128)(2,1)S(1)} %get-tuple-element.155), channel_id=1, source_target_pairs={{0,4},{4,8},{8,12},{12,16},{16,20},{20,24},{24,28},{28,0},{1,5},{5... | collective-permute-start | bytes 1572872 | tf_op jit(solution)/shard_map/ppermute | solution.py:29
  (41 other events, 574.6 us)
Sparse Core Ops, SparseCore 0:
  9.8 32.8 all-gather.12
  44.6 30.1 all-gather.14
  76.6 49.6 all-gather.16
  128.0 29.5 all-gather.8
  159.2 29.1 all-gather.10
